TPU v7x, 512 devices: a whole 4x4x16 slice. The times are simulated.
512 devices in a mesh: chan: 4 (over x), filt: 32 (over z_hi, y, core), space: 4 (over z_lo).
Axes of the slice: x: 4, y: 4, z: 16 (z_hi: 4, z_lo: 4; z = z_hi * 4 + z_lo), core: 2. Of those that a mesh axis runs over, the one named last changes fastest.
Arguments:
- activations: bfloat16 [32, 32, 32, 512], P('filt', 'space', None, 'chan'), may hold values from -6 to 6
- weight: bfloat16 [27, 512, 512], P(None, 'chan', 'space'), may hold values from -0.0546875 to 0.0546875
- output_grad: bfloat16 [32, 32, 32, 512], P('filt', 'space', None, 'chan'), may hold values from -6 to 6
Outputs:
- output: bfloat16 [32, 32, 32, 512], P('filt', 'space', None, 'chan')
- input_grad: bfloat16 [32, 32, 32, 512], P('filt', 'space', None, 'chan')
- weight_grad: float32 [27, 512, 512], P(None, 'chan', 'space')
All inputs are finite; a program needn't handle non-finite values.
Results may differ from a plain program's by a relative error of at most 0.0011.
Values may be sent and summed in bfloat16 or wider, within the bound.
No kernel may reach another device: no remote copies, remote signals or barrier semaphores. Data moves between devices by JAX's collectives and lax.ppermute only.
A program may use at most 64 MiB of HBM per device.

v0:
```python
import math

import jax
import jax.numpy as jnp
from jax import lax
from jax.sharding import PartitionSpec as P

forward_specs = ("NWDHC", "WDHIO", "NWDHC")
backward_specs = ("NWDHC", "WDHOI", "NWDHC")
filter_specs = ("CWDHN", "IWDHO", "WDHNC")


def extended(block, sides, width):
    for axis, dim in sides:
        count = lax.axis_size(axis)
        forward = [(i, i + 1) for i in range(count - 1)]
        backward = [(target, source) for source, target in forward]
        low = lax.ppermute(
            lax.slice_in_dim(block, block.shape[dim] - width, None, axis=dim), axis, forward
        )
        high = lax.ppermute(lax.slice_in_dim(block, 0, width, axis=dim), axis, backward)
        block = jnp.concatenate([low, block, high], axis=dim)
    return block


def correlate(data, kernel, pads, specs):
    result = lax.conv_general_dilated(
        data[None],
        kernel,
        (1, 1, 1),
        pads,
        dimension_numbers=specs,
        preferred_element_type=jnp.float32,
    )
    return result[0]


def shards(activations, weight, output_grad):
    planes = activations.shape[1]
    all_blocks = lax.all_gather(weight, "space", axis=2, tiled=True)
    kernel = all_blocks.reshape(3, 3, 3, all_blocks.shape[1], all_blocks.shape[2])
    rimmed = extended(activations, (("filt", 0), ("space", 1)), 1)
    deep_column = lax.all_gather(rimmed[:, 1 : planes + 1], "space", axis=1, tiled=True)
    forward = correlate(rimmed, kernel, ((0, 0), (0, 0), (1, 1)), forward_specs)
    output = lax.psum_scatter(forward, "chan", scatter_dimension=3, tiled=True).astype(jnp.bfloat16)
    grad_rimmed = extended(output_grad, (("filt", 0), ("space", 1)), 1)
    grad_full = lax.all_gather(grad_rimmed, "chan", axis=3, tiled=True)
    flipped = jnp.flip(kernel, (0, 1, 2))
    input_grad = correlate(grad_full, flipped, ((0, 0), (0, 0), (1, 1)), backward_specs).astype(
        jnp.bfloat16
    )
    centre = grad_full[1:2, 1 : planes + 1]
    grad_deep = lax.all_to_all(centre, "space", split_axis=3, concat_axis=1, tiled=True)
    padded = jnp.pad(deep_column, ((0, 0), (1, 1), (1, 1), (0, 0)))
    local_sum = lax.conv_general_dilated(
        padded[None],
        grad_deep[None],
        (1, 1, 1),
        ((0, 0), (0, 0), (0, 0)),
        dimension_numbers=filter_specs,
        preferred_element_type=jnp.float32,
    )
    local_sum = local_sum.reshape(27, weight.shape[1], weight.shape[2])
    totals = lax.psum(local_sum, "filt")
    cell_count = (
        activations.shape[0] * lax.axis_size("filt") * deep_column.shape[1] * deep_column.shape[2]
    )
    weight_grad = totals / math.sqrt(cell_count)
    return (output, input_grad, weight_grad)


def solution(mesh):
    in_specs = (
        P("filt", "space", None, "chan"),
        P(None, "chan", "space"),
        P("filt", "space", None, "chan"),
    )
    out_specs = (
        P("filt", "space", None, "chan"),
        P("filt", "space", None, "chan"),
        P(None, "chan", "space"),
    )
    return jax.shard_map(shards, mesh=mesh, in_specs=in_specs, out_specs=out_specs, check_vma=False)
```

profile of v0, /device:TPU:1, one launch (start us, length us, event | category | flops | bytes accessed | tf_op | source)
XLA Modules:
  0.0 502.3 jit_solution(7896800465269733082)
XLA Ops:
  8.0 4.6 collective-permute-start.4
  12.6 5.5 %collective-permute-start.5 = (bf16[1,8,32,128]{3,2,1,0:T(8,128)(2,1)}, bf16[1,8,32,128]{3,2,1,0:T(8,128)(2,1)S(1)}, u32[]{:S(2)}, u32[]{:S(2)}) collective-permute-start(bf16[1,8,32,128]{3,2,1,0:T(8,128)(2,1)} %param.5), channel_id=1, source_target_pairs={{4,0},{8,4},{12,8},{16,12},{20,16},{24,20},{28,24},{32,28},{36,32}... | collective-permute-start | bytes 196616 | tf_op jit(solution)/shard_map/ppermute | solution.py:21
  18.1 0.0 collective-permute-done.4
  18.1 0.9 constant_dynamic-update-slice_fusion.4
  19.0 0.2 collective-permute-done.5
  19.2 2.8 collective-permute-start.6
  22.0 1.3 collective-permute-start.7
  23.3 2.3 collective-permute-start
  25.5 0.0 collective-permute-done.6
  25.6 1.2 collective-permute-done.7
  26.8 20.6 %all_gather.10 = bf16[3,10,32,512]{3,2,1,0:T(8,128)(2,1)S(1)} all-gather(bf16[3,10,32,128]{3,2,1,0:T(8,128)(2,1)S(1)} %pad_maximum_fusion), channel_id=1, replica_groups=mesh['chan'=4,'filt'=32,'space'=4] {'chan'}, dimensions={3}, use_global_device_ids=true | all-gather | bytes 1228800 | tf_op jit(solution)/shard_map/all_gather | solution.py:47
  47.4 0.0 copy-start
  47.4 1.0 copy-done
  48.4 0.0 copy-start.4
  48.4 0.8 copy.50
  49.2 1.7 reshape.56
  50.8 4.9 all-to-all-start
  55.7 0.0 all-gather.2.cloned.1.call-start
  55.7 0.0 copy-done.4
  55.7 2.9 collective-permute-start.1
  58.7 0.0 all-gather.2.cloned.1.call-update
  58.7 0.0 all-reduce.3.cloned.1.call-start
  58.8 0.0 collective-permute-done
  58.8 3.3 collective-permute-done.1
  62.1 0.0 copy-start.2
  62.1 0.7 copy-done.2
  62.8 18.7 %all_gather.11 = bf16[3,32,32,128]{3,2,1,0:T(8,128)(2,1)S(1)} all-gather(bf16[3,8,32,128]{3,2,1,0:T(8,128)(2,1)S(1)} %constant_dynamic-update-slice_fusion), channel_id=1, replica_groups=mesh['chan'=4,'filt'=32,'space'=4] {'space'}, dimensions={1}, use_global_device_ids=true | all-gather | bytes 983040 | tf_op jit(solution)/shard_map/all_gather | solution.py:43
  81.5 0.3 pad_bitcast_fusion
  81.8 0.0 all-to-all-done
  81.8 0.5 reshape.57
  82.3 0.8 copy.57
  83.1 9.2 %fusion.1 = f32[3,3,3,128,128]{4,3,2,1,0:T(8,128)} fusion(bf16[1,3,34,34,128]{4,3,2,1,0:T(8,128)(2,1)S(1)} %pad_bitcast_fusion, bf16[1,1,32,32,128]{4,3,2,1,0:T(8,128)(2,1)S(1)} %bitcast.45), kind=kOutput, calls=%fused_computation.2 | convolution fusion | flops 905969664 | bytes 2919424 | tf_op jit(solution)/shard_map/conv_general_dilated | solution.py:55
  92.3 0.0 copy-start.3
  92.3 0.0 all-reduce.3.cloned.1.call-update
  92.3 0.0 copy-start.6
  92.3 0.0 reduce-scatter.2.cloned.1.call-start
  92.4 0.8 copy-done.3
  93.2 1.3 collective-permute-start.2
  94.5 1.5 collective-permute-start.3
  96.0 0.0 collective-permute-done.2
  96.0 6.4 %collective-permute-done.3 = bf16[3,1,32,128]{3,2,1,0:T(8,128)(2,1)S(1)} collective-permute-done((bf16[3,1,32,128]{3,2,1,0:T(8,128)(2,1)S(1)}, bf16[3,1,32,128]{3,2,1,0:T(8,128)(2,1)S(1)}, u32[]{:S(2)}, u32[]{:S(2)}) %collective-permute-start.3) | collective-permute-done | bytes 24608 | tf_op jit(solution)/shard_map/ppermute | solution.py:21
  102.4 0.1 pad.5
  102.5 0.1 reshape.30
  102.7 47.0 %all-gather.2.cloned.1.call-done = bf16[27,128,512]{2,1,0:T(8,128)(2,1)} async-done(((bf16[27,128,128]{2,1,0:T(8,128)(2,1)}), bf16[27,128,512]{2,1,0:T(8,128)(2,1)}) %all-gather.2.cloned.1.call-update) | async-done | bytes 3538960 | tf_op jit(solution)/shard_map/all_gather | solution.py:40
  149.7 0.0 copy-done.6
  149.7 3.3 convolution_select_fusion
  153.1 0.0 copy-start.1
  153.1 0.4 copy.46
  153.5 0.8 slice_bitcast_fusion
  154.3 0.0 reduce-scatter.2.cloned.1.call-update
  154.3 0.0 copy-done.1
  154.3 0.6 pad.7
  154.9 0.5 reshape.37
  155.4 0.6 copy.48
  156.0 0.1 slice.30
  156.1 330.9 %all-reduce.3.cloned.1.call-done = f32[27,128,128]{2,1,0:T(8,128)} async-done(((f32[27,128,128]{2,1,0:T(8,128)}), f32[27,128,128]{2,1,0:T(8,128)}) %all-reduce.3.cloned.1.call-update) | async-done | bytes 1769488 | tf_op jit(solution)/shard_map/psum | solution.py:64
  487.1 0.0 copy-start.5
  487.1 3.1 broadcast_multiply_fusion
  490.1 0.0 copy-done.5
  490.1 2.5 fusion.13
  492.6 0.6 copy.56
  493.3 0.0 reduce-scatter.2.cloned.1.call-done
  493.3 0.9 convert_element_type.19
  494.2 0.6 copy.55
  (15 shorter events, 0.3 us)
Async XLA Ops:
  8.0 10.1 %collective-permute-start.4 = (bf16[1,8,32,128]{3,2,1,0:T(8,128)(2,1)}, bf16[1,8,32,128]{3,2,1,0:T(8,128)(2,1)S(1)}, u32[]{:S(2)}, u32[]{:S(2)}) collective-permute-start(bf16[1,8,32,128]{3,2,1,0:T(8,128)(2,1)} %param.5), channel_id=1, source_target_pairs={{0,4},{4,8},{8,12},{12,16},{16,20},{20,24},{24,28},{28,32},{32,36}... | collective-permute-start | bytes 196616 | tf_op jit(solution)/shard_map/ppermute | solution.py:18
  12.6 6.6 %collective-permute-start.5 = (bf16[1,8,32,128]{3,2,1,0:T(8,128)(2,1)}, bf16[1,8,32,128]{3,2,1,0:T(8,128)(2,1)S(1)}, u32[]{:S(2)}, u32[]{:S(2)}) collective-permute-start(bf16[1,8,32,128]{3,2,1,0:T(8,128)(2,1)} %param.5), channel_id=1, source_target_pairs={{4,0},{8,4},{12,8},{16,12},{20,16},{24,20},{28,24},{32,28},{36,32}... | collective-permute-start | bytes 196616 | tf_op jit(solution)/shard_map/ppermute | solution.py:21
  19.2 6.3 %collective-permute-start.6 = (bf16[3,1,32,128]{3,2,1,0:T(8,128)(2,1)S(1)}, bf16[3,1,32,128]{3,2,1,0:T(8,128)(2,1)S(1)}, u32[]{:S(2)}, u32[]{:S(2)}) collective-permute-start(bf16[3,1,32,128]{3,2,1,0:T(8,128)(2,1)S(1)} %get-tuple-element.15), channel_id=1, source_target_pairs={{0,1},{1,2},{2,3},{4,5},{5,6},{6,7},{8,9},{9,10},{10,11},{12,13},{... | collective-permute-start | bytes 73736 | tf_op jit(solution)/shard_map/ppermute | solution.py:18
  22.0 4.8 collective-permute-start.7
  23.3 35.5 %collective-permute-start = (bf16[1,8,32,128]{3,2,1,0:T(8,128)(2,1)}, bf16[1,8,32,128]{3,2,1,0:T(8,128)(2,1)S(1)}, u32[]{:S(2)}, u32[]{:S(2)}) collective-permute-start(bf16[1,8,32,128]{3,2,1,0:T(8,128)(2,1)} %param.3), channel_id=1, source_target_pairs={{0,4},{4,8},{8,12},{12,16},{16,20},{20,24},{24,28},{28,32},{32,36}... | collective-permute-start | bytes 196616 | tf_op jit(solution)/shard_map/ppermute | solution.py:18
  47.4 1.0 copy-start
  48.4 7.4 %copy-start.4 = (bf16[1,8,32,128]{3,2,1,0:T(8,128)(2,1)S(1)}, bf16[1,8,32,128]{3,2,1,0:T(8,128)(2,1)}, u32[]{:S(2)}) copy-start(bf16[1,8,32,128]{3,2,1,0:T(8,128)(2,1)} %param.3) | copy-start | bytes 196612
  50.8 30.9 %all-to-all-start = ((bf16[4,2,16384]{2,1,0:T(2,128)(2,1)}), bf16[4,2,16384]{2,1,0:T(2,128)(2,1)S(1)}, u32[]{:S(2)}, u32[]{:S(2)}) async-start(bf16[4,2,16384]{2,1,0:T(2,128)(2,1)} %reshape.56), calls=%async_computation.1 | async-start | bytes 524288 | tf_op jit(solution)/shard_map/all_to_all | solution.py:53
  55.7 94.0 %all-gather.2.cloned.1.call-start = ((), (), s32[]{:S(2)}) async-start(), calls=%async_computation.2 | async-start | bytes 4423680 | tf_op jit(solution)/shard_map/all_gather | solution.py:40
  55.7 6.3 %collective-permute-start.1 = (bf16[1,8,32,128]{3,2,1,0:T(8,128)(2,1)S(1)}, bf16[1,8,32,128]{3,2,1,0:T(8,128)(2,1)S(1)}, u32[]{:S(2)}, u32[]{:S(2)}) collective-permute-start(bf16[1,8,32,128]{3,2,1,0:T(8,128)(2,1)S(1)} %copy-done.4), channel_id=1, source_target_pairs={{4,0},{8,4},{12,8},{16,12},{20,16},{24,20},{28,24},{32,28},{36,32}... | collective-permute-start | bytes 196616 | tf_op jit(solution)/shard_map/ppermute | solution.py:21
  58.7 428.4 %all-reduce.3.cloned.1.call-start = ((), (), s32[]{:S(2)}) async-start(), calls=%async_computation.4 | async-start | bytes 3538944 | tf_op jit(solution)/shard_map/psum | solution.py:64
  62.1 0.7 copy-start.2
  92.3 0.9 copy-start.3
  92.3 57.4 %copy-start.6 = (pred[8,5]{0,1:T(8,128)(4,1)S(1)}, pred[8,5]{0,1:T(8,128)(4,1)}, u32[]{:S(2)}) copy-start(pred[8,5]{0,1:T(8,128)(4,1)} %constant.18) | copy-start | bytes 124
  92.3 401.0 %reduce-scatter.2.cloned.1.call-start = ((), (), s32[]{:S(2)}) async-start(), calls=%async_computation.3 | async-start | bytes 655360 | tf_op jit(solution)/shard_map/reduce_scatter | solution.py:45
  93.2 2.8 collective-permute-start.2
  94.5 7.9 %collective-permute-start.3 = (bf16[3,1,32,128]{3,2,1,0:T(8,128)(2,1)S(1)}, bf16[3,1,32,128]{3,2,1,0:T(8,128)(2,1)S(1)}, u32[]{:S(2)}, u32[]{:S(2)}) collective-permute-start(bf16[3,1,32,128]{3,2,1,0:T(8,128)(2,1)S(1)} %get-tuple-element.18), channel_id=1, source_target_pairs={{1,0},{2,1},{3,2},{5,4},{6,5},{7,6},{9,8},{10,9},{11,10},{13,12},{... | collective-permute-start | bytes 73736 | tf_op jit(solution)/shard_map/ppermute | solution.py:21
  153.1 1.3 copy-start.1
  487.1 3.1 copy-start.5
Sparse Core Ops, SparseCore 0:
  58.8 90.8 all-gather.1
  154.4 31.0 reduce-scatter.1
Sparse Core Ops, SparseCore 1:
  92.4 394.6 all-reduce.2
where the time goes:
time: 505 us; the launch traced here: 502 us
  waiting for transfers between devices  389 us (77%)
  blocking collectives  39.3 us (8%)
  starting transfers between devices  27 us (5%)
  between operations  15.8 us (3%)
  matrix products  14.9 us (3%)
  local copies, waits for them, and re-layouts  12.1 us (2%)
    psum x1, waiting for transfers between devices, shards(): totals = lax.psum(local_sum, 'filt')  331 us
    all_gather x1, waiting for transfers between devices, shards(): all_blocks = lax.all_gather(weight, 'space', axis=2, tiled=True)  47 us
    all_gather x1, blocking collectives, shards(): grad_full = lax.all_gather(grad_rimmed, 'chan', axis=3, tiled=True)  20.6 us
    all_gather x1, blocking collectives, shards(): lax.all_gather(rimmed[:, 1:planes + 1], 'space', axis=1, tiled=True)  18.7 us
    ppermute x4, starting transfers between devices, extended(): lax.ppermute(lax.slice_in_dim(block, 0, width, axis=dim), axis, backward)  11.2 us
    ppermute x4, waiting for transfers between devices, extended(): lax.ppermute(lax.slice_in_dim(block, 0, width, axis=dim), axis, backward)  11.1 us
    ppermute x4, starting transfers between devices, extended(): lax.ppermute(lax.slice_in_dim(block, block.shape[dim] - width, None, axis...  10.9 us
  transfers between devices with their start and end apart: 12, of which 6 were waited for; matrix products, arithmetic and copies ran while one was open for 5% of the time, Pallas kernels for 0%

commit v1 on v0

v1 whole, which is shorter than its diff:
```python
import functools
import math

import jax
import jax.numpy as jnp
import numpy as np
from jax import lax
from jax.experimental import pallas as pl
from jax.experimental.pallas import tpu as pltpu
from jax.sharding import Mesh, PartitionSpec as P

AXES = ("chan", "zhi", "ring", "core", "space")
F32 = jnp.float32
BF16 = jnp.bfloat16
VMEM = pl.BlockSpec(memory_space=pltpu.VMEM)
SMEM = pl.BlockSpec(memory_space=pltpu.SMEM)


def permutation(sizes, move):
    pairs = []
    for source in range(math.prod(sizes)):
        target = move(*(int(v) for v in np.unravel_index(source, sizes)))
        if target is not None:
            pairs.append((source, int(np.ravel_multi_index(target, sizes))))
    return pairs


def column_move(sizes, step, swap):
    _, zhis, rings, cores, _ = sizes

    def move(chan, zhi, ring, core, space):
        column = (zhi * rings + ring) * cores + core + step
        if not 0 <= column < zhis * rings * cores:
            return None
        rest = (column // (rings * cores), column // cores % rings, column % cores)
        return (space, *rest, chan) if swap else (chan, *rest, space)

    return permutation(sizes, move)


def height_mask(rows, height, at):
    return lax.broadcasted_iota(jnp.int32, (rows, 128), 0) % height == at


def shifted(value, height, step):
    rows = value.shape[0]
    edge = 0 if step < 0 else height - 1
    rolled = pltpu.roll(value, (-step) % rows, 0)
    return jnp.where(height_mask(rows, height, edge), 0.0, rolled)


def fill_padded(padded, block):
    columns, planes, height, lanes = block.shape
    zero = jnp.zeros((columns, 1, height, lanes), BF16)
    padded[:, 0:1] = zero
    padded[:, planes + 1 : planes + 2] = zero
    padded[:, 1 : planes + 1] = block[...]


def conv_kernel(backward, block, weight, out, padded, flat):
    slabs, rows, lanes = out.shape
    height = block.shape[2]
    planes = rows // height
    fill_padded(padded, block)
    for cell in range(9):
        for r in range(3):
            if backward:
                flat[r * lanes : (r + 1) * lanes, cell * lanes : (cell + 1) * lanes] = weight[3 * cell + r]
            else:
                flat[cell * lanes : (cell + 1) * lanes, r * lanes : (r + 1) * lanes] = weight[3 * cell + r]
    for slab in range(slabs):
        pieces = []
        for p in range(3):
            for q in range(3):
                column, plane = (2 - p, 2 - q) if backward else (p, q)
                start = slab * planes + plane
                pieces.append(padded[column, start : start + planes].reshape(rows, lanes))
        lhs = jnp.concatenate(pieces, axis=1)
        dims = (((1,), (1 if backward else 0,)), ((), ()))
        taps = lax.dot_general(lhs, flat[...], dims, preferred_element_type=F32)
        low, high = (2, 0) if backward else (0, 2)
        total = taps[:, lanes : 2 * lanes]
        total += shifted(taps[:, low * lanes : (low + 1) * lanes], height, -1)
        total += shifted(taps[:, high * lanes : (high + 1) * lanes], height, 1)
        out[slab] = total


def convolve(backward, block, weight, slabs):
    columns, planes, height, lanes = block.shape
    rows = planes * height
    flat = (3 * lanes, 9 * lanes) if backward else (9 * lanes, 3 * lanes)
    return pl.pallas_call(
        functools.partial(conv_kernel, backward),
        out_shape=jax.ShapeDtypeStruct((slabs, rows // slabs, lanes), F32),
        in_specs=[VMEM, VMEM],
        out_specs=VMEM,
        scratch_shapes=[
            pltpu.VMEM((columns, planes + 2, height, lanes), BF16),
            pltpu.VMEM(flat, BF16),
        ],
        compiler_params=pltpu.CompilerParams(vmem_limit_bytes=40 << 20),
        cost_estimate=pl.CostEstimate(
            flops=2 * 27 * rows * lanes * lanes, bytes_accessed=3 << 20, transcendentals=0
        ),
        name="input_grad" if backward else "forward",
    )(block, weight)


def filter_kernel(core, data, grad, keep, send, padded, turned, taps):
    planes, height, lanes = data.shape
    rows = planes * height
    fill_padded(padded, grad)
    flat = data[...].reshape(rows, lanes).astype(F32)
    turned[0:lanes] = shifted(flat, height, -1).T.astype(BF16)
    turned[lanes : 2 * lanes] = flat.T.astype(BF16)
    turned[2 * lanes : 3 * lanes] = shifted(flat, height, 1).T.astype(BF16)
    for p in range(3):
        pieces = [padded[2 - p, 2 - q : 2 - q + planes].reshape(rows, lanes) for q in range(3)]
        rhs = jnp.concatenate(pieces, axis=1)
        result = jnp.dot(turned[...], rhs, preferred_element_type=F32)
        for q in range(3):
            for r in range(3):
                tap = 9 * p + 3 * q + r
                taps[tap * lanes : (tap + 1) * lanes] = result[
                    r * lanes : (r + 1) * lanes, q * lanes : (q + 1) * lanes
                ]
    taps[27 * lanes :] = jnp.zeros((lanes, lanes), F32)
    half = keep.shape[0]

    @pl.when(core[0] == 0)
    def _():
        keep[...] = taps[0:half]
        send[...] = taps[half : 2 * half]

    @pl.when(core[0] == 1)
    def _():
        keep[...] = taps[half : 2 * half]
        send[...] = taps[0:half]


def filter_partial(data, grad, core):
    planes, height, lanes = data.shape
    rows = planes * height
    half = jax.ShapeDtypeStruct((14 * lanes, lanes), F32)
    return pl.pallas_call(
        filter_kernel,
        out_shape=(half, half),
        in_specs=[SMEM, VMEM, VMEM],
        out_specs=(VMEM, VMEM),
        scratch_shapes=[
            pltpu.VMEM((3, planes + 2, height, lanes), BF16),
            pltpu.VMEM((3 * lanes, rows), BF16),
            pltpu.VMEM((28 * lanes, lanes), F32),
        ],
        compiler_params=pltpu.CompilerParams(vmem_limit_bytes=40 << 20),
        cost_estimate=pl.CostEstimate(
            flops=2 * 27 * rows * lanes * lanes, bytes_accessed=3 << 20, transcendentals=0
        ),
        name="filter_grad",
    )(core, data, grad)


def exchange(block, axis):
    return lax.all_to_all(block, axis, split_axis=0, concat_axis=0, tiled=True)


def shards(sizes, activations, weight, output_grad):
    _, zhis, rings, cores, spaces = sizes
    act_low = lax.ppermute(activations, AXES, column_move(sizes, 1, False))
    act_high = lax.ppermute(activations, AXES, column_move(sizes, -1, False))
    grad_low = lax.ppermute(output_grad, AXES, column_move(sizes, 1, True))
    grad_mid = lax.ppermute(output_grad, AXES, column_move(sizes, 0, True))
    grad_high = lax.ppermute(output_grad, AXES, column_move(sizes, -1, True))
    grad = jnp.concatenate([grad_low, grad_mid, grad_high], axis=0)
    grad = lax.all_gather(grad, "chan", axis=1, tiled=True)
    data = jnp.concatenate([act_low, activations, act_high], axis=0)
    data = lax.all_gather(data, "space", axis=1, tiled=True)
    lanes = activations.shape[3]
    core = lax.axis_index("core").reshape(1)

    keep, send = filter_partial(data[1], grad, core)
    half = keep + lax.ppermute(send, "core", [(0, 1), (1, 0)])
    quarter = exchange(half.reshape(rings, -1, lanes), "ring").sum(0)
    part = exchange(quarter.reshape(zhis, -1, lanes), "zhi").sum(0)
    cell_count = sizes[1] * rings * cores * grad.shape[1] * grad.shape[2]
    part = part / math.sqrt(cell_count)
    quarter = lax.all_gather(part, "zhi", axis=0, tiled=True)
    half = lax.all_gather(quarter, "ring", axis=0, tiled=True)
    other = lax.ppermute(half, "core", [(0, 1), (1, 0)])
    first = core[0] == 0
    low = jnp.where(first, half, other)
    high = jnp.where(first, other, half)
    taps = weight.shape[0]
    filter_grad = jnp.concatenate([low, high[: taps * lanes - low.shape[0]]], axis=0)
    filter_grad = filter_grad.reshape(weight.shape)

    forward = exchange(convolve(False, data, weight, spaces), "chan").sum(0).astype(BF16)
    output = lax.ppermute(forward, AXES, column_move(sizes, 0, True)).reshape(activations.shape)
    back = exchange(convolve(True, grad, weight, spaces), "space").sum(0).astype(BF16)
    input_grad = back.reshape(activations.shape)
    return output, input_grad, filter_grad


def solution(mesh):
    chans, filts, spaces = (mesh.shape[name] for name in ("chan", "filt", "space"))
    sizes = (chans, filts // 8, 4, 2, spaces)
    fine = Mesh(mesh.devices.reshape(sizes), AXES)
    cells = P(("zhi", "ring", "core"), "space", None, "chan")
    filters = P(None, "chan", "space")
    return jax.shard_map(
        functools.partial(shards, sizes),
        mesh=fine,
        in_specs=(cells, filters, cells),
        out_specs=(cells, cells, filters),
        check_vma=False,
    )
```

time: 505 us -> 188 us (0.37)
  the two profiles are of different devices: /device:TPU:1 before, /device:TPU:38 now
where the time goes in v1:
time: 188 us
  blocking collectives  97.3 us (52%)
  starting transfers between devices  49.4 us (26%)
  waiting for transfers between devices  29.5 us (16%)
  Pallas kernels  6.24 us (3%)
  other arithmetic  3.93 us (2%)
    all_gather x1, blocking collectives, shards(): quarter = lax.all_gather(part, 'zhi', axis=0, tiled=True)  26.5 us
    all_to_all x3, starting transfers between devices, exchange(): return lax.all_to_all(block, axis, split_axis=0, concat_axis=0, tiled=True)  25 us
    all_to_all x1, blocking collectives, exchange(): return lax.all_to_all(block, axis, split_axis=0, concat_axis=0, tiled=True)  24.6 us
    all_to_all x3, waiting for transfers between devices, exchange(): return lax.all_to_all(block, axis, split_axis=0, concat_axis=0, tiled=True)  19.4 us
    all_gather x1, blocking collectives, shards(): data = lax.all_gather(data, 'space', axis=1, tiled=True)  18.1 us
    all_gather x1, blocking collectives, shards(): half = lax.all_gather(quarter, 'ring', axis=0, tiled=True)  14.7 us
    all_gather x1, blocking collectives, shards(): grad = lax.all_gather(grad, 'chan', axis=1, tiled=True)  13.3 us
    ppermute x1, waiting for transfers between devices, shards(): lax.ppermute(forward, AXES, column_move(sizes, 0, True))  8.04 us
  transfers between devices with their start and end apart: 11, of which 4 were waited for; matrix products, arithmetic and copies ran while one was open for 0% of the time, Pallas kernels for 2%

profile of v1, /device:TPU:38, one launch (start us, length us, event | category | flops | bytes accessed | tf_op | source)
XLA Modules:
  0.0 187.8 jit_solution(8383728823336657319)
XLA Ops:
  0.6 5.5 %collective-permute-start.3 = (bf16[1,8,32,128]{3,2,1,0:T(8,128)(2,1)}, bf16[1,8,32,128]{3,2,1,0:T(8,128)(2,1)S(1)}, u32[]{:S(2)}, u32[]{:S(2)}) collective-permute-start(bf16[1,8,32,128]{3,2,1,0:T(8,128)(2,1)} %param.5), channel_id=1, source_target_pairs={{0,4},{1,132},{2,260},{3,388},{4,8},{5,136},{6,264},{7,392},{8,12}... | collective-permute-start | bytes 196616 | tf_op jit(solution)/shard_map/ppermute | solution.py:171
  6.1 1.3 collective-permute-start.5
  7.4 3.1 %collective-permute-start.4 = (bf16[1,8,32,128]{3,2,1,0:T(8,128)(2,1)}, bf16[1,8,32,128]{3,2,1,0:T(8,128)(2,1)S(1)}, u32[]{:S(2)}, u32[]{:S(2)}) collective-permute-start(bf16[1,8,32,128]{3,2,1,0:T(8,128)(2,1)} %param.5), channel_id=1, source_target_pairs={{0,0},{1,128},{2,256},{3,384},{4,4},{5,132},{6,260},{7,388},{8,8},... | collective-permute-start | bytes 196616 | tf_op jit(solution)/shard_map/ppermute | solution.py:172
  10.5 6.5 %collective-permute-start = (bf16[1,8,32,128]{3,2,1,0:T(8,128)(2,1)}, bf16[1,8,32,128]{3,2,1,0:T(8,128)(2,1)S(1)}, u32[]{:S(2)}, u32[]{:S(2)}) collective-permute-start(bf16[1,8,32,128]{3,2,1,0:T(8,128)(2,1)} %param.3), channel_id=1, source_target_pairs={{0,4},{1,5},{2,6},{3,7},{4,8},{5,9},{6,10},{7,11},{8,12},{9,13},{1... | collective-permute-start | bytes 196616 | tf_op jit(solution)/shard_map/ppermute | solution.py:169
  17.0 1.3 collective-permute-start.1
  18.3 0.0 collective-permute-done.3
  18.3 0.0 collective-permute-done.5
  18.3 0.0 collective-permute-done.4
  18.4 13.3 %all_gather.13.block.grad = bf16[3,32,32,128]{3,2,1,0:T(8,128)(2,1)S(1)} all-gather(bf16[3,8,32,128]{3,2,1,0:T(8,128)(2,1)S(1)} %pad_maximum_fusion.2), channel_id=1, replica_groups=mesh['chan'=4,'zhi'=4,'ring'=4,'core'=2,'space'=4] {'chan'}, dimensions={1}, use_global_device_ids=true | all-gather | bytes 983040 | tf_op jit(solution)/shard_map/all_gather | solution.py:175
  31.7 0.0 collective-permute-done
  31.7 0.0 collective-permute-done.1
  31.7 0.9 pad_maximum_fusion.1
  32.6 18.1 %all_gather.12.block = bf16[3,32,32,128]{3,2,1,0:T(8,128)(2,1)S(1)} all-gather(bf16[3,8,32,128]{3,2,1,0:T(8,128)(2,1)S(1)} %pad_maximum_fusion.1), channel_id=1, replica_groups=mesh['chan'=4,'zhi'=4,'ring'=4,'core'=2,'space'=4] {'space'}, dimensions={1}, use_global_device_ids=true | all-gather | bytes 983040 | tf_op jit(solution)/shard_map/all_gather | solution.py:177
  50.7 1.6 filter_grad.1
  52.3 3.0 %collective-permute-start.6 = (f32[1792,128]{1,0:T(8,128)S(1)}, f32[1792,128]{1,0:T(8,128)S(1)}, u32[]{:S(2)}, u32[]{:S(2)}) collective-permute-start(f32[1792,128]{1,0:T(8,128)S(1)} %get-tuple-element.6), channel_id=1, source_target_pairs={{0,4},{4,0},{1,5},{5,1},{2,6},{6,2},{3,7},{7,3},{8,12},{12,8},{9,1... | collective-permute-start | bytes 2752520 | tf_op jit(solution)/shard_map/ppermute | solution.py:182
  55.3 2.1 %collective-permute-done.6 = f32[1792,128]{1,0:T(8,128)S(1)} collective-permute-done((f32[1792,128]{1,0:T(8,128)S(1)}, f32[1792,128]{1,0:T(8,128)S(1)}, u32[]{:S(2)}, u32[]{:S(2)}) %collective-permute-start.6) | collective-permute-done | bytes 917536 | tf_op jit(solution)/shard_map/ppermute | solution.py:182
  57.4 0.1 add.3
  57.5 0.0 copy-start
  57.5 24.6 %all_to_all.20 = f32[4,448,128]{2,1,0:T(8,128)S(1)} all-to-all(f32[4,448,128]{2,1,0:T(8,128)S(1)} %bitcast.8), channel_id=1, replica_groups=mesh['chan'=4,'zhi'=4,'ring'=4,'core'=2,'space'=4] {'ring'}, dimensions={0} | all-to-all | bytes 1835008 | tf_op jit(solution)/shard_map/all_to_all | solution.py:164
  82.1 0.7 reduce_sum.38
  82.8 15.4 %all-to-all-start.3 = ((f32[4,112,128]{2,1,0:T(8,128)}), f32[4,112,128]{2,1,0:T(8,128)S(1)}, u32[]{:S(2)}, u32[]{:S(2)}) async-start(f32[4,112,128]{2,1,0:T(8,128)} %bitcast.10), calls=%async_computation.3 | async-start | bytes 458752 | tf_op jit(solution)/shard_map/all_to_all | solution.py:164
  98.2 0.0 copy-done
  98.2 2.3 %forward.1 = f32[4,256,128]{2,1,0:T(8,128)} custom-call(bf16[3,32,32,128]{3,2,1,0:T(8,128)(2,1)S(1)} %all_gather.12.block, bf16[27,128,128]{2,1,0:T(8,128)(2,1)S(1)} %copy-done), custom_call_target="tpu_custom_call" | custom-call | flops 905969664 | bytes 3145728 | tf_op jit(solution)/shard_map/forward/pallas_call | solution.py:92
  100.5 15.7 %all-to-all-done.3 = f32[4,112,128]{2,1,0:T(8,128)S(1)} async-done(((f32[4,112,128]{2,1,0:T(8,128)}), f32[4,112,128]{2,1,0:T(8,128)S(1)}, u32[]{:S(2)}, u32[]{:S(2)}) %all-to-all-start.3) | async-done | bytes 229408 | tf_op jit(solution)/shard_map/all_to_all | solution.py:164
  116.2 4.5 %all-to-all-start = ((f32[4,256,128]{2,1,0:T(8,128)}), f32[4,256,128]{2,1,0:T(8,128)S(1)}, u32[]{:S(2)}, u32[]{:S(2)}) async-start(f32[4,256,128]{2,1,0:T(8,128)} %forward.1), calls=%async_computation | async-start | bytes 1048576 | tf_op jit(solution)/shard_map/all_to_all | solution.py:164
  120.7 2.4 %input_grad.1 = f32[4,256,128]{2,1,0:T(8,128)} custom-call(bf16[3,32,32,128]{3,2,1,0:T(8,128)(2,1)S(1)} %all_gather.13.block.grad, bf16[27,128,128]{2,1,0:T(8,128)(2,1)S(1)} %copy-done), custom_call_target="tpu_custom_call" | custom-call | flops 905969664 | bytes 3145728 | tf_op jit(solution)/shard_map/input_grad/pallas_call | solution.py:92
  123.1 3.6 %all-to-all-done = f32[4,256,128]{2,1,0:T(8,128)S(1)} async-done(((f32[4,256,128]{2,1,0:T(8,128)}), f32[4,256,128]{2,1,0:T(8,128)S(1)}, u32[]{:S(2)}, u32[]{:S(2)}) %all-to-all-start) | async-done | bytes 524320 | tf_op jit(solution)/shard_map/all_to_all | solution.py:164
  126.8 5.1 %all-to-all-start.1 = ((f32[4,256,128]{2,1,0:T(8,128)}), f32[4,256,128]{2,1,0:T(8,128)S(1)}, u32[]{:S(2)}, u32[]{:S(2)}) async-start(f32[4,256,128]{2,1,0:T(8,128)} %input_grad.1), calls=%async_computation.1 | async-start | bytes 1048576 | tf_op jit(solution)/shard_map/all_to_all | solution.py:164
  131.9 26.5 %all_gather.14 = f32[448,128]{1,0:T(8,128)S(1)} all-gather(f32[112,128]{1,0:T(8,128)S(1)} %broadcast_multiply_fusion), channel_id=1, replica_groups=mesh['chan'=4,'zhi'=4,'ring'=4,'core'=2,'space'=4] {'zhi'}, dimensions={0}, use_global_device_ids=true | all-gather | bytes 286720 | tf_op jit(solution)/shard_map/all_gather | solution.py:187
  158.3 14.7 %all_gather.15 = f32[1792,128]{1,0:T(8,128)S(1)} all-gather(f32[448,128]{1,0:T(8,128)S(1)} %all_gather.14), channel_id=1, replica_groups=mesh['chan'=4,'zhi'=4,'ring'=4,'core'=2,'space'=4] {'ring'}, dimensions={0}, use_global_device_ids=true | all-gather | bytes 1146880 | tf_op jit(solution)/shard_map/all_gather | solution.py:188
  173.1 1.9 %collective-permute-start.7 = (f32[1792,128]{1,0:T(8,128)S(1)}, f32[1792,128]{1,0:T(8,128)S(1)}, u32[]{:S(2)}, u32[]{:S(2)}) collective-permute-start(f32[1792,128]{1,0:T(8,128)S(1)} %all_gather.15), channel_id=1, source_target_pairs={{0,4},{4,0},{1,5},{5,1},{2,6},{6,2},{3,7},{7,3},{8,12},{12,8},{9,1... | collective-permute-start | bytes 2752520 | tf_op jit(solution)/shard_map/ppermute | solution.py:189
  175.0 1.9 %collective-permute-start.2 = (bf16[256,128]{1,0:T(8,128)(2,1)S(1)}, bf16[256,128]{1,0:T(8,128)(2,1)S(1)}, u32[]{:S(2)}, u32[]{:S(2)}) collective-permute-start(bf16[256,128]{1,0:T(8,128)(2,1)S(1)} %reduce_sum.36), channel_id=1, source_target_pairs={{0,0},{1,128},{2,256},{3,384},{4,4},{5,132},{6,260},{7,388},{8,8},... | collective-permute-start | bytes 196616 | tf_op jit(solution)/shard_map/ppermute | solution.py:198
  177.0 8.0 %collective-permute-done.2 = bf16[256,128]{1,0:T(8,128)(2,1)S(1)} collective-permute-done((bf16[256,128]{1,0:T(8,128)(2,1)S(1)}, bf16[256,128]{1,0:T(8,128)(2,1)S(1)}, u32[]{:S(2)}, u32[]{:S(2)}) %collective-permute-start.2) | collective-permute-done | bytes 65568 | tf_op jit(solution)/shard_map/ppermute | solution.py:198
  185.0 0.0 all-to-all-done.1
  185.0 0.7 reduce_sum.37
  185.7 0.0 collective-permute-done.7
  185.7 0.1 slice_select_fusion
  185.8 0.1 broadcast_select_fusion
  185.9 1.3 pad_maximum_fusion
  187.2 0.6 copy.7
  (5 shorter events, 0.1 us)
Async XLA Ops:
  0.6 17.7 %collective-permute-start.3 = (bf16[1,8,32,128]{3,2,1,0:T(8,128)(2,1)}, bf16[1,8,32,128]{3,2,1,0:T(8,128)(2,1)S(1)}, u32[]{:S(2)}, u32[]{:S(2)}) collective-permute-start(bf16[1,8,32,128]{3,2,1,0:T(8,128)(2,1)} %param.5), channel_id=1, source_target_pairs={{0,4},{1,132},{2,260},{3,388},{4,8},{5,136},{6,264},{7,392},{8,12}... | collective-permute-start | bytes 196616 | tf_op jit(solution)/shard_map/ppermute | solution.py:171
  6.1 12.2 %collective-permute-start.5 = (bf16[1,8,32,128]{3,2,1,0:T(8,128)(2,1)}, bf16[1,8,32,128]{3,2,1,0:T(8,128)(2,1)S(1)}, u32[]{:S(2)}, u32[]{:S(2)}) collective-permute-start(bf16[1,8,32,128]{3,2,1,0:T(8,128)(2,1)} %param.5), channel_id=1, source_target_pairs={{4,0},{5,128},{6,256},{7,384},{8,4},{9,132},{10,260},{11,388},{12,... | collective-permute-start | bytes 196616 | tf_op jit(solution)/shard_map/ppermute | solution.py:173
  7.4 10.9 %collective-permute-start.4 = (bf16[1,8,32,128]{3,2,1,0:T(8,128)(2,1)}, bf16[1,8,32,128]{3,2,1,0:T(8,128)(2,1)S(1)}, u32[]{:S(2)}, u32[]{:S(2)}) collective-permute-start(bf16[1,8,32,128]{3,2,1,0:T(8,128)(2,1)} %param.5), channel_id=1, source_target_pairs={{0,0},{1,128},{2,256},{3,384},{4,4},{5,132},{6,260},{7,388},{8,8},... | collective-permute-start | bytes 196616 | tf_op jit(solution)/shard_map/ppermute | solution.py:172
  10.5 21.2 %collective-permute-start = (bf16[1,8,32,128]{3,2,1,0:T(8,128)(2,1)}, bf16[1,8,32,128]{3,2,1,0:T(8,128)(2,1)S(1)}, u32[]{:S(2)}, u32[]{:S(2)}) collective-permute-start(bf16[1,8,32,128]{3,2,1,0:T(8,128)(2,1)} %param.3), channel_id=1, source_target_pairs={{0,4},{1,5},{2,6},{3,7},{4,8},{5,9},{6,10},{7,11},{8,12},{9,13},{1... | collective-permute-start | bytes 196616 | tf_op jit(solution)/shard_map/ppermute | solution.py:169
  17.0 14.7 %collective-permute-start.1 = (bf16[1,8,32,128]{3,2,1,0:T(8,128)(2,1)}, bf16[1,8,32,128]{3,2,1,0:T(8,128)(2,1)S(1)}, u32[]{:S(2)}, u32[]{:S(2)}) collective-permute-start(bf16[1,8,32,128]{3,2,1,0:T(8,128)(2,1)} %param.3), channel_id=1, source_target_pairs={{4,0},{5,1},{6,2},{7,3},{8,4},{9,5},{10,6},{11,7},{12,8},{13,9},{1... | collective-permute-start | bytes 196616 | tf_op jit(solution)/shard_map/ppermute | solution.py:170
  52.3 5.1 %collective-permute-start.6 = (f32[1792,128]{1,0:T(8,128)S(1)}, f32[1792,128]{1,0:T(8,128)S(1)}, u32[]{:S(2)}, u32[]{:S(2)}) collective-permute-start(f32[1792,128]{1,0:T(8,128)S(1)} %get-tuple-element.6), channel_id=1, source_target_pairs={{0,4},{4,0},{1,5},{5,1},{2,6},{6,2},{3,7},{7,3},{8,12},{12,8},{9,1... | collective-permute-start | bytes 2752520 | tf_op jit(solution)/shard_map/ppermute | solution.py:182
  57.5 40.7 %copy-start = (bf16[27,128,128]{2,1,0:T(8,128)(2,1)S(1)}, bf16[27,128,128]{2,1,0:T(8,128)(2,1)}, u32[]{:S(2)}) copy-start(bf16[27,128,128]{2,1,0:T(8,128)(2,1)} %weight.3) | copy-start | bytes 2654212
  82.8 33.4 %all-to-all-start.3 = ((f32[4,112,128]{2,1,0:T(8,128)}), f32[4,112,128]{2,1,0:T(8,128)S(1)}, u32[]{:S(2)}, u32[]{:S(2)}) async-start(f32[4,112,128]{2,1,0:T(8,128)} %bitcast.10), calls=%async_computation.3 | async-start | bytes 458752 | tf_op jit(solution)/shard_map/all_to_all | solution.py:164
  116.2 10.5 %all-to-all-start = ((f32[4,256,128]{2,1,0:T(8,128)}), f32[4,256,128]{2,1,0:T(8,128)S(1)}, u32[]{:S(2)}, u32[]{:S(2)}) async-start(f32[4,256,128]{2,1,0:T(8,128)} %forward.1), calls=%async_computation | async-start | bytes 1048576 | tf_op jit(solution)/shard_map/all_to_all | solution.py:164
  126.8 58.3 %all-to-all-start.1 = ((f32[4,256,128]{2,1,0:T(8,128)}), f32[4,256,128]{2,1,0:T(8,128)S(1)}, u32[]{:S(2)}, u32[]{:S(2)}) async-start(f32[4,256,128]{2,1,0:T(8,128)} %input_grad.1), calls=%async_computation.1 | async-start | bytes 1048576 | tf_op jit(solution)/shard_map/all_to_all | solution.py:164
  173.1 12.6 %collective-permute-start.7 = (f32[1792,128]{1,0:T(8,128)S(1)}, f32[1792,128]{1,0:T(8,128)S(1)}, u32[]{:S(2)}, u32[]{:S(2)}) collective-permute-start(f32[1792,128]{1,0:T(8,128)S(1)} %all_gather.15), channel_id=1, source_target_pairs={{0,4},{4,0},{1,5},{5,1},{2,6},{6,2},{3,7},{7,3},{8,12},{12,8},{9,1... | collective-permute-start | bytes 2752520 | tf_op jit(solution)/shard_map/ppermute | solution.py:189
  175.0 10.0 %collective-permute-start.2 = (bf16[256,128]{1,0:T(8,128)(2,1)S(1)}, bf16[256,128]{1,0:T(8,128)(2,1)S(1)}, u32[]{:S(2)}, u32[]{:S(2)}) collective-permute-start(bf16[256,128]{1,0:T(8,128)(2,1)S(1)} %reduce_sum.36), channel_id=1, source_target_pairs={{0,0},{1,128},{2,256},{3,384},{4,4},{5,132},{6,260},{7,388},{8,8},... | collective-permute-start | bytes 196616 | tf_op jit(solution)/shard_map/ppermute | solution.py:198

commit v2 on v1

--- a/solution.py
+++ b/solution.py
@@ -164,40 +164,69 @@
     return lax.all_to_all(block, axis, split_axis=0, concat_axis=0, tiled=True)
 
 
+def gather(block, axis):
+    count = lax.axis_size(axis)
+    return exchange(jnp.broadcast_to(block[None], (count, *block.shape)), axis)
+
+
+def after(value, *others):
+    return lax.optimization_barrier((value, *others))[0]
+
+
 def shards(sizes, activations, weight, output_grad):
     _, zhis, rings, cores, spaces = sizes
-    act_low = lax.ppermute(activations, AXES, column_move(sizes, 1, False))
-    act_high = lax.ppermute(activations, AXES, column_move(sizes, -1, False))
-    grad_low = lax.ppermute(output_grad, AXES, column_move(sizes, 1, True))
-    grad_mid = lax.ppermute(output_grad, AXES, column_move(sizes, 0, True))
-    grad_high = lax.ppermute(output_grad, AXES, column_move(sizes, -1, True))
-    grad = jnp.concatenate([grad_low, grad_mid, grad_high], axis=0)
-    grad = lax.all_gather(grad, "chan", axis=1, tiled=True)
-    data = jnp.concatenate([act_low, activations, act_high], axis=0)
-    data = lax.all_gather(data, "space", axis=1, tiled=True)
-    lanes = activations.shape[3]
+    planes, height, lanes = activations.shape[1:]
     core = lax.axis_index("core").reshape(1)
-
-    keep, send = filter_partial(data[1], grad, core)
-    half = keep + lax.ppermute(send, "core", [(0, 1), (1, 0)])
-    quarter = exchange(half.reshape(rings, -1, lanes), "ring").sum(0)
-    part = exchange(quarter.reshape(zhis, -1, lanes), "zhi").sum(0)
+    swap = [(0, 1), (1, 0)]
+
+    own = gather(activations[0], "space").reshape(-1, height, lanes)
+    grads = [
+        lax.ppermute(output_grad, AXES, column_move(sizes, step, True)) for step in (1, 0, -1)
+    ]
+    grad = lax.all_gather(jnp.concatenate(grads, axis=0), "chan", axis=1, tiled=True)
+
+    keep, send = filter_partial(own, grad, core)
+    moved = lax.ppermute(send, "core", swap)
+    edge = after(activations, send)
+    low = lax.ppermute(edge, AXES, column_move(sizes, 1, False))
+    high = lax.ppermute(edge, AXES, column_move(sizes, -1, False))
+    half = keep + moved
+    half = after(half, low, high)
+
+    moved = exchange(half.reshape(rings, -1, lanes), "ring")
+    sides = jnp.concatenate([after(low, half), high], axis=0)
+    sides = lax.all_gather(sides, "space", axis=1, tiled=True)
+    quarter = moved.sum(0)
+    quarter = after(quarter, sides)
+
+    moved = exchange(quarter.reshape(zhis, -1, lanes), "zhi")
+    data = jnp.stack([after(sides, quarter)[0], own, sides[1]], axis=0)
+    forward = convolve(False, data, weight, spaces)
+    back = convolve(True, after(grad, quarter), weight, spaces)
+    forward = exchange(forward, "chan")
     cell_count = sizes[1] * rings * cores * grad.shape[1] * grad.shape[2]
-    part = part / math.sqrt(cell_count)
-    quarter = lax.all_gather(part, "zhi", axis=0, tiled=True)
-    half = lax.all_gather(quarter, "ring", axis=0, tiled=True)
-    other = lax.ppermute(half, "core", [(0, 1), (1, 0)])
+    part = moved.sum(0) / math.sqrt(cell_count)
+    part = after(part, back, forward)
+
+    moved = gather(part, "zhi")
+    forward = after(forward, part).sum(0).astype(BF16)
+    output = lax.ppermute(forward, AXES, column_move(sizes, 0, True)).reshape(activations.shape)
+    quarter = moved.reshape(-1, lanes)
+    quarter = after(quarter, output)
+
+    moved = gather(quarter, "ring")
+    back = exchange(after(back, quarter), "space").sum(0).astype(BF16)
+    input_grad = back.reshape(activations.shape)
+    half = moved.reshape(-1, lanes)
+    half = after(half, input_grad)
+
+    other = lax.ppermute(half, "core", swap)
     first = core[0] == 0
     low = jnp.where(first, half, other)
     high = jnp.where(first, other, half)
     taps = weight.shape[0]
     filter_grad = jnp.concatenate([low, high[: taps * lanes - low.shape[0]]], axis=0)
     filter_grad = filter_grad.reshape(weight.shape)
-
-    forward = exchange(convolve(False, data, weight, spaces), "chan").sum(0).astype(BF16)
-    output = lax.ppermute(forward, AXES, column_move(sizes, 0, True)).reshape(activations.shape)
-    back = exchange(convolve(True, grad, weight, spaces), "space").sum(0).astype(BF16)
-    input_grad = back.reshape(activations.shape)
     return output, input_grad, filter_grad
 
 

time: 188 us -> 187 us (level)
  the two profiles are of different devices: /device:TPU:38 before, /device:TPU:1 now
where the time goes in v2:
time: 187 us; the launch traced here: 186 us
  starting transfers between devices  80.8 us (43%)
  blocking collectives  50.4 us (27%)
  waiting for transfers between devices  40.8 us (22%)
  Pallas kernels  5.46 us (3%)
  other arithmetic  4.1 us (2%)
  local copies, waits for them, and re-layouts  3.94 us (2%)
    all_to_all x6, starting transfers between devices, exchange(): return lax.all_to_all(block, axis, split_axis=0, concat_axis=0, tiled=True)  42.2 us
    all_to_all x6, waiting for transfers between devices, exchange(): return lax.all_to_all(block, axis, split_axis=0, concat_axis=0, tiled=True)  36.9 us
    all_gather x1, blocking collectives, shards(): lax.all_gather(jnp.concatenate(grads, axis=0), 'chan', axis=1, tiled=True)  21.4 us
    ppermute x1, starting transfers between devices, shards(): other = lax.ppermute(half, 'core', swap)  18.9 us
    all_to_all x1, blocking collectives, exchange(): return lax.all_to_all(block, axis, split_axis=0, concat_axis=0, tiled=True)  14.8 us
    all_gather x1, blocking collectives, shards(): sides = lax.all_gather(sides, 'space', axis=1, tiled=True)  14.2 us
    ppermute x3, starting transfers between devices, shards(): lax.ppermute(output_grad, AXES, column_move(sizes, step, True))  8.55 us
    ppermute x1, starting transfers between devices, shards(): low = lax.ppermute(edge, AXES, column_move(sizes, 1, False))  6.18 us
  transfers between devices with their start and end apart: 14, of which 7 were waited for; matrix products, arithmetic and copies ran while one was open for 1% of the time, Pallas kernels for 2%

profile of v2, /device:TPU:1, one launch (start us, length us, event | category | flops | bytes accessed | tf_op | source)
XLA Modules:
  0.0 186.3 jit_solution(10531513922524522880)
XLA Ops:
  0.6 1.6 broadcast_in_dim.9
  2.2 6.4 %all-to-all-start = ((bf16[4,8,32,128]{3,2,1,0:T(8,128)(2,1)}), bf16[4,8,32,128]{3,2,1,0:T(8,128)(2,1)S(1)}, u32[]{:S(2)}, u32[]{:S(2)}) async-start(bf16[4,8,32,128]{3,2,1,0:T(8,128)(2,1)} %broadcast_in_dim.9), calls=%async_computation | async-start | bytes 524288 | tf_op jit(solution)/shard_map/all_to_all | solution.py:164
  8.7 4.0 %collective-permute-start = (bf16[1,8,32,128]{3,2,1,0:T(8,128)(2,1)}, bf16[1,8,32,128]{3,2,1,0:T(8,128)(2,1)S(1)}, u32[]{:S(2)}, u32[]{:S(2)}) collective-permute-start(bf16[1,8,32,128]{3,2,1,0:T(8,128)(2,1)} %param.5), channel_id=1, source_target_pairs={{0,4},{1,132},{2,260},{3,388},{4,8},{5,136},{6,264},{7,392},{8,12}... | collective-permute-start | bytes 196616 | tf_op jit(solution)/shard_map/ppermute | solution.py:184
  12.7 3.0 %collective-permute-start.2 = (bf16[1,8,32,128]{3,2,1,0:T(8,128)(2,1)}, bf16[1,8,32,128]{3,2,1,0:T(8,128)(2,1)S(1)}, u32[]{:S(2)}, u32[]{:S(2)}) collective-permute-start(bf16[1,8,32,128]{3,2,1,0:T(8,128)(2,1)} %param.5), channel_id=1, source_target_pairs={{4,0},{5,128},{6,256},{7,384},{8,4},{9,132},{10,260},{11,388},{12,... | collective-permute-start | bytes 196616 | tf_op jit(solution)/shard_map/ppermute | solution.py:184
  15.7 1.5 collective-permute-start.1
  17.2 0.0 collective-permute-done
  17.2 1.6 collective-permute-done.2
  18.8 0.0 collective-permute-done.1
  18.8 21.4 %all_gather.6.grad.block = bf16[3,32,32,128]{3,2,1,0:T(8,128)(2,1)S(1)} all-gather(bf16[3,8,32,128]{3,2,1,0:T(8,128)(2,1)S(1)} %pad_maximum_fusion.2), channel_id=1, replica_groups=mesh['chan'=4,'zhi'=4,'ring'=4,'core'=2,'space'=4] {'chan'}, dimensions={1}, use_global_device_ids=true | all-gather | bytes 983040 | tf_op jit(solution)/shard_map/all_gather | solution.py:186
  40.2 0.0 copy-start.1
  40.2 0.0 all-to-all-done
  40.2 1.6 filter_grad.1
  41.8 2.5 %collective-permute-start.4 = (f32[1792,128]{1,0:T(8,128)S(1)}, f32[1792,128]{1,0:T(8,128)S(1)}, u32[]{:S(2)}, u32[]{:S(2)}) collective-permute-start(f32[1792,128]{1,0:T(8,128)S(1)} %get-tuple-element.16), channel_id=1, source_target_pairs={{0,4},{4,0},{1,5},{5,1},{2,6},{6,2},{3,7},{7,3},{8,12},{12,8},{9,1... | collective-permute-start | bytes 2752520 | tf_op jit(solution)/shard_map/ppermute | solution.py:189
  44.3 0.0 copy-done.1
  44.3 1.9 %collective-permute-start.5 = (bf16[1,8,32,128]{3,2,1,0:T(8,128)(2,1)S(1)}, bf16[1,8,32,128]{3,2,1,0:T(8,128)(2,1)S(1)}, u32[]{:S(2)}, u32[]{:S(2)}) collective-permute-start(bf16[1,8,32,128]{3,2,1,0:T(8,128)(2,1)S(1)} %copy-done.1), channel_id=1, source_target_pairs={{4,0},{5,1},{6,2},{7,3},{8,4},{9,5},{10,6},{11,7},{12,8},{13,9},{1... | collective-permute-start | bytes 196616 | tf_op jit(solution)/shard_map/ppermute | solution.py:192
  46.2 6.2 %collective-permute-start.3 = (bf16[1,8,32,128]{3,2,1,0:T(8,128)(2,1)S(1)}, bf16[1,8,32,128]{3,2,1,0:T(8,128)(2,1)S(1)}, u32[]{:S(2)}, u32[]{:S(2)}) collective-permute-start(bf16[1,8,32,128]{3,2,1,0:T(8,128)(2,1)S(1)} %copy-done.1), channel_id=1, source_target_pairs={{0,4},{1,5},{2,6},{3,7},{4,8},{5,9},{6,10},{7,11},{8,12},{9,13},{1... | collective-permute-start | bytes 196616 | tf_op jit(solution)/shard_map/ppermute | solution.py:191
  52.4 0.0 collective-permute-done.4
  52.4 1.0 add.3
  53.5 0.0 collective-permute-done.5
  53.5 0.3 collective-permute-done.3
  53.7 15.7 %all-to-all-start.1 = ((f32[4,448,128]{2,1,0:T(8,128)}), f32[4,448,128]{2,1,0:T(8,128)S(1)}, u32[]{:S(2)}, u32[]{:S(2)}) async-start(f32[4,448,128]{2,1,0:T(8,128)} %bitcast.3), calls=%async_computation.1 | async-start | bytes 1835008 | tf_op jit(solution)/shard_map/all_to_all | solution.py:164
  69.5 14.2 %all_gather.7 = bf16[2,32,32,128]{3,2,1,0:T(8,128)(2,1)S(1)} all-gather(bf16[2,8,32,128]{3,2,1,0:T(8,128)(2,1)S(1)} %pad_maximum_fusion.3), channel_id=1, replica_groups=mesh['chan'=4,'zhi'=4,'ring'=4,'core'=2,'space'=4] {'space'}, dimensions={1}, use_global_device_ids=true | all-gather | bytes 655360 | tf_op jit(solution)/shard_map/all_gather | solution.py:198
  83.7 0.0 all-to-all-done.1
  83.7 0.7 reduce_sum.36
  84.4 0.0 copy-start
  84.4 8.0 %all-to-all-start.3 = ((f32[4,112,128]{2,1,0:T(8,128)}), f32[4,112,128]{2,1,0:T(8,128)S(1)}, u32[]{:S(2)}, u32[]{:S(2)}) async-start(f32[4,112,128]{2,1,0:T(8,128)} %bitcast.5), calls=%async_computation.3 | async-start | bytes 458752 | tf_op jit(solution)/shard_map/all_to_all | solution.py:164
  92.4 0.1 pad_maximum_fusion.1.block
  92.5 0.0 copy-done
  92.5 2.3 %forward.1 = f32[4,256,128]{2,1,0:T(8,128)} custom-call(bf16[3,32,32,128]{3,2,1,0:T(8,128)(2,1)S(1)} %pad_maximum_fusion.1.block, bf16[27,128,128]{2,1,0:T(8,128)(2,1)S(1)} %copy-done), custom_call_target="tpu_custom_call" | custom-call | flops 905969664 | bytes 3145728 | tf_op jit(solution)/shard_map/forward/pallas_call | solution.py:92
  94.8 11.3 %all-to-all-done.3 = f32[4,112,128]{2,1,0:T(8,128)S(1)} async-done(((f32[4,112,128]{2,1,0:T(8,128)}), f32[4,112,128]{2,1,0:T(8,128)S(1)}, u32[]{:S(2)}, u32[]{:S(2)}) %all-to-all-start.3) | async-done | bytes 229408 | tf_op jit(solution)/shard_map/all_to_all | solution.py:164
  106.2 3.5 %all-to-all-start.2 = ((f32[4,256,128]{2,1,0:T(8,128)}), f32[4,256,128]{2,1,0:T(8,128)S(1)}, u32[]{:S(2)}, u32[]{:S(2)}) async-start(f32[4,256,128]{2,1,0:T(8,128)} %forward.1), calls=%async_computation.2 | async-start | bytes 1048576 | tf_op jit(solution)/shard_map/all_to_all | solution.py:164
  109.6 1.6 input_grad.1
  111.2 5.3 %all-to-all-done.2 = f32[4,256,128]{2,1,0:T(8,128)S(1)} async-done(((f32[4,256,128]{2,1,0:T(8,128)}), f32[4,256,128]{2,1,0:T(8,128)S(1)}, u32[]{:S(2)}, u32[]{:S(2)}) %all-to-all-start.2) | async-done | bytes 524320 | tf_op jit(solution)/shard_map/all_to_all | solution.py:164
  116.5 0.7 broadcast_in_dim.10
  117.2 3.9 %all-to-all-start.4 = ((f32[4,112,128]{2,1,0:T(8,128)}), f32[4,112,128]{2,1,0:T(8,128)S(1)}, u32[]{:S(2)}, u32[]{:S(2)}) async-start(f32[4,112,128]{2,1,0:T(8,128)} %broadcast_in_dim.10), calls=%async_computation.4 | async-start | bytes 458752 | tf_op jit(solution)/shard_map/all_to_all | solution.py:164
  121.1 0.7 collective-permute-start.6
  121.8 0.0 collective-permute-done.6
  121.8 11.9 %all-to-all-done.4 = f32[4,112,128]{2,1,0:T(8,128)S(1)} async-done(((f32[4,112,128]{2,1,0:T(8,128)}), f32[4,112,128]{2,1,0:T(8,128)S(1)}, u32[]{:S(2)}, u32[]{:S(2)}) %all-to-all-start.4) | async-done | bytes 229408 | tf_op jit(solution)/shard_map/all_to_all | solution.py:164
  133.7 14.8 %all_to_all.35 = f32[4,256,128]{2,1,0:T(8,128)S(1)} all-to-all(f32[4,256,128]{2,1,0:T(8,128)S(1)} %input_grad.1), channel_id=1, replica_groups=mesh['chan'=4,'zhi'=4,'ring'=4,'core'=2,'space'=4] {'space'}, dimensions={0} | all-to-all | bytes 1048576 | tf_op jit(solution)/shard_map/all_to_all | solution.py:164
  148.5 1.0 broadcast_in_dim.22
  149.5 4.7 %all-to-all-start.6 = ((f32[4,448,128]{2,1,0:T(8,128)}), f32[4,448,128]{2,1,0:T(8,128)S(1)}, u32[]{:S(2)}, u32[]{:S(2)}) async-start(f32[4,448,128]{2,1,0:T(8,128)} %broadcast_in_dim.22), calls=%async_computation.6 | async-start | bytes 1835008 | tf_op jit(solution)/shard_map/all_to_all | solution.py:164
  154.2 0.7 reduce_sum.39
  154.8 8.4 %all-to-all-done.6 = f32[4,448,128]{2,1,0:T(8,128)S(1)} async-done(((f32[4,448,128]{2,1,0:T(8,128)}), f32[4,448,128]{2,1,0:T(8,128)S(1)}, u32[]{:S(2)}, u32[]{:S(2)}) %all-to-all-start.6) | async-done | bytes 917536 | tf_op jit(solution)/shard_map/all_to_all | solution.py:164
  163.2 18.9 %collective-permute-start.7 = (f32[1792,128]{1,0:T(8,128)S(1)}, f32[1792,128]{1,0:T(8,128)S(1)}, u32[]{:S(2)}, u32[]{:S(2)}) collective-permute-start(f32[1792,128]{1,0:T(8,128)S(1)} %bitcast.13), channel_id=1, source_target_pairs={{0,4},{4,0},{1,5},{5,1},{2,6},{6,2},{3,7},{7,3},{8,12},{12,8},{9,1... | collective-permute-start | bytes 2752520 | tf_op jit(solution)/shard_map/ppermute | solution.py:223
  182.1 2.1 %collective-permute-done.7 = f32[1792,128]{1,0:T(8,128)S(1)} collective-permute-done((f32[1792,128]{1,0:T(8,128)S(1)}, f32[1792,128]{1,0:T(8,128)S(1)}, u32[]{:S(2)}, u32[]{:S(2)}) %collective-permute-start.7) | collective-permute-done | bytes 917536 | tf_op jit(solution)/shard_map/ppermute | solution.py:223
  184.2 0.1 slice_select_fusion
  184.3 0.1 broadcast_select_fusion
  184.4 1.3 pad_maximum_fusion
  185.7 0.6 copy.7
  (7 shorter events, 0.1 us)
Async XLA Ops:
  2.2 38.0 %all-to-all-start = ((bf16[4,8,32,128]{3,2,1,0:T(8,128)(2,1)}), bf16[4,8,32,128]{3,2,1,0:T(8,128)(2,1)S(1)}, u32[]{:S(2)}, u32[]{:S(2)}) async-start(bf16[4,8,32,128]{3,2,1,0:T(8,128)(2,1)} %broadcast_in_dim.9), calls=%async_computation | async-start | bytes 524288 | tf_op jit(solution)/shard_map/all_to_all | solution.py:164
  8.7 8.6 %collective-permute-start = (bf16[1,8,32,128]{3,2,1,0:T(8,128)(2,1)}, bf16[1,8,32,128]{3,2,1,0:T(8,128)(2,1)S(1)}, u32[]{:S(2)}, u32[]{:S(2)}) collective-permute-start(bf16[1,8,32,128]{3,2,1,0:T(8,128)(2,1)} %param.5), channel_id=1, source_target_pairs={{0,4},{1,132},{2,260},{3,388},{4,8},{5,136},{6,264},{7,392},{8,12}... | collective-permute-start | bytes 196616 | tf_op jit(solution)/shard_map/ppermute | solution.py:184
  12.7 6.1 %collective-permute-start.2 = (bf16[1,8,32,128]{3,2,1,0:T(8,128)(2,1)}, bf16[1,8,32,128]{3,2,1,0:T(8,128)(2,1)S(1)}, u32[]{:S(2)}, u32[]{:S(2)}) collective-permute-start(bf16[1,8,32,128]{3,2,1,0:T(8,128)(2,1)} %param.5), channel_id=1, source_target_pairs={{4,0},{5,128},{6,256},{7,384},{8,4},{9,132},{10,260},{11,388},{12,... | collective-permute-start | bytes 196616 | tf_op jit(solution)/shard_map/ppermute | solution.py:184
  15.7 3.1 %collective-permute-start.1 = (bf16[1,8,32,128]{3,2,1,0:T(8,128)(2,1)}, bf16[1,8,32,128]{3,2,1,0:T(8,128)(2,1)S(1)}, u32[]{:S(2)}, u32[]{:S(2)}) collective-permute-start(bf16[1,8,32,128]{3,2,1,0:T(8,128)(2,1)} %param.5), channel_id=1, source_target_pairs={{0,0},{1,128},{2,256},{3,384},{4,4},{5,132},{6,260},{7,388},{8,8},... | collective-permute-start | bytes 196616 | tf_op jit(solution)/shard_map/ppermute | solution.py:184
  40.2 4.1 %copy-start.1 = (bf16[1,8,32,128]{3,2,1,0:T(8,128)(2,1)S(1)}, bf16[1,8,32,128]{3,2,1,0:T(8,128)(2,1)}, u32[]{:S(2)}) copy-start(bf16[1,8,32,128]{3,2,1,0:T(8,128)(2,1)} %param.3) | copy-start | bytes 196612
  41.8 10.6 %collective-permute-start.4 = (f32[1792,128]{1,0:T(8,128)S(1)}, f32[1792,128]{1,0:T(8,128)S(1)}, u32[]{:S(2)}, u32[]{:S(2)}) collective-permute-start(f32[1792,128]{1,0:T(8,128)S(1)} %get-tuple-element.16), channel_id=1, source_target_pairs={{0,4},{4,0},{1,5},{5,1},{2,6},{6,2},{3,7},{7,3},{8,12},{12,8},{9,1... | collective-permute-start | bytes 2752520 | tf_op jit(solution)/shard_map/ppermute | solution.py:189
  44.3 9.2 %collective-permute-start.5 = (bf16[1,8,32,128]{3,2,1,0:T(8,128)(2,1)S(1)}, bf16[1,8,32,128]{3,2,1,0:T(8,128)(2,1)S(1)}, u32[]{:S(2)}, u32[]{:S(2)}) collective-permute-start(bf16[1,8,32,128]{3,2,1,0:T(8,128)(2,1)S(1)} %copy-done.1), channel_id=1, source_target_pairs={{4,0},{5,1},{6,2},{7,3},{8,4},{9,5},{10,6},{11,7},{12,8},{13,9},{1... | collective-permute-start | bytes 196616 | tf_op jit(solution)/shard_map/ppermute | solution.py:192
  46.2 7.5 %collective-permute-start.3 = (bf16[1,8,32,128]{3,2,1,0:T(8,128)(2,1)S(1)}, bf16[1,8,32,128]{3,2,1,0:T(8,128)(2,1)S(1)}, u32[]{:S(2)}, u32[]{:S(2)}) collective-permute-start(bf16[1,8,32,128]{3,2,1,0:T(8,128)(2,1)S(1)} %copy-done.1), channel_id=1, source_target_pairs={{0,4},{1,5},{2,6},{3,7},{4,8},{5,9},{6,10},{7,11},{8,12},{9,13},{1... | collective-permute-start | bytes 196616 | tf_op jit(solution)/shard_map/ppermute | solution.py:191
  53.7 29.9 %all-to-all-start.1 = ((f32[4,448,128]{2,1,0:T(8,128)}), f32[4,448,128]{2,1,0:T(8,128)S(1)}, u32[]{:S(2)}, u32[]{:S(2)}) async-start(f32[4,448,128]{2,1,0:T(8,128)} %bitcast.3), calls=%async_computation.1 | async-start | bytes 1835008 | tf_op jit(solution)/shard_map/all_to_all | solution.py:164
  84.4 8.1 %copy-start = (bf16[27,128,128]{2,1,0:T(8,128)(2,1)S(1)}, bf16[27,128,128]{2,1,0:T(8,128)(2,1)}, u32[]{:S(2)}) copy-start(bf16[27,128,128]{2,1,0:T(8,128)(2,1)} %weight.3) | copy-start | bytes 2654212
  84.4 21.7 %all-to-all-start.3 = ((f32[4,112,128]{2,1,0:T(8,128)}), f32[4,112,128]{2,1,0:T(8,128)S(1)}, u32[]{:S(2)}, u32[]{:S(2)}) async-start(f32[4,112,128]{2,1,0:T(8,128)} %bitcast.5), calls=%async_computation.3 | async-start | bytes 458752 | tf_op jit(solution)/shard_map/all_to_all | solution.py:164
  106.2 10.4 %all-to-all-start.2 = ((f32[4,256,128]{2,1,0:T(8,128)}), f32[4,256,128]{2,1,0:T(8,128)S(1)}, u32[]{:S(2)}, u32[]{:S(2)}) async-start(f32[4,256,128]{2,1,0:T(8,128)} %forward.1), calls=%async_computation.2 | async-start | bytes 1048576 | tf_op jit(solution)/shard_map/all_to_all | solution.py:164
  117.2 16.5 %all-to-all-start.4 = ((f32[4,112,128]{2,1,0:T(8,128)}), f32[4,112,128]{2,1,0:T(8,128)S(1)}, u32[]{:S(2)}, u32[]{:S(2)}) async-start(f32[4,112,128]{2,1,0:T(8,128)} %broadcast_in_dim.10), calls=%async_computation.4 | async-start | bytes 458752 | tf_op jit(solution)/shard_map/all_to_all | solution.py:164
  121.1 0.7 collective-permute-start.6
  149.5 13.7 %all-to-all-start.6 = ((f32[4,448,128]{2,1,0:T(8,128)}), f32[4,448,128]{2,1,0:T(8,128)S(1)}, u32[]{:S(2)}, u32[]{:S(2)}) async-start(f32[4,448,128]{2,1,0:T(8,128)} %broadcast_in_dim.22), calls=%async_computation.6 | async-start | bytes 1835008 | tf_op jit(solution)/shard_map/all_to_all | solution.py:164
  163.2 20.9 %collective-permute-start.7 = (f32[1792,128]{1,0:T(8,128)S(1)}, f32[1792,128]{1,0:T(8,128)S(1)}, u32[]{:S(2)}, u32[]{:S(2)}) collective-permute-start(f32[1792,128]{1,0:T(8,128)S(1)} %bitcast.13), channel_id=1, source_target_pairs={{0,4},{4,0},{1,5},{5,1},{2,6},{6,2},{3,7},{7,3},{8,12},{12,8},{9,1... | collective-permute-start | bytes 2752520 | tf_op jit(solution)/shard_map/ppermute | solution.py:223

commit v3 on v2

--- a/solution.py
+++ b/solution.py
@@ -50,11 +50,12 @@
 
 
 def fill_padded(padded, block):
-    columns, planes, height, lanes = block.shape
+    _, planes, height, lanes = block.shape
+    columns = padded.shape[0]
     zero = jnp.zeros((columns, 1, height, lanes), BF16)
     padded[:, 0:1] = zero
     padded[:, planes + 1 : planes + 2] = zero
-    padded[:, 1 : planes + 1] = block[...]
+    padded[:, 1 : planes + 1] = block[0:columns]
 
 
 def conv_kernel(backward, block, weight, out, padded, flat):
@@ -86,7 +87,7 @@
 
 
 def convolve(backward, block, weight, slabs):
-    columns, planes, height, lanes = block.shape
+    _, planes, height, lanes = block.shape
     rows = planes * height
     flat = (3 * lanes, 9 * lanes) if backward else (9 * lanes, 3 * lanes)
     return pl.pallas_call(
@@ -95,7 +96,7 @@
         in_specs=[VMEM, VMEM],
         out_specs=VMEM,
         scratch_shapes=[
-            pltpu.VMEM((columns, planes + 2, height, lanes), BF16),
+            pltpu.VMEM((3, planes + 2, height, lanes), BF16),
             pltpu.VMEM(flat, BF16),
         ],
         compiler_params=pltpu.CompilerParams(vmem_limit_bytes=40 << 20),
@@ -183,42 +184,36 @@
     grads = [
         lax.ppermute(output_grad, AXES, column_move(sizes, step, True)) for step in (1, 0, -1)
     ]
-    grad = lax.all_gather(jnp.concatenate(grads, axis=0), "chan", axis=1, tiled=True)
+    low = lax.ppermute(activations, AXES, column_move(sizes, 1, False))
+    high = lax.ppermute(activations, AXES, column_move(sizes, -1, False))
+    sides = jnp.concatenate([low, activations, high, low], axis=0)
+    data = lax.all_gather(sides, "space", axis=1, tiled=True)
+    grad = after(jnp.concatenate(grads, axis=0), sides)
+    grad = lax.all_gather(grad, "chan", axis=1, tiled=True)
 
     keep, send = filter_partial(own, grad, core)
     moved = lax.ppermute(send, "core", swap)
-    edge = after(activations, send)
-    low = lax.ppermute(edge, AXES, column_move(sizes, 1, False))
-    high = lax.ppermute(edge, AXES, column_move(sizes, -1, False))
-    half = keep + moved
-    half = after(half, low, high)
+    back = convolve(True, after(grad, send), weight, spaces)
+    half = after(keep + moved, back)
+    back = lax.psum_scatter(back, "space", scatter_dimension=0, tiled=True)
 
     moved = exchange(half.reshape(rings, -1, lanes), "ring")
-    sides = jnp.concatenate([after(low, half), high], axis=0)
-    sides = lax.all_gather(sides, "space", axis=1, tiled=True)
-    quarter = moved.sum(0)
-    quarter = after(quarter, sides)
+    quarter, data = lax.optimization_barrier((moved.sum(0), data))
 
     moved = exchange(quarter.reshape(zhis, -1, lanes), "zhi")
-    data = jnp.stack([after(sides, quarter)[0], own, sides[1]], axis=0)
     forward = convolve(False, data, weight, spaces)
-    back = convolve(True, after(grad, quarter), weight, spaces)
-    forward = exchange(forward, "chan")
     cell_count = sizes[1] * rings * cores * grad.shape[1] * grad.shape[2]
     part = moved.sum(0) / math.sqrt(cell_count)
-    part = after(part, back, forward)
-
-    moved = gather(part, "zhi")
-    forward = after(forward, part).sum(0).astype(BF16)
+    part, back = lax.optimization_barrier((after(part, forward), back))
+    forward = lax.psum_scatter(forward, "chan", scatter_dimension=0, tiled=True)
+
+    quarter = gather(part, "zhi").reshape(-1, lanes)
+
+    half = gather(quarter, "ring").reshape(-1, lanes)
+    half, forward = lax.optimization_barrier((half, forward))
+    forward = forward[0].astype(BF16)
     output = lax.ppermute(forward, AXES, column_move(sizes, 0, True)).reshape(activations.shape)
-    quarter = moved.reshape(-1, lanes)
-    quarter = after(quarter, output)
-
-    moved = gather(quarter, "ring")
-    back = exchange(after(back, quarter), "space").sum(0).astype(BF16)
-    input_grad = back.reshape(activations.shape)
-    half = moved.reshape(-1, lanes)
-    half = after(half, input_grad)
+    input_grad = back[0].astype(BF16).reshape(activations.shape)
 
     other = lax.ppermute(half, "core", swap)
     first = core[0] == 0

time: 187 us -> 186 us (level)
  the two profiles are of different devices: /device:TPU:1 before, /device:TPU:5 now
where the time goes in v3:
time: 186 us; the launch traced here: 185 us
  starting transfers between devices  77 us (41%)
  waiting for transfers between devices  62.4 us (34%)
  between operations  14 us (8%)
  blocking collectives  12.6 us (7%)
  local copies, waits for them, and re-layouts  6.72 us (4%)
  Pallas kernels  6.27 us (3%)
  other arithmetic  6.04 us (3%)
    all_to_all x5, starting transfers between devices, exchange(): return lax.all_to_all(block, axis, split_axis=0, concat_axis=0, tiled=True)  43.7 us
    all_to_all x5, waiting for transfers between devices, exchange(): return lax.all_to_all(block, axis, split_axis=0, concat_axis=0, tiled=True)  36.1 us
    ppermute x3, starting transfers between devices, shards(): lax.ppermute(output_grad, AXES, column_move(sizes, step, True))  13.7 us
    all_gather x1, blocking collectives, shards(): grad = lax.all_gather(grad, 'chan', axis=1, tiled=True)  12.6 us
    reduce_scatter x1, waiting for transfers between devices, shards(): forward = lax.psum_scatter(forward, 'chan', scatter_dimension=0, tiled=True)  10.6 us
    reduce_scatter x1, waiting for transfers between devices, shards(): back = lax.psum_scatter(back, 'space', scatter_dimension=0, tiled=True)  10.4 us
    ppermute x1, starting transfers between devices, shards(): lax.ppermute(forward, AXES, column_move(sizes, 0, True))  6.06 us
    ppermute x1, starting transfers between devices, shards(): other = lax.ppermute(half, 'core', swap)  5.89 us
  transfers between devices with their start and end apart: 16, of which 7 were waited for; matrix products, arithmetic and copies ran while one was open for 4% of the time, Pallas kernels for 3%

profile of v3, /device:TPU:5, one launch (start us, length us, event | category | flops | bytes accessed | tf_op | source)
XLA Modules:
  0.0 185.0 jit_solution(4287871112949057332)
XLA Ops:
  7.2 3.8 %collective-permute-start.3 = (bf16[1,8,32,128]{3,2,1,0:T(8,128)(2,1)}, bf16[1,8,32,128]{3,2,1,0:T(8,128)(2,1)S(1)}, u32[]{:S(2)}, u32[]{:S(2)}) collective-permute-start(bf16[1,8,32,128]{3,2,1,0:T(8,128)(2,1)} %param.3), channel_id=1, source_target_pairs={{0,4},{1,5},{2,6},{3,7},{4,8},{5,9},{6,10},{7,11},{8,12},{9,13},{1... | collective-permute-start | bytes 196616 | tf_op jit(solution)/shard_map/ppermute | solution.py:187
  10.9 4.6 %collective-permute-start = (bf16[1,8,32,128]{3,2,1,0:T(8,128)(2,1)}, bf16[1,8,32,128]{3,2,1,0:T(8,128)(2,1)S(1)}, u32[]{:S(2)}, u32[]{:S(2)}) collective-permute-start(bf16[1,8,32,128]{3,2,1,0:T(8,128)(2,1)} %param.5), channel_id=1, source_target_pairs={{0,4},{1,132},{2,260},{3,388},{4,8},{5,136},{6,264},{7,392},{8,12}... | collective-permute-start | bytes 196616 | tf_op jit(solution)/shard_map/ppermute | solution.py:185
  15.5 4.3 %collective-permute-start.2 = (bf16[1,8,32,128]{3,2,1,0:T(8,128)(2,1)}, bf16[1,8,32,128]{3,2,1,0:T(8,128)(2,1)S(1)}, u32[]{:S(2)}, u32[]{:S(2)}) collective-permute-start(bf16[1,8,32,128]{3,2,1,0:T(8,128)(2,1)} %param.5), channel_id=1, source_target_pairs={{4,0},{5,128},{6,256},{7,384},{8,4},{9,132},{10,260},{11,388},{12,... | collective-permute-start | bytes 196616 | tf_op jit(solution)/shard_map/ppermute | solution.py:185
  19.8 4.8 %collective-permute-start.1 = (bf16[1,8,32,128]{3,2,1,0:T(8,128)(2,1)}, bf16[1,8,32,128]{3,2,1,0:T(8,128)(2,1)S(1)}, u32[]{:S(2)}, u32[]{:S(2)}) collective-permute-start(bf16[1,8,32,128]{3,2,1,0:T(8,128)(2,1)} %param.5), channel_id=1, source_target_pairs={{0,0},{1,128},{2,256},{3,384},{4,4},{5,132},{6,260},{7,388},{8,8},... | collective-permute-start | bytes 196616 | tf_op jit(solution)/shard_map/ppermute | solution.py:185
  24.7 1.9 %collective-permute-start.4 = (bf16[1,8,32,128]{3,2,1,0:T(8,128)(2,1)}, bf16[1,8,32,128]{3,2,1,0:T(8,128)(2,1)S(1)}, u32[]{:S(2)}, u32[]{:S(2)}) collective-permute-start(bf16[1,8,32,128]{3,2,1,0:T(8,128)(2,1)} %param.3), channel_id=1, source_target_pairs={{4,0},{5,1},{6,2},{7,3},{8,4},{9,5},{10,6},{11,7},{12,8},{13,9},{1... | collective-permute-start | bytes 196616 | tf_op jit(solution)/shard_map/ppermute | solution.py:188
  26.6 1.6 broadcast_in_dim.21
  28.2 3.4 %all-to-all-start = ((bf16[4,8,32,128]{3,2,1,0:T(8,128)(2,1)}), bf16[4,8,32,128]{3,2,1,0:T(8,128)(2,1)S(1)}, u32[]{:S(2)}, u32[]{:S(2)}) async-start(bf16[4,8,32,128]{3,2,1,0:T(8,128)(2,1)} %broadcast_in_dim.21), calls=%async_computation | async-start | bytes 524288 | tf_op jit(solution)/shard_map/all_to_all | solution.py:165
  31.6 0.0 all-gather.2.cloned.1.call-start
  31.6 0.0 collective-permute-done.3
  31.7 0.9 constant_dynamic-update-slice_fusion.2
  32.5 0.0 collective-permute-done.4
  32.6 0.0 copy-start.3
  32.6 0.7 copy-done.3
  33.3 0.0 all-gather.2.cloned.1.call-update
  33.3 0.0 collective-permute-done
  33.3 0.0 collective-permute-done.2
  33.3 0.0 collective-permute-done.1
  33.4 12.6 %all_gather.6.grad.block = bf16[3,32,32,128]{3,2,1,0:T(8,128)(2,1)S(1)} all-gather(bf16[3,8,32,128]{3,2,1,0:T(8,128)(2,1)S(1)} %pad_maximum_fusion.1), channel_id=1, replica_groups=mesh['chan'=4,'zhi'=4,'ring'=4,'core'=2,'space'=4] {'chan'}, dimensions={1}, use_global_device_ids=true | all-gather | bytes 983040 | tf_op jit(solution)/shard_map/all_gather | solution.py:192
  45.9 0.0 all-to-all-done
  46.0 0.0 copy-start.1
  46.0 1.6 filter_grad.1
  47.5 1.9 %collective-permute-start.5 = (f32[1792,128]{1,0:T(8,128)S(1)}, f32[1792,128]{1,0:T(8,128)}, u32[]{:S(2)}, u32[]{:S(2)}) collective-permute-start(f32[1792,128]{1,0:T(8,128)S(1)} %get-tuple-element.17), channel_id=1, source_target_pairs={{0,4},{4,0},{1,5},{5,1},{2,6},{6,2},{3,7},{7,3},{8,12},{12,8},{9,1... | collective-permute-start | bytes 2752520 | tf_op jit(solution)/shard_map/ppermute | solution.py:195
  49.5 0.0 copy-done.1
  49.5 2.4 %input_grad.1 = f32[4,256,128]{2,1,0:T(8,128)} custom-call(bf16[3,32,32,128]{3,2,1,0:T(8,128)(2,1)S(1)} %all_gather.6.grad.block, bf16[27,128,128]{2,1,0:T(8,128)(2,1)S(1)} %copy-done.1), custom_call_target="tpu_custom_call" | custom-call | flops 905969664 | bytes 3145728 | tf_op jit(solution)/shard_map/input_grad/pallas_call | solution.py:93
  51.9 0.2 collective-permute-done.5
  52.0 2.2 %add.7 = f32[1792,128]{1,0:T(8,128)} add(f32[1792,128]{1,0:T(8,128)S(1)} %get-tuple-element.16, f32[1792,128]{1,0:T(8,128)} %collective-permute-done.5) | non-fusion elementwise | flops 229376 | bytes 2752512 | tf_op jit(solution)/shard_map/add | solution.py:197
  54.2 0.0 copy-start.2
  54.2 12.6 %all-to-all-start.1 = ((f32[4,448,128]{2,1,0:T(8,128)}), f32[4,448,128]{2,1,0:T(8,128)S(1)}, u32[]{:S(2)}, u32[]{:S(2)}) async-start(f32[4,448,128]{2,1,0:T(8,128)} %bitcast.3), calls=%async_computation.1 | async-start | bytes 1835008 | tf_op jit(solution)/shard_map/all_to_all | solution.py:165
  66.8 0.0 reduce-scatter.3.cloned.1.call-start
  66.8 0.7 reduce-scatter.3.cloned.1.call-update
  67.6 12.5 %all-to-all-done.1 = f32[4,448,128]{2,1,0:T(8,128)S(1)} async-done(((f32[4,448,128]{2,1,0:T(8,128)}), f32[4,448,128]{2,1,0:T(8,128)S(1)}, u32[]{:S(2)}, u32[]{:S(2)}) %all-to-all-start.1) | async-done | bytes 917536 | tf_op jit(solution)/shard_map/all_to_all | solution.py:165
  80.1 0.7 reduce_sum.18
  80.8 0.0 all-gather.2.cloned.1.call-done.block
  80.8 13.7 %all-to-all-start.2 = ((f32[4,112,128]{2,1,0:T(8,128)}), f32[4,112,128]{2,1,0:T(8,128)S(1)}, u32[]{:S(2)}, u32[]{:S(2)}) async-start(f32[4,112,128]{2,1,0:T(8,128)} %bitcast.4), calls=%async_computation.2 | async-start | bytes 458752 | tf_op jit(solution)/shard_map/all_to_all | solution.py:165
  94.5 0.0 copy-done.2
  94.5 0.0 copy-start
  94.5 1.2 copy-done
  95.8 2.3 %forward.1 = f32[4,256,128]{2,1,0:T(8,128)} custom-call(bf16[4,32,32,128]{3,2,1,0:T(8,128)(2,1)S(1)} %copy-done, bf16[27,128,128]{2,1,0:T(8,128)(2,1)S(1)} %copy-done.2), custom_call_target="tpu_custom_call" | custom-call | flops 905969664 | bytes 3145728 | tf_op jit(solution)/shard_map/forward/pallas_call | solution.py:93
  98.1 9.6 %all-to-all-done.2 = f32[4,112,128]{2,1,0:T(8,128)S(1)} async-done(((f32[4,112,128]{2,1,0:T(8,128)}), f32[4,112,128]{2,1,0:T(8,128)S(1)}, u32[]{:S(2)}, u32[]{:S(2)}) %all-to-all-start.2) | async-done | bytes 229408 | tf_op jit(solution)/shard_map/all_to_all | solution.py:165
  107.7 10.4 %reduce-scatter.3.cloned.1.call-done = f32[1,256,128]{2,1,0:T(8,128)} async-done(((f32[4,256,128]{2,1,0:T(8,128)}), f32[1,256,128]{2,1,0:T(8,128)}) %reduce-scatter.3.cloned.1.call-update) | async-done | bytes 131088 | tf_op jit(solution)/shard_map/reduce_scatter | solution.py:198
  118.1 0.7 broadcast_in_dim.22
  118.8 10.5 %all-to-all-start.3 = ((f32[4,112,128]{2,1,0:T(8,128)}), f32[4,112,128]{2,1,0:T(8,128)S(1)}, u32[]{:S(2)}, u32[]{:S(2)}) async-start(f32[4,112,128]{2,1,0:T(8,128)} %broadcast_in_dim.22), calls=%async_computation.4 | async-start | bytes 458752 | tf_op jit(solution)/shard_map/all_to_all | solution.py:165
  129.3 0.0 copy-start.4
  129.3 0.0 reduce-scatter.5.cloned.1.call-start
  129.3 0.7 reduce-scatter.5.cloned.1.call-update
  130.0 14.0 %all-to-all-done.3 = f32[4,112,128]{2,1,0:T(8,128)S(1)} async-done(((f32[4,112,128]{2,1,0:T(8,128)}), f32[4,112,128]{2,1,0:T(8,128)S(1)}, u32[]{:S(2)}, u32[]{:S(2)}) %all-to-all-start.3) | async-done | bytes 229408 | tf_op jit(solution)/shard_map/all_to_all | solution.py:165
  144.0 1.0 broadcast_in_dim.24
  145.0 3.5 %all-to-all-start.4 = ((f32[4,448,128]{2,1,0:T(8,128)}), f32[4,448,128]{2,1,0:T(8,128)S(1)}, u32[]{:S(2)}, u32[]{:S(2)}) async-start(f32[4,448,128]{2,1,0:T(8,128)} %broadcast_in_dim.24), calls=%async_computation.5 | async-start | bytes 1835008 | tf_op jit(solution)/shard_map/all_to_all | solution.py:165
  148.5 10.6 %reduce-scatter.5.cloned.1.call-done = f32[1,256,128]{2,1,0:T(8,128)} async-done(((f32[4,256,128]{2,1,0:T(8,128)}), f32[1,256,128]{2,1,0:T(8,128)}) %reduce-scatter.5.cloned.1.call-update) | async-done | bytes 131088 | tf_op jit(solution)/shard_map/reduce_scatter | solution.py:208
  159.1 0.0 all-to-all-done.4
  159.1 5.9 %collective-permute-start.7 = (f32[1792,128]{1,0:T(8,128)S(1)}, f32[1792,128]{1,0:T(8,128)S(1)}, u32[]{:S(2)}, u32[]{:S(2)}) collective-permute-start(f32[1792,128]{1,0:T(8,128)S(1)} %bitcast.13), channel_id=1, source_target_pairs={{0,4},{4,0},{1,5},{5,1},{2,6},{6,2},{3,7},{7,3},{8,12},{12,8},{9,1... | collective-permute-start | bytes 2752520 | tf_op jit(solution)/shard_map/ppermute | solution.py:218
  165.0 0.9 convert_bitcast_fusion
  166.0 6.1 %collective-permute-start.6 = (bf16[256,128]{1,0:T(8,128)(2,1)S(1)}, bf16[256,128]{1,0:T(8,128)(2,1)S(1)}, u32[]{:S(2)}, u32[]{:S(2)}) collective-permute-start(bf16[256,128]{1,0:T(8,128)(2,1)S(1)} %convert_bitcast_fusion), channel_id=1, source_target_pairs={{0,0},{1,128},{2,256},{3,384},{4,4},{5,132},{6,260},{7,388},{8,8},... | collective-permute-start | bytes 196616 | tf_op jit(solution)/shard_map/ppermute | solution.py:215
  172.0 0.0 copy-done.4
  172.0 0.6 convert_element_type.21
  172.7 3.6 %collective-permute-done.6 = bf16[256,128]{1,0:T(8,128)(2,1)S(1)} collective-permute-done((bf16[256,128]{1,0:T(8,128)(2,1)S(1)}, bf16[256,128]{1,0:T(8,128)(2,1)S(1)}, u32[]{:S(2)}, u32[]{:S(2)}) %collective-permute-start.6) | collective-permute-done | bytes 65568 | tf_op jit(solution)/shard_map/ppermute | solution.py:215
  176.3 0.0 collective-permute-done.7
  176.3 0.1 slice_select_fusion
  176.4 0.1 broadcast_select_fusion
  176.5 1.3 pad_maximum_fusion
  177.8 0.6 copy.10
  (6 shorter events, 0.1 us)
Async XLA Ops:
  7.2 24.5 %collective-permute-start.3 = (bf16[1,8,32,128]{3,2,1,0:T(8,128)(2,1)}, bf16[1,8,32,128]{3,2,1,0:T(8,128)(2,1)S(1)}, u32[]{:S(2)}, u32[]{:S(2)}) collective-permute-start(bf16[1,8,32,128]{3,2,1,0:T(8,128)(2,1)} %param.3), channel_id=1, source_target_pairs={{0,4},{1,5},{2,6},{3,7},{4,8},{5,9},{6,10},{7,11},{8,12},{9,13},{1... | collective-permute-start | bytes 196616 | tf_op jit(solution)/shard_map/ppermute | solution.py:187
  10.9 22.4 %collective-permute-start = (bf16[1,8,32,128]{3,2,1,0:T(8,128)(2,1)}, bf16[1,8,32,128]{3,2,1,0:T(8,128)(2,1)S(1)}, u32[]{:S(2)}, u32[]{:S(2)}) collective-permute-start(bf16[1,8,32,128]{3,2,1,0:T(8,128)(2,1)} %param.5), channel_id=1, source_target_pairs={{0,4},{1,132},{2,260},{3,388},{4,8},{5,136},{6,264},{7,392},{8,12}... | collective-permute-start | bytes 196616 | tf_op jit(solution)/shard_map/ppermute | solution.py:185
  15.5 17.8 %collective-permute-start.2 = (bf16[1,8,32,128]{3,2,1,0:T(8,128)(2,1)}, bf16[1,8,32,128]{3,2,1,0:T(8,128)(2,1)S(1)}, u32[]{:S(2)}, u32[]{:S(2)}) collective-permute-start(bf16[1,8,32,128]{3,2,1,0:T(8,128)(2,1)} %param.5), channel_id=1, source_target_pairs={{4,0},{5,128},{6,256},{7,384},{8,4},{9,132},{10,260},{11,388},{12,... | collective-permute-start | bytes 196616 | tf_op jit(solution)/shard_map/ppermute | solution.py:185
  19.8 13.5 %collective-permute-start.1 = (bf16[1,8,32,128]{3,2,1,0:T(8,128)(2,1)}, bf16[1,8,32,128]{3,2,1,0:T(8,128)(2,1)S(1)}, u32[]{:S(2)}, u32[]{:S(2)}) collective-permute-start(bf16[1,8,32,128]{3,2,1,0:T(8,128)(2,1)} %param.5), channel_id=1, source_target_pairs={{0,0},{1,128},{2,256},{3,384},{4,4},{5,132},{6,260},{7,388},{8,8},... | collective-permute-start | bytes 196616 | tf_op jit(solution)/shard_map/ppermute | solution.py:185
  24.7 7.9 %collective-permute-start.4 = (bf16[1,8,32,128]{3,2,1,0:T(8,128)(2,1)}, bf16[1,8,32,128]{3,2,1,0:T(8,128)(2,1)S(1)}, u32[]{:S(2)}, u32[]{:S(2)}) collective-permute-start(bf16[1,8,32,128]{3,2,1,0:T(8,128)(2,1)} %param.3), channel_id=1, source_target_pairs={{4,0},{5,1},{6,2},{7,3},{8,4},{9,5},{10,6},{11,7},{12,8},{13,9},{1... | collective-permute-start | bytes 196616 | tf_op jit(solution)/shard_map/ppermute | solution.py:188
  28.2 17.8 %all-to-all-start = ((bf16[4,8,32,128]{3,2,1,0:T(8,128)(2,1)}), bf16[4,8,32,128]{3,2,1,0:T(8,128)(2,1)S(1)}, u32[]{:S(2)}, u32[]{:S(2)}) async-start(bf16[4,8,32,128]{3,2,1,0:T(8,128)(2,1)} %broadcast_in_dim.21), calls=%async_computation | async-start | bytes 524288 | tf_op jit(solution)/shard_map/all_to_all | solution.py:165
  31.6 49.2 %all-gather.2.cloned.1.call-start = ((), (), s32[]{:S(2)}) async-start(), calls=%async_computation.7 | async-start | bytes 1310720 | tf_op jit(solution)/shard_map/all_gather | solution.py:190
  32.6 0.7 copy-start.3
  46.0 3.5 %copy-start.1 = (bf16[27,128,128]{2,1,0:T(8,128)(2,1)S(1)}, bf16[27,128,128]{2,1,0:T(8,128)(2,1)}, u32[]{:S(2)}) copy-start(bf16[27,128,128]{2,1,0:T(8,128)(2,1)} %weight.3) | copy-start | bytes 2654212
  47.5 4.5 %collective-permute-start.5 = (f32[1792,128]{1,0:T(8,128)S(1)}, f32[1792,128]{1,0:T(8,128)}, u32[]{:S(2)}, u32[]{:S(2)}) collective-permute-start(f32[1792,128]{1,0:T(8,128)S(1)} %get-tuple-element.17), channel_id=1, source_target_pairs={{0,4},{4,0},{1,5},{5,1},{2,6},{6,2},{3,7},{7,3},{8,12},{12,8},{9,1... | collective-permute-start | bytes 2752520 | tf_op jit(solution)/shard_map/ppermute | solution.py:195
  54.2 40.3 %copy-start.2 = (bf16[27,128,128]{2,1,0:T(8,128)(2,1)S(1)}, bf16[27,128,128]{2,1,0:T(8,128)(2,1)}, u32[]{:S(2)}) copy-start(bf16[27,128,128]{2,1,0:T(8,128)(2,1)} %weight.3) | copy-start | bytes 2654212
  54.2 25.8 %all-to-all-start.1 = ((f32[4,448,128]{2,1,0:T(8,128)}), f32[4,448,128]{2,1,0:T(8,128)S(1)}, u32[]{:S(2)}, u32[]{:S(2)}) async-start(f32[4,448,128]{2,1,0:T(8,128)} %bitcast.3), calls=%async_computation.1 | async-start | bytes 1835008 | tf_op jit(solution)/shard_map/all_to_all | solution.py:165
  66.8 51.3 %reduce-scatter.3.cloned.1.call-start = ((), (), s32[]{:S(2)}) async-start(), calls=%async_computation.8 | async-start | bytes 655360 | tf_op jit(solution)/shard_map/reduce_scatter | solution.py:198
  80.8 26.9 %all-to-all-start.2 = ((f32[4,112,128]{2,1,0:T(8,128)}), f32[4,112,128]{2,1,0:T(8,128)S(1)}, u32[]{:S(2)}, u32[]{:S(2)}) async-start(f32[4,112,128]{2,1,0:T(8,128)} %bitcast.4), calls=%async_computation.2 | async-start | bytes 458752 | tf_op jit(solution)/shard_map/all_to_all | solution.py:165
  94.5 1.2 copy-start
  118.8 25.2 %all-to-all-start.3 = ((f32[4,112,128]{2,1,0:T(8,128)}), f32[4,112,128]{2,1,0:T(8,128)S(1)}, u32[]{:S(2)}, u32[]{:S(2)}) async-start(f32[4,112,128]{2,1,0:T(8,128)} %broadcast_in_dim.22), calls=%async_computation.4 | async-start | bytes 458752 | tf_op jit(solution)/shard_map/all_to_all | solution.py:165
  129.3 42.7 %copy-start.4 = (f32[1,256,128]{2,1,0:T(8,128)S(1)}, f32[1,256,128]{2,1,0:T(8,128)}, u32[]{:S(2)}) copy-start(f32[1,256,128]{2,1,0:T(8,128)} %reduce-scatter.3.cloned.1.call-done) | copy-start | bytes 393220
  129.3 29.8 %reduce-scatter.5.cloned.1.call-start = ((), (), s32[]{:S(2)}) async-start(), calls=%async_computation.9 | async-start | bytes 655360 | tf_op jit(solution)/shard_map/reduce_scatter | solution.py:208
  145.0 14.1 %all-to-all-start.4 = ((f32[4,448,128]{2,1,0:T(8,128)}), f32[4,448,128]{2,1,0:T(8,128)S(1)}, u32[]{:S(2)}, u32[]{:S(2)}) async-start(f32[4,448,128]{2,1,0:T(8,128)} %broadcast_in_dim.24), calls=%async_computation.5 | async-start | bytes 1835008 | tf_op jit(solution)/shard_map/all_to_all | solution.py:165
  159.1 17.1 %collective-permute-start.7 = (f32[1792,128]{1,0:T(8,128)S(1)}, f32[1792,128]{1,0:T(8,128)S(1)}, u32[]{:S(2)}, u32[]{:S(2)}) collective-permute-start(f32[1792,128]{1,0:T(8,128)S(1)} %bitcast.13), channel_id=1, source_target_pairs={{0,4},{4,0},{1,5},{5,1},{2,6},{6,2},{3,7},{7,3},{8,12},{12,8},{9,1... | collective-permute-start | bytes 2752520 | tf_op jit(solution)/shard_map/ppermute | solution.py:218
  166.0 10.3 %collective-permute-start.6 = (bf16[256,128]{1,0:T(8,128)(2,1)S(1)}, bf16[256,128]{1,0:T(8,128)(2,1)S(1)}, u32[]{:S(2)}, u32[]{:S(2)}) collective-permute-start(bf16[256,128]{1,0:T(8,128)(2,1)S(1)} %convert_bitcast_fusion), channel_id=1, source_target_pairs={{0,0},{1,128},{2,256},{3,384},{4,4},{5,132},{6,260},{7,388},{8,8},... | collective-permute-start | bytes 196616 | tf_op jit(solution)/shard_map/ppermute | solution.py:215
Sparse Core Ops, SparseCore 0:
  34.5 45.5 all-gather.1
  83.0 35.0 reduce-scatter.2
  132.9 26.1 reduce-scatter.4

commit v4 on v3

--- a/solution.py
+++ b/solution.py
@@ -50,17 +50,24 @@
 
 
 def fill_padded(padded, block):
-    _, planes, height, lanes = block.shape
-    columns = padded.shape[0]
+    columns, planes, height, lanes = padded.shape
+    planes -= 2
     zero = jnp.zeros((columns, 1, height, lanes), BF16)
     padded[:, 0:1] = zero
     padded[:, planes + 1 : planes + 2] = zero
-    padded[:, 1 : planes + 1] = block[0:columns]
-
-
-def conv_kernel(backward, block, weight, out, padded, flat):
-    slabs, rows, lanes = out.shape
-    height = block.shape[2]
+    if len(block.shape) == 4:
+        padded[:, 1 : planes + 1] = block[...]
+    else:
+        slabs, _, depth = block.shape[:3]
+        for slab in range(slabs):
+            padded[:, 1 + slab * depth : 1 + (slab + 1) * depth] = block[slab]
+
+
+def conv_kernel(backward, me, block, weight, *refs):
+    *outs, padded, flat = refs
+    slabs = len(outs)
+    rows, lanes = outs[0].shape
+    height = block.shape[-2]
     planes = rows // height
     fill_padded(padded, block)
     for cell in range(9):
@@ -69,13 +76,14 @@
                 flat[r * lanes : (r + 1) * lanes, cell * lanes : (cell + 1) * lanes] = weight[3 * cell + r]
             else:
                 flat[cell * lanes : (cell + 1) * lanes, r * lanes : (r + 1) * lanes] = weight[3 * cell + r]
-    for slab in range(slabs):
+    for step, out in enumerate(outs):
+        slab = lax.rem(me[0] + step, slabs)
         pieces = []
         for p in range(3):
             for q in range(3):
                 column, plane = (2 - p, 2 - q) if backward else (p, q)
                 start = slab * planes + plane
-                pieces.append(padded[column, start : start + planes].reshape(rows, lanes))
+                pieces.append(padded[column, pl.ds(start, planes)].reshape(rows, lanes))
         lhs = jnp.concatenate(pieces, axis=1)
         dims = (((1,), (1 if backward else 0,)), ((), ()))
         taps = lax.dot_general(lhs, flat[...], dims, preferred_element_type=F32)
@@ -83,35 +91,36 @@
         total = taps[:, lanes : 2 * lanes]
         total += shifted(taps[:, low * lanes : (low + 1) * lanes], height, -1)
         total += shifted(taps[:, high * lanes : (high + 1) * lanes], height, 1)
-        out[slab] = total
-
-
-def convolve(backward, block, weight, slabs):
-    _, planes, height, lanes = block.shape
-    rows = planes * height
+        out[...] = total
+
+
+def convolve(backward, block, weight, slabs, me):
+    height, lanes = block.shape[-2:]
+    rows = block.size // (3 * lanes)
+    planes = rows // height
     flat = (3 * lanes, 9 * lanes) if backward else (9 * lanes, 3 * lanes)
     return pl.pallas_call(
         functools.partial(conv_kernel, backward),
-        out_shape=jax.ShapeDtypeStruct((slabs, rows // slabs, lanes), F32),
-        in_specs=[VMEM, VMEM],
-        out_specs=VMEM,
+        out_shape=[jax.ShapeDtypeStruct((rows // slabs, lanes), F32)] * slabs,
+        in_specs=[SMEM, VMEM, VMEM],
+        out_specs=[VMEM] * slabs,
         scratch_shapes=[
             pltpu.VMEM((3, planes + 2, height, lanes), BF16),
             pltpu.VMEM(flat, BF16),
         ],
-        compiler_params=pltpu.CompilerParams(vmem_limit_bytes=40 << 20),
+        compiler_params=pltpu.CompilerParams(vmem_limit_bytes=14 << 20),
         cost_estimate=pl.CostEstimate(
             flops=2 * 27 * rows * lanes * lanes, bytes_accessed=3 << 20, transcendentals=0
         ),
         name="input_grad" if backward else "forward",
-    )(block, weight)
+    )(me, block, weight)
 
 
 def filter_kernel(core, data, grad, keep, send, padded, turned, taps):
-    planes, height, lanes = data.shape
+    planes, height, lanes = grad.shape[1:]
     rows = planes * height
     fill_padded(padded, grad)
-    flat = data[...].reshape(rows, lanes).astype(F32)
+    flat = data[:, 1].reshape(rows, lanes).astype(F32)
     turned[0:lanes] = shifted(flat, height, -1).T.astype(BF16)
     turned[lanes : 2 * lanes] = flat.T.astype(BF16)
     turned[2 * lanes : 3 * lanes] = shifted(flat, height, 1).T.astype(BF16)
@@ -140,7 +149,7 @@
 
 
 def filter_partial(data, grad, core):
-    planes, height, lanes = data.shape
+    planes, height, lanes = grad.shape[1:]
     rows = planes * height
     half = jax.ShapeDtypeStruct((14 * lanes, lanes), F32)
     return pl.pallas_call(
@@ -153,7 +162,7 @@
             pltpu.VMEM((3 * lanes, rows), BF16),
             pltpu.VMEM((28 * lanes, lanes), F32),
         ],
-        compiler_params=pltpu.CompilerParams(vmem_limit_bytes=40 << 20),
+        compiler_params=pltpu.CompilerParams(vmem_limit_bytes=14 << 20),
         cost_estimate=pl.CostEstimate(
             flops=2 * 27 * rows * lanes * lanes, bytes_accessed=3 << 20, transcendentals=0
         ),
@@ -170,6 +179,14 @@
     return exchange(jnp.broadcast_to(block[None], (count, *block.shape)), axis)
 
 
+def reduced(blocks, axis):
+    count = len(blocks)
+    total = blocks[0]
+    for step in range(1, count):
+        total += lax.ppermute(blocks[step], axis, [(i, (i + step) % count) for i in range(count)])
+    return total
+
+
 def after(value, *others):
     return lax.optimization_barrier((value, *others))[0]
 
@@ -180,40 +197,38 @@
     core = lax.axis_index("core").reshape(1)
     swap = [(0, 1), (1, 0)]
 
-    own = gather(activations[0], "space").reshape(-1, height, lanes)
-    grads = [
-        lax.ppermute(output_grad, AXES, column_move(sizes, step, True)) for step in (1, 0, -1)
-    ]
     low = lax.ppermute(activations, AXES, column_move(sizes, 1, False))
     high = lax.ppermute(activations, AXES, column_move(sizes, -1, False))
-    sides = jnp.concatenate([low, activations, high, low], axis=0)
-    data = lax.all_gather(sides, "space", axis=1, tiled=True)
-    grad = after(jnp.concatenate(grads, axis=0), sides)
+    sides = jnp.concatenate([low, activations, high], axis=0)
+    data = gather(sides, "space")
+    cotangent = after(output_grad, sides)
+    grads = [lax.ppermute(cotangent, AXES, column_move(sizes, step, True)) for step in (1, 0, -1)]
+    grad = jnp.concatenate(grads, axis=0)
     grad = lax.all_gather(grad, "chan", axis=1, tiled=True)
 
-    keep, send = filter_partial(own, grad, core)
+    keep, send = filter_partial(data, grad, core)
     moved = lax.ppermute(send, "core", swap)
-    back = convolve(True, after(grad, send), weight, spaces)
-    half = after(keep + moved, back)
-    back = lax.psum_scatter(back, "space", scatter_dimension=0, tiled=True)
+    me = lax.axis_index("space").reshape(1)
+    back = convolve(True, after(grad, send), weight, spaces, me)
+    half, *back = lax.optimization_barrier((keep + moved, *back))
 
     moved = exchange(half.reshape(rings, -1, lanes), "ring")
-    quarter, data = lax.optimization_barrier((moved.sum(0), data))
+    input_grad = reduced(back, "space").astype(BF16).reshape(activations.shape)
+    quarter, input_grad = lax.optimization_barrier((moved.sum(0), input_grad))
 
     moved = exchange(quarter.reshape(zhis, -1, lanes), "zhi")
-    forward = convolve(False, data, weight, spaces)
+    me = lax.axis_index("chan").reshape(1)
+    forward = convolve(False, after(data, quarter), weight, spaces, me)
+    forward = reduced(forward, "chan").astype(BF16)
     cell_count = sizes[1] * rings * cores * grad.shape[1] * grad.shape[2]
     part = moved.sum(0) / math.sqrt(cell_count)
-    part, back = lax.optimization_barrier((after(part, forward), back))
-    forward = lax.psum_scatter(forward, "chan", scatter_dimension=0, tiled=True)
+    part, forward = lax.optimization_barrier((part, forward))
 
     quarter = gather(part, "zhi").reshape(-1, lanes)
+    output = lax.ppermute(forward, AXES, column_move(sizes, 0, True)).reshape(activations.shape)
+    quarter, output = lax.optimization_barrier((quarter, output))
 
     half = gather(quarter, "ring").reshape(-1, lanes)
-    half, forward = lax.optimization_barrier((half, forward))
-    forward = forward[0].astype(BF16)
-    output = lax.ppermute(forward, AXES, column_move(sizes, 0, True)).reshape(activations.shape)
-    input_grad = back[0].astype(BF16).reshape(activations.shape)
 
     other = lax.ppermute(half, "core", swap)
     first = core[0] == 0

time: 186 us -> 184 us (0.989)
  the two profiles are of different devices: /device:TPU:5 before, /device:TPU:33 now
where the time goes in v4:
time: 184 us; the launch traced here: 183 us
  starting transfers between devices  93.8 us (51%)
  blocking collectives  36.9 us (20%)
  waiting for transfers between devices  35.4 us (19%)
  local copies, waits for them, and re-layouts  6.41 us (3%)
  other arithmetic  5.22 us (3%)
  Pallas kernels  4.76 us (3%)
    all_to_all x4, starting transfers between devices, exchange(): return lax.all_to_all(block, axis, split_axis=0, concat_axis=0, tiled=True)  38.1 us
    all_gather x1, blocking collectives, shards(): grad = lax.all_gather(grad, 'chan', axis=1, tiled=True)  23.8 us
    ppermute x6, starting transfers between devices, reduced(): lax.ppermute(blocks[step], axis, [(i, (i + step) % count) for i in range(...  18.1 us
    ppermute x1, starting transfers between devices, shards(): other = lax.ppermute(half, 'core', swap)  14.5 us
    all_to_all x1, blocking collectives, exchange(): return lax.all_to_all(block, axis, split_axis=0, concat_axis=0, tiled=True)  13.1 us
    ppermute x6, waiting for transfers between devices, reduced(): lax.ppermute(blocks[step], axis, [(i, (i + step) % count) for i in range(...  11.8 us
    ppermute x3, starting transfers between devices, shards(): lax.ppermute(cotangent, AXES, column_move(sizes, step, True))  10.5 us
    ppermute x1, waiting for transfers between devices, shards(): lax.ppermute(forward, AXES, column_move(sizes, 0, True))  9.53 us
  transfers between devices with their start and end apart: 18, of which 10 were waited for; matrix products, arithmetic and copies ran while one was open for 1% of the time, Pallas kernels for 2%

profile of v4, /device:TPU:33, one launch (start us, length us, event | category | flops | bytes accessed | tf_op | source)
XLA Modules:
  0.0 183.4 jit_solution(7091753467451414120)
XLA Ops:
  0.6 0.0 copy-start.8
  0.6 3.9 %collective-permute-start = (bf16[1,8,32,128]{3,2,1,0:T(8,128)(2,1)}, bf16[1,8,32,128]{3,2,1,0:T(8,128)(2,1)S(1)}, u32[]{:S(2)}, u32[]{:S(2)}) collective-permute-start(bf16[1,8,32,128]{3,2,1,0:T(8,128)(2,1)} %param.3), channel_id=1, source_target_pairs={{0,4},{1,5},{2,6},{3,7},{4,8},{5,9},{6,10},{7,11},{8,12},{9,13},{1... | collective-permute-start | bytes 196616 | tf_op jit(solution)/shard_map/ppermute | solution.py:200
  4.5 1.9 %collective-permute-start.1 = (bf16[1,8,32,128]{3,2,1,0:T(8,128)(2,1)}, bf16[1,8,32,128]{3,2,1,0:T(8,128)(2,1)S(1)}, u32[]{:S(2)}, u32[]{:S(2)}) collective-permute-start(bf16[1,8,32,128]{3,2,1,0:T(8,128)(2,1)} %param.3), channel_id=1, source_target_pairs={{4,0},{5,1},{6,2},{7,3},{8,4},{9,5},{10,6},{11,7},{12,8},{13,9},{1... | collective-permute-start | bytes 196616 | tf_op jit(solution)/shard_map/ppermute | solution.py:201
  6.5 0.0 collective-permute-done
  6.5 0.9 constant_dynamic-update-slice_fusion.1
  7.4 3.0 %collective-permute-done.1 = bf16[1,8,32,128]{3,2,1,0:T(8,128)(2,1)S(1)} collective-permute-done((bf16[1,8,32,128]{3,2,1,0:T(8,128)(2,1)}, bf16[1,8,32,128]{3,2,1,0:T(8,128)(2,1)S(1)}, u32[]{:S(2)}, u32[]{:S(2)}) %collective-permute-start.1) | collective-permute-done | bytes 65568 | tf_op jit(solution)/shard_map/ppermute | solution.py:201
  10.4 1.0 broadcast_in_dim.6
  11.4 5.4 %all-to-all-start = ((bf16[4,3,8,32,128]{4,3,2,1,0:T(8,128)(2,1)}), bf16[4,3,8,32,128]{4,3,2,1,0:T(8,128)(2,1)S(1)}, u32[]{:S(2)}, u32[]{:S(2)}) async-start(bf16[4,3,8,32,128]{4,3,2,1,0:T(8,128)(2,1)} %broadcast_in_dim.6), calls=%async_computation | async-start | bytes 1572864 | tf_op jit(solution)/shard_map/all_to_all | solution.py:174
  16.8 0.0 copy-done.8
  16.8 1.9 %collective-permute-start.4 = (bf16[1,8,32,128]{3,2,1,0:T(8,128)(2,1)S(1)}, bf16[1,8,32,128]{3,2,1,0:T(8,128)(2,1)S(1)}, u32[]{:S(2)}, u32[]{:S(2)}) collective-permute-start(bf16[1,8,32,128]{3,2,1,0:T(8,128)(2,1)S(1)} %copy-done.8), channel_id=1, source_target_pairs={{4,0},{5,128},{6,256},{7,384},{8,4},{9,132},{10,260},{11,388},{12,... | collective-permute-start | bytes 196616 | tf_op jit(solution)/shard_map/ppermute | solution.py:205
  18.7 3.4 %collective-permute-start.3 = (bf16[1,8,32,128]{3,2,1,0:T(8,128)(2,1)S(1)}, bf16[1,8,32,128]{3,2,1,0:T(8,128)(2,1)S(1)}, u32[]{:S(2)}, u32[]{:S(2)}) collective-permute-start(bf16[1,8,32,128]{3,2,1,0:T(8,128)(2,1)S(1)} %copy-done.8), channel_id=1, source_target_pairs={{0,0},{1,128},{2,256},{3,384},{4,4},{5,132},{6,260},{7,388},{8,8},... | collective-permute-start | bytes 196616 | tf_op jit(solution)/shard_map/ppermute | solution.py:205
  22.2 5.1 %collective-permute-start.2 = (bf16[1,8,32,128]{3,2,1,0:T(8,128)(2,1)S(1)}, bf16[1,8,32,128]{3,2,1,0:T(8,128)(2,1)S(1)}, u32[]{:S(2)}, u32[]{:S(2)}) collective-permute-start(bf16[1,8,32,128]{3,2,1,0:T(8,128)(2,1)S(1)} %copy-done.8), channel_id=1, source_target_pairs={{0,4},{1,132},{2,260},{3,388},{4,8},{5,136},{6,264},{7,392},{8,12}... | collective-permute-start | bytes 196616 | tf_op jit(solution)/shard_map/ppermute | solution.py:205
  27.3 5.4 %collective-permute-done.4 = bf16[1,8,32,128]{3,2,1,0:T(8,128)(2,1)S(1)} collective-permute-done((bf16[1,8,32,128]{3,2,1,0:T(8,128)(2,1)S(1)}, bf16[1,8,32,128]{3,2,1,0:T(8,128)(2,1)S(1)}, u32[]{:S(2)}, u32[]{:S(2)}) %collective-permute-start.4) | collective-permute-done | bytes 65568 | tf_op jit(solution)/shard_map/ppermute | solution.py:205
  32.7 0.0 collective-permute-done.3
  32.7 0.0 collective-permute-done.2
  32.8 23.8 %all_gather.3.grad.block = bf16[3,32,32,128]{3,2,1,0:T(8,128)(2,1)S(1)} all-gather(bf16[3,8,32,128]{3,2,1,0:T(8,128)(2,1)S(1)} %pad_maximum_fusion.1), channel_id=1, replica_groups=mesh['chan'=4,'zhi'=4,'ring'=4,'core'=2,'space'=4] {'chan'}, dimensions={1}, use_global_device_ids=true | all-gather | bytes 983040 | tf_op jit(solution)/shard_map/all_gather | solution.py:207
  56.6 0.0 all-to-all-done.data.block
  56.6 1.6 filter_grad.1
  58.1 3.8 %collective-permute-start.5 = (f32[1792,128]{1,0:T(8,128)S(1)}, f32[1792,128]{1,0:T(8,128)}, u32[]{:S(2)}, u32[]{:S(2)}) collective-permute-start(f32[1792,128]{1,0:T(8,128)S(1)} %get-tuple-element.29), channel_id=1, source_target_pairs={{0,4},{4,0},{1,5},{5,1},{2,6},{6,2},{3,7},{7,3},{8,12},{12,8},{9,1... | collective-permute-start | bytes 2752520 | tf_op jit(solution)/shard_map/ppermute | solution.py:210
  61.9 0.0 copy-start
  61.9 1.2 copy-done
  63.1 1.6 input_grad.1
  64.7 0.0 copy-start.2
  64.7 0.6 copy-done.2
  65.4 0.6 copy-done.4
  66.0 0.7 copy-done.6
  66.6 0.0 collective-permute-done.5
  66.7 2.2 %add.21 = f32[1792,128]{1,0:T(8,128)} add(f32[1792,128]{1,0:T(8,128)S(1)} %get-tuple-element.28, f32[1792,128]{1,0:T(8,128)} %collective-permute-done.5) | non-fusion elementwise | flops 229376 | bytes 2752512 | tf_op jit(solution)/shard_map/add | solution.py:213
  68.9 10.1 %all-to-all-start.1 = ((f32[4,448,128]{2,1,0:T(8,128)}), f32[4,448,128]{2,1,0:T(8,128)S(1)}, u32[]{:S(2)}, u32[]{:S(2)}) async-start(f32[4,448,128]{2,1,0:T(8,128)} %bitcast.13), calls=%async_computation.1 | async-start | bytes 1835008 | tf_op jit(solution)/shard_map/all_to_all | solution.py:174
  79.0 0.0 copy-done.7
  79.1 1.9 %collective-permute-start.6 = (f32[256,128]{1,0:T(8,128)S(1)}, f32[256,128]{1,0:T(8,128)S(1)}, u32[]{:S(2)}, u32[]{:S(2)}) collective-permute-start(f32[256,128]{1,0:T(8,128)S(1)} %copy-done.7), channel_id=1, source_target_pairs={{0,1},{1,2},{2,3},{3,0},{4,5},{5,6},{6,7},{7,4},{8,9},{9,10},{10,1... | collective-permute-start | bytes 393224 | tf_op jit(solution)/shard_map/ppermute | solution.py:186
  81.0 0.0 copy-done.5
  81.0 5.3 %collective-permute-start.7 = (f32[256,128]{1,0:T(8,128)S(1)}, f32[256,128]{1,0:T(8,128)S(1)}, u32[]{:S(2)}, u32[]{:S(2)}) collective-permute-start(f32[256,128]{1,0:T(8,128)S(1)} %copy-done.5), channel_id=1, source_target_pairs={{0,2},{1,3},{2,0},{3,1},{4,6},{5,7},{6,4},{7,5},{8,10},{9,11},{10,... | collective-permute-start | bytes 393224 | tf_op jit(solution)/shard_map/ppermute | solution.py:186
  86.3 0.0 copy-done.3
  86.3 1.9 %collective-permute-start.8 = (f32[256,128]{1,0:T(8,128)S(1)}, f32[256,128]{1,0:T(8,128)S(1)}, u32[]{:S(2)}, u32[]{:S(2)}) collective-permute-start(f32[256,128]{1,0:T(8,128)S(1)} %copy-done.3), channel_id=1, source_target_pairs={{0,3},{1,0},{2,1},{3,2},{4,7},{5,4},{6,5},{7,6},{8,11},{9,8},{10,9... | collective-permute-start | bytes 393224 | tf_op jit(solution)/shard_map/ppermute | solution.py:186
  88.3 0.0 collective-permute-done.6
  88.3 5.5 %collective-permute-done.7 = f32[256,128]{1,0:T(8,128)S(1)} collective-permute-done((f32[256,128]{1,0:T(8,128)S(1)}, f32[256,128]{1,0:T(8,128)S(1)}, u32[]{:S(2)}, u32[]{:S(2)}) %collective-permute-start.7) | collective-permute-done | bytes 131104 | tf_op jit(solution)/shard_map/ppermute | solution.py:186
  93.8 3.0 %collective-permute-done.8 = f32[256,128]{1,0:T(8,128)S(1)} collective-permute-done((f32[256,128]{1,0:T(8,128)S(1)}, f32[256,128]{1,0:T(8,128)S(1)}, u32[]{:S(2)}, u32[]{:S(2)}) %collective-permute-start.8) | collective-permute-done | bytes 131104 | tf_op jit(solution)/shard_map/ppermute | solution.py:186
  96.8 0.7 add_convert_fusion.1
  97.5 0.0 all-to-all-done.1
  97.5 0.7 reduce_sum.18
  98.2 14.0 %all-to-all-start.2 = ((f32[4,112,128]{2,1,0:T(8,128)}), f32[4,112,128]{2,1,0:T(8,128)S(1)}, u32[]{:S(2)}, u32[]{:S(2)}) async-start(f32[4,112,128]{2,1,0:T(8,128)} %bitcast.4), calls=%async_computation.2 | async-start | bytes 458752 | tf_op jit(solution)/shard_map/all_to_all | solution.py:174
  112.2 0.0 copy-done.1
  112.2 1.6 forward.1
  113.8 1.9 %collective-permute-start.9 = (f32[256,128]{1,0:T(8,128)S(1)}, f32[256,128]{1,0:T(8,128)S(1)}, u32[]{:S(2)}, u32[]{:S(2)}) collective-permute-start(f32[256,128]{1,0:T(8,128)S(1)} %get-tuple-element.43), channel_id=1, source_target_pairs={{0,128},{128,256},{256,384},{384,0},{1,129},{129,257},{257,385},{3... | collective-permute-start | bytes 393224 | tf_op jit(solution)/shard_map/ppermute | solution.py:186
  115.7 4.3 %collective-permute-start.10 = (f32[256,128]{1,0:T(8,128)S(1)}, f32[256,128]{1,0:T(8,128)S(1)}, u32[]{:S(2)}, u32[]{:S(2)}) collective-permute-start(f32[256,128]{1,0:T(8,128)S(1)} %get-tuple-element.44), channel_id=1, source_target_pairs={{0,256},{128,384},{256,0},{384,128},{1,257},{129,385},{257,1},{385... | collective-permute-start | bytes 393224 | tf_op jit(solution)/shard_map/ppermute | solution.py:186
  120.0 2.7 %collective-permute-start.11 = (f32[256,128]{1,0:T(8,128)S(1)}, f32[256,128]{1,0:T(8,128)S(1)}, u32[]{:S(2)}, u32[]{:S(2)}) collective-permute-start(f32[256,128]{1,0:T(8,128)S(1)} %get-tuple-element.45), channel_id=1, source_target_pairs={{0,384},{128,0},{256,128},{384,256},{1,385},{129,1},{257,129},{385... | collective-permute-start | bytes 393224 | tf_op jit(solution)/shard_map/ppermute | solution.py:186
  122.8 0.0 collective-permute-done.9
  122.8 1.0 collective-permute-done.10
  123.8 2.3 %collective-permute-done.11 = f32[256,128]{1,0:T(8,128)S(1)} collective-permute-done((f32[256,128]{1,0:T(8,128)S(1)}, f32[256,128]{1,0:T(8,128)S(1)}, u32[]{:S(2)}, u32[]{:S(2)}) %collective-permute-start.11) | collective-permute-done | bytes 131104 | tf_op jit(solution)/shard_map/ppermute | solution.py:186
  126.1 3.2 %all-to-all-done.2 = f32[4,112,128]{2,1,0:T(8,128)S(1)} async-done(((f32[4,112,128]{2,1,0:T(8,128)}), f32[4,112,128]{2,1,0:T(8,128)S(1)}, u32[]{:S(2)}, u32[]{:S(2)}) %all-to-all-start.2) | async-done | bytes 229408 | tf_op jit(solution)/shard_map/all_to_all | solution.py:174
  129.3 0.7 broadcast_in_dim.7
  130.0 8.6 %all-to-all-start.3 = ((f32[4,112,128]{2,1,0:T(8,128)}), f32[4,112,128]{2,1,0:T(8,128)S(1)}, u32[]{:S(2)}, u32[]{:S(2)}) async-start(f32[4,112,128]{2,1,0:T(8,128)} %broadcast_in_dim.7), calls=%async_computation.3 | async-start | bytes 458752 | tf_op jit(solution)/shard_map/all_to_all | solution.py:174
  138.6 3.0 %collective-permute-start.12 = (bf16[256,128]{1,0:T(8,128)(2,1)S(1)}, bf16[256,128]{1,0:T(8,128)(2,1)S(1)}, u32[]{:S(2)}, u32[]{:S(2)}) collective-permute-start(bf16[256,128]{1,0:T(8,128)(2,1)S(1)} %add_convert_fusion), channel_id=1, source_target_pairs={{0,0},{1,128},{2,256},{3,384},{4,4},{5,132},{6,260},{7,388},{8,8},... | collective-permute-start | bytes 196616 | tf_op jit(solution)/shard_map/ppermute | solution.py:228
  141.6 9.5 %collective-permute-done.12 = bf16[256,128]{1,0:T(8,128)(2,1)S(1)} collective-permute-done((bf16[256,128]{1,0:T(8,128)(2,1)S(1)}, bf16[256,128]{1,0:T(8,128)(2,1)S(1)}, u32[]{:S(2)}, u32[]{:S(2)}) %collective-permute-start.12) | collective-permute-done | bytes 65568 | tf_op jit(solution)/shard_map/ppermute | solution.py:228
  151.1 0.5 all-to-all-done.3
  151.5 0.1 broadcast_in_dim.8
  151.6 13.1 %all_to_all.25 = f32[4,448,128]{2,1,0:T(8,128)S(1)} all-to-all(f32[4,448,128]{2,1,0:T(8,128)S(1)} %broadcast_in_dim.8), channel_id=1, replica_groups=mesh['chan'=4,'zhi'=4,'ring'=4,'core'=2,'space'=4] {'ring'}, dimensions={0} | all-to-all | bytes 1835008 | tf_op jit(solution)/shard_map/all_to_all | solution.py:174
  164.7 14.5 %collective-permute-start.13 = (f32[1792,128]{1,0:T(8,128)S(1)}, f32[1792,128]{1,0:T(8,128)S(1)}, u32[]{:S(2)}, u32[]{:S(2)}) collective-permute-start(f32[1792,128]{1,0:T(8,128)S(1)} %bitcast.11), channel_id=1, source_target_pairs={{0,4},{4,0},{1,5},{5,1},{2,6},{6,2},{3,7},{7,3},{8,12},{12,8},{9,1... | collective-permute-start | bytes 2752520 | tf_op jit(solution)/shard_map/ppermute | solution.py:233
  179.2 2.1 %collective-permute-done.13 = f32[1792,128]{1,0:T(8,128)S(1)} collective-permute-done((f32[1792,128]{1,0:T(8,128)S(1)}, f32[1792,128]{1,0:T(8,128)S(1)}, u32[]{:S(2)}, u32[]{:S(2)}) %collective-permute-start.13) | collective-permute-done | bytes 917536 | tf_op jit(solution)/shard_map/ppermute | solution.py:233
  181.3 0.1 slice_select_fusion
  181.4 0.1 broadcast_select_fusion
  181.5 1.3 pad_maximum_fusion
  182.8 0.6 copy.9
  (12 shorter events, 0.1 us)
Async XLA Ops:
  0.6 16.2 %copy-start.8 = (bf16[1,8,32,128]{3,2,1,0:T(8,128)(2,1)S(1)}, bf16[1,8,32,128]{3,2,1,0:T(8,128)(2,1)}, u32[]{:S(2)}) copy-start(bf16[1,8,32,128]{3,2,1,0:T(8,128)(2,1)} %param.5) | copy-start | bytes 196612
  0.6 5.8 %collective-permute-start = (bf16[1,8,32,128]{3,2,1,0:T(8,128)(2,1)}, bf16[1,8,32,128]{3,2,1,0:T(8,128)(2,1)S(1)}, u32[]{:S(2)}, u32[]{:S(2)}) collective-permute-start(bf16[1,8,32,128]{3,2,1,0:T(8,128)(2,1)} %param.3), channel_id=1, source_target_pairs={{0,4},{1,5},{2,6},{3,7},{4,8},{5,9},{6,10},{7,11},{8,12},{9,13},{1... | collective-permute-start | bytes 196616 | tf_op jit(solution)/shard_map/ppermute | solution.py:200
  4.5 5.8 %collective-permute-start.1 = (bf16[1,8,32,128]{3,2,1,0:T(8,128)(2,1)}, bf16[1,8,32,128]{3,2,1,0:T(8,128)(2,1)S(1)}, u32[]{:S(2)}, u32[]{:S(2)}) collective-permute-start(bf16[1,8,32,128]{3,2,1,0:T(8,128)(2,1)} %param.3), channel_id=1, source_target_pairs={{4,0},{5,1},{6,2},{7,3},{8,4},{9,5},{10,6},{11,7},{12,8},{13,9},{1... | collective-permute-start | bytes 196616 | tf_op jit(solution)/shard_map/ppermute | solution.py:201
  11.4 45.2 %all-to-all-start = ((bf16[4,3,8,32,128]{4,3,2,1,0:T(8,128)(2,1)}), bf16[4,3,8,32,128]{4,3,2,1,0:T(8,128)(2,1)S(1)}, u32[]{:S(2)}, u32[]{:S(2)}) async-start(bf16[4,3,8,32,128]{4,3,2,1,0:T(8,128)(2,1)} %broadcast_in_dim.6), calls=%async_computation | async-start | bytes 1572864 | tf_op jit(solution)/shard_map/all_to_all | solution.py:174
  16.8 15.9 %collective-permute-start.4 = (bf16[1,8,32,128]{3,2,1,0:T(8,128)(2,1)S(1)}, bf16[1,8,32,128]{3,2,1,0:T(8,128)(2,1)S(1)}, u32[]{:S(2)}, u32[]{:S(2)}) collective-permute-start(bf16[1,8,32,128]{3,2,1,0:T(8,128)(2,1)S(1)} %copy-done.8), channel_id=1, source_target_pairs={{4,0},{5,128},{6,256},{7,384},{8,4},{9,132},{10,260},{11,388},{12,... | collective-permute-start | bytes 196616 | tf_op jit(solution)/shard_map/ppermute | solution.py:205
  18.7 14.0 %collective-permute-start.3 = (bf16[1,8,32,128]{3,2,1,0:T(8,128)(2,1)S(1)}, bf16[1,8,32,128]{3,2,1,0:T(8,128)(2,1)S(1)}, u32[]{:S(2)}, u32[]{:S(2)}) collective-permute-start(bf16[1,8,32,128]{3,2,1,0:T(8,128)(2,1)S(1)} %copy-done.8), channel_id=1, source_target_pairs={{0,0},{1,128},{2,256},{3,384},{4,4},{5,132},{6,260},{7,388},{8,8},... | collective-permute-start | bytes 196616 | tf_op jit(solution)/shard_map/ppermute | solution.py:205
  22.2 10.6 %collective-permute-start.2 = (bf16[1,8,32,128]{3,2,1,0:T(8,128)(2,1)S(1)}, bf16[1,8,32,128]{3,2,1,0:T(8,128)(2,1)S(1)}, u32[]{:S(2)}, u32[]{:S(2)}) collective-permute-start(bf16[1,8,32,128]{3,2,1,0:T(8,128)(2,1)S(1)} %copy-done.8), channel_id=1, source_target_pairs={{0,4},{1,132},{2,260},{3,388},{4,8},{5,136},{6,264},{7,392},{8,12}... | collective-permute-start | bytes 196616 | tf_op jit(solution)/shard_map/ppermute | solution.py:205
  58.1 8.5 %collective-permute-start.5 = (f32[1792,128]{1,0:T(8,128)S(1)}, f32[1792,128]{1,0:T(8,128)}, u32[]{:S(2)}, u32[]{:S(2)}) collective-permute-start(f32[1792,128]{1,0:T(8,128)S(1)} %get-tuple-element.29), channel_id=1, source_target_pairs={{0,4},{4,0},{1,5},{5,1},{2,6},{6,2},{3,7},{7,3},{8,12},{12,8},{9,1... | collective-permute-start | bytes 2752520 | tf_op jit(solution)/shard_map/ppermute | solution.py:210
  61.9 1.2 copy-start
  64.7 0.7 copy-start.2
  65.3 0.6 copy-start.4
  66.0 0.7 copy-start.6
  66.6 12.4 %copy-start.7 = (f32[256,128]{1,0:T(8,128)S(1)}, f32[256,128]{1,0:T(8,128)}, u32[]{:S(2)}) copy-start(f32[256,128]{1,0:T(8,128)} %copy-done.6) | copy-start | bytes 393220
  66.7 14.3 %copy-start.5 = (f32[256,128]{1,0:T(8,128)S(1)}, f32[256,128]{1,0:T(8,128)}, u32[]{:S(2)}) copy-start(f32[256,128]{1,0:T(8,128)} %copy-done.4) | copy-start | bytes 393220
  66.7 19.7 %copy-start.3 = (f32[256,128]{1,0:T(8,128)S(1)}, f32[256,128]{1,0:T(8,128)}, u32[]{:S(2)}) copy-start(f32[256,128]{1,0:T(8,128)} %copy-done.2) | copy-start | bytes 393220
  68.9 43.3 %copy-start.1 = (bf16[27,128,128]{2,1,0:T(8,128)(2,1)S(1)}, bf16[27,128,128]{2,1,0:T(8,128)(2,1)}, u32[]{:S(2)}) copy-start(bf16[27,128,128]{2,1,0:T(8,128)(2,1)} %weight.3) | copy-start | bytes 2654212
  68.9 28.6 %all-to-all-start.1 = ((f32[4,448,128]{2,1,0:T(8,128)}), f32[4,448,128]{2,1,0:T(8,128)S(1)}, u32[]{:S(2)}, u32[]{:S(2)}) async-start(f32[4,448,128]{2,1,0:T(8,128)} %bitcast.13), calls=%async_computation.1 | async-start | bytes 1835008 | tf_op jit(solution)/shard_map/all_to_all | solution.py:174
  79.1 9.2 %collective-permute-start.6 = (f32[256,128]{1,0:T(8,128)S(1)}, f32[256,128]{1,0:T(8,128)S(1)}, u32[]{:S(2)}, u32[]{:S(2)}) collective-permute-start(f32[256,128]{1,0:T(8,128)S(1)} %copy-done.7), channel_id=1, source_target_pairs={{0,1},{1,2},{2,3},{3,0},{4,5},{5,6},{6,7},{7,4},{8,9},{9,10},{10,1... | collective-permute-start | bytes 393224 | tf_op jit(solution)/shard_map/ppermute | solution.py:186
  81.0 12.8 %collective-permute-start.7 = (f32[256,128]{1,0:T(8,128)S(1)}, f32[256,128]{1,0:T(8,128)S(1)}, u32[]{:S(2)}, u32[]{:S(2)}) collective-permute-start(f32[256,128]{1,0:T(8,128)S(1)} %copy-done.5), channel_id=1, source_target_pairs={{0,2},{1,3},{2,0},{3,1},{4,6},{5,7},{6,4},{7,5},{8,10},{9,11},{10,... | collective-permute-start | bytes 393224 | tf_op jit(solution)/shard_map/ppermute | solution.py:186
  86.3 10.5 %collective-permute-start.8 = (f32[256,128]{1,0:T(8,128)S(1)}, f32[256,128]{1,0:T(8,128)S(1)}, u32[]{:S(2)}, u32[]{:S(2)}) collective-permute-start(f32[256,128]{1,0:T(8,128)S(1)} %copy-done.3), channel_id=1, source_target_pairs={{0,3},{1,0},{2,1},{3,2},{4,7},{5,4},{6,5},{7,6},{8,11},{9,8},{10,9... | collective-permute-start | bytes 393224 | tf_op jit(solution)/shard_map/ppermute | solution.py:186
  98.2 31.1 %all-to-all-start.2 = ((f32[4,112,128]{2,1,0:T(8,128)}), f32[4,112,128]{2,1,0:T(8,128)S(1)}, u32[]{:S(2)}, u32[]{:S(2)}) async-start(f32[4,112,128]{2,1,0:T(8,128)} %bitcast.4), calls=%async_computation.2 | async-start | bytes 458752 | tf_op jit(solution)/shard_map/all_to_all | solution.py:174
  113.8 9.0 %collective-permute-start.9 = (f32[256,128]{1,0:T(8,128)S(1)}, f32[256,128]{1,0:T(8,128)S(1)}, u32[]{:S(2)}, u32[]{:S(2)}) collective-permute-start(f32[256,128]{1,0:T(8,128)S(1)} %get-tuple-element.43), channel_id=1, source_target_pairs={{0,128},{128,256},{256,384},{384,0},{1,129},{129,257},{257,385},{3... | collective-permute-start | bytes 393224 | tf_op jit(solution)/shard_map/ppermute | solution.py:186
  115.7 8.1 %collective-permute-start.10 = (f32[256,128]{1,0:T(8,128)S(1)}, f32[256,128]{1,0:T(8,128)S(1)}, u32[]{:S(2)}, u32[]{:S(2)}) collective-permute-start(f32[256,128]{1,0:T(8,128)S(1)} %get-tuple-element.44), channel_id=1, source_target_pairs={{0,256},{128,384},{256,0},{384,128},{1,257},{129,385},{257,1},{385... | collective-permute-start | bytes 393224 | tf_op jit(solution)/shard_map/ppermute | solution.py:186
  120.0 6.0 %collective-permute-start.11 = (f32[256,128]{1,0:T(8,128)S(1)}, f32[256,128]{1,0:T(8,128)S(1)}, u32[]{:S(2)}, u32[]{:S(2)}) collective-permute-start(f32[256,128]{1,0:T(8,128)S(1)} %get-tuple-element.45), channel_id=1, source_target_pairs={{0,384},{128,0},{256,128},{384,256},{1,385},{129,1},{257,129},{385... | collective-permute-start | bytes 393224 | tf_op jit(solution)/shard_map/ppermute | solution.py:186
  130.0 21.6 %all-to-all-start.3 = ((f32[4,112,128]{2,1,0:T(8,128)}), f32[4,112,128]{2,1,0:T(8,128)S(1)}, u32[]{:S(2)}, u32[]{:S(2)}) async-start(f32[4,112,128]{2,1,0:T(8,128)} %broadcast_in_dim.7), calls=%async_computation.3 | async-start | bytes 458752 | tf_op jit(solution)/shard_map/all_to_all | solution.py:174
  138.6 12.5 %collective-permute-start.12 = (bf16[256,128]{1,0:T(8,128)(2,1)S(1)}, bf16[256,128]{1,0:T(8,128)(2,1)S(1)}, u32[]{:S(2)}, u32[]{:S(2)}) collective-permute-start(bf16[256,128]{1,0:T(8,128)(2,1)S(1)} %add_convert_fusion), channel_id=1, source_target_pairs={{0,0},{1,128},{2,256},{3,384},{4,4},{5,132},{6,260},{7,388},{8,8},... | collective-permute-start | bytes 196616 | tf_op jit(solution)/shard_map/ppermute | solution.py:228
  164.7 16.6 %collective-permute-start.13 = (f32[1792,128]{1,0:T(8,128)S(1)}, f32[1792,128]{1,0:T(8,128)S(1)}, u32[]{:S(2)}, u32[]{:S(2)}) collective-permute-start(f32[1792,128]{1,0:T(8,128)S(1)} %bitcast.11), channel_id=1, source_target_pairs={{0,4},{4,0},{1,5},{5,1},{2,6},{6,2},{3,7},{7,3},{8,12},{12,8},{9,1... | collective-permute-start | bytes 2752520 | tf_op jit(solution)/shard_map/ppermute | solution.py:233

commit v5 on v3

--- a/solution.py
+++ b/solution.py
@@ -25,17 +25,21 @@
     return pairs
 
 
-def column_move(sizes, step, swap):
+def outer_neighbour(sizes):
     _, zhis, rings, cores, _ = sizes
 
     def move(chan, zhi, ring, core, space):
-        column = (zhi * rings + ring) * cores + core + step
+        column = (zhi * rings + ring) * cores + core
+        column += 1 if column % 2 else -1
         if not 0 <= column < zhis * rings * cores:
             return None
-        rest = (column // (rings * cores), column // cores % rings, column % cores)
-        return (space, *rest, chan) if swap else (chan, *rest, space)
+        return (chan, column // (rings * cores), column // cores % rings, column % cores, space)
 
     return permutation(sizes, move)
+
+
+def transposed(sizes):
+    return permutation(sizes, lambda chan, zhi, ring, core, space: (space, zhi, ring, core, chan))
 
 
 def height_mask(rows, height, at):
@@ -49,20 +53,27 @@
     return jnp.where(height_mask(rows, height, edge), 0.0, rolled)
 
 
-def fill_padded(padded, block):
-    _, planes, height, lanes = block.shape
-    columns = padded.shape[0]
+def fill_padded(padded, block, core):
+    columns, planes, height, lanes = padded.shape
+    planes -= 2
     zero = jnp.zeros((columns, 1, height, lanes), BF16)
     padded[:, 0:1] = zero
     padded[:, planes + 1 : planes + 2] = zero
-    padded[:, 1 : planes + 1] = block[0:columns]
-
-
-def conv_kernel(backward, block, weight, out, padded, flat):
+    low = 2 - core
+    for column, source in enumerate((low, 0, 3 - low)):
+        if len(block.shape) == 4:
+            padded[column, 1 : planes + 1] = block[source]
+        else:
+            slabs, _, depth = block.shape[:3]
+            for slab in range(slabs):
+                padded[column, 1 + slab * depth : 1 + (slab + 1) * depth] = block[slab, source]
+
+
+def conv_kernel(backward, core, block, weight, out, padded, flat):
     slabs, rows, lanes = out.shape
-    height = block.shape[2]
+    height = block.shape[-2]
     planes = rows // height
-    fill_padded(padded, block)
+    fill_padded(padded, block, core[0])
     for cell in range(9):
         for r in range(3):
             if backward:
@@ -86,32 +97,33 @@
         out[slab] = total
 
 
-def convolve(backward, block, weight, slabs):
-    _, planes, height, lanes = block.shape
-    rows = planes * height
+def convolve(backward, core, block, weight, slabs):
+    height, lanes = block.shape[-2:]
+    rows = block.size // (3 * lanes)
+    planes = rows // height
     flat = (3 * lanes, 9 * lanes) if backward else (9 * lanes, 3 * lanes)
     return pl.pallas_call(
         functools.partial(conv_kernel, backward),
         out_shape=jax.ShapeDtypeStruct((slabs, rows // slabs, lanes), F32),
-        in_specs=[VMEM, VMEM],
+        in_specs=[SMEM, VMEM, VMEM],
         out_specs=VMEM,
         scratch_shapes=[
             pltpu.VMEM((3, planes + 2, height, lanes), BF16),
             pltpu.VMEM(flat, BF16),
         ],
-        compiler_params=pltpu.CompilerParams(vmem_limit_bytes=40 << 20),
+        compiler_params=pltpu.CompilerParams(vmem_limit_bytes=14 << 20),
         cost_estimate=pl.CostEstimate(
             flops=2 * 27 * rows * lanes * lanes, bytes_accessed=3 << 20, transcendentals=0
         ),
         name="input_grad" if backward else "forward",
-    )(block, weight)
+    )(core, block, weight)
 
 
 def filter_kernel(core, data, grad, keep, send, padded, turned, taps):
-    planes, height, lanes = data.shape
+    planes, height, lanes = grad.shape[1:]
     rows = planes * height
-    fill_padded(padded, grad)
-    flat = data[...].reshape(rows, lanes).astype(F32)
+    fill_padded(padded, grad, core[0])
+    flat = data[:, 0].reshape(rows, lanes).astype(F32)
     turned[0:lanes] = shifted(flat, height, -1).T.astype(BF16)
     turned[lanes : 2 * lanes] = flat.T.astype(BF16)
     turned[2 * lanes : 3 * lanes] = shifted(flat, height, 1).T.astype(BF16)
@@ -140,7 +152,7 @@
 
 
 def filter_partial(data, grad, core):
-    planes, height, lanes = data.shape
+    planes, height, lanes = grad.shape[1:]
     rows = planes * height
     half = jax.ShapeDtypeStruct((14 * lanes, lanes), F32)
     return pl.pallas_call(
@@ -153,7 +165,7 @@
             pltpu.VMEM((3 * lanes, rows), BF16),
             pltpu.VMEM((28 * lanes, lanes), F32),
         ],
-        compiler_params=pltpu.CompilerParams(vmem_limit_bytes=40 << 20),
+        compiler_params=pltpu.CompilerParams(vmem_limit_bytes=14 << 20),
         cost_estimate=pl.CostEstimate(
             flops=2 * 27 * rows * lanes * lanes, bytes_accessed=3 << 20, transcendentals=0
         ),
@@ -180,40 +192,34 @@
     core = lax.axis_index("core").reshape(1)
     swap = [(0, 1), (1, 0)]
 
-    own = gather(activations[0], "space").reshape(-1, height, lanes)
-    grads = [
-        lax.ppermute(output_grad, AXES, column_move(sizes, step, True)) for step in (1, 0, -1)
-    ]
-    low = lax.ppermute(activations, AXES, column_move(sizes, 1, False))
-    high = lax.ppermute(activations, AXES, column_move(sizes, -1, False))
-    sides = jnp.concatenate([low, activations, high, low], axis=0)
-    data = lax.all_gather(sides, "space", axis=1, tiled=True)
-    grad = after(jnp.concatenate(grads, axis=0), sides)
+    both = jnp.concatenate([activations, output_grad], axis=0)
+    inner = lax.ppermute(both, "core", swap)
+    outer = lax.ppermute(both, AXES, outer_neighbour(sizes))
+    data = gather(jnp.concatenate([activations, inner[:1], outer[:1]], axis=0), "space")
+    grad = jnp.concatenate([output_grad, inner[1:], outer[1:]], axis=0)
+    grad = lax.ppermute(grad, AXES, transposed(sizes))
     grad = lax.all_gather(grad, "chan", axis=1, tiled=True)
 
-    keep, send = filter_partial(own, grad, core)
+    keep, send = filter_partial(data, grad, core)
     moved = lax.ppermute(send, "core", swap)
-    back = convolve(True, after(grad, send), weight, spaces)
-    half = after(keep + moved, back)
+    back = convolve(True, core, after(grad, send), weight, spaces)
+    forward = convolve(False, core, after(data, back), weight, spaces)
+    half, back, forward = lax.optimization_barrier((keep + moved, back, forward))
     back = lax.psum_scatter(back, "space", scatter_dimension=0, tiled=True)
-
-    moved = exchange(half.reshape(rings, -1, lanes), "ring")
-    quarter, data = lax.optimization_barrier((moved.sum(0), data))
-
-    moved = exchange(quarter.reshape(zhis, -1, lanes), "zhi")
-    forward = convolve(False, data, weight, spaces)
+    forward = lax.psum_scatter(forward, "chan", scatter_dimension=0, tiled=True)
+
+    quarter = exchange(half.reshape(rings, -1, lanes), "ring").sum(0)
+    part = exchange(quarter.reshape(zhis, -1, lanes), "zhi").sum(0)
     cell_count = sizes[1] * rings * cores * grad.shape[1] * grad.shape[2]
-    part = moved.sum(0) / math.sqrt(cell_count)
-    part, back = lax.optimization_barrier((after(part, forward), back))
-    forward = lax.psum_scatter(forward, "chan", scatter_dimension=0, tiled=True)
+    part = part / math.sqrt(cell_count)
+    part, forward = lax.optimization_barrier((part, forward))
 
     quarter = gather(part, "zhi").reshape(-1, lanes)
-
+    output = lax.ppermute(forward[0].astype(BF16), AXES, transposed(sizes))
+    output = output.reshape(activations.shape)
+    quarter, back, output = lax.optimization_barrier((quarter, back, output))
+    input_grad = back[0].astype(BF16).reshape(activations.shape)
     half = gather(quarter, "ring").reshape(-1, lanes)
-    half, forward = lax.optimization_barrier((half, forward))
-    forward = forward[0].astype(BF16)
-    output = lax.ppermute(forward, AXES, column_move(sizes, 0, True)).reshape(activations.shape)
-    input_grad = back[0].astype(BF16).reshape(activations.shape)
 
     other = lax.ppermute(half, "core", swap)
     first = core[0] == 0

time: 186 us -> 190 us (1.022)
  the two profiles are of different devices: /device:TPU:5 before, /device:TPU:1 now
where the time goes in v5:
time: 190 us; the launch traced here: 189 us
  waiting for transfers between devices  56 us (29%)
  starting transfers between devices  50.2 us (26%)
  blocking collectives  49.7 us (26%)
  between operations  14.2 us (7%)
  other arithmetic  6.9 us (4%)
  Pallas kernels  6.3 us (3%)
  local copies, waits for them, and re-layouts  5.31 us (3%)
    all_gather x1, blocking collectives, shards(): grad = lax.all_gather(grad, 'chan', axis=1, tiled=True)  35.8 us
    all_to_all x4, starting transfers between devices, exchange(): return lax.all_to_all(block, axis, split_axis=0, concat_axis=0, tiled=True)  30.7 us
    all_to_all x4, waiting for transfers between devices, exchange(): return lax.all_to_all(block, axis, split_axis=0, concat_axis=0, tiled=True)  26 us
    reduce_scatter x1, waiting for transfers between devices, shards(): back = lax.psum_scatter(back, 'space', scatter_dimension=0, tiled=True)  22.8 us
    all_to_all x1, blocking collectives, exchange(): return lax.all_to_all(block, axis, split_axis=0, concat_axis=0, tiled=True)  13.9 us
    ppermute x1, starting transfers between devices, shards(): inner = lax.ppermute(both, 'core', swap)  8.92 us
    ppermute x1, starting transfers between devices, shards(): other = lax.ppermute(half, 'core', swap)  5.06 us
    pallas_call x2, Pallas kernels, convolve(): pl.pallas_call(functools.partial(conv_kernel, backward), out_shape=jax.Sh...  4.72 us
  transfers between devices with their start and end apart: 12, of which 5 were waited for; matrix products, arithmetic and copies ran while one was open for 2% of the time, Pallas kernels for 3%

profile of v5, /device:TPU:1, one launch (start us, length us, event | category | flops | bytes accessed | tf_op | source)
XLA Modules:
  0.0 188.7 jit_solution(6778411328918710875)
XLA Ops:
  7.2 0.8 constant_dynamic-update-slice_fusion.1
  8.0 0.9 constant_dynamic-update-slice_fusion
  8.9 0.0 copy-start.2
  8.9 8.9 %collective-permute-start = (bf16[2,8,32,128]{3,2,1,0:T(8,128)(2,1)S(1)}, bf16[2,8,32,128]{3,2,1,0:T(8,128)(2,1)S(1)}, u32[]{:S(2)}, u32[]{:S(2)}) collective-permute-start(bf16[2,8,32,128]{3,2,1,0:T(8,128)(2,1)S(1)} %constant_dynamic-update-slice_fusion), channel_id=1, source_target_pairs={{0,4},{4,0},{1,5},{5,1},{2,6},{6,2},{3,7},{7,3},{8,12},{12,8},{9,1... | collective-permute-start | bytes 393224 | tf_op jit(solution)/shard_map/ppermute | solution.py:196
  17.8 1.9 %collective-permute-start.1 = (bf16[2,8,32,128]{3,2,1,0:T(8,128)(2,1)S(1)}, bf16[2,8,32,128]{3,2,1,0:T(8,128)(2,1)S(1)}, u32[]{:S(2)}, u32[]{:S(2)}) collective-permute-start(bf16[2,8,32,128]{3,2,1,0:T(8,128)(2,1)S(1)} %constant_dynamic-update-slice_fusion), channel_id=1, source_target_pairs={{4,8},{5,9},{6,10},{7,11},{8,4},{9,5},{10,6},{11,7},{12,16},{13,17... | collective-permute-start | bytes 393224 | tf_op jit(solution)/shard_map/ppermute | solution.py:197
  19.7 0.0 collective-permute-done
  19.8 4.3 %collective-permute-done.1 = bf16[2,8,32,128]{3,2,1,0:T(8,128)(2,1)S(1)} collective-permute-done((bf16[2,8,32,128]{3,2,1,0:T(8,128)(2,1)S(1)}, bf16[2,8,32,128]{3,2,1,0:T(8,128)(2,1)S(1)}, u32[]{:S(2)}, u32[]{:S(2)}) %collective-permute-start.1) | collective-permute-done | bytes 131104 | tf_op jit(solution)/shard_map/ppermute | solution.py:197
  24.1 0.9 pad_maximum_fusion.1
  25.0 1.0 broadcast_in_dim.6
  26.0 3.5 %all-to-all-start = ((bf16[4,3,8,32,128]{4,3,2,1,0:T(8,128)(2,1)}), bf16[4,3,8,32,128]{4,3,2,1,0:T(8,128)(2,1)S(1)}, u32[]{:S(2)}, u32[]{:S(2)}) async-start(bf16[4,3,8,32,128]{4,3,2,1,0:T(8,128)(2,1)} %broadcast_in_dim.6), calls=%async_computation | async-start | bytes 1572864 | tf_op jit(solution)/shard_map/all_to_all | solution.py:177
  29.5 0.0 copy-done.2
  29.5 0.7 collective-permute-start.2
  30.2 0.0 collective-permute-done.2
  30.2 35.8 %all_gather.3.grad.block = bf16[3,32,32,128]{3,2,1,0:T(8,128)(2,1)S(1)} all-gather(bf16[3,8,32,128]{3,2,1,0:T(8,128)(2,1)S(1)} %collective-permute-done.2), channel_id=1, replica_groups=mesh['chan'=4,'zhi'=4,'ring'=4,'core'=2,'space'=4] {'chan'}, dimensions={1}, use_global_device_ids=true | all-gather | bytes 983040 | tf_op jit(solution)/shard_map/all_gather | solution.py:201
  66.1 0.0 all-to-all-done.data.block
  66.1 0.0 copy-start
  66.1 1.6 filter_grad.1
  67.7 2.3 %collective-permute-start.3 = (f32[1792,128]{1,0:T(8,128)S(1)}, f32[1792,128]{1,0:T(8,128)}, u32[]{:S(2)}, u32[]{:S(2)}) collective-permute-start(f32[1792,128]{1,0:T(8,128)S(1)} %get-tuple-element.16), channel_id=1, source_target_pairs={{0,4},{4,0},{1,5},{5,1},{2,6},{6,2},{3,7},{7,3},{8,12},{12,8},{9,1... | collective-permute-start | bytes 2752520 | tf_op jit(solution)/shard_map/ppermute | solution.py:204
  70.0 0.0 copy-done
  70.0 2.4 %input_grad.1 = f32[4,256,128]{2,1,0:T(8,128)} custom-call(s32[1]{0:T(128)} %bitcast.core, bf16[3,32,32,128]{3,2,1,0:T(8,128)(2,1)S(1)} %all_gather.3.grad.block, bf16[27,128,128]{2,1,0:T(8,128)(2,1)S(1)} %copy-done), custom_call_target="tpu_custom_call" | custom-call | flops 905969664 | bytes 3145728 | tf_op jit(solution)/shard_map/input_grad/pallas_call | solution.py:105
  72.4 0.0 copy-start.1
  72.4 1.2 copy-done.1
  73.5 2.3 %forward.1 = f32[4,256,128]{2,1,0:T(8,128)} custom-call(s32[1]{0:T(128)} %bitcast.core, bf16[4,3,8,32,128]{4,3,2,1,0:T(8,128)(2,1)S(1)} %all-to-all-done.data.block, bf16[27,128,128]{2,1,0:T(8,128)(2,1)S(1)} %copy-done.1), custom_call_target="tpu_custom_call" | custom-call | flops 905969664 | bytes 3145728 | tf_op jit(solution)/shard_map/forward/pallas_call | solution.py:105
  75.9 0.0 collective-permute-done.3
  75.9 2.2 %add.7 = f32[1792,128]{1,0:T(8,128)} add(f32[1792,128]{1,0:T(8,128)S(1)} %get-tuple-element.15, f32[1792,128]{1,0:T(8,128)} %collective-permute-done.3) | non-fusion elementwise | flops 229376 | bytes 2752512 | tf_op jit(solution)/shard_map/add | solution.py:207
  78.1 7.7 %all-to-all-start.1 = ((f32[4,448,128]{2,1,0:T(8,128)}), f32[4,448,128]{2,1,0:T(8,128)S(1)}, u32[]{:S(2)}, u32[]{:S(2)}) async-start(f32[4,448,128]{2,1,0:T(8,128)} %bitcast.1), calls=%async_computation.1 | async-start | bytes 1835008 | tf_op jit(solution)/shard_map/all_to_all | solution.py:177
  85.8 0.0 reduce-scatter.3.cloned.1.call-start
  85.8 0.7 reduce-scatter.3.cloned.1.call-update
  86.5 12.8 %all-to-all-done.1 = f32[4,448,128]{2,1,0:T(8,128)S(1)} async-done(((f32[4,448,128]{2,1,0:T(8,128)}), f32[4,448,128]{2,1,0:T(8,128)S(1)}, u32[]{:S(2)}, u32[]{:S(2)}) %all-to-all-start.1) | async-done | bytes 917536 | tf_op jit(solution)/shard_map/all_to_all | solution.py:177
  99.3 0.7 reduce_sum.18
  100.1 13.1 %all-to-all-start.2 = ((f32[4,112,128]{2,1,0:T(8,128)}), f32[4,112,128]{2,1,0:T(8,128)S(1)}, u32[]{:S(2)}, u32[]{:S(2)}) async-start(f32[4,112,128]{2,1,0:T(8,128)} %bitcast.2), calls=%async_computation.2 | async-start | bytes 458752 | tf_op jit(solution)/shard_map/all_to_all | solution.py:177
  113.2 0.0 reduce-scatter.5.cloned.1.call-start
  113.2 0.7 reduce-scatter.5.cloned.1.call-update
  114.0 13.2 %all-to-all-done.2 = f32[4,112,128]{2,1,0:T(8,128)S(1)} async-done(((f32[4,112,128]{2,1,0:T(8,128)}), f32[4,112,128]{2,1,0:T(8,128)S(1)}, u32[]{:S(2)}, u32[]{:S(2)}) %all-to-all-start.2) | async-done | bytes 229408 | tf_op jit(solution)/shard_map/all_to_all | solution.py:177
  127.2 0.0 reduce-scatter.3.cloned.1.call-done
  127.2 0.7 broadcast_in_dim.7
  127.9 6.3 %all-to-all-start.3 = ((f32[4,112,128]{2,1,0:T(8,128)}), f32[4,112,128]{2,1,0:T(8,128)S(1)}, u32[]{:S(2)}, u32[]{:S(2)}) async-start(f32[4,112,128]{2,1,0:T(8,128)} %broadcast_in_dim.7), calls=%async_computation.4 | async-start | bytes 458752 | tf_op jit(solution)/shard_map/all_to_all | solution.py:177
  134.2 0.9 convert_bitcast_fusion
  135.1 0.7 collective-permute-start.4
  135.8 22.8 %reduce-scatter.5.cloned.1.call-done = f32[1,256,128]{2,1,0:T(8,128)} async-done(((f32[4,256,128]{2,1,0:T(8,128)}), f32[1,256,128]{2,1,0:T(8,128)}) %reduce-scatter.5.cloned.1.call-update) | async-done | bytes 131088 | tf_op jit(solution)/shard_map/reduce_scatter | solution.py:208
  158.6 0.0 copy-start.3
  158.6 0.0 collective-permute-done.4
  158.6 0.0 all-to-all-done.3
  158.6 0.1 broadcast_in_dim.8
  158.6 13.9 %all_to_all.25 = f32[4,448,128]{2,1,0:T(8,128)S(1)} all-to-all(f32[4,448,128]{2,1,0:T(8,128)S(1)} %broadcast_in_dim.8), channel_id=1, replica_groups=mesh['chan'=4,'zhi'=4,'ring'=4,'core'=2,'space'=4] {'ring'}, dimensions={0} | all-to-all | bytes 1835008 | tf_op jit(solution)/shard_map/all_to_all | solution.py:177
  172.5 5.1 %collective-permute-start.5 = (f32[1792,128]{1,0:T(8,128)S(1)}, f32[1792,128]{1,0:T(8,128)S(1)}, u32[]{:S(2)}, u32[]{:S(2)}) collective-permute-start(f32[1792,128]{1,0:T(8,128)S(1)} %bitcast.11), channel_id=1, source_target_pairs={{0,4},{4,0},{1,5},{5,1},{2,6},{6,2},{3,7},{7,3},{8,12},{12,8},{9,1... | collective-permute-start | bytes 2752520 | tf_op jit(solution)/shard_map/ppermute | solution.py:224
  177.6 0.0 copy-done.3
  177.6 0.6 convert_element_type.21
  178.3 1.4 collective-permute-done.5
  179.7 0.1 broadcast_select_fusion
  179.8 0.1 slice_select_fusion
  179.9 1.3 pad_maximum_fusion
  181.2 0.6 copy.8
  (5 shorter events, 0.1 us)
Async XLA Ops:
  8.9 20.6 %copy-start.2 = (bf16[1,8,32,128]{3,2,1,0:T(8,128)(2,1)S(1)}, bf16[1,8,32,128]{3,2,1,0:T(8,128)(2,1)}, u32[]{:S(2)}) copy-start(bf16[1,8,32,128]{3,2,1,0:T(8,128)(2,1)} %param.5) | copy-start | bytes 196612
  8.9 10.9 %collective-permute-start = (bf16[2,8,32,128]{3,2,1,0:T(8,128)(2,1)S(1)}, bf16[2,8,32,128]{3,2,1,0:T(8,128)(2,1)S(1)}, u32[]{:S(2)}, u32[]{:S(2)}) collective-permute-start(bf16[2,8,32,128]{3,2,1,0:T(8,128)(2,1)S(1)} %constant_dynamic-update-slice_fusion), channel_id=1, source_target_pairs={{0,4},{4,0},{1,5},{5,1},{2,6},{6,2},{3,7},{7,3},{8,12},{12,8},{9,1... | collective-permute-start | bytes 393224 | tf_op jit(solution)/shard_map/ppermute | solution.py:196
  17.8 6.3 %collective-permute-start.1 = (bf16[2,8,32,128]{3,2,1,0:T(8,128)(2,1)S(1)}, bf16[2,8,32,128]{3,2,1,0:T(8,128)(2,1)S(1)}, u32[]{:S(2)}, u32[]{:S(2)}) collective-permute-start(bf16[2,8,32,128]{3,2,1,0:T(8,128)(2,1)S(1)} %constant_dynamic-update-slice_fusion), channel_id=1, source_target_pairs={{4,8},{5,9},{6,10},{7,11},{8,4},{9,5},{10,6},{11,7},{12,16},{13,17... | collective-permute-start | bytes 393224 | tf_op jit(solution)/shard_map/ppermute | solution.py:197
  26.0 40.1 %all-to-all-start = ((bf16[4,3,8,32,128]{4,3,2,1,0:T(8,128)(2,1)}), bf16[4,3,8,32,128]{4,3,2,1,0:T(8,128)(2,1)S(1)}, u32[]{:S(2)}, u32[]{:S(2)}) async-start(bf16[4,3,8,32,128]{4,3,2,1,0:T(8,128)(2,1)} %broadcast_in_dim.6), calls=%async_computation | async-start | bytes 1572864 | tf_op jit(solution)/shard_map/all_to_all | solution.py:177
  29.5 0.7 collective-permute-start.2
  66.1 3.9 %copy-start = (bf16[27,128,128]{2,1,0:T(8,128)(2,1)S(1)}, bf16[27,128,128]{2,1,0:T(8,128)(2,1)}, u32[]{:S(2)}) copy-start(bf16[27,128,128]{2,1,0:T(8,128)(2,1)} %weight.3) | copy-start | bytes 2654212
  67.7 8.2 %collective-permute-start.3 = (f32[1792,128]{1,0:T(8,128)S(1)}, f32[1792,128]{1,0:T(8,128)}, u32[]{:S(2)}, u32[]{:S(2)}) collective-permute-start(f32[1792,128]{1,0:T(8,128)S(1)} %get-tuple-element.16), channel_id=1, source_target_pairs={{0,4},{4,0},{1,5},{5,1},{2,6},{6,2},{3,7},{7,3},{8,12},{12,8},{9,1... | collective-permute-start | bytes 2752520 | tf_op jit(solution)/shard_map/ppermute | solution.py:204
  72.4 1.2 copy-start.1
  78.1 21.3 %all-to-all-start.1 = ((f32[4,448,128]{2,1,0:T(8,128)}), f32[4,448,128]{2,1,0:T(8,128)S(1)}, u32[]{:S(2)}, u32[]{:S(2)}) async-start(f32[4,448,128]{2,1,0:T(8,128)} %bitcast.1), calls=%async_computation.1 | async-start | bytes 1835008 | tf_op jit(solution)/shard_map/all_to_all | solution.py:177
  85.8 41.4 %reduce-scatter.3.cloned.1.call-start = ((), (), s32[]{:S(2)}) async-start(), calls=%async_computation.7 | async-start | bytes 655360 | tf_op jit(solution)/shard_map/reduce_scatter | solution.py:209
  100.1 27.0 %all-to-all-start.2 = ((f32[4,112,128]{2,1,0:T(8,128)}), f32[4,112,128]{2,1,0:T(8,128)S(1)}, u32[]{:S(2)}, u32[]{:S(2)}) async-start(f32[4,112,128]{2,1,0:T(8,128)} %bitcast.2), calls=%async_computation.2 | async-start | bytes 458752 | tf_op jit(solution)/shard_map/all_to_all | solution.py:177
  113.2 45.3 %reduce-scatter.5.cloned.1.call-start = ((), (), s32[]{:S(2)}) async-start(), calls=%async_computation.8 | async-start | bytes 655360 | tf_op jit(solution)/shard_map/reduce_scatter | solution.py:208
  127.9 30.7 %all-to-all-start.3 = ((f32[4,112,128]{2,1,0:T(8,128)}), f32[4,112,128]{2,1,0:T(8,128)S(1)}, u32[]{:S(2)}, u32[]{:S(2)}) async-start(f32[4,112,128]{2,1,0:T(8,128)} %broadcast_in_dim.7), calls=%async_computation.4 | async-start | bytes 458752 | tf_op jit(solution)/shard_map/all_to_all | solution.py:177
  135.1 23.4 %collective-permute-start.4 = (bf16[256,128]{1,0:T(8,128)(2,1)S(1)}, bf16[256,128]{1,0:T(8,128)(2,1)S(1)}, u32[]{:S(2)}, u32[]{:S(2)}) collective-permute-start(bf16[256,128]{1,0:T(8,128)(2,1)S(1)} %convert_bitcast_fusion), channel_id=1, source_target_pairs={{0,0},{1,128},{2,256},{3,384},{4,4},{5,132},{6,260},{7,388},{8,8},... | collective-permute-start | bytes 196616 | tf_op jit(solution)/shard_map/ppermute | solution.py:218
  158.6 19.0 %copy-start.3 = (f32[1,256,128]{2,1,0:T(8,128)S(1)}, f32[1,256,128]{2,1,0:T(8,128)}, u32[]{:S(2)}) copy-start(f32[1,256,128]{2,1,0:T(8,128)} %reduce-scatter.5.cloned.1.call-done) | copy-start | bytes 393220
  172.5 7.1 %collective-permute-start.5 = (f32[1792,128]{1,0:T(8,128)S(1)}, f32[1792,128]{1,0:T(8,128)S(1)}, u32[]{:S(2)}, u32[]{:S(2)}) collective-permute-start(f32[1792,128]{1,0:T(8,128)S(1)} %bitcast.11), channel_id=1, source_target_pairs={{0,4},{4,0},{1,5},{5,1},{2,6},{6,2},{3,7},{7,3},{8,12},{12,8},{9,1... | collective-permute-start | bytes 2752520 | tf_op jit(solution)/shard_map/ppermute | solution.py:224
Sparse Core Ops, SparseCore 0:
  89.4 28.4 reduce-scatter.2
  120.7 37.7 reduce-scatter.4

commit v6 on v4

--- a/solution.py
+++ b/solution.py
@@ -25,17 +25,21 @@
     return pairs
 
 
-def column_move(sizes, step, swap):
+def outer_neighbour(sizes):
     _, zhis, rings, cores, _ = sizes
 
     def move(chan, zhi, ring, core, space):
-        column = (zhi * rings + ring) * cores + core + step
+        column = (zhi * rings + ring) * cores + core
+        column += 1 if column % 2 else -1
         if not 0 <= column < zhis * rings * cores:
             return None
-        rest = (column // (rings * cores), column // cores % rings, column % cores)
-        return (space, *rest, chan) if swap else (chan, *rest, space)
+        return (chan, column // (rings * cores), column // cores % rings, column % cores, space)
 
     return permutation(sizes, move)
+
+
+def transposed(sizes):
+    return permutation(sizes, lambda chan, zhi, ring, core, space: (space, zhi, ring, core, chan))
 
 
 def height_mask(rows, height, at):
@@ -49,27 +53,29 @@
     return jnp.where(height_mask(rows, height, edge), 0.0, rolled)
 
 
-def fill_padded(padded, block):
-    columns, planes, height, lanes = padded.shape
+def fill_padded(padded, pair, inner, core):
+    planes, height, lanes = padded.shape[1:]
     planes -= 2
-    zero = jnp.zeros((columns, 1, height, lanes), BF16)
+    zero = jnp.zeros((3, 1, height, lanes), BF16)
     padded[:, 0:1] = zero
     padded[:, planes + 1 : planes + 2] = zero
-    if len(block.shape) == 4:
-        padded[:, 1 : planes + 1] = block[...]
-    else:
-        slabs, _, depth = block.shape[:3]
-        for slab in range(slabs):
-            padded[:, 1 + slab * depth : 1 + (slab + 1) * depth] = block[slab]
-
-
-def conv_kernel(backward, me, block, weight, *refs):
+    for column, source in ((1, 0), (2 * core, 1)):
+        if len(pair.shape) == 4:
+            padded[column, 1 : planes + 1] = pair[source]
+        else:
+            slabs, _, depth = pair.shape[:3]
+            for slab in range(slabs):
+                padded[column, 1 + slab * depth : 1 + (slab + 1) * depth] = pair[slab, source]
+    padded[2 - 2 * core, 1 : planes + 1] = inner[...]
+
+
+def conv_kernel(backward, place, pair, inner, weight, *refs):
     *outs, padded, flat = refs
     slabs = len(outs)
     rows, lanes = outs[0].shape
-    height = block.shape[-2]
+    height = inner.shape[1]
     planes = rows // height
-    fill_padded(padded, block)
+    fill_padded(padded, pair, inner, place[0])
     for cell in range(9):
         for r in range(3):
             if backward:
@@ -77,7 +83,7 @@
             else:
                 flat[cell * lanes : (cell + 1) * lanes, r * lanes : (r + 1) * lanes] = weight[3 * cell + r]
     for step, out in enumerate(outs):
-        slab = lax.rem(me[0] + step, slabs)
+        slab = lax.rem(place[1] + step, slabs)
         pieces = []
         for p in range(3):
             for q in range(3):
@@ -94,15 +100,14 @@
         out[...] = total
 
 
-def convolve(backward, block, weight, slabs, me):
-    height, lanes = block.shape[-2:]
-    rows = block.size // (3 * lanes)
-    planes = rows // height
+def convolve(backward, core, me, pair, inner, weight, slabs):
+    planes, height, lanes = inner.shape
+    rows = planes * height
     flat = (3 * lanes, 9 * lanes) if backward else (9 * lanes, 3 * lanes)
     return pl.pallas_call(
         functools.partial(conv_kernel, backward),
         out_shape=[jax.ShapeDtypeStruct((rows // slabs, lanes), F32)] * slabs,
-        in_specs=[SMEM, VMEM, VMEM],
+        in_specs=[SMEM, VMEM, VMEM, VMEM],
         out_specs=[VMEM] * slabs,
         scratch_shapes=[
             pltpu.VMEM((3, planes + 2, height, lanes), BF16),
@@ -113,14 +118,14 @@
             flops=2 * 27 * rows * lanes * lanes, bytes_accessed=3 << 20, transcendentals=0
         ),
         name="input_grad" if backward else "forward",
-    )(me, block, weight)
-
-
-def filter_kernel(core, data, grad, keep, send, padded, turned, taps):
-    planes, height, lanes = grad.shape[1:]
+    )(jnp.stack([core, me]), pair, inner, weight)
+
+
+def filter_kernel(core, data, pair, inner, keep, send, padded, turned, taps):
+    planes, height, lanes = inner.shape
     rows = planes * height
-    fill_padded(padded, grad)
-    flat = data[:, 1].reshape(rows, lanes).astype(F32)
+    fill_padded(padded, pair, inner, core[0])
+    flat = data[:, 0].reshape(rows, lanes).astype(F32)
     turned[0:lanes] = shifted(flat, height, -1).T.astype(BF16)
     turned[lanes : 2 * lanes] = flat.T.astype(BF16)
     turned[2 * lanes : 3 * lanes] = shifted(flat, height, 1).T.astype(BF16)
@@ -148,14 +153,14 @@
         send[...] = taps[0:half]
 
 
-def filter_partial(data, grad, core):
-    planes, height, lanes = grad.shape[1:]
+def filter_partial(core, data, pair, inner):
+    planes, height, lanes = inner.shape
     rows = planes * height
     half = jax.ShapeDtypeStruct((14 * lanes, lanes), F32)
     return pl.pallas_call(
         filter_kernel,
         out_shape=(half, half),
-        in_specs=[SMEM, VMEM, VMEM],
+        in_specs=[SMEM, VMEM, VMEM, VMEM],
         out_specs=(VMEM, VMEM),
         scratch_shapes=[
             pltpu.VMEM((3, planes + 2, height, lanes), BF16),
@@ -167,7 +172,7 @@
             flops=2 * 27 * rows * lanes * lanes, bytes_accessed=3 << 20, transcendentals=0
         ),
         name="filter_grad",
-    )(core, data, grad)
+    )(core.reshape(1), data, pair, inner)
 
 
 def exchange(block, axis):
@@ -179,11 +184,11 @@
     return exchange(jnp.broadcast_to(block[None], (count, *block.shape)), axis)
 
 
-def reduced(blocks, axis):
-    count = len(blocks)
-    total = blocks[0]
+def reduced(terms, axis):
+    count = len(terms)
+    total = terms[0]
     for step in range(1, count):
-        total += lax.ppermute(blocks[step], axis, [(i, (i + step) % count) for i in range(count)])
+        total += lax.ppermute(terms[step], axis, [(i, (i + step) % count) for i in range(count)])
     return total
 
 
@@ -194,44 +199,46 @@
 def shards(sizes, activations, weight, output_grad):
     _, zhis, rings, cores, spaces = sizes
     planes, height, lanes = activations.shape[1:]
-    core = lax.axis_index("core").reshape(1)
+    core = lax.axis_index("core")
     swap = [(0, 1), (1, 0)]
 
-    low = lax.ppermute(activations, AXES, column_move(sizes, 1, False))
-    high = lax.ppermute(activations, AXES, column_move(sizes, -1, False))
-    sides = jnp.concatenate([low, activations, high], axis=0)
-    data = gather(sides, "space")
-    cotangent = after(output_grad, sides)
-    grads = [lax.ppermute(cotangent, AXES, column_move(sizes, step, True)) for step in (1, 0, -1)]
-    grad = jnp.concatenate(grads, axis=0)
-    grad = lax.all_gather(grad, "chan", axis=1, tiled=True)
-
-    keep, send = filter_partial(data, grad, core)
+    outer = lax.ppermute(output_grad, AXES, outer_neighbour(sizes))
+    grad = jnp.concatenate([output_grad, outer], axis=0)
+    grad, later = lax.optimization_barrier((grad, activations))
+    grad = lax.ppermute(grad, AXES, transposed(sizes))
+    outer = lax.ppermute(later, AXES, outer_neighbour(sizes))
+    data = gather(jnp.concatenate([activations, outer], axis=0), "space")
+    grad = lax.all_gather(after(grad, outer), "chan", axis=1, tiled=True)
+    grad_inner = lax.ppermute(grad[0], "core", swap)
+
+    keep, send = filter_partial(core, data, grad, grad_inner)
     moved = lax.ppermute(send, "core", swap)
-    me = lax.axis_index("space").reshape(1)
-    back = convolve(True, after(grad, send), weight, spaces, me)
-    half, *back = lax.optimization_barrier((keep + moved, *back))
+    own = after(data[:, 0].reshape(grad_inner.shape), send)
+    data_inner = lax.ppermute(own, "core", swap)
+    half, data_inner = lax.optimization_barrier((keep + moved, data_inner))
 
     moved = exchange(half.reshape(rings, -1, lanes), "ring")
+    me = lax.axis_index("space")
+    back = convolve(True, core, me, after(grad, half), grad_inner, weight, spaces)
     input_grad = reduced(back, "space").astype(BF16).reshape(activations.shape)
     quarter, input_grad = lax.optimization_barrier((moved.sum(0), input_grad))
 
     moved = exchange(quarter.reshape(zhis, -1, lanes), "zhi")
-    me = lax.axis_index("chan").reshape(1)
-    forward = convolve(False, after(data, quarter), weight, spaces, me)
+    me = lax.axis_index("chan")
+    forward = convolve(False, core, me, after(data, quarter), data_inner, weight, spaces)
     forward = reduced(forward, "chan").astype(BF16)
     cell_count = sizes[1] * rings * cores * grad.shape[1] * grad.shape[2]
     part = moved.sum(0) / math.sqrt(cell_count)
     part, forward = lax.optimization_barrier((part, forward))
 
     quarter = gather(part, "zhi").reshape(-1, lanes)
-    output = lax.ppermute(forward, AXES, column_move(sizes, 0, True)).reshape(activations.shape)
+    output = lax.ppermute(forward, AXES, transposed(sizes)).reshape(activations.shape)
     quarter, output = lax.optimization_barrier((quarter, output))
 
     half = gather(quarter, "ring").reshape(-1, lanes)
 
     other = lax.ppermute(half, "core", swap)
-    first = core[0] == 0
+    first = core == 0
     low = jnp.where(first, half, other)
     high = jnp.where(first, other, half)
     taps = weight.shape[0]

time: 184 us -> 185 us (level)
  the two profiles are of different devices: /device:TPU:33 before, /device:TPU:1 now
where the time goes in v6:
time: 185 us; the launch traced here: 181 us
  starting transfers between devices  93.6 us (51%)
  blocking collectives  39.7 us (21%)
  waiting for transfers between devices  33.2 us (18%)
  other arithmetic  5.83 us (3%)
  Pallas kernels  5.82 us (3%)
  local copies, waits for them, and re-layouts  2.32 us (1%)
    all_to_all x4, starting transfers between devices, exchange(): return lax.all_to_all(block, axis, split_axis=0, concat_axis=0, tiled=True)  51.7 us
    all_gather x1, blocking collectives, shards(): grad = lax.all_gather(after(grad, outer), 'chan', axis=1, tiled=True)  26.5 us
    ppermute x6, starting transfers between devices, reduced(): lax.ppermute(terms[step], axis, [(i, (i + step) % count) for i in range(c...  18.5 us
    all_to_all x4, waiting for transfers between devices, exchange(): return lax.all_to_all(block, axis, split_axis=0, concat_axis=0, tiled=True)  15.1 us
    all_to_all x1, blocking collectives, exchange(): return lax.all_to_all(block, axis, split_axis=0, concat_axis=0, tiled=True)  13.2 us
    ppermute x6, waiting for transfers between devices, reduced(): lax.ppermute(terms[step], axis, [(i, (i + step) % count) for i in range(c...  10.3 us
    ppermute x1, starting transfers between devices, shards(): other = lax.ppermute(half, 'core', swap)  7.27 us
    ppermute x1, starting transfers between devices, shards(): outer = lax.ppermute(output_grad, AXES, outer_neighbour(sizes))  4.59 us
  transfers between devices with their start and end apart: 18, of which 10 were waited for; matrix products, arithmetic and copies ran while one was open for 1% of the time, Pallas kernels for 2%

profile of v6, /device:TPU:1, one launch (start us, length us, event | category | flops | bytes accessed | tf_op | source)
XLA Modules:
  0.0 181.4 jit_solution(17515375827120625985)
XLA Ops:
  0.6 4.6 %collective-permute-start = (bf16[1,8,32,128]{3,2,1,0:T(8,128)(2,1)}, bf16[1,8,32,128]{3,2,1,0:T(8,128)(2,1)S(1)}, u32[]{:S(2)}, u32[]{:S(2)}) collective-permute-start(bf16[1,8,32,128]{3,2,1,0:T(8,128)(2,1)} %param.5), channel_id=1, source_target_pairs={{4,8},{5,9},{6,10},{7,11},{8,4},{9,5},{10,6},{11,7},{12,16},{13,17... | collective-permute-start | bytes 196616 | tf_op jit(solution)/shard_map/ppermute | solution.py:205
  5.2 2.1 %collective-permute-done = bf16[1,8,32,128]{3,2,1,0:T(8,128)(2,1)S(1)} collective-permute-done((bf16[1,8,32,128]{3,2,1,0:T(8,128)(2,1)}, bf16[1,8,32,128]{3,2,1,0:T(8,128)(2,1)S(1)}, u32[]{:S(2)}, u32[]{:S(2)}) %collective-permute-start) | collective-permute-done | bytes 65568 | tf_op jit(solution)/shard_map/ppermute | solution.py:205
  7.4 0.9 pad_maximum_fusion.1
  8.2 3.6 %collective-permute-start.1 = (bf16[1,8,32,128]{3,2,1,0:T(8,128)(2,1)}, bf16[1,8,32,128]{3,2,1,0:T(8,128)(2,1)S(1)}, u32[]{:S(2)}, u32[]{:S(2)}) collective-permute-start(bf16[1,8,32,128]{3,2,1,0:T(8,128)(2,1)} %param.3), channel_id=1, source_target_pairs={{4,8},{5,9},{6,10},{7,11},{8,4},{9,5},{10,6},{11,7},{12,16},{13,17... | collective-permute-start | bytes 196616 | tf_op jit(solution)/shard_map/ppermute | solution.py:209
  11.9 2.1 %collective-permute-done.1 = bf16[1,8,32,128]{3,2,1,0:T(8,128)(2,1)S(1)} collective-permute-done((bf16[1,8,32,128]{3,2,1,0:T(8,128)(2,1)}, bf16[1,8,32,128]{3,2,1,0:T(8,128)(2,1)S(1)}, u32[]{:S(2)}, u32[]{:S(2)}) %collective-permute-start.1) | collective-permute-done | bytes 65568 | tf_op jit(solution)/shard_map/ppermute | solution.py:209
  14.0 0.9 pad_maximum_fusion.2
  14.9 0.9 broadcast_in_dim.6
  15.8 5.6 %all-to-all-start = ((bf16[4,2,8,32,128]{4,3,2,1,0:T(8,128)(2,1)}), bf16[4,2,8,32,128]{4,3,2,1,0:T(8,128)(2,1)S(1)}, u32[]{:S(2)}, u32[]{:S(2)}) async-start(bf16[4,2,8,32,128]{4,3,2,1,0:T(8,128)(2,1)} %broadcast_in_dim.6), calls=%async_computation | async-start | bytes 1048576 | tf_op jit(solution)/shard_map/all_to_all | solution.py:179
  21.4 0.7 collective-permute-start.2
  22.0 0.0 collective-permute-done.2
  22.1 26.5 %all_gather.3.pair = bf16[2,32,32,128]{3,2,1,0:T(8,128)(2,1)S(1)} all-gather(bf16[2,8,32,128]{3,2,1,0:T(8,128)(2,1)S(1)} %collective-permute-done.2), channel_id=1, replica_groups=mesh['chan'=4,'zhi'=4,'ring'=4,'core'=2,'space'=4] {'chan'}, dimensions={1}, use_global_device_ids=true | all-gather | bytes 655360 | tf_op jit(solution)/shard_map/all_gather | solution.py:211
  48.6 2.3 %collective-permute-start.3 = (bf16[32,32,128]{2,1,0:T(8,128)(2,1)S(1)}, bf16[32,32,128]{2,1,0:T(8,128)(2,1)S(1)}, u32[]{:S(2)}, u32[]{:S(2)}) collective-permute-start(bf16[32,32,128]{2,1,0:T(8,128)(2,1)S(1)} %slice_bitcast_fusion), channel_id=1, source_target_pairs={{0,4},{4,0},{1,5},{5,1},{2,6},{6,2},{3,7},{7,3},{8,12},{12,8},{9,1... | collective-permute-start | bytes 786440 | tf_op jit(solution)/shard_map/ppermute | solution.py:212
  50.9 1.1 collective-permute-done.3.inner
  52.0 0.0 all-to-all-done.data.pair
  52.0 1.6 filter_grad.1
  53.6 2.3 %collective-permute-start.4 = (f32[1792,128]{1,0:T(8,128)S(1)}, f32[1792,128]{1,0:T(8,128)S(1)}, u32[]{:S(2)}, u32[]{:S(2)}) collective-permute-start(f32[1792,128]{1,0:T(8,128)S(1)} %get-tuple-element.31), channel_id=1, source_target_pairs={{0,4},{4,0},{1,5},{5,1},{2,6},{6,2},{3,7},{7,3},{8,12},{12,8},{9,1... | collective-permute-start | bytes 2752520 | tf_op jit(solution)/shard_map/ppermute | solution.py:215
  55.9 2.1 %collective-permute-start.5 = (bf16[32,32,128]{2,1,0:T(8,128)(2,1)S(1)}, bf16[32,32,128]{2,1,0:T(8,128)(2,1)S(1)}, u32[]{:S(2)}, u32[]{:S(2)}) collective-permute-start(bf16[32,32,128]{2,1,0:T(8,128)(2,1)S(1)} %bitcast.19), channel_id=1, source_target_pairs={{0,4},{4,0},{1,5},{5,1},{2,6},{6,2},{3,7},{7,3},{8,12},{12,8},{9,1... | collective-permute-start | bytes 786440 | tf_op jit(solution)/shard_map/ppermute | solution.py:217
  58.0 0.0 collective-permute-done.4
  58.0 0.0 copy-start
  58.0 1.0 add.21
  59.0 0.3 collective-permute-done.5.inner
  59.4 11.1 %all-to-all-start.1 = ((f32[4,448,128]{2,1,0:T(8,128)}), f32[4,448,128]{2,1,0:T(8,128)S(1)}, u32[]{:S(2)}, u32[]{:S(2)}) async-start(f32[4,448,128]{2,1,0:T(8,128)} %bitcast.16), calls=%async_computation.1 | async-start | bytes 1835008 | tf_op jit(solution)/shard_map/all_to_all | solution.py:179
  70.4 0.1 pad_add_fusion.place
  70.5 0.0 copy-done
  70.5 2.2 %input_grad.1 = (f32[256,128]{1,0:T(8,128)S(1)}, f32[256,128]{1,0:T(8,128)S(1)}, f32[256,128]{1,0:T(8,128)S(1)}, f32[256,128]{1,0:T(8,128)S(1)}) custom-call(s32[2]{0:T(128)S(1)} %pad_add_fusion.place, bf16[2,32,32,128]{3,2,1,0:T(8,128)(2,1)S(1)} %all_gather.3.pair, bf16[32,32,128]{2,1,0:T(8,128)(2,1)S(1)} %collective-permute-done.3.inner, ...), custom_call_target="tpu_custom_call" | custom-call | flops 905969664 | bytes 3145728 | tf_op jit(solution)/shard_map/input_grad/pallas_call | solution.py:107
  72.7 2.4 %collective-permute-start.6 = (f32[256,128]{1,0:T(8,128)S(1)}, f32[256,128]{1,0:T(8,128)S(1)}, u32[]{:S(2)}, u32[]{:S(2)}) collective-permute-start(f32[256,128]{1,0:T(8,128)S(1)} %get-tuple-element.36), channel_id=1, source_target_pairs={{0,1},{1,2},{2,3},{3,0},{4,5},{5,6},{6,7},{7,4},{8,9},{9,10},{10,1... | collective-permute-start | bytes 393224 | tf_op jit(solution)/shard_map/ppermute | solution.py:191
  75.1 4.4 %collective-permute-start.7 = (f32[256,128]{1,0:T(8,128)S(1)}, f32[256,128]{1,0:T(8,128)S(1)}, u32[]{:S(2)}, u32[]{:S(2)}) collective-permute-start(f32[256,128]{1,0:T(8,128)S(1)} %get-tuple-element.37), channel_id=1, source_target_pairs={{0,2},{1,3},{2,0},{3,1},{4,6},{5,7},{6,4},{7,5},{8,10},{9,11},{10,... | collective-permute-start | bytes 393224 | tf_op jit(solution)/shard_map/ppermute | solution.py:191
  79.5 2.6 %collective-permute-start.8 = (f32[256,128]{1,0:T(8,128)S(1)}, f32[256,128]{1,0:T(8,128)S(1)}, u32[]{:S(2)}, u32[]{:S(2)}) collective-permute-start(f32[256,128]{1,0:T(8,128)S(1)} %get-tuple-element.38), channel_id=1, source_target_pairs={{0,3},{1,0},{2,1},{3,2},{4,7},{5,4},{6,5},{7,6},{8,11},{9,8},{10,9... | collective-permute-start | bytes 393224 | tf_op jit(solution)/shard_map/ppermute | solution.py:191
  82.2 0.0 collective-permute-done.6
  82.2 5.3 %collective-permute-done.7 = f32[256,128]{1,0:T(8,128)S(1)} collective-permute-done((f32[256,128]{1,0:T(8,128)S(1)}, f32[256,128]{1,0:T(8,128)S(1)}, u32[]{:S(2)}, u32[]{:S(2)}) %collective-permute-start.7) | collective-permute-done | bytes 131104 | tf_op jit(solution)/shard_map/ppermute | solution.py:191
  87.4 1.3 collective-permute-done.8
  88.7 0.7 add_convert_fusion.1
  89.3 0.0 all-to-all-done.1
  89.3 0.7 reduce_sum.18
  90.1 23.6 %all-to-all-start.2 = ((f32[4,112,128]{2,1,0:T(8,128)}), f32[4,112,128]{2,1,0:T(8,128)S(1)}, u32[]{:S(2)}, u32[]{:S(2)}) async-start(f32[4,112,128]{2,1,0:T(8,128)} %bitcast.6), calls=%async_computation.2 | async-start | bytes 458752 | tf_op jit(solution)/shard_map/all_to_all | solution.py:179
  113.7 0.1 pad_add_fusion.1.place
  113.7 2.1 %forward.1 = (f32[256,128]{1,0:T(8,128)S(1)}, f32[256,128]{1,0:T(8,128)S(1)}, f32[256,128]{1,0:T(8,128)S(1)}, f32[256,128]{1,0:T(8,128)S(1)}) custom-call(s32[2]{0:T(128)S(1)} %pad_add_fusion.1.place, bf16[4,2,8,32,128]{4,3,2,1,0:T(8,128)(2,1)S(1)} %all-to-all-done.data.pair, bf16[32,32,128]{2,1,0:T(8,128)(2,1)S(1)} %collective-permute-done.5.inner, ...), custom_call_target="tpu_custom_call" | custom-call | flops 905969664 | bytes 3145728 | tf_op jit(solution)/shard_map/forward/pallas_call | solution.py:107
  115.8 2.2 %collective-permute-start.9 = (f32[256,128]{1,0:T(8,128)S(1)}, f32[256,128]{1,0:T(8,128)S(1)}, u32[]{:S(2)}, u32[]{:S(2)}) collective-permute-start(f32[256,128]{1,0:T(8,128)S(1)} %get-tuple-element.43), channel_id=1, source_target_pairs={{0,128},{128,256},{256,384},{384,0},{1,129},{129,257},{257,385},{3... | collective-permute-start | bytes 393224 | tf_op jit(solution)/shard_map/ppermute | solution.py:191
  118.0 4.3 %collective-permute-start.10 = (f32[256,128]{1,0:T(8,128)S(1)}, f32[256,128]{1,0:T(8,128)S(1)}, u32[]{:S(2)}, u32[]{:S(2)}) collective-permute-start(f32[256,128]{1,0:T(8,128)S(1)} %get-tuple-element.44), channel_id=1, source_target_pairs={{0,256},{128,384},{256,0},{384,128},{1,257},{129,385},{257,1},{385... | collective-permute-start | bytes 393224 | tf_op jit(solution)/shard_map/ppermute | solution.py:191
  122.3 2.5 %collective-permute-start.11 = (f32[256,128]{1,0:T(8,128)S(1)}, f32[256,128]{1,0:T(8,128)S(1)}, u32[]{:S(2)}, u32[]{:S(2)}) collective-permute-start(f32[256,128]{1,0:T(8,128)S(1)} %get-tuple-element.45), channel_id=1, source_target_pairs={{0,384},{128,0},{256,128},{384,256},{1,385},{129,1},{257,129},{385... | collective-permute-start | bytes 393224 | tf_op jit(solution)/shard_map/ppermute | solution.py:191
  124.8 0.0 collective-permute-done.9
  124.8 1.0 collective-permute-done.10
  125.9 2.8 %collective-permute-done.11 = f32[256,128]{1,0:T(8,128)S(1)} collective-permute-done((f32[256,128]{1,0:T(8,128)S(1)}, f32[256,128]{1,0:T(8,128)S(1)}, u32[]{:S(2)}, u32[]{:S(2)}) %collective-permute-start.11) | collective-permute-done | bytes 131104 | tf_op jit(solution)/shard_map/ppermute | solution.py:191
  128.7 0.0 all-to-all-done.2
  128.8 0.7 broadcast_in_dim.7
  129.5 11.4 %all-to-all-start.3 = ((f32[4,112,128]{2,1,0:T(8,128)}), f32[4,112,128]{2,1,0:T(8,128)S(1)}, u32[]{:S(2)}, u32[]{:S(2)}) async-start(f32[4,112,128]{2,1,0:T(8,128)} %broadcast_in_dim.7), calls=%async_computation.3 | async-start | bytes 458752 | tf_op jit(solution)/shard_map/all_to_all | solution.py:179
  140.9 0.7 collective-permute-start.12
  141.6 0.0 collective-permute-done.12
  141.6 15.1 %all-to-all-done.3 = f32[4,112,128]{2,1,0:T(8,128)S(1)} async-done(((f32[4,112,128]{2,1,0:T(8,128)}), f32[4,112,128]{2,1,0:T(8,128)S(1)}, u32[]{:S(2)}, u32[]{:S(2)}) %all-to-all-start.3) | async-done | bytes 229408 | tf_op jit(solution)/shard_map/all_to_all | solution.py:179
  156.6 0.1 broadcast_in_dim.8
  156.7 13.2 %all_to_all.25 = f32[4,448,128]{2,1,0:T(8,128)S(1)} all-to-all(f32[4,448,128]{2,1,0:T(8,128)S(1)} %broadcast_in_dim.8), channel_id=1, replica_groups=mesh['chan'=4,'zhi'=4,'ring'=4,'core'=2,'space'=4] {'ring'}, dimensions={0} | all-to-all | bytes 1835008 | tf_op jit(solution)/shard_map/all_to_all | solution.py:179
  169.9 7.3 %collective-permute-start.13 = (f32[1792,128]{1,0:T(8,128)S(1)}, f32[1792,128]{1,0:T(8,128)S(1)}, u32[]{:S(2)}, u32[]{:S(2)}) collective-permute-start(f32[1792,128]{1,0:T(8,128)S(1)} %bitcast.14), channel_id=1, source_target_pairs={{0,4},{4,0},{1,5},{5,1},{2,6},{6,2},{3,7},{7,3},{8,12},{12,8},{9,1... | collective-permute-start | bytes 2752520 | tf_op jit(solution)/shard_map/ppermute | solution.py:240
  177.1 2.1 %collective-permute-done.13 = f32[1792,128]{1,0:T(8,128)S(1)} collective-permute-done((f32[1792,128]{1,0:T(8,128)S(1)}, f32[1792,128]{1,0:T(8,128)S(1)}, u32[]{:S(2)}, u32[]{:S(2)}) %collective-permute-start.13) | collective-permute-done | bytes 917536 | tf_op jit(solution)/shard_map/ppermute | solution.py:240
  179.2 0.1 slice_select_fusion
  179.3 0.1 broadcast_select_fusion
  179.4 1.3 pad_maximum_fusion
  180.7 0.6 copy.7
  (5 shorter events, 0.1 us)
Async XLA Ops:
  0.6 6.7 %collective-permute-start = (bf16[1,8,32,128]{3,2,1,0:T(8,128)(2,1)}, bf16[1,8,32,128]{3,2,1,0:T(8,128)(2,1)S(1)}, u32[]{:S(2)}, u32[]{:S(2)}) collective-permute-start(bf16[1,8,32,128]{3,2,1,0:T(8,128)(2,1)} %param.5), channel_id=1, source_target_pairs={{4,8},{5,9},{6,10},{7,11},{8,4},{9,5},{10,6},{11,7},{12,16},{13,17... | collective-permute-start | bytes 196616 | tf_op jit(solution)/shard_map/ppermute | solution.py:205
  8.2 5.8 %collective-permute-start.1 = (bf16[1,8,32,128]{3,2,1,0:T(8,128)(2,1)}, bf16[1,8,32,128]{3,2,1,0:T(8,128)(2,1)S(1)}, u32[]{:S(2)}, u32[]{:S(2)}) collective-permute-start(bf16[1,8,32,128]{3,2,1,0:T(8,128)(2,1)} %param.3), channel_id=1, source_target_pairs={{4,8},{5,9},{6,10},{7,11},{8,4},{9,5},{10,6},{11,7},{12,16},{13,17... | collective-permute-start | bytes 196616 | tf_op jit(solution)/shard_map/ppermute | solution.py:209
  15.8 36.3 %all-to-all-start = ((bf16[4,2,8,32,128]{4,3,2,1,0:T(8,128)(2,1)}), bf16[4,2,8,32,128]{4,3,2,1,0:T(8,128)(2,1)S(1)}, u32[]{:S(2)}, u32[]{:S(2)}) async-start(bf16[4,2,8,32,128]{4,3,2,1,0:T(8,128)(2,1)} %broadcast_in_dim.6), calls=%async_computation | async-start | bytes 1048576 | tf_op jit(solution)/shard_map/all_to_all | solution.py:179
  21.4 0.7 collective-permute-start.2
  48.6 3.5 %collective-permute-start.3 = (bf16[32,32,128]{2,1,0:T(8,128)(2,1)S(1)}, bf16[32,32,128]{2,1,0:T(8,128)(2,1)S(1)}, u32[]{:S(2)}, u32[]{:S(2)}) collective-permute-start(bf16[32,32,128]{2,1,0:T(8,128)(2,1)S(1)} %slice_bitcast_fusion), channel_id=1, source_target_pairs={{0,4},{4,0},{1,5},{5,1},{2,6},{6,2},{3,7},{7,3},{8,12},{12,8},{9,1... | collective-permute-start | bytes 786440 | tf_op jit(solution)/shard_map/ppermute | solution.py:212
  53.6 4.4 %collective-permute-start.4 = (f32[1792,128]{1,0:T(8,128)S(1)}, f32[1792,128]{1,0:T(8,128)S(1)}, u32[]{:S(2)}, u32[]{:S(2)}) collective-permute-start(f32[1792,128]{1,0:T(8,128)S(1)} %get-tuple-element.31), channel_id=1, source_target_pairs={{0,4},{4,0},{1,5},{5,1},{2,6},{6,2},{3,7},{7,3},{8,12},{12,8},{9,1... | collective-permute-start | bytes 2752520 | tf_op jit(solution)/shard_map/ppermute | solution.py:215
  55.9 3.4 %collective-permute-start.5 = (bf16[32,32,128]{2,1,0:T(8,128)(2,1)S(1)}, bf16[32,32,128]{2,1,0:T(8,128)(2,1)S(1)}, u32[]{:S(2)}, u32[]{:S(2)}) collective-permute-start(bf16[32,32,128]{2,1,0:T(8,128)(2,1)S(1)} %bitcast.19), channel_id=1, source_target_pairs={{0,4},{4,0},{1,5},{5,1},{2,6},{6,2},{3,7},{7,3},{8,12},{12,8},{9,1... | collective-permute-start | bytes 786440 | tf_op jit(solution)/shard_map/ppermute | solution.py:217
  58.0 12.5 %copy-start = (bf16[27,128,128]{2,1,0:T(8,128)(2,1)S(1)}, bf16[27,128,128]{2,1,0:T(8,128)(2,1)}, u32[]{:S(2)}) copy-start(bf16[27,128,128]{2,1,0:T(8,128)(2,1)} %weight.3) | copy-start | bytes 2654212
  59.4 30.0 %all-to-all-start.1 = ((f32[4,448,128]{2,1,0:T(8,128)}), f32[4,448,128]{2,1,0:T(8,128)S(1)}, u32[]{:S(2)}, u32[]{:S(2)}) async-start(f32[4,448,128]{2,1,0:T(8,128)} %bitcast.16), calls=%async_computation.1 | async-start | bytes 1835008 | tf_op jit(solution)/shard_map/all_to_all | solution.py:179
  72.7 9.5 %collective-permute-start.6 = (f32[256,128]{1,0:T(8,128)S(1)}, f32[256,128]{1,0:T(8,128)S(1)}, u32[]{:S(2)}, u32[]{:S(2)}) collective-permute-start(f32[256,128]{1,0:T(8,128)S(1)} %get-tuple-element.36), channel_id=1, source_target_pairs={{0,1},{1,2},{2,3},{3,0},{4,5},{5,6},{6,7},{7,4},{8,9},{9,10},{10,1... | collective-permute-start | bytes 393224 | tf_op jit(solution)/shard_map/ppermute | solution.py:191
  75.1 12.3 %collective-permute-start.7 = (f32[256,128]{1,0:T(8,128)S(1)}, f32[256,128]{1,0:T(8,128)S(1)}, u32[]{:S(2)}, u32[]{:S(2)}) collective-permute-start(f32[256,128]{1,0:T(8,128)S(1)} %get-tuple-element.37), channel_id=1, source_target_pairs={{0,2},{1,3},{2,0},{3,1},{4,6},{5,7},{6,4},{7,5},{8,10},{9,11},{10,... | collective-permute-start | bytes 393224 | tf_op jit(solution)/shard_map/ppermute | solution.py:191
  79.5 9.2 %collective-permute-start.8 = (f32[256,128]{1,0:T(8,128)S(1)}, f32[256,128]{1,0:T(8,128)S(1)}, u32[]{:S(2)}, u32[]{:S(2)}) collective-permute-start(f32[256,128]{1,0:T(8,128)S(1)} %get-tuple-element.38), channel_id=1, source_target_pairs={{0,3},{1,0},{2,1},{3,2},{4,7},{5,4},{6,5},{7,6},{8,11},{9,8},{10,9... | collective-permute-start | bytes 393224 | tf_op jit(solution)/shard_map/ppermute | solution.py:191
  90.1 38.6 %all-to-all-start.2 = ((f32[4,112,128]{2,1,0:T(8,128)}), f32[4,112,128]{2,1,0:T(8,128)S(1)}, u32[]{:S(2)}, u32[]{:S(2)}) async-start(f32[4,112,128]{2,1,0:T(8,128)} %bitcast.6), calls=%async_computation.2 | async-start | bytes 458752 | tf_op jit(solution)/shard_map/all_to_all | solution.py:179
  115.8 9.0 %collective-permute-start.9 = (f32[256,128]{1,0:T(8,128)S(1)}, f32[256,128]{1,0:T(8,128)S(1)}, u32[]{:S(2)}, u32[]{:S(2)}) collective-permute-start(f32[256,128]{1,0:T(8,128)S(1)} %get-tuple-element.43), channel_id=1, source_target_pairs={{0,128},{128,256},{256,384},{384,0},{1,129},{129,257},{257,385},{3... | collective-permute-start | bytes 393224 | tf_op jit(solution)/shard_map/ppermute | solution.py:191
  118.0 7.9 %collective-permute-start.10 = (f32[256,128]{1,0:T(8,128)S(1)}, f32[256,128]{1,0:T(8,128)S(1)}, u32[]{:S(2)}, u32[]{:S(2)}) collective-permute-start(f32[256,128]{1,0:T(8,128)S(1)} %get-tuple-element.44), channel_id=1, source_target_pairs={{0,256},{128,384},{256,0},{384,128},{1,257},{129,385},{257,1},{385... | collective-permute-start | bytes 393224 | tf_op jit(solution)/shard_map/ppermute | solution.py:191
  122.3 6.3 %collective-permute-start.11 = (f32[256,128]{1,0:T(8,128)S(1)}, f32[256,128]{1,0:T(8,128)S(1)}, u32[]{:S(2)}, u32[]{:S(2)}) collective-permute-start(f32[256,128]{1,0:T(8,128)S(1)} %get-tuple-element.45), channel_id=1, source_target_pairs={{0,384},{128,0},{256,128},{384,256},{1,385},{129,1},{257,129},{385... | collective-permute-start | bytes 393224 | tf_op jit(solution)/shard_map/ppermute | solution.py:191
  129.5 27.2 %all-to-all-start.3 = ((f32[4,112,128]{2,1,0:T(8,128)}), f32[4,112,128]{2,1,0:T(8,128)S(1)}, u32[]{:S(2)}, u32[]{:S(2)}) async-start(f32[4,112,128]{2,1,0:T(8,128)} %broadcast_in_dim.7), calls=%async_computation.3 | async-start | bytes 458752 | tf_op jit(solution)/shard_map/all_to_all | solution.py:179
  140.9 0.7 collective-permute-start.12
  169.9 9.4 %collective-permute-start.13 = (f32[1792,128]{1,0:T(8,128)S(1)}, f32[1792,128]{1,0:T(8,128)S(1)}, u32[]{:S(2)}, u32[]{:S(2)}) collective-permute-start(f32[1792,128]{1,0:T(8,128)S(1)} %bitcast.14), channel_id=1, source_target_pairs={{0,4},{4,0},{1,5},{5,1},{2,6},{6,2},{3,7},{7,3},{8,12},{12,8},{9,1... | collective-permute-start | bytes 2752520 | tf_op jit(solution)/shard_map/ppermute | solution.py:240

commit v7 on v6

--- a/solution.py
+++ b/solution.py
@@ -69,27 +69,24 @@
     padded[2 - 2 * core, 1 : planes + 1] = inner[...]
 
 
-def conv_kernel(backward, place, pair, inner, weight, *refs):
-    *outs, padded, flat = refs
-    slabs = len(outs)
-    rows, lanes = outs[0].shape
+def conv_kernel(backward, core, pair, inner, weight, out, padded, flat):
+    slabs, rows, lanes = out.shape
     height = inner.shape[1]
     planes = rows // height
-    fill_padded(padded, pair, inner, place[0])
+    fill_padded(padded, pair, inner, core[0])
     for cell in range(9):
         for r in range(3):
             if backward:
                 flat[r * lanes : (r + 1) * lanes, cell * lanes : (cell + 1) * lanes] = weight[3 * cell + r]
             else:
                 flat[cell * lanes : (cell + 1) * lanes, r * lanes : (r + 1) * lanes] = weight[3 * cell + r]
-    for step, out in enumerate(outs):
-        slab = lax.rem(place[1] + step, slabs)
+    for slab in range(slabs):
         pieces = []
         for p in range(3):
             for q in range(3):
                 column, plane = (2 - p, 2 - q) if backward else (p, q)
                 start = slab * planes + plane
-                pieces.append(padded[column, pl.ds(start, planes)].reshape(rows, lanes))
+                pieces.append(padded[column, start : start + planes].reshape(rows, lanes))
         lhs = jnp.concatenate(pieces, axis=1)
         dims = (((1,), (1 if backward else 0,)), ((), ()))
         taps = lax.dot_general(lhs, flat[...], dims, preferred_element_type=F32)
@@ -97,18 +94,18 @@
         total = taps[:, lanes : 2 * lanes]
         total += shifted(taps[:, low * lanes : (low + 1) * lanes], height, -1)
         total += shifted(taps[:, high * lanes : (high + 1) * lanes], height, 1)
-        out[...] = total
-
-
-def convolve(backward, core, me, pair, inner, weight, slabs):
+        out[slab] = total
+
+
+def convolve(backward, core, pair, inner, weight, slabs):
     planes, height, lanes = inner.shape
     rows = planes * height
     flat = (3 * lanes, 9 * lanes) if backward else (9 * lanes, 3 * lanes)
     return pl.pallas_call(
         functools.partial(conv_kernel, backward),
-        out_shape=[jax.ShapeDtypeStruct((rows // slabs, lanes), F32)] * slabs,
+        out_shape=jax.ShapeDtypeStruct((slabs, rows // slabs, lanes), F32),
         in_specs=[SMEM, VMEM, VMEM, VMEM],
-        out_specs=[VMEM] * slabs,
+        out_specs=VMEM,
         scratch_shapes=[
             pltpu.VMEM((3, planes + 2, height, lanes), BF16),
             pltpu.VMEM(flat, BF16),
@@ -118,7 +115,7 @@
             flops=2 * 27 * rows * lanes * lanes, bytes_accessed=3 << 20, transcendentals=0
         ),
         name="input_grad" if backward else "forward",
-    )(jnp.stack([core, me]), pair, inner, weight)
+    )(core.reshape(1), pair, inner, weight)
 
 
 def filter_kernel(core, data, pair, inner, keep, send, padded, turned, taps):
@@ -184,14 +181,6 @@
     return exchange(jnp.broadcast_to(block[None], (count, *block.shape)), axis)
 
 
-def reduced(terms, axis):
-    count = len(terms)
-    total = terms[0]
-    for step in range(1, count):
-        total += lax.ppermute(terms[step], axis, [(i, (i + step) % count) for i in range(count)])
-    return total
-
-
 def after(value, *others):
     return lax.optimization_barrier((value, *others))[0]
 
@@ -203,39 +192,40 @@
     swap = [(0, 1), (1, 0)]
 
     outer = lax.ppermute(output_grad, AXES, outer_neighbour(sizes))
-    grad = jnp.concatenate([output_grad, outer], axis=0)
-    grad, later = lax.optimization_barrier((grad, activations))
+    outer_data = lax.ppermute(activations, AXES, outer_neighbour(sizes))
+    grad, outer_data = lax.optimization_barrier(
+        (jnp.concatenate([output_grad, outer], axis=0), outer_data)
+    )
     grad = lax.ppermute(grad, AXES, transposed(sizes))
-    outer = lax.ppermute(later, AXES, outer_neighbour(sizes))
-    data = gather(jnp.concatenate([activations, outer], axis=0), "space")
-    grad = lax.all_gather(after(grad, outer), "chan", axis=1, tiled=True)
+    data = jnp.concatenate([activations, outer_data], axis=0)
+    grad, data = lax.optimization_barrier((grad, data))
+    data = gather(data, "space")
+    grad = lax.all_gather(grad, "chan", axis=1, tiled=True)
     grad_inner = lax.ppermute(grad[0], "core", swap)
 
     keep, send = filter_partial(core, data, grad, grad_inner)
     moved = lax.ppermute(send, "core", swap)
     own = after(data[:, 0].reshape(grad_inner.shape), send)
     data_inner = lax.ppermute(own, "core", swap)
-    half, data_inner = lax.optimization_barrier((keep + moved, data_inner))
+    back = convolve(True, core, after(grad, send), grad_inner, weight, spaces)
+    half, data_inner, back = lax.optimization_barrier((keep + moved, data_inner, back))
+    back = lax.psum_scatter(back, "space", scatter_dimension=0, tiled=True)
 
     moved = exchange(half.reshape(rings, -1, lanes), "ring")
-    me = lax.axis_index("space")
-    back = convolve(True, core, me, after(grad, half), grad_inner, weight, spaces)
-    input_grad = reduced(back, "space").astype(BF16).reshape(activations.shape)
-    quarter, input_grad = lax.optimization_barrier((moved.sum(0), input_grad))
-
-    moved = exchange(quarter.reshape(zhis, -1, lanes), "zhi")
-    me = lax.axis_index("chan")
-    forward = convolve(False, core, me, after(data, quarter), data_inner, weight, spaces)
-    forward = reduced(forward, "chan").astype(BF16)
+    forward = convolve(False, core, after(data, half), data_inner, weight, spaces)
+    quarter, forward = lax.optimization_barrier((moved.sum(0), forward))
+    forward = lax.psum_scatter(forward, "chan", scatter_dimension=0, tiled=True)
+
+    part = exchange(quarter.reshape(zhis, -1, lanes), "zhi").sum(0)
     cell_count = sizes[1] * rings * cores * grad.shape[1] * grad.shape[2]
-    part = moved.sum(0) / math.sqrt(cell_count)
-    part, forward = lax.optimization_barrier((part, forward))
-
-    quarter = gather(part, "zhi").reshape(-1, lanes)
-    output = lax.ppermute(forward, AXES, transposed(sizes)).reshape(activations.shape)
-    quarter, output = lax.optimization_barrier((quarter, output))
+    part, back = lax.optimization_barrier((part / math.sqrt(cell_count), back))
+    quarter, forward = lax.optimization_barrier((gather(part, "zhi").reshape(-1, lanes), forward))
 
     half = gather(quarter, "ring").reshape(-1, lanes)
+    output = lax.ppermute(forward[0].astype(BF16), AXES, transposed(sizes))
+    output = output.reshape(activations.shape)
+    input_grad = back[0].astype(BF16).reshape(activations.shape)
+    half, output, input_grad = lax.optimization_barrier((half, output, input_grad))
 
     other = lax.ppermute(half, "core", swap)
     first = core == 0

time: 185 us -> 189 us (1.022); the launches traced: 181 us -> 188 us
  waiting for transfers between devices: 33.2 us -> 69.6 us
  blocking collectives: 39.7 us -> 10.9 us
  starting transfers between devices: 93.6 us -> 76.2 us
  between operations: 0.89 us -> 14.2 us
    all_to_all x4 -> x5, waiting for transfers between devices: 15.1 us -> 39.2 us  [exchange(): return lax.all_to_all(block, axis, split_axis=0, concat_axis=0, tiled=True)]
    reduce_scatter x0 -> x2, waiting for transfers between devices: none -> 22.4 us  [the longest x1 22.4 us: shards(): forward = lax.psum_scatter(forward, 'chan', scatter_dimension=0, tiled=True)]
    ppermute x8 -> x2, starting transfers between devices: 22.8 us -> 2.59 us  [the longest x1 1.92 us: shards(): outer_data = lax.ppermute(activations, AXES, outer_neighbour(sizes))]
    all_gather x1, blocking collectives: 26.5 us -> 10.9 us  [shards(): grad = lax.all_gather(grad, 'chan', axis=1, tiled=True)]
    all_to_all x1 -> x0, blocking collectives: 13.2 us -> none  [exchange(): return lax.all_to_all(block, axis, split_axis=0, concat_axis=0, tiled=True)]
    ppermute x8 -> x2, waiting for transfers between devices: 12.5 us -> 2.8 us  [the longest x1 2.8 us: shards(): outer_data = lax.ppermute(activations, AXES, outer_neighbour(sizes))]
    all_to_all x4 -> x5, starting transfers between devices: 51.7 us -> 56.5 us  [exchange(): return lax.all_to_all(block, axis, split_axis=0, concat_axis=0, tiled=True)]
    ppermute x1, waiting for transfers between devices: 2.15 us -> 0.21 us  [shards(): outer = lax.ppermute(output_grad, AXES, outer_neighbour(sizes))]
  transfers between devices with their start and end apart: 18 -> 15, of which waited for: 10 -> 8; matrix products, arithmetic and copies ran while one was open for 1% -> 4% of each run, Pallas kernels for 2% -> 3%
where the time goes in v7:
time: 189 us; the launch traced here: 188 us
  starting transfers between devices  76.2 us (40%)
  waiting for transfers between devices  69.6 us (37%)
  between operations  14.2 us (8%)
  blocking collectives  10.9 us (6%)
  other arithmetic  6.82 us (4%)
  Pallas kernels  6.35 us (3%)
  local copies, waits for them, and re-layouts  3.94 us (2%)
    all_to_all x5, starting transfers between devices, exchange(): return lax.all_to_all(block, axis, split_axis=0, concat_axis=0, tiled=True)  56.5 us
    all_to_all x5, waiting for transfers between devices, exchange(): return lax.all_to_all(block, axis, split_axis=0, concat_axis=0, tiled=True)  39.2 us
    reduce_scatter x1, waiting for transfers between devices, shards(): forward = lax.psum_scatter(forward, 'chan', scatter_dimension=0, tiled=True)  22.4 us
    all_gather x1, blocking collectives, shards(): grad = lax.all_gather(grad, 'chan', axis=1, tiled=True)  10.9 us
    ppermute x1, starting transfers between devices, shards(): other = lax.ppermute(half, 'core', swap)  5.63 us
    pallas_call x2, Pallas kernels, convolve(): pl.pallas_call(functools.partial(conv_kernel, backward), out_shape=jax.Sh...  4.78 us
    ppermute x1, starting transfers between devices, shards(): outer = lax.ppermute(output_grad, AXES, outer_neighbour(sizes))  4.59 us
  transfers between devices with their start and end apart: 15, of which 8 were waited for; matrix products, arithmetic and copies ran while one was open for 4% of the time, Pallas kernels for 3%

profile of v7, /device:TPU:1, one launch (start us, length us, event | category | flops | bytes accessed | tf_op | source)
XLA Modules:
  0.0 188.0 jit_solution(6089708739337224448)
XLA Ops:
  7.2 4.6 %collective-permute-start = (bf16[1,8,32,128]{3,2,1,0:T(8,128)(2,1)}, bf16[1,8,32,128]{3,2,1,0:T(8,128)(2,1)S(1)}, u32[]{:S(2)}, u32[]{:S(2)}) collective-permute-start(bf16[1,8,32,128]{3,2,1,0:T(8,128)(2,1)} %param.5), channel_id=1, source_target_pairs={{4,8},{5,9},{6,10},{7,11},{8,4},{9,5},{10,6},{11,7},{12,16},{13,17... | collective-permute-start | bytes 196616 | tf_op jit(solution)/shard_map/ppermute | solution.py:194
  11.8 1.9 %collective-permute-start.1 = (bf16[1,8,32,128]{3,2,1,0:T(8,128)(2,1)}, bf16[1,8,32,128]{3,2,1,0:T(8,128)(2,1)S(1)}, u32[]{:S(2)}, u32[]{:S(2)}) collective-permute-start(bf16[1,8,32,128]{3,2,1,0:T(8,128)(2,1)} %param.3), channel_id=1, source_target_pairs={{4,8},{5,9},{6,10},{7,11},{8,4},{9,5},{10,6},{11,7},{12,16},{13,17... | collective-permute-start | bytes 196616 | tf_op jit(solution)/shard_map/ppermute | solution.py:195
  13.7 0.2 collective-permute-done
  13.9 0.9 pad_maximum_fusion.1
  14.8 2.8 %collective-permute-done.1 = bf16[1,8,32,128]{3,2,1,0:T(8,128)(2,1)S(1)} collective-permute-done((bf16[1,8,32,128]{3,2,1,0:T(8,128)(2,1)}, bf16[1,8,32,128]{3,2,1,0:T(8,128)(2,1)S(1)}, u32[]{:S(2)}, u32[]{:S(2)}) %collective-permute-start.1) | collective-permute-done | bytes 65568 | tf_op jit(solution)/shard_map/ppermute | solution.py:195
  17.6 0.7 collective-permute-start.2
  18.2 0.9 pad_maximum_fusion.2
  19.1 0.0 collective-permute-done.2
  19.1 0.9 broadcast_in_dim.6
  20.0 13.9 %all-to-all-start = ((bf16[4,2,8,32,128]{4,3,2,1,0:T(8,128)(2,1)}), bf16[4,2,8,32,128]{4,3,2,1,0:T(8,128)(2,1)S(1)}, u32[]{:S(2)}, u32[]{:S(2)}) async-start(bf16[4,2,8,32,128]{4,3,2,1,0:T(8,128)(2,1)} %broadcast_in_dim.6), calls=%async_computation | async-start | bytes 1048576 | tf_op jit(solution)/shard_map/all_to_all | solution.py:176
  33.9 10.9 %all_gather.3.pair = bf16[2,32,32,128]{3,2,1,0:T(8,128)(2,1)S(1)} all-gather(bf16[2,8,32,128]{3,2,1,0:T(8,128)(2,1)S(1)} %collective-permute-done.2), channel_id=1, replica_groups=mesh['chan'=4,'zhi'=4,'ring'=4,'core'=2,'space'=4] {'chan'}, dimensions={1}, use_global_device_ids=true | all-gather | bytes 655360 | tf_op jit(solution)/shard_map/all_gather | solution.py:203
  44.8 1.9 %collective-permute-start.3 = (bf16[32,32,128]{2,1,0:T(8,128)(2,1)S(1)}, bf16[32,32,128]{2,1,0:T(8,128)(2,1)S(1)}, u32[]{:S(2)}, u32[]{:S(2)}) collective-permute-start(bf16[32,32,128]{2,1,0:T(8,128)(2,1)S(1)} %slice_bitcast_fusion), channel_id=1, source_target_pairs={{0,4},{4,0},{1,5},{5,1},{2,6},{6,2},{3,7},{7,3},{8,12},{12,8},{9,1... | collective-permute-start | bytes 786440 | tf_op jit(solution)/shard_map/ppermute | solution.py:204
  46.7 1.5 collective-permute-done.3.inner
  48.2 0.0 all-to-all-done.data.pair
  48.2 0.0 copy-start
  48.2 1.6 filter_grad.1
  49.8 2.0 %collective-permute-start.4 = (f32[1792,128]{1,0:T(8,128)S(1)}, f32[1792,128]{1,0:T(8,128)}, u32[]{:S(2)}, u32[]{:S(2)}) collective-permute-start(f32[1792,128]{1,0:T(8,128)S(1)} %get-tuple-element.29), channel_id=1, source_target_pairs={{0,4},{4,0},{1,5},{5,1},{2,6},{6,2},{3,7},{7,3},{8,12},{12,8},{9,1... | collective-permute-start | bytes 2752520 | tf_op jit(solution)/shard_map/ppermute | solution.py:207
  51.8 0.7 slice.13
  52.5 2.3 %collective-permute-start.5 = (bf16[32,32,128]{2,1,0:T(8,128)(2,1)}, bf16[32,32,128]{2,1,0:T(8,128)(2,1)S(1)}, u32[]{:S(2)}, u32[]{:S(2)}) collective-permute-start(bf16[32,32,128]{2,1,0:T(8,128)(2,1)} %bitcast.2), channel_id=1, source_target_pairs={{0,4},{4,0},{1,5},{5,1},{2,6},{6,2},{3,7},{7,3},{8,12},{12,8},{9,1... | collective-permute-start | bytes 786440 | tf_op jit(solution)/shard_map/ppermute | solution.py:209
  54.8 0.0 copy-done
  54.8 2.4 %input_grad.1 = f32[4,256,128]{2,1,0:T(8,128)} custom-call(s32[1]{0:T(128)} %bitcast.core, bf16[2,32,32,128]{3,2,1,0:T(8,128)(2,1)S(1)} %all_gather.3.pair, bf16[32,32,128]{2,1,0:T(8,128)(2,1)S(1)} %collective-permute-done.3.inner, bf16[27,128,128]{2,1,0:T(8,128)(2,1)S(1)} %copy-done), custom_call_target="tpu_custom_call" | custom-call | flops 905969664 | bytes 3145728 | tf_op jit(solution)/shard_map/input_grad/pallas_call | solution.py:104
  57.3 0.0 collective-permute-done.4
  57.3 2.2 %add.7 = f32[1792,128]{1,0:T(8,128)} add(f32[1792,128]{1,0:T(8,128)S(1)} %get-tuple-element.28, f32[1792,128]{1,0:T(8,128)} %collective-permute-done.4) | non-fusion elementwise | flops 229376 | bytes 2752512 | tf_op jit(solution)/shard_map/add | solution.py:211
  59.5 0.0 copy-start.1
  59.5 0.0 collective-permute-done.5.inner
  59.5 16.6 %all-to-all-start.1 = ((f32[4,448,128]{2,1,0:T(8,128)}), f32[4,448,128]{2,1,0:T(8,128)S(1)}, u32[]{:S(2)}, u32[]{:S(2)}) async-start(f32[4,448,128]{2,1,0:T(8,128)} %bitcast.3), calls=%async_computation.1 | async-start | bytes 1835008 | tf_op jit(solution)/shard_map/all_to_all | solution.py:176
  76.0 0.0 reduce-scatter.3.cloned.1.call-start
  76.0 0.7 reduce-scatter.3.cloned.1.call-update
  76.7 0.0 copy-done.1
  76.7 2.3 %forward.1 = f32[4,256,128]{2,1,0:T(8,128)} custom-call(s32[1]{0:T(128)} %bitcast.core, bf16[4,2,8,32,128]{4,3,2,1,0:T(8,128)(2,1)S(1)} %all-to-all-done.data.pair, bf16[32,32,128]{2,1,0:T(8,128)(2,1)S(1)} %collective-permute-done.5.inner, bf16[27,128,128]{2,1,0:T(8,128)(2,1)S(1)} %copy-done.1), custom_call_target="tpu_custom_call" | custom-call | flops 905969664 | bytes 3145728 | tf_op jit(solution)/shard_map/forward/pallas_call | solution.py:104
  79.1 10.4 %all-to-all-done.1 = f32[4,448,128]{2,1,0:T(8,128)S(1)} async-done(((f32[4,448,128]{2,1,0:T(8,128)}), f32[4,448,128]{2,1,0:T(8,128)S(1)}, u32[]{:S(2)}, u32[]{:S(2)}) %all-to-all-start.1) | async-done | bytes 917536 | tf_op jit(solution)/shard_map/all_to_all | solution.py:176
  89.5 0.7 reduce_sum.18
  90.2 16.0 %all-to-all-start.2 = ((f32[4,112,128]{2,1,0:T(8,128)}), f32[4,112,128]{2,1,0:T(8,128)S(1)}, u32[]{:S(2)}, u32[]{:S(2)}) async-start(f32[4,112,128]{2,1,0:T(8,128)} %bitcast.4), calls=%async_computation.2 | async-start | bytes 458752 | tf_op jit(solution)/shard_map/all_to_all | solution.py:176
  106.2 0.0 reduce-scatter.5.cloned.1.call-start
  106.2 0.7 reduce-scatter.5.cloned.1.call-update
  106.9 19.2 %all-to-all-done.2 = f32[4,112,128]{2,1,0:T(8,128)S(1)} async-done(((f32[4,112,128]{2,1,0:T(8,128)}), f32[4,112,128]{2,1,0:T(8,128)S(1)}, u32[]{:S(2)}, u32[]{:S(2)}) %all-to-all-start.2) | async-done | bytes 229408 | tf_op jit(solution)/shard_map/all_to_all | solution.py:176
  126.2 0.0 reduce-scatter.3.cloned.1.call-done
  126.2 0.7 broadcast_in_dim.7
  126.9 0.0 copy-start.2
  126.9 6.1 %all-to-all-start.3 = ((f32[4,112,128]{2,1,0:T(8,128)}), f32[4,112,128]{2,1,0:T(8,128)S(1)}, u32[]{:S(2)}, u32[]{:S(2)}) async-start(f32[4,112,128]{2,1,0:T(8,128)} %broadcast_in_dim.7), calls=%async_computation.4 | async-start | bytes 458752 | tf_op jit(solution)/shard_map/all_to_all | solution.py:176
  133.0 22.4 %reduce-scatter.5.cloned.1.call-done = f32[1,256,128]{2,1,0:T(8,128)} async-done(((f32[4,256,128]{2,1,0:T(8,128)}), f32[1,256,128]{2,1,0:T(8,128)}) %reduce-scatter.5.cloned.1.call-update) | async-done | bytes 131088 | tf_op jit(solution)/shard_map/reduce_scatter | solution.py:217
  155.4 0.0 copy-start.3
  155.4 0.0 all-to-all-done.3
  155.4 1.0 broadcast_in_dim.8
  156.3 4.0 %all-to-all-start.4 = ((f32[4,448,128]{2,1,0:T(8,128)}), f32[4,448,128]{2,1,0:T(8,128)S(1)}, u32[]{:S(2)}, u32[]{:S(2)}) async-start(f32[4,448,128]{2,1,0:T(8,128)} %broadcast_in_dim.8), calls=%async_computation.6 | async-start | bytes 1835008 | tf_op jit(solution)/shard_map/all_to_all | solution.py:176
  160.4 0.0 copy-done.3
  160.4 0.7 collective-permute-start.6
  161.0 0.0 copy-done.2
  161.1 0.6 convert_element_type.21
  161.7 0.0 collective-permute-done.6
  161.7 9.6 %all-to-all-done.4 = f32[4,448,128]{2,1,0:T(8,128)S(1)} async-done(((f32[4,448,128]{2,1,0:T(8,128)}), f32[4,448,128]{2,1,0:T(8,128)S(1)}, u32[]{:S(2)}, u32[]{:S(2)}) %all-to-all-start.4) | async-done | bytes 917536 | tf_op jit(solution)/shard_map/all_to_all | solution.py:176
  171.3 5.6 %collective-permute-start.7 = (f32[1792,128]{1,0:T(8,128)S(1)}, f32[1792,128]{1,0:T(8,128)S(1)}, u32[]{:S(2)}, u32[]{:S(2)}) collective-permute-start(f32[1792,128]{1,0:T(8,128)S(1)} %bitcast.13), channel_id=1, source_target_pairs={{0,4},{4,0},{1,5},{5,1},{2,6},{6,2},{3,7},{7,3},{8,12},{12,8},{9,1... | collective-permute-start | bytes 2752520 | tf_op jit(solution)/shard_map/ppermute | solution.py:230
  176.9 2.1 %collective-permute-done.7 = f32[1792,128]{1,0:T(8,128)S(1)} collective-permute-done((f32[1792,128]{1,0:T(8,128)S(1)}, f32[1792,128]{1,0:T(8,128)S(1)}, u32[]{:S(2)}, u32[]{:S(2)}) %collective-permute-start.7) | collective-permute-done | bytes 917536 | tf_op jit(solution)/shard_map/ppermute | solution.py:230
  179.0 0.1 slice_select_fusion
  179.1 0.1 broadcast_select_fusion
  179.2 1.3 pad_maximum_fusion
  180.5 0.6 copy.7
  (4 shorter events, 0.0 us)
Async XLA Ops:
  7.2 6.7 %collective-permute-start = (bf16[1,8,32,128]{3,2,1,0:T(8,128)(2,1)}, bf16[1,8,32,128]{3,2,1,0:T(8,128)(2,1)S(1)}, u32[]{:S(2)}, u32[]{:S(2)}) collective-permute-start(bf16[1,8,32,128]{3,2,1,0:T(8,128)(2,1)} %param.5), channel_id=1, source_target_pairs={{4,8},{5,9},{6,10},{7,11},{8,4},{9,5},{10,6},{11,7},{12,16},{13,17... | collective-permute-start | bytes 196616 | tf_op jit(solution)/shard_map/ppermute | solution.py:194
  11.8 5.8 %collective-permute-start.1 = (bf16[1,8,32,128]{3,2,1,0:T(8,128)(2,1)}, bf16[1,8,32,128]{3,2,1,0:T(8,128)(2,1)S(1)}, u32[]{:S(2)}, u32[]{:S(2)}) collective-permute-start(bf16[1,8,32,128]{3,2,1,0:T(8,128)(2,1)} %param.3), channel_id=1, source_target_pairs={{4,8},{5,9},{6,10},{7,11},{8,4},{9,5},{10,6},{11,7},{12,16},{13,17... | collective-permute-start | bytes 196616 | tf_op jit(solution)/shard_map/ppermute | solution.py:195
  17.6 1.5 collective-permute-start.2
  20.0 28.2 %all-to-all-start = ((bf16[4,2,8,32,128]{4,3,2,1,0:T(8,128)(2,1)}), bf16[4,2,8,32,128]{4,3,2,1,0:T(8,128)(2,1)S(1)}, u32[]{:S(2)}, u32[]{:S(2)}) async-start(bf16[4,2,8,32,128]{4,3,2,1,0:T(8,128)(2,1)} %broadcast_in_dim.6), calls=%async_computation | async-start | bytes 1048576 | tf_op jit(solution)/shard_map/all_to_all | solution.py:176
  44.8 3.4 %collective-permute-start.3 = (bf16[32,32,128]{2,1,0:T(8,128)(2,1)S(1)}, bf16[32,32,128]{2,1,0:T(8,128)(2,1)S(1)}, u32[]{:S(2)}, u32[]{:S(2)}) collective-permute-start(bf16[32,32,128]{2,1,0:T(8,128)(2,1)S(1)} %slice_bitcast_fusion), channel_id=1, source_target_pairs={{0,4},{4,0},{1,5},{5,1},{2,6},{6,2},{3,7},{7,3},{8,12},{12,8},{9,1... | collective-permute-start | bytes 786440 | tf_op jit(solution)/shard_map/ppermute | solution.py:204
  48.2 6.6 %copy-start = (bf16[27,128,128]{2,1,0:T(8,128)(2,1)S(1)}, bf16[27,128,128]{2,1,0:T(8,128)(2,1)}, u32[]{:S(2)}) copy-start(bf16[27,128,128]{2,1,0:T(8,128)(2,1)} %weight.3) | copy-start | bytes 2654212
  49.8 7.5 %collective-permute-start.4 = (f32[1792,128]{1,0:T(8,128)S(1)}, f32[1792,128]{1,0:T(8,128)}, u32[]{:S(2)}, u32[]{:S(2)}) collective-permute-start(f32[1792,128]{1,0:T(8,128)S(1)} %get-tuple-element.29), channel_id=1, source_target_pairs={{0,4},{4,0},{1,5},{5,1},{2,6},{6,2},{3,7},{7,3},{8,12},{12,8},{9,1... | collective-permute-start | bytes 2752520 | tf_op jit(solution)/shard_map/ppermute | solution.py:207
  52.5 6.9 %collective-permute-start.5 = (bf16[32,32,128]{2,1,0:T(8,128)(2,1)}, bf16[32,32,128]{2,1,0:T(8,128)(2,1)S(1)}, u32[]{:S(2)}, u32[]{:S(2)}) collective-permute-start(bf16[32,32,128]{2,1,0:T(8,128)(2,1)} %bitcast.2), channel_id=1, source_target_pairs={{0,4},{4,0},{1,5},{5,1},{2,6},{6,2},{3,7},{7,3},{8,12},{12,8},{9,1... | collective-permute-start | bytes 786440 | tf_op jit(solution)/shard_map/ppermute | solution.py:209
  59.5 17.3 %copy-start.1 = (bf16[27,128,128]{2,1,0:T(8,128)(2,1)S(1)}, bf16[27,128,128]{2,1,0:T(8,128)(2,1)}, u32[]{:S(2)}) copy-start(bf16[27,128,128]{2,1,0:T(8,128)(2,1)} %weight.3) | copy-start | bytes 2654212
  59.5 30.0 %all-to-all-start.1 = ((f32[4,448,128]{2,1,0:T(8,128)}), f32[4,448,128]{2,1,0:T(8,128)S(1)}, u32[]{:S(2)}, u32[]{:S(2)}) async-start(f32[4,448,128]{2,1,0:T(8,128)} %bitcast.3), calls=%async_computation.1 | async-start | bytes 1835008 | tf_op jit(solution)/shard_map/all_to_all | solution.py:176
  76.0 50.2 %reduce-scatter.3.cloned.1.call-start = ((), (), s32[]{:S(2)}) async-start(), calls=%async_computation.7 | async-start | bytes 655360 | tf_op jit(solution)/shard_map/reduce_scatter | solution.py:212
  90.2 36.0 %all-to-all-start.2 = ((f32[4,112,128]{2,1,0:T(8,128)}), f32[4,112,128]{2,1,0:T(8,128)S(1)}, u32[]{:S(2)}, u32[]{:S(2)}) async-start(f32[4,112,128]{2,1,0:T(8,128)} %bitcast.4), calls=%async_computation.2 | async-start | bytes 458752 | tf_op jit(solution)/shard_map/all_to_all | solution.py:176
  106.2 49.1 %reduce-scatter.5.cloned.1.call-start = ((), (), s32[]{:S(2)}) async-start(), calls=%async_computation.8 | async-start | bytes 655360 | tf_op jit(solution)/shard_map/reduce_scatter | solution.py:217
  126.9 34.1 %copy-start.2 = (f32[1,256,128]{2,1,0:T(8,128)S(1)}, f32[1,256,128]{2,1,0:T(8,128)}, u32[]{:S(2)}) copy-start(f32[1,256,128]{2,1,0:T(8,128)} %reduce-scatter.3.cloned.1.call-done) | copy-start | bytes 393220
  126.9 28.4 %all-to-all-start.3 = ((f32[4,112,128]{2,1,0:T(8,128)}), f32[4,112,128]{2,1,0:T(8,128)S(1)}, u32[]{:S(2)}, u32[]{:S(2)}) async-start(f32[4,112,128]{2,1,0:T(8,128)} %broadcast_in_dim.7), calls=%async_computation.4 | async-start | bytes 458752 | tf_op jit(solution)/shard_map/all_to_all | solution.py:176
  155.4 5.0 %copy-start.3 = (f32[1,256,128]{2,1,0:T(8,128)S(1)}, f32[1,256,128]{2,1,0:T(8,128)}, u32[]{:S(2)}) copy-start(f32[1,256,128]{2,1,0:T(8,128)} %reduce-scatter.5.cloned.1.call-done) | copy-start | bytes 393220
  156.3 14.9 %all-to-all-start.4 = ((f32[4,448,128]{2,1,0:T(8,128)}), f32[4,448,128]{2,1,0:T(8,128)S(1)}, u32[]{:S(2)}, u32[]{:S(2)}) async-start(f32[4,448,128]{2,1,0:T(8,128)} %broadcast_in_dim.8), calls=%async_computation.6 | async-start | bytes 1835008 | tf_op jit(solution)/shard_map/all_to_all | solution.py:176
  160.4 1.3 collective-permute-start.6
  171.3 7.7 %collective-permute-start.7 = (f32[1792,128]{1,0:T(8,128)S(1)}, f32[1792,128]{1,0:T(8,128)S(1)}, u32[]{:S(2)}, u32[]{:S(2)}) collective-permute-start(f32[1792,128]{1,0:T(8,128)S(1)} %bitcast.13), channel_id=1, source_target_pairs={{0,4},{4,0},{1,5},{5,1},{2,6},{6,2},{3,7},{7,3},{8,12},{12,8},{9,1... | collective-permute-start | bytes 2752520 | tf_op jit(solution)/shard_map/ppermute | solution.py:230
Sparse Core Ops, SparseCore 0:
  79.7 41.3 reduce-scatter.2
  123.8 31.4 reduce-scatter.4

commit v8 on v6

--- a/solution.py
+++ b/solution.py
@@ -184,12 +184,9 @@
     return exchange(jnp.broadcast_to(block[None], (count, *block.shape)), axis)
 
 
-def reduced(terms, axis):
-    count = len(terms)
-    total = terms[0]
-    for step in range(1, count):
-        total += lax.ppermute(terms[step], axis, [(i, (i + step) % count) for i in range(count)])
-    return total
+def rotate(term, axis, step):
+    count = lax.axis_size(axis)
+    return lax.ppermute(term, axis, [(i, (i + step) % count) for i in range(count)])
 
 
 def after(value, *others):
@@ -203,39 +200,46 @@
     swap = [(0, 1), (1, 0)]
 
     outer = lax.ppermute(output_grad, AXES, outer_neighbour(sizes))
-    grad = jnp.concatenate([output_grad, outer], axis=0)
-    grad, later = lax.optimization_barrier((grad, activations))
+    outer_data = lax.ppermute(activations, AXES, outer_neighbour(sizes))
+    grad, outer_data = lax.optimization_barrier(
+        (jnp.concatenate([output_grad, outer], axis=0), outer_data)
+    )
     grad = lax.ppermute(grad, AXES, transposed(sizes))
-    outer = lax.ppermute(later, AXES, outer_neighbour(sizes))
-    data = gather(jnp.concatenate([activations, outer], axis=0), "space")
-    grad = lax.all_gather(after(grad, outer), "chan", axis=1, tiled=True)
+    data = jnp.concatenate([activations, outer_data], axis=0)
+    grad, data = lax.optimization_barrier((grad, data))
+    data = gather(data, "space")
+    grad = lax.all_gather(grad, "chan", axis=1, tiled=True)
     grad_inner = lax.ppermute(grad[0], "core", swap)
 
     keep, send = filter_partial(core, data, grad, grad_inner)
-    moved = lax.ppermute(send, "core", swap)
-    own = after(data[:, 0].reshape(grad_inner.shape), send)
-    data_inner = lax.ppermute(own, "core", swap)
-    half, data_inner = lax.optimization_barrier((keep + moved, data_inner))
+    half = keep + lax.ppermute(send, "core", swap)
 
     moved = exchange(half.reshape(rings, -1, lanes), "ring")
     me = lax.axis_index("space")
     back = convolve(True, core, me, after(grad, half), grad_inner, weight, spaces)
-    input_grad = reduced(back, "space").astype(BF16).reshape(activations.shape)
-    quarter, input_grad = lax.optimization_barrier((moved.sum(0), input_grad))
+    back = [back[0], rotate(back[1], "space", 1), rotate(back[2], "space", 2), back[3]]
+    quarter, *back = lax.optimization_barrier((moved.sum(0), *back))
 
     moved = exchange(quarter.reshape(zhis, -1, lanes), "zhi")
+    own = after(data[:, 0].reshape(grad_inner.shape), quarter)
+    data_inner = lax.ppermute(own, "core", swap)
     me = lax.axis_index("chan")
     forward = convolve(False, core, me, after(data, quarter), data_inner, weight, spaces)
-    forward = reduced(forward, "chan").astype(BF16)
+    forward = [forward[0], rotate(forward[1], "chan", 1), *forward[2:]]
+    back[3] = rotate(back[3], "space", 3)
     cell_count = sizes[1] * rings * cores * grad.shape[1] * grad.shape[2]
     part = moved.sum(0) / math.sqrt(cell_count)
-    part, forward = lax.optimization_barrier((part, forward))
+    part, back, forward = lax.optimization_barrier((part, back, forward))
 
     quarter = gather(part, "zhi").reshape(-1, lanes)
-    output = lax.ppermute(forward, AXES, transposed(sizes)).reshape(activations.shape)
-    quarter, output = lax.optimization_barrier((quarter, output))
+    forward = [*forward[:2], rotate(forward[2], "chan", 2), rotate(forward[3], "chan", 3)]
+    input_grad = sum(back).astype(BF16).reshape(activations.shape)
+    quarter, forward, input_grad = lax.optimization_barrier((quarter, forward, input_grad))
 
     half = gather(quarter, "ring").reshape(-1, lanes)
+    output = lax.ppermute(sum(forward).astype(BF16), AXES, transposed(sizes))
+    output = output.reshape(activations.shape)
+    half, output = lax.optimization_barrier((half, output))
 
     other = lax.ppermute(half, "core", swap)
     first = core == 0

time: 185 us -> 169 us (0.914); the launches traced: 181 us -> 168 us
  blocking collectives: 39.7 us -> 10.9 us
  starting transfers between devices: 93.6 us -> 106 us
    all_gather x1, blocking collectives: 26.5 us -> 10.9 us  [shards(): grad = lax.all_gather(grad, 'chan', axis=1, tiled=True)]
    all_to_all x1 -> x0, blocking collectives: 13.2 us -> none  [exchange(): return lax.all_to_all(block, axis, split_axis=0, concat_axis=0, tiled=True)]
    all_to_all x4 -> x5, starting transfers between devices: 51.7 us -> 62.9 us  [exchange(): return lax.all_to_all(block, axis, split_axis=0, concat_axis=0, tiled=True)]
    all_to_all x4 -> x5, waiting for transfers between devices: 15.1 us -> 18 us  [exchange(): return lax.all_to_all(block, axis, split_axis=0, concat_axis=0, tiled=True)]
    ppermute x1, waiting for transfers between devices: 2.15 us -> 0.21 us  [shards(): outer = lax.ppermute(output_grad, AXES, outer_neighbour(sizes))]
  transfers between devices with their start and end apart: 18 -> 19, of which waited for: 10 -> 14; matrix products, arithmetic and copies ran while one was open for 1% -> 3% of each run, Pallas kernels for 2% -> 3%
where the time goes in v8:
time: 169 us; the launch traced here: 168 us
  starting transfers between devices  106 us (63%)
  waiting for transfers between devices  34.1 us (20%)
  blocking collectives  10.9 us (6%)
  other arithmetic  7.03 us (4%)
  Pallas kernels  5.82 us (3%)
  local copies, waits for them, and re-layouts  3.23 us (2%)
    all_to_all x5, starting transfers between devices, exchange(): return lax.all_to_all(block, axis, split_axis=0, concat_axis=0, tiled=True)  62.9 us
    ppermute x6, starting transfers between devices, rotate(): lax.ppermute(term, axis, [(i, (i + step) % count) for i in range(count)])  20.4 us
    all_to_all x5, waiting for transfers between devices, exchange(): return lax.all_to_all(block, axis, split_axis=0, concat_axis=0, tiled=True)  18 us
    all_gather x1, blocking collectives, shards(): grad = lax.all_gather(grad, 'chan', axis=1, tiled=True)  10.9 us
    ppermute x1, starting transfers between devices, shards(): other = lax.ppermute(half, 'core', swap)  7.46 us
    ppermute x6, waiting for transfers between devices, rotate(): lax.ppermute(term, axis, [(i, (i + step) % count) for i in range(count)])  7.18 us
    ppermute x1, starting transfers between devices, shards(): outer = lax.ppermute(output_grad, AXES, outer_neighbour(sizes))  4.59 us
    pallas_call x2, Pallas kernels, convolve(): pl.pallas_call(functools.partial(conv_kernel, backward), out_shape=[jax.S...  4.25 us
  transfers between devices with their start and end apart: 19, of which 14 were waited for; matrix products, arithmetic and copies ran while one was open for 3% of the time, Pallas kernels for 3%

profile of v8, /device:TPU:1, one launch (start us, length us, event | category | flops | bytes accessed | tf_op | source)
XLA Modules:
  0.0 167.7 jit_solution(15936609192470800289)
XLA Ops:
  0.6 4.6 %collective-permute-start = (bf16[1,8,32,128]{3,2,1,0:T(8,128)(2,1)}, bf16[1,8,32,128]{3,2,1,0:T(8,128)(2,1)S(1)}, u32[]{:S(2)}, u32[]{:S(2)}) collective-permute-start(bf16[1,8,32,128]{3,2,1,0:T(8,128)(2,1)} %param.5), channel_id=1, source_target_pairs={{4,8},{5,9},{6,10},{7,11},{8,4},{9,5},{10,6},{11,7},{12,16},{13,17... | collective-permute-start | bytes 196616 | tf_op jit(solution)/shard_map/ppermute | solution.py:202
  5.2 1.9 %collective-permute-start.1 = (bf16[1,8,32,128]{3,2,1,0:T(8,128)(2,1)}, bf16[1,8,32,128]{3,2,1,0:T(8,128)(2,1)S(1)}, u32[]{:S(2)}, u32[]{:S(2)}) collective-permute-start(bf16[1,8,32,128]{3,2,1,0:T(8,128)(2,1)} %param.3), channel_id=1, source_target_pairs={{4,8},{5,9},{6,10},{7,11},{8,4},{9,5},{10,6},{11,7},{12,16},{13,17... | collective-permute-start | bytes 196616 | tf_op jit(solution)/shard_map/ppermute | solution.py:203
  7.2 0.2 collective-permute-done
  7.4 0.9 pad_maximum_fusion.1
  8.2 2.8 %collective-permute-done.1 = bf16[1,8,32,128]{3,2,1,0:T(8,128)(2,1)S(1)} collective-permute-done((bf16[1,8,32,128]{3,2,1,0:T(8,128)(2,1)}, bf16[1,8,32,128]{3,2,1,0:T(8,128)(2,1)S(1)}, u32[]{:S(2)}, u32[]{:S(2)}) %collective-permute-start.1) | collective-permute-done | bytes 65568 | tf_op jit(solution)/shard_map/ppermute | solution.py:203
  11.0 0.7 collective-permute-start.2
  11.7 0.9 pad_maximum_fusion.2
  12.6 0.0 collective-permute-done.2
  12.6 0.9 broadcast_in_dim.6
  13.4 13.9 %all-to-all-start = ((bf16[4,2,8,32,128]{4,3,2,1,0:T(8,128)(2,1)}), bf16[4,2,8,32,128]{4,3,2,1,0:T(8,128)(2,1)S(1)}, u32[]{:S(2)}, u32[]{:S(2)}) async-start(bf16[4,2,8,32,128]{4,3,2,1,0:T(8,128)(2,1)} %broadcast_in_dim.6), calls=%async_computation | async-start | bytes 1048576 | tf_op jit(solution)/shard_map/all_to_all | solution.py:179
  27.3 10.9 %all_gather.3.pair = bf16[2,32,32,128]{3,2,1,0:T(8,128)(2,1)S(1)} all-gather(bf16[2,8,32,128]{3,2,1,0:T(8,128)(2,1)S(1)} %collective-permute-done.2), channel_id=1, replica_groups=mesh['chan'=4,'zhi'=4,'ring'=4,'core'=2,'space'=4] {'chan'}, dimensions={1}, use_global_device_ids=true | all-gather | bytes 655360 | tf_op jit(solution)/shard_map/all_gather | solution.py:211
  38.2 1.9 %collective-permute-start.3 = (bf16[32,32,128]{2,1,0:T(8,128)(2,1)S(1)}, bf16[32,32,128]{2,1,0:T(8,128)(2,1)S(1)}, u32[]{:S(2)}, u32[]{:S(2)}) collective-permute-start(bf16[32,32,128]{2,1,0:T(8,128)(2,1)S(1)} %slice_bitcast_fusion), channel_id=1, source_target_pairs={{0,4},{4,0},{1,5},{5,1},{2,6},{6,2},{3,7},{7,3},{8,12},{12,8},{9,1... | collective-permute-start | bytes 786440 | tf_op jit(solution)/shard_map/ppermute | solution.py:212
  40.2 1.5 collective-permute-done.3.inner
  41.7 0.0 all-to-all-done.data.pair
  41.7 1.6 filter_grad.1
  43.2 2.0 %collective-permute-start.4 = (f32[1792,128]{1,0:T(8,128)S(1)}, f32[1792,128]{1,0:T(8,128)S(1)}, u32[]{:S(2)}, u32[]{:S(2)}) collective-permute-start(f32[1792,128]{1,0:T(8,128)S(1)} %get-tuple-element.47), channel_id=1, source_target_pairs={{0,4},{4,0},{1,5},{5,1},{2,6},{6,2},{3,7},{7,3},{8,12},{12,8},{9,1... | collective-permute-start | bytes 2752520 | tf_op jit(solution)/shard_map/ppermute | solution.py:215
  45.3 2.3 %collective-permute-done.4 = f32[1792,128]{1,0:T(8,128)S(1)} collective-permute-done((f32[1792,128]{1,0:T(8,128)S(1)}, f32[1792,128]{1,0:T(8,128)S(1)}, u32[]{:S(2)}, u32[]{:S(2)}) %collective-permute-start.4) | collective-permute-done | bytes 917536 | tf_op jit(solution)/shard_map/ppermute | solution.py:215
  47.6 0.0 copy-start
  47.6 1.0 add.21
  48.6 16.4 %all-to-all-start.1 = ((f32[4,448,128]{2,1,0:T(8,128)}), f32[4,448,128]{2,1,0:T(8,128)}, u32[]{:S(2)}, u32[]{:S(2)}) async-start(f32[4,448,128]{2,1,0:T(8,128)} %bitcast.2), calls=%async_computation.1 | async-start | bytes 1835008 | tf_op jit(solution)/shard_map/all_to_all | solution.py:179
  65.0 0.1 pad_add_fusion.place
  65.1 0.0 copy-done
  65.1 2.2 %input_grad.1 = (f32[256,128]{1,0:T(8,128)S(1)}, f32[256,128]{1,0:T(8,128)S(1)}, f32[256,128]{1,0:T(8,128)S(1)}, f32[256,128]{1,0:T(8,128)S(1)}) custom-call(s32[2]{0:T(128)S(1)} %pad_add_fusion.place, bf16[2,32,32,128]{3,2,1,0:T(8,128)(2,1)S(1)} %all_gather.3.pair, bf16[32,32,128]{2,1,0:T(8,128)(2,1)S(1)} %collective-permute-done.3.inner, ...), custom_call_target="tpu_custom_call" | custom-call | flops 905969664 | bytes 3145728 | tf_op jit(solution)/shard_map/input_grad/pallas_call | solution.py:107
  67.2 3.4 %collective-permute-start.5 = (f32[256,128]{1,0:T(8,128)S(1)}, f32[256,128]{1,0:T(8,128)S(1)}, u32[]{:S(2)}, u32[]{:S(2)}) collective-permute-start(f32[256,128]{1,0:T(8,128)S(1)} %get-tuple-element.50), channel_id=1, source_target_pairs={{0,1},{1,2},{2,3},{3,0},{4,5},{5,6},{6,7},{7,4},{8,9},{9,10},{10,1... | collective-permute-start | bytes 393224 | tf_op jit(solution)/shard_map/ppermute | solution.py:189
  70.6 4.0 %collective-permute-start.6 = (f32[256,128]{1,0:T(8,128)S(1)}, f32[256,128]{1,0:T(8,128)S(1)}, u32[]{:S(2)}, u32[]{:S(2)}) collective-permute-start(f32[256,128]{1,0:T(8,128)S(1)} %get-tuple-element.51), channel_id=1, source_target_pairs={{0,2},{1,3},{2,0},{3,1},{4,6},{5,7},{6,4},{7,5},{8,10},{9,11},{10,... | collective-permute-start | bytes 393224 | tf_op jit(solution)/shard_map/ppermute | solution.py:189
  74.6 3.9 %all-to-all-done.1 = f32[4,448,128]{2,1,0:T(8,128)} async-done(((f32[4,448,128]{2,1,0:T(8,128)}), f32[4,448,128]{2,1,0:T(8,128)}, u32[]{:S(2)}, u32[]{:S(2)}) %all-to-all-start.1) | async-done | bytes 917536 | tf_op jit(solution)/shard_map/all_to_all | solution.py:179
  78.5 1.9 %reduce_sum.18 = f32[448,128]{1,0:T(8,128)} reduce(f32[4,448,128]{2,1,0:T(8,128)} %all-to-all-done.1, f32[]{:T(128)} %constant.15.clone.1), dimensions={0}, to_apply=%region_0.0 | reduce | flops 172032 | bytes 1146884 | tf_op jit(solution)/shard_map/reduce_sum | solution.py:221
  80.4 0.0 collective-permute-done.5
  80.4 1.0 collective-permute-done.6
  81.4 17.1 %all-to-all-start.2 = ((f32[4,112,128]{2,1,0:T(8,128)}), f32[4,112,128]{2,1,0:T(8,128)S(1)}, u32[]{:S(2)}, u32[]{:S(2)}) async-start(f32[4,112,128]{2,1,0:T(8,128)} %bitcast.4), calls=%async_computation.2 | async-start | bytes 458752 | tf_op jit(solution)/shard_map/all_to_all | solution.py:179
  98.5 3.3 %collective-permute-start.8 = (bf16[32,32,128]{2,1,0:T(8,128)(2,1)S(1)}, bf16[32,32,128]{2,1,0:T(8,128)(2,1)S(1)}, u32[]{:S(2)}, u32[]{:S(2)}) collective-permute-start(bf16[32,32,128]{2,1,0:T(8,128)(2,1)S(1)} %bitcast.18), channel_id=1, source_target_pairs={{0,4},{4,0},{1,5},{5,1},{2,6},{6,2},{3,7},{7,3},{8,12},{12,8},{9,1... | collective-permute-start | bytes 786440 | tf_op jit(solution)/shard_map/ppermute | solution.py:225
  101.8 0.1 pad_add_fusion.1.place
  101.8 4.3 %collective-permute-start.7 = (f32[256,128]{1,0:T(8,128)S(1)}, f32[256,128]{1,0:T(8,128)S(1)}, u32[]{:S(2)}, u32[]{:S(2)}) collective-permute-start(f32[256,128]{1,0:T(8,128)S(1)} %get-tuple-element.57), channel_id=1, source_target_pairs={{0,3},{1,0},{2,1},{3,2},{4,7},{5,4},{6,5},{7,6},{8,11},{9,8},{10,9... | collective-permute-start | bytes 393224 | tf_op jit(solution)/shard_map/ppermute | solution.py:189
  106.2 0.0 collective-permute-done.8.inner
  106.2 2.1 %forward.1 = (f32[256,128]{1,0:T(8,128)S(1)}, f32[256,128]{1,0:T(8,128)S(1)}, f32[256,128]{1,0:T(8,128)S(1)}, f32[256,128]{1,0:T(8,128)S(1)}) custom-call(s32[2]{0:T(128)S(1)} %pad_add_fusion.1.place, bf16[4,2,8,32,128]{4,3,2,1,0:T(8,128)(2,1)S(1)} %all-to-all-done.data.pair, bf16[32,32,128]{2,1,0:T(8,128)(2,1)S(1)} %collective-permute-done.8.inner, ...), custom_call_target="tpu_custom_call" | custom-call | flops 905969664 | bytes 3145728 | tf_op jit(solution)/shard_map/forward/pallas_call | solution.py:107
  108.3 2.8 %collective-permute-start.9 = (f32[256,128]{1,0:T(8,128)S(1)}, f32[256,128]{1,0:T(8,128)S(1)}, u32[]{:S(2)}, u32[]{:S(2)}) collective-permute-start(f32[256,128]{1,0:T(8,128)S(1)} %get-tuple-element.61), channel_id=1, source_target_pairs={{0,128},{128,256},{256,384},{384,0},{1,129},{129,257},{257,385},{3... | collective-permute-start | bytes 393224 | tf_op jit(solution)/shard_map/ppermute | solution.py:189
  111.1 1.7 all-to-all-done.2
  112.8 0.4 collective-permute-done.7
  113.2 3.0 %collective-permute-done.9 = f32[256,128]{1,0:T(8,128)S(1)} collective-permute-done((f32[256,128]{1,0:T(8,128)S(1)}, f32[256,128]{1,0:T(8,128)S(1)}, u32[]{:S(2)}, u32[]{:S(2)}) %collective-permute-start.9) | collective-permute-done | bytes 131104 | tf_op jit(solution)/shard_map/ppermute | solution.py:189
  116.2 0.7 broadcast_in_dim.7
  116.9 11.7 %all-to-all-start.3 = ((f32[4,112,128]{2,1,0:T(8,128)}), f32[4,112,128]{2,1,0:T(8,128)S(1)}, u32[]{:S(2)}, u32[]{:S(2)}) async-start(f32[4,112,128]{2,1,0:T(8,128)} %broadcast_in_dim.7), calls=%async_computation.3 | async-start | bytes 458752 | tf_op jit(solution)/shard_map/all_to_all | solution.py:179
  128.6 2.0 %collective-permute-start.10 = (f32[256,128]{1,0:T(8,128)S(1)}, f32[256,128]{1,0:T(8,128)S(1)}, u32[]{:S(2)}, u32[]{:S(2)}) collective-permute-start(f32[256,128]{1,0:T(8,128)S(1)} %get-tuple-element.67), channel_id=1, source_target_pairs={{0,256},{128,384},{256,0},{384,128},{1,257},{129,385},{257,1},{385... | collective-permute-start | bytes 393224 | tf_op jit(solution)/shard_map/ppermute | solution.py:189
  130.6 3.9 %collective-permute-start.11 = (f32[256,128]{1,0:T(8,128)S(1)}, f32[256,128]{1,0:T(8,128)S(1)}, u32[]{:S(2)}, u32[]{:S(2)}) collective-permute-start(f32[256,128]{1,0:T(8,128)S(1)} %get-tuple-element.68), channel_id=1, source_target_pairs={{0,384},{128,0},{256,128},{384,256},{1,385},{129,1},{257,129},{385... | collective-permute-start | bytes 393224 | tf_op jit(solution)/shard_map/ppermute | solution.py:189
  134.5 0.7 add_convert_fusion.1
  135.2 0.6 collective-permute-done.10
  135.8 2.2 %collective-permute-done.11 = f32[256,128]{1,0:T(8,128)S(1)} collective-permute-done((f32[256,128]{1,0:T(8,128)S(1)}, f32[256,128]{1,0:T(8,128)S(1)}, u32[]{:S(2)}, u32[]{:S(2)}) %collective-permute-start.11) | collective-permute-done | bytes 131104 | tf_op jit(solution)/shard_map/ppermute | solution.py:189
  138.0 4.1 %all-to-all-done.3 = f32[4,112,128]{2,1,0:T(8,128)S(1)} async-done(((f32[4,112,128]{2,1,0:T(8,128)}), f32[4,112,128]{2,1,0:T(8,128)S(1)}, u32[]{:S(2)}, u32[]{:S(2)}) %all-to-all-start.3) | async-done | bytes 229408 | tf_op jit(solution)/shard_map/all_to_all | solution.py:179
  142.1 1.0 broadcast_in_dim.8
  143.1 3.8 %all-to-all-start.4 = ((f32[4,448,128]{2,1,0:T(8,128)}), f32[4,448,128]{2,1,0:T(8,128)S(1)}, u32[]{:S(2)}, u32[]{:S(2)}) async-start(f32[4,448,128]{2,1,0:T(8,128)} %broadcast_in_dim.8), calls=%async_computation.4 | async-start | bytes 1835008 | tf_op jit(solution)/shard_map/all_to_all | solution.py:179
  146.9 0.7 collective-permute-start.12
  147.6 0.0 collective-permute-done.12
  147.6 8.4 %all-to-all-done.4 = f32[4,448,128]{2,1,0:T(8,128)S(1)} async-done(((f32[4,448,128]{2,1,0:T(8,128)}), f32[4,448,128]{2,1,0:T(8,128)S(1)}, u32[]{:S(2)}, u32[]{:S(2)}) %all-to-all-start.4) | async-done | bytes 917536 | tf_op jit(solution)/shard_map/all_to_all | solution.py:179
  156.0 7.5 %collective-permute-start.13 = (f32[1792,128]{1,0:T(8,128)S(1)}, f32[1792,128]{1,0:T(8,128)S(1)}, u32[]{:S(2)}, u32[]{:S(2)}) collective-permute-start(f32[1792,128]{1,0:T(8,128)S(1)} %bitcast.13), channel_id=1, source_target_pairs={{0,4},{4,0},{1,5},{5,1},{2,6},{6,2},{3,7},{7,3},{8,12},{12,8},{9,1... | collective-permute-start | bytes 2752520 | tf_op jit(solution)/shard_map/ppermute | solution.py:244
  163.5 2.1 %collective-permute-done.13 = f32[1792,128]{1,0:T(8,128)S(1)} collective-permute-done((f32[1792,128]{1,0:T(8,128)S(1)}, f32[1792,128]{1,0:T(8,128)S(1)}, u32[]{:S(2)}, u32[]{:S(2)}) %collective-permute-start.13) | collective-permute-done | bytes 917536 | tf_op jit(solution)/shard_map/ppermute | solution.py:244
  165.5 0.1 slice_select_fusion
  165.6 0.1 broadcast_select_fusion
  165.7 1.3 pad_maximum_fusion
  167.1 0.6 copy.7
  (5 shorter events, 0.1 us)
Async XLA Ops:
  0.6 6.7 %collective-permute-start = (bf16[1,8,32,128]{3,2,1,0:T(8,128)(2,1)}, bf16[1,8,32,128]{3,2,1,0:T(8,128)(2,1)S(1)}, u32[]{:S(2)}, u32[]{:S(2)}) collective-permute-start(bf16[1,8,32,128]{3,2,1,0:T(8,128)(2,1)} %param.5), channel_id=1, source_target_pairs={{4,8},{5,9},{6,10},{7,11},{8,4},{9,5},{10,6},{11,7},{12,16},{13,17... | collective-permute-start | bytes 196616 | tf_op jit(solution)/shard_map/ppermute | solution.py:202
  5.2 5.8 %collective-permute-start.1 = (bf16[1,8,32,128]{3,2,1,0:T(8,128)(2,1)}, bf16[1,8,32,128]{3,2,1,0:T(8,128)(2,1)S(1)}, u32[]{:S(2)}, u32[]{:S(2)}) collective-permute-start(bf16[1,8,32,128]{3,2,1,0:T(8,128)(2,1)} %param.3), channel_id=1, source_target_pairs={{4,8},{5,9},{6,10},{7,11},{8,4},{9,5},{10,6},{11,7},{12,16},{13,17... | collective-permute-start | bytes 196616 | tf_op jit(solution)/shard_map/ppermute | solution.py:203
  11.0 1.5 collective-permute-start.2
  13.4 28.2 %all-to-all-start = ((bf16[4,2,8,32,128]{4,3,2,1,0:T(8,128)(2,1)}), bf16[4,2,8,32,128]{4,3,2,1,0:T(8,128)(2,1)S(1)}, u32[]{:S(2)}, u32[]{:S(2)}) async-start(bf16[4,2,8,32,128]{4,3,2,1,0:T(8,128)(2,1)} %broadcast_in_dim.6), calls=%async_computation | async-start | bytes 1048576 | tf_op jit(solution)/shard_map/all_to_all | solution.py:179
  38.2 3.4 %collective-permute-start.3 = (bf16[32,32,128]{2,1,0:T(8,128)(2,1)S(1)}, bf16[32,32,128]{2,1,0:T(8,128)(2,1)S(1)}, u32[]{:S(2)}, u32[]{:S(2)}) collective-permute-start(bf16[32,32,128]{2,1,0:T(8,128)(2,1)S(1)} %slice_bitcast_fusion), channel_id=1, source_target_pairs={{0,4},{4,0},{1,5},{5,1},{2,6},{6,2},{3,7},{7,3},{8,12},{12,8},{9,1... | collective-permute-start | bytes 786440 | tf_op jit(solution)/shard_map/ppermute | solution.py:212
  43.2 4.4 %collective-permute-start.4 = (f32[1792,128]{1,0:T(8,128)S(1)}, f32[1792,128]{1,0:T(8,128)S(1)}, u32[]{:S(2)}, u32[]{:S(2)}) collective-permute-start(f32[1792,128]{1,0:T(8,128)S(1)} %get-tuple-element.47), channel_id=1, source_target_pairs={{0,4},{4,0},{1,5},{5,1},{2,6},{6,2},{3,7},{7,3},{8,12},{12,8},{9,1... | collective-permute-start | bytes 2752520 | tf_op jit(solution)/shard_map/ppermute | solution.py:215
  47.6 17.5 %copy-start = (bf16[27,128,128]{2,1,0:T(8,128)(2,1)S(1)}, bf16[27,128,128]{2,1,0:T(8,128)(2,1)}, u32[]{:S(2)}) copy-start(bf16[27,128,128]{2,1,0:T(8,128)(2,1)} %weight.3) | copy-start | bytes 2654212
  48.6 29.9 %all-to-all-start.1 = ((f32[4,448,128]{2,1,0:T(8,128)}), f32[4,448,128]{2,1,0:T(8,128)}, u32[]{:S(2)}, u32[]{:S(2)}) async-start(f32[4,448,128]{2,1,0:T(8,128)} %bitcast.2), calls=%async_computation.1 | async-start | bytes 1835008 | tf_op jit(solution)/shard_map/all_to_all | solution.py:179
  67.2 13.2 %collective-permute-start.5 = (f32[256,128]{1,0:T(8,128)S(1)}, f32[256,128]{1,0:T(8,128)S(1)}, u32[]{:S(2)}, u32[]{:S(2)}) collective-permute-start(f32[256,128]{1,0:T(8,128)S(1)} %get-tuple-element.50), channel_id=1, source_target_pairs={{0,1},{1,2},{2,3},{3,0},{4,5},{5,6},{6,7},{7,4},{8,9},{9,10},{10,1... | collective-permute-start | bytes 393224 | tf_op jit(solution)/shard_map/ppermute | solution.py:189
  70.6 10.8 %collective-permute-start.6 = (f32[256,128]{1,0:T(8,128)S(1)}, f32[256,128]{1,0:T(8,128)S(1)}, u32[]{:S(2)}, u32[]{:S(2)}) collective-permute-start(f32[256,128]{1,0:T(8,128)S(1)} %get-tuple-element.51), channel_id=1, source_target_pairs={{0,2},{1,3},{2,0},{3,1},{4,6},{5,7},{6,4},{7,5},{8,10},{9,11},{10,... | collective-permute-start | bytes 393224 | tf_op jit(solution)/shard_map/ppermute | solution.py:189
  81.4 31.4 %all-to-all-start.2 = ((f32[4,112,128]{2,1,0:T(8,128)}), f32[4,112,128]{2,1,0:T(8,128)S(1)}, u32[]{:S(2)}, u32[]{:S(2)}) async-start(f32[4,112,128]{2,1,0:T(8,128)} %bitcast.4), calls=%async_computation.2 | async-start | bytes 458752 | tf_op jit(solution)/shard_map/all_to_all | solution.py:179
  98.5 7.7 %collective-permute-start.8 = (bf16[32,32,128]{2,1,0:T(8,128)(2,1)S(1)}, bf16[32,32,128]{2,1,0:T(8,128)(2,1)S(1)}, u32[]{:S(2)}, u32[]{:S(2)}) collective-permute-start(bf16[32,32,128]{2,1,0:T(8,128)(2,1)S(1)} %bitcast.18), channel_id=1, source_target_pairs={{0,4},{4,0},{1,5},{5,1},{2,6},{6,2},{3,7},{7,3},{8,12},{12,8},{9,1... | collective-permute-start | bytes 786440 | tf_op jit(solution)/shard_map/ppermute | solution.py:225
  101.8 11.4 %collective-permute-start.7 = (f32[256,128]{1,0:T(8,128)S(1)}, f32[256,128]{1,0:T(8,128)S(1)}, u32[]{:S(2)}, u32[]{:S(2)}) collective-permute-start(f32[256,128]{1,0:T(8,128)S(1)} %get-tuple-element.57), channel_id=1, source_target_pairs={{0,3},{1,0},{2,1},{3,2},{4,7},{5,4},{6,5},{7,6},{8,11},{9,8},{10,9... | collective-permute-start | bytes 393224 | tf_op jit(solution)/shard_map/ppermute | solution.py:189
  108.3 7.9 %collective-permute-start.9 = (f32[256,128]{1,0:T(8,128)S(1)}, f32[256,128]{1,0:T(8,128)S(1)}, u32[]{:S(2)}, u32[]{:S(2)}) collective-permute-start(f32[256,128]{1,0:T(8,128)S(1)} %get-tuple-element.61), channel_id=1, source_target_pairs={{0,128},{128,256},{256,384},{384,0},{1,129},{129,257},{257,385},{3... | collective-permute-start | bytes 393224 | tf_op jit(solution)/shard_map/ppermute | solution.py:189
  116.9 25.2 %all-to-all-start.3 = ((f32[4,112,128]{2,1,0:T(8,128)}), f32[4,112,128]{2,1,0:T(8,128)S(1)}, u32[]{:S(2)}, u32[]{:S(2)}) async-start(f32[4,112,128]{2,1,0:T(8,128)} %broadcast_in_dim.7), calls=%async_computation.3 | async-start | bytes 458752 | tf_op jit(solution)/shard_map/all_to_all | solution.py:179
  128.6 7.2 %collective-permute-start.10 = (f32[256,128]{1,0:T(8,128)S(1)}, f32[256,128]{1,0:T(8,128)S(1)}, u32[]{:S(2)}, u32[]{:S(2)}) collective-permute-start(f32[256,128]{1,0:T(8,128)S(1)} %get-tuple-element.67), channel_id=1, source_target_pairs={{0,256},{128,384},{256,0},{384,128},{1,257},{129,385},{257,1},{385... | collective-permute-start | bytes 393224 | tf_op jit(solution)/shard_map/ppermute | solution.py:189
  130.6 7.4 %collective-permute-start.11 = (f32[256,128]{1,0:T(8,128)S(1)}, f32[256,128]{1,0:T(8,128)S(1)}, u32[]{:S(2)}, u32[]{:S(2)}) collective-permute-start(f32[256,128]{1,0:T(8,128)S(1)} %get-tuple-element.68), channel_id=1, source_target_pairs={{0,384},{128,0},{256,128},{384,256},{1,385},{129,1},{257,129},{385... | collective-permute-start | bytes 393224 | tf_op jit(solution)/shard_map/ppermute | solution.py:189
  143.1 12.9 %all-to-all-start.4 = ((f32[4,448,128]{2,1,0:T(8,128)}), f32[4,448,128]{2,1,0:T(8,128)S(1)}, u32[]{:S(2)}, u32[]{:S(2)}) async-start(f32[4,448,128]{2,1,0:T(8,128)} %broadcast_in_dim.8), calls=%async_computation.4 | async-start | bytes 1835008 | tf_op jit(solution)/shard_map/all_to_all | solution.py:179
  146.9 0.7 collective-permute-start.12
  156.0 9.5 %collective-permute-start.13 = (f32[1792,128]{1,0:T(8,128)S(1)}, f32[1792,128]{1,0:T(8,128)S(1)}, u32[]{:S(2)}, u32[]{:S(2)}) collective-permute-start(f32[1792,128]{1,0:T(8,128)S(1)} %bitcast.13), channel_id=1, source_target_pairs={{0,4},{4,0},{1,5},{5,1},{2,6},{6,2},{3,7},{7,3},{8,12},{12,8},{9,1... | collective-permute-start | bytes 2752520 | tf_op jit(solution)/shard_map/ppermute | solution.py:244

commit v9 on v8

--- a/solution.py
+++ b/solution.py
@@ -25,21 +25,20 @@
     return pairs
 
 
-def outer_neighbour(sizes):
+def neighbour(sizes, outer, turn):
     _, zhis, rings, cores, _ = sizes
 
     def move(chan, zhi, ring, core, space):
         column = (zhi * rings + ring) * cores + core
-        column += 1 if column % 2 else -1
+        if outer:
+            column += 1 if column % 2 else -1
         if not 0 <= column < zhis * rings * cores:
             return None
+        if turn:
+            chan, space = space, chan
         return (chan, column // (rings * cores), column // cores % rings, column % cores, space)
 
     return permutation(sizes, move)
-
-
-def transposed(sizes):
-    return permutation(sizes, lambda chan, zhi, ring, core, space: (space, zhi, ring, core, chan))
 
 
 def height_mask(rows, height, at):
@@ -121,10 +120,11 @@
     )(jnp.stack([core, me]), pair, inner, weight)
 
 
-def filter_kernel(core, data, pair, inner, keep, send, padded, turned, taps):
+def filter_kernel(core, data, pair, inner, keep, send, own, padded, turned, taps):
     planes, height, lanes = inner.shape
     rows = planes * height
     fill_padded(padded, pair, inner, core[0])
+    own[...] = data[:, 0].reshape(own.shape)
     flat = data[:, 0].reshape(rows, lanes).astype(F32)
     turned[0:lanes] = shifted(flat, height, -1).T.astype(BF16)
     turned[lanes : 2 * lanes] = flat.T.astype(BF16)
@@ -159,9 +159,9 @@
     half = jax.ShapeDtypeStruct((14 * lanes, lanes), F32)
     return pl.pallas_call(
         filter_kernel,
-        out_shape=(half, half),
+        out_shape=(half, half, jax.ShapeDtypeStruct(inner.shape, BF16)),
         in_specs=[SMEM, VMEM, VMEM, VMEM],
-        out_specs=(VMEM, VMEM),
+        out_specs=(VMEM, VMEM, VMEM),
         scratch_shapes=[
             pltpu.VMEM((3, planes + 2, height, lanes), BF16),
             pltpu.VMEM((3 * lanes, rows), BF16),
@@ -199,20 +199,19 @@
     core = lax.axis_index("core")
     swap = [(0, 1), (1, 0)]
 
-    outer = lax.ppermute(output_grad, AXES, outer_neighbour(sizes))
-    outer_data = lax.ppermute(activations, AXES, outer_neighbour(sizes))
-    grad, outer_data = lax.optimization_barrier(
-        (jnp.concatenate([output_grad, outer], axis=0), outer_data)
-    )
-    grad = lax.ppermute(grad, AXES, transposed(sizes))
-    data = jnp.concatenate([activations, outer_data], axis=0)
+    outer = lax.ppermute(activations, AXES, neighbour(sizes, True, False))
+    grads = [lax.ppermute(output_grad, AXES, neighbour(sizes, far, True)) for far in (False, True)]
+    grad = jnp.concatenate(grads, axis=0)
+    data = jnp.concatenate([activations, outer], axis=0)
     grad, data = lax.optimization_barrier((grad, data))
     data = gather(data, "space")
     grad = lax.all_gather(grad, "chan", axis=1, tiled=True)
     grad_inner = lax.ppermute(grad[0], "core", swap)
 
-    keep, send = filter_partial(core, data, grad, grad_inner)
-    half = keep + lax.ppermute(send, "core", swap)
+    keep, send, own = filter_partial(core, data, grad, grad_inner)
+    moved = lax.ppermute(send, "core", swap)
+    data_inner = lax.ppermute(after(own, send), "core", swap)
+    half, data_inner = lax.optimization_barrier((keep + moved, data_inner))
 
     moved = exchange(half.reshape(rings, -1, lanes), "ring")
     me = lax.axis_index("space")
@@ -221,8 +220,6 @@
     quarter, *back = lax.optimization_barrier((moved.sum(0), *back))
 
     moved = exchange(quarter.reshape(zhis, -1, lanes), "zhi")
-    own = after(data[:, 0].reshape(grad_inner.shape), quarter)
-    data_inner = lax.ppermute(own, "core", swap)
     me = lax.axis_index("chan")
     forward = convolve(False, core, me, after(data, quarter), data_inner, weight, spaces)
     forward = [forward[0], rotate(forward[1], "chan", 1), *forward[2:]]
@@ -234,12 +231,13 @@
     quarter = gather(part, "zhi").reshape(-1, lanes)
     forward = [*forward[:2], rotate(forward[2], "chan", 2), rotate(forward[3], "chan", 3)]
     input_grad = sum(back).astype(BF16).reshape(activations.shape)
-    quarter, forward, input_grad = lax.optimization_barrier((quarter, forward, input_grad))
+    quarter, forward, _ = lax.optimization_barrier((quarter, forward, input_grad))
 
     half = gather(quarter, "ring").reshape(-1, lanes)
-    output = lax.ppermute(sum(forward).astype(BF16), AXES, transposed(sizes))
-    output = output.reshape(activations.shape)
-    half, output = lax.optimization_barrier((half, output))
+    output = lax.ppermute(
+        sum(forward).astype(BF16).reshape(activations.shape), AXES, neighbour(sizes, False, True)
+    )
+    half = after(half, output)
 
     other = lax.ppermute(half, "core", swap)
     first = core == 0

time: 169 us -> 160 us (0.947)
  starting transfers between devices: 106 us -> 96.4 us
    all_to_all x5, starting transfers between devices: 62.9 us -> 54.7 us  [exchange(): return lax.all_to_all(block, axis, split_axis=0, concat_axis=0, tiled=True)]
    all_to_all x5, waiting for transfers between devices: 18 us -> 22.4 us  [exchange(): return lax.all_to_all(block, axis, split_axis=0, concat_axis=0, tiled=True)]
    ppermute x6, waiting for transfers between devices: 5.35 us -> 3.12 us  [the longest x2 2.99 us: shards(): lax.ppermute(output_grad, AXES, neighbour(sizes, far, True))]
  transfers between devices with their start and end apart: 19 -> 19, of which waited for: 14 -> 12; matrix products, arithmetic and copies ran while one was open for 3% -> 3% of each run, Pallas kernels for 3% -> 3%
where the time goes in v9:
time: 160 us; the launch traced here: 159 us
  starting transfers between devices  96.4 us (60%)
  waiting for transfers between devices  34.9 us (22%)
  blocking collectives  11.2 us (7%)
  other arithmetic  6.19 us (4%)
  Pallas kernels  5.82 us (4%)
  local copies, waits for them, and re-layouts  3.22 us (2%)
    all_to_all x5, starting transfers between devices, exchange(): return lax.all_to_all(block, axis, split_axis=0, concat_axis=0, tiled=True)  54.7 us
    all_to_all x5, waiting for transfers between devices, exchange(): return lax.all_to_all(block, axis, split_axis=0, concat_axis=0, tiled=True)  22.4 us
    ppermute x6, starting transfers between devices, rotate(): lax.ppermute(term, axis, [(i, (i + step) % count) for i in range(count)])  19.7 us
    all_gather x1, blocking collectives, shards(): grad = lax.all_gather(grad, 'chan', axis=1, tiled=True)  11.2 us
    ppermute x1, starting transfers between devices, shards(): other = lax.ppermute(half, 'core', swap)  7.1 us
    ppermute x6, waiting for transfers between devices, rotate(): lax.ppermute(term, axis, [(i, (i + step) % count) for i in range(count)])  5.86 us
    ppermute x1, starting transfers between devices, shards(): outer = lax.ppermute(activations, AXES, neighbour(sizes, True, False))  4.59 us
    pallas_call x2, Pallas kernels, convolve(): pl.pallas_call(functools.partial(conv_kernel, backward), out_shape=[jax.S...  4.24 us
  transfers between devices with their start and end apart: 19, of which 12 were waited for; matrix products, arithmetic and copies ran while one was open for 3% of the time, Pallas kernels for 3%

profile of v9, /device:TPU:1, one launch (start us, length us, event | category | flops | bytes accessed | tf_op | source)
XLA Modules:
  0.0 158.7 jit_solution(6044492278757576513)
XLA Ops:
  0.6 4.6 %collective-permute-start.2 = (bf16[1,8,32,128]{3,2,1,0:T(8,128)(2,1)}, bf16[1,8,32,128]{3,2,1,0:T(8,128)(2,1)S(1)}, u32[]{:S(2)}, u32[]{:S(2)}) collective-permute-start(bf16[1,8,32,128]{3,2,1,0:T(8,128)(2,1)} %param.3), channel_id=1, source_target_pairs={{4,8},{5,9},{6,10},{7,11},{8,4},{9,5},{10,6},{11,7},{12,16},{13,17... | collective-permute-start | bytes 196616 | tf_op jit(solution)/shard_map/ppermute | solution.py:202
  5.2 1.5 collective-permute-start
  6.7 1.9 %collective-permute-start.1 = (bf16[1,8,32,128]{3,2,1,0:T(8,128)(2,1)}, bf16[1,8,32,128]{3,2,1,0:T(8,128)(2,1)S(1)}, u32[]{:S(2)}, u32[]{:S(2)}) collective-permute-start(bf16[1,8,32,128]{3,2,1,0:T(8,128)(2,1)} %param.5), channel_id=1, source_target_pairs={{4,8},{5,136},{6,264},{7,392},{8,4},{9,132},{10,260},{11,388},{12,... | collective-permute-start | bytes 196616 | tf_op jit(solution)/shard_map/ppermute | solution.py:203
  8.6 0.0 collective-permute-done.2
  8.7 0.9 pad_maximum_fusion.2
  9.5 0.0 collective-permute-done
  9.5 3.0 %collective-permute-done.1 = bf16[1,8,32,128]{3,2,1,0:T(8,128)(2,1)S(1)} collective-permute-done((bf16[1,8,32,128]{3,2,1,0:T(8,128)(2,1)}, bf16[1,8,32,128]{3,2,1,0:T(8,128)(2,1)S(1)}, u32[]{:S(2)}, u32[]{:S(2)}) %collective-permute-start.1) | collective-permute-done | bytes 65568 | tf_op jit(solution)/shard_map/ppermute | solution.py:203
  12.5 0.9 broadcast_in_dim.6
  13.4 12.4 %all-to-all-start = ((bf16[4,2,8,32,128]{4,3,2,1,0:T(8,128)(2,1)}), bf16[4,2,8,32,128]{4,3,2,1,0:T(8,128)(2,1)S(1)}, u32[]{:S(2)}, u32[]{:S(2)}) async-start(bf16[4,2,8,32,128]{4,3,2,1,0:T(8,128)(2,1)} %broadcast_in_dim.6), calls=%async_computation | async-start | bytes 1048576 | tf_op jit(solution)/shard_map/all_to_all | solution.py:179
  25.8 11.2 %all_gather.3.pair = bf16[2,32,32,128]{3,2,1,0:T(8,128)(2,1)S(1)} all-gather(bf16[2,8,32,128]{3,2,1,0:T(8,128)(2,1)S(1)} %pad_maximum_fusion.1), channel_id=1, replica_groups=mesh['chan'=4,'zhi'=4,'ring'=4,'core'=2,'space'=4] {'chan'}, dimensions={1}, use_global_device_ids=true | all-gather | bytes 655360 | tf_op jit(solution)/shard_map/all_gather | solution.py:208
  37.0 1.9 %collective-permute-start.3 = (bf16[32,32,128]{2,1,0:T(8,128)(2,1)S(1)}, bf16[32,32,128]{2,1,0:T(8,128)(2,1)S(1)}, u32[]{:S(2)}, u32[]{:S(2)}) collective-permute-start(bf16[32,32,128]{2,1,0:T(8,128)(2,1)S(1)} %slice_bitcast_fusion), channel_id=1, source_target_pairs={{0,4},{4,0},{1,5},{5,1},{2,6},{6,2},{3,7},{7,3},{8,12},{12,8},{9,1... | collective-permute-start | bytes 786440 | tf_op jit(solution)/shard_map/ppermute | solution.py:209
  39.0 1.5 collective-permute-done.3.inner
  40.5 0.0 all-to-all-done.data.pair
  40.5 1.6 filter_grad.1
  42.1 2.0 %collective-permute-start.4 = (f32[1792,128]{1,0:T(8,128)S(1)}, f32[1792,128]{1,0:T(8,128)S(1)}, u32[]{:S(2)}, u32[]{:S(2)}) collective-permute-start(f32[1792,128]{1,0:T(8,128)S(1)} %get-tuple-element.44), channel_id=1, source_target_pairs={{0,4},{4,0},{1,5},{5,1},{2,6},{6,2},{3,7},{7,3},{8,12},{12,8},{9,1... | collective-permute-start | bytes 2752520 | tf_op jit(solution)/shard_map/ppermute | solution.py:212
  44.1 2.3 %collective-permute-start.5 = (bf16[32,32,128]{2,1,0:T(8,128)(2,1)S(1)}, bf16[32,32,128]{2,1,0:T(8,128)(2,1)S(1)}, u32[]{:S(2)}, u32[]{:S(2)}) collective-permute-start(bf16[32,32,128]{2,1,0:T(8,128)(2,1)S(1)} %get-tuple-element.46), channel_id=1, source_target_pairs={{0,4},{4,0},{1,5},{5,1},{2,6},{6,2},{3,7},{7,3},{8,12},{12,8},{9,1... | collective-permute-start | bytes 786440 | tf_op jit(solution)/shard_map/ppermute | solution.py:213
  46.4 0.0 collective-permute-done.4
  46.4 0.0 copy-start
  46.4 1.0 add.21
  47.4 0.1 collective-permute-done.5.inner
  47.5 15.3 %all-to-all-start.1 = ((f32[4,448,128]{2,1,0:T(8,128)}), f32[4,448,128]{2,1,0:T(8,128)}, u32[]{:S(2)}, u32[]{:S(2)}) async-start(f32[4,448,128]{2,1,0:T(8,128)} %bitcast.2), calls=%async_computation.1 | async-start | bytes 1835008 | tf_op jit(solution)/shard_map/all_to_all | solution.py:179
  62.8 0.1 pad_add_fusion.place
  62.9 0.0 copy-done
  62.9 2.2 %input_grad.1 = (f32[256,128]{1,0:T(8,128)S(1)}, f32[256,128]{1,0:T(8,128)S(1)}, f32[256,128]{1,0:T(8,128)S(1)}, f32[256,128]{1,0:T(8,128)S(1)}) custom-call(s32[2]{0:T(128)S(1)} %pad_add_fusion.place, bf16[2,32,32,128]{3,2,1,0:T(8,128)(2,1)S(1)} %all_gather.3.pair, bf16[32,32,128]{2,1,0:T(8,128)(2,1)S(1)} %collective-permute-done.3.inner, ...), custom_call_target="tpu_custom_call" | custom-call | flops 905969664 | bytes 3145728 | tf_op jit(solution)/shard_map/input_grad/pallas_call | solution.py:106
  65.0 3.3 %collective-permute-start.6 = (f32[256,128]{1,0:T(8,128)S(1)}, f32[256,128]{1,0:T(8,128)S(1)}, u32[]{:S(2)}, u32[]{:S(2)}) collective-permute-start(f32[256,128]{1,0:T(8,128)S(1)} %get-tuple-element.50), channel_id=1, source_target_pairs={{0,1},{1,2},{2,3},{3,0},{4,5},{5,6},{6,7},{7,4},{8,9},{9,10},{10,1... | collective-permute-start | bytes 393224 | tf_op jit(solution)/shard_map/ppermute | solution.py:189
  68.4 4.0 %collective-permute-start.7 = (f32[256,128]{1,0:T(8,128)S(1)}, f32[256,128]{1,0:T(8,128)S(1)}, u32[]{:S(2)}, u32[]{:S(2)}) collective-permute-start(f32[256,128]{1,0:T(8,128)S(1)} %get-tuple-element.51), channel_id=1, source_target_pairs={{0,2},{1,3},{2,0},{3,1},{4,6},{5,7},{6,4},{7,5},{8,10},{9,11},{10,... | collective-permute-start | bytes 393224 | tf_op jit(solution)/shard_map/ppermute | solution.py:189
  72.4 3.7 %all-to-all-done.1 = f32[4,448,128]{2,1,0:T(8,128)} async-done(((f32[4,448,128]{2,1,0:T(8,128)}), f32[4,448,128]{2,1,0:T(8,128)}, u32[]{:S(2)}, u32[]{:S(2)}) %all-to-all-start.1) | async-done | bytes 917536 | tf_op jit(solution)/shard_map/all_to_all | solution.py:179
  76.0 1.9 %reduce_sum.18 = f32[448,128]{1,0:T(8,128)} reduce(f32[4,448,128]{2,1,0:T(8,128)} %all-to-all-done.1, f32[]{:T(128)} %constant.15.clone.1), dimensions={0}, to_apply=%region_0.0 | reduce | flops 172032 | bytes 1146884 | tf_op jit(solution)/shard_map/reduce_sum | solution.py:220
  78.0 0.0 collective-permute-done.6
  78.0 1.2 collective-permute-done.7
  79.2 13.3 %all-to-all-start.2 = ((f32[4,112,128]{2,1,0:T(8,128)}), f32[4,112,128]{2,1,0:T(8,128)S(1)}, u32[]{:S(2)}, u32[]{:S(2)}) async-start(f32[4,112,128]{2,1,0:T(8,128)} %bitcast.4), calls=%async_computation.2 | async-start | bytes 458752 | tf_op jit(solution)/shard_map/all_to_all | solution.py:179
  92.5 0.1 pad_add_fusion.1.place
  92.5 2.1 %forward.1 = (f32[256,128]{1,0:T(8,128)S(1)}, f32[256,128]{1,0:T(8,128)S(1)}, f32[256,128]{1,0:T(8,128)S(1)}, f32[256,128]{1,0:T(8,128)S(1)}) custom-call(s32[2]{0:T(128)S(1)} %pad_add_fusion.1.place, bf16[4,2,8,32,128]{4,3,2,1,0:T(8,128)(2,1)S(1)} %all-to-all-done.data.pair, bf16[32,32,128]{2,1,0:T(8,128)(2,1)S(1)} %collective-permute-done.5.inner, ...), custom_call_target="tpu_custom_call" | custom-call | flops 905969664 | bytes 3145728 | tf_op jit(solution)/shard_map/forward/pallas_call | solution.py:106
  94.6 2.0 %collective-permute-start.9 = (f32[256,128]{1,0:T(8,128)S(1)}, f32[256,128]{1,0:T(8,128)S(1)}, u32[]{:S(2)}, u32[]{:S(2)}) collective-permute-start(f32[256,128]{1,0:T(8,128)S(1)} %get-tuple-element.61), channel_id=1, source_target_pairs={{0,128},{128,256},{256,384},{384,0},{1,129},{129,257},{257,385},{3... | collective-permute-start | bytes 393224 | tf_op jit(solution)/shard_map/ppermute | solution.py:189
  96.6 4.3 %collective-permute-start.8 = (f32[256,128]{1,0:T(8,128)S(1)}, f32[256,128]{1,0:T(8,128)S(1)}, u32[]{:S(2)}, u32[]{:S(2)}) collective-permute-start(f32[256,128]{1,0:T(8,128)S(1)} %get-tuple-element.57), channel_id=1, source_target_pairs={{0,3},{1,0},{2,1},{3,2},{4,7},{5,4},{6,5},{7,6},{8,11},{9,8},{10,9... | collective-permute-start | bytes 393224 | tf_op jit(solution)/shard_map/ppermute | solution.py:189
  100.9 4.3 %all-to-all-done.2 = f32[4,112,128]{2,1,0:T(8,128)S(1)} async-done(((f32[4,112,128]{2,1,0:T(8,128)}), f32[4,112,128]{2,1,0:T(8,128)S(1)}, u32[]{:S(2)}, u32[]{:S(2)}) %all-to-all-start.2) | async-done | bytes 229408 | tf_op jit(solution)/shard_map/all_to_all | solution.py:179
  105.2 0.0 collective-permute-done.9
  105.3 2.5 %collective-permute-done.8 = f32[256,128]{1,0:T(8,128)S(1)} collective-permute-done((f32[256,128]{1,0:T(8,128)S(1)}, f32[256,128]{1,0:T(8,128)S(1)}, u32[]{:S(2)}, u32[]{:S(2)}) %collective-permute-start.8) | collective-permute-done | bytes 131104 | tf_op jit(solution)/shard_map/ppermute | solution.py:189
  107.8 0.7 broadcast_in_dim.7
  108.5 10.3 %all-to-all-start.3 = ((f32[4,112,128]{2,1,0:T(8,128)}), f32[4,112,128]{2,1,0:T(8,128)S(1)}, u32[]{:S(2)}, u32[]{:S(2)}) async-start(f32[4,112,128]{2,1,0:T(8,128)} %broadcast_in_dim.7), calls=%async_computation.3 | async-start | bytes 458752 | tf_op jit(solution)/shard_map/all_to_all | solution.py:179
  118.7 2.6 %collective-permute-start.10 = (f32[256,128]{1,0:T(8,128)S(1)}, f32[256,128]{1,0:T(8,128)S(1)}, u32[]{:S(2)}, u32[]{:S(2)}) collective-permute-start(f32[256,128]{1,0:T(8,128)S(1)} %get-tuple-element.67), channel_id=1, source_target_pairs={{0,256},{128,384},{256,0},{384,128},{1,257},{129,385},{257,1},{385... | collective-permute-start | bytes 393224 | tf_op jit(solution)/shard_map/ppermute | solution.py:189
  121.3 3.5 %collective-permute-start.11 = (f32[256,128]{1,0:T(8,128)S(1)}, f32[256,128]{1,0:T(8,128)S(1)}, u32[]{:S(2)}, u32[]{:S(2)}) collective-permute-start(f32[256,128]{1,0:T(8,128)S(1)} %get-tuple-element.68), channel_id=1, source_target_pairs={{0,384},{128,0},{256,128},{384,256},{1,385},{129,1},{257,129},{385... | collective-permute-start | bytes 393224 | tf_op jit(solution)/shard_map/ppermute | solution.py:189
  124.9 0.7 add_convert_fusion.1
  125.5 0.4 collective-permute-done.10
  125.9 1.7 %collective-permute-done.11 = f32[256,128]{1,0:T(8,128)S(1)} collective-permute-done((f32[256,128]{1,0:T(8,128)S(1)}, f32[256,128]{1,0:T(8,128)S(1)}, u32[]{:S(2)}, u32[]{:S(2)}) %collective-permute-start.11) | collective-permute-done | bytes 131104 | tf_op jit(solution)/shard_map/ppermute | solution.py:189
  127.6 5.8 %all-to-all-done.3 = f32[4,112,128]{2,1,0:T(8,128)S(1)} async-done(((f32[4,112,128]{2,1,0:T(8,128)}), f32[4,112,128]{2,1,0:T(8,128)S(1)}, u32[]{:S(2)}, u32[]{:S(2)}) %all-to-all-start.3) | async-done | bytes 229408 | tf_op jit(solution)/shard_map/all_to_all | solution.py:179
  133.4 1.0 broadcast_in_dim.8
  134.4 3.5 %all-to-all-start.4 = ((f32[4,448,128]{2,1,0:T(8,128)}), f32[4,448,128]{2,1,0:T(8,128)S(1)}, u32[]{:S(2)}, u32[]{:S(2)}) async-start(f32[4,448,128]{2,1,0:T(8,128)} %broadcast_in_dim.8), calls=%async_computation.4 | async-start | bytes 1835008 | tf_op jit(solution)/shard_map/all_to_all | solution.py:179
  137.9 0.7 collective-permute-start.12
  138.6 0.0 collective-permute-done.12
  138.6 8.7 %all-to-all-done.4 = f32[4,448,128]{2,1,0:T(8,128)S(1)} async-done(((f32[4,448,128]{2,1,0:T(8,128)}), f32[4,448,128]{2,1,0:T(8,128)S(1)}, u32[]{:S(2)}, u32[]{:S(2)}) %all-to-all-start.4) | async-done | bytes 917536 | tf_op jit(solution)/shard_map/all_to_all | solution.py:179
  147.3 7.1 %collective-permute-start.13 = (f32[1792,128]{1,0:T(8,128)S(1)}, f32[1792,128]{1,0:T(8,128)S(1)}, u32[]{:S(2)}, u32[]{:S(2)}) collective-permute-start(f32[1792,128]{1,0:T(8,128)S(1)} %bitcast.12), channel_id=1, source_target_pairs={{0,4},{4,0},{1,5},{5,1},{2,6},{6,2},{3,7},{7,3},{8,12},{12,8},{9,1... | collective-permute-start | bytes 2752520 | tf_op jit(solution)/shard_map/ppermute | solution.py:242
  154.4 2.1 %collective-permute-done.13 = f32[1792,128]{1,0:T(8,128)S(1)} collective-permute-done((f32[1792,128]{1,0:T(8,128)S(1)}, f32[1792,128]{1,0:T(8,128)S(1)}, u32[]{:S(2)}, u32[]{:S(2)}) %collective-permute-start.13) | collective-permute-done | bytes 917536 | tf_op jit(solution)/shard_map/ppermute | solution.py:242
  156.5 0.1 broadcast_select_fusion
  156.6 0.1 slice_select_fusion
  156.7 1.3 pad_maximum_fusion
  158.0 0.6 copy.7
  (5 shorter events, 0.1 us)
Async XLA Ops:
  0.6 8.0 %collective-permute-start.2 = (bf16[1,8,32,128]{3,2,1,0:T(8,128)(2,1)}, bf16[1,8,32,128]{3,2,1,0:T(8,128)(2,1)S(1)}, u32[]{:S(2)}, u32[]{:S(2)}) collective-permute-start(bf16[1,8,32,128]{3,2,1,0:T(8,128)(2,1)} %param.3), channel_id=1, source_target_pairs={{4,8},{5,9},{6,10},{7,11},{8,4},{9,5},{10,6},{11,7},{12,16},{13,17... | collective-permute-start | bytes 196616 | tf_op jit(solution)/shard_map/ppermute | solution.py:202
  5.2 4.3 %collective-permute-start = (bf16[1,8,32,128]{3,2,1,0:T(8,128)(2,1)}, bf16[1,8,32,128]{3,2,1,0:T(8,128)(2,1)S(1)}, u32[]{:S(2)}, u32[]{:S(2)}) collective-permute-start(bf16[1,8,32,128]{3,2,1,0:T(8,128)(2,1)} %param.5), channel_id=1, source_target_pairs={{0,0},{1,128},{2,256},{3,384},{4,4},{5,132},{6,260},{7,388},{8,8},... | collective-permute-start | bytes 196616 | tf_op jit(solution)/shard_map/ppermute | solution.py:203
  6.7 5.8 %collective-permute-start.1 = (bf16[1,8,32,128]{3,2,1,0:T(8,128)(2,1)}, bf16[1,8,32,128]{3,2,1,0:T(8,128)(2,1)S(1)}, u32[]{:S(2)}, u32[]{:S(2)}) collective-permute-start(bf16[1,8,32,128]{3,2,1,0:T(8,128)(2,1)} %param.5), channel_id=1, source_target_pairs={{4,8},{5,136},{6,264},{7,392},{8,4},{9,132},{10,260},{11,388},{12,... | collective-permute-start | bytes 196616 | tf_op jit(solution)/shard_map/ppermute | solution.py:203
  13.4 27.1 %all-to-all-start = ((bf16[4,2,8,32,128]{4,3,2,1,0:T(8,128)(2,1)}), bf16[4,2,8,32,128]{4,3,2,1,0:T(8,128)(2,1)S(1)}, u32[]{:S(2)}, u32[]{:S(2)}) async-start(bf16[4,2,8,32,128]{4,3,2,1,0:T(8,128)(2,1)} %broadcast_in_dim.6), calls=%async_computation | async-start | bytes 1048576 | tf_op jit(solution)/shard_map/all_to_all | solution.py:179
  37.0 3.4 %collective-permute-start.3 = (bf16[32,32,128]{2,1,0:T(8,128)(2,1)S(1)}, bf16[32,32,128]{2,1,0:T(8,128)(2,1)S(1)}, u32[]{:S(2)}, u32[]{:S(2)}) collective-permute-start(bf16[32,32,128]{2,1,0:T(8,128)(2,1)S(1)} %slice_bitcast_fusion), channel_id=1, source_target_pairs={{0,4},{4,0},{1,5},{5,1},{2,6},{6,2},{3,7},{7,3},{8,12},{12,8},{9,1... | collective-permute-start | bytes 786440 | tf_op jit(solution)/shard_map/ppermute | solution.py:209
  42.1 4.4 %collective-permute-start.4 = (f32[1792,128]{1,0:T(8,128)S(1)}, f32[1792,128]{1,0:T(8,128)S(1)}, u32[]{:S(2)}, u32[]{:S(2)}) collective-permute-start(f32[1792,128]{1,0:T(8,128)S(1)} %get-tuple-element.44), channel_id=1, source_target_pairs={{0,4},{4,0},{1,5},{5,1},{2,6},{6,2},{3,7},{7,3},{8,12},{12,8},{9,1... | collective-permute-start | bytes 2752520 | tf_op jit(solution)/shard_map/ppermute | solution.py:212
  44.1 3.4 %collective-permute-start.5 = (bf16[32,32,128]{2,1,0:T(8,128)(2,1)S(1)}, bf16[32,32,128]{2,1,0:T(8,128)(2,1)S(1)}, u32[]{:S(2)}, u32[]{:S(2)}) collective-permute-start(bf16[32,32,128]{2,1,0:T(8,128)(2,1)S(1)} %get-tuple-element.46), channel_id=1, source_target_pairs={{0,4},{4,0},{1,5},{5,1},{2,6},{6,2},{3,7},{7,3},{8,12},{12,8},{9,1... | collective-permute-start | bytes 786440 | tf_op jit(solution)/shard_map/ppermute | solution.py:213
  46.4 16.5 %copy-start = (bf16[27,128,128]{2,1,0:T(8,128)(2,1)S(1)}, bf16[27,128,128]{2,1,0:T(8,128)(2,1)}, u32[]{:S(2)}) copy-start(bf16[27,128,128]{2,1,0:T(8,128)(2,1)} %weight.3) | copy-start | bytes 2654212
  47.5 28.5 %all-to-all-start.1 = ((f32[4,448,128]{2,1,0:T(8,128)}), f32[4,448,128]{2,1,0:T(8,128)}, u32[]{:S(2)}, u32[]{:S(2)}) async-start(f32[4,448,128]{2,1,0:T(8,128)} %bitcast.2), calls=%async_computation.1 | async-start | bytes 1835008 | tf_op jit(solution)/shard_map/all_to_all | solution.py:179
  65.0 12.9 %collective-permute-start.6 = (f32[256,128]{1,0:T(8,128)S(1)}, f32[256,128]{1,0:T(8,128)S(1)}, u32[]{:S(2)}, u32[]{:S(2)}) collective-permute-start(f32[256,128]{1,0:T(8,128)S(1)} %get-tuple-element.50), channel_id=1, source_target_pairs={{0,1},{1,2},{2,3},{3,0},{4,5},{5,6},{6,7},{7,4},{8,9},{9,10},{10,1... | collective-permute-start | bytes 393224 | tf_op jit(solution)/shard_map/ppermute | solution.py:189
  68.4 10.8 %collective-permute-start.7 = (f32[256,128]{1,0:T(8,128)S(1)}, f32[256,128]{1,0:T(8,128)S(1)}, u32[]{:S(2)}, u32[]{:S(2)}) collective-permute-start(f32[256,128]{1,0:T(8,128)S(1)} %get-tuple-element.51), channel_id=1, source_target_pairs={{0,2},{1,3},{2,0},{3,1},{4,6},{5,7},{6,4},{7,5},{8,10},{9,11},{10,... | collective-permute-start | bytes 393224 | tf_op jit(solution)/shard_map/ppermute | solution.py:189
  79.2 26.0 %all-to-all-start.2 = ((f32[4,112,128]{2,1,0:T(8,128)}), f32[4,112,128]{2,1,0:T(8,128)S(1)}, u32[]{:S(2)}, u32[]{:S(2)}) async-start(f32[4,112,128]{2,1,0:T(8,128)} %bitcast.4), calls=%async_computation.2 | async-start | bytes 458752 | tf_op jit(solution)/shard_map/all_to_all | solution.py:179
  94.6 10.6 %collective-permute-start.9 = (f32[256,128]{1,0:T(8,128)S(1)}, f32[256,128]{1,0:T(8,128)S(1)}, u32[]{:S(2)}, u32[]{:S(2)}) collective-permute-start(f32[256,128]{1,0:T(8,128)S(1)} %get-tuple-element.61), channel_id=1, source_target_pairs={{0,128},{128,256},{256,384},{384,0},{1,129},{129,257},{257,385},{3... | collective-permute-start | bytes 393224 | tf_op jit(solution)/shard_map/ppermute | solution.py:189
  96.6 11.1 %collective-permute-start.8 = (f32[256,128]{1,0:T(8,128)S(1)}, f32[256,128]{1,0:T(8,128)S(1)}, u32[]{:S(2)}, u32[]{:S(2)}) collective-permute-start(f32[256,128]{1,0:T(8,128)S(1)} %get-tuple-element.57), channel_id=1, source_target_pairs={{0,3},{1,0},{2,1},{3,2},{4,7},{5,4},{6,5},{7,6},{8,11},{9,8},{10,9... | collective-permute-start | bytes 393224 | tf_op jit(solution)/shard_map/ppermute | solution.py:189
  108.5 24.9 %all-to-all-start.3 = ((f32[4,112,128]{2,1,0:T(8,128)}), f32[4,112,128]{2,1,0:T(8,128)S(1)}, u32[]{:S(2)}, u32[]{:S(2)}) async-start(f32[4,112,128]{2,1,0:T(8,128)} %broadcast_in_dim.7), calls=%async_computation.3 | async-start | bytes 458752 | tf_op jit(solution)/shard_map/all_to_all | solution.py:179
  118.7 7.2 %collective-permute-start.10 = (f32[256,128]{1,0:T(8,128)S(1)}, f32[256,128]{1,0:T(8,128)S(1)}, u32[]{:S(2)}, u32[]{:S(2)}) collective-permute-start(f32[256,128]{1,0:T(8,128)S(1)} %get-tuple-element.67), channel_id=1, source_target_pairs={{0,256},{128,384},{256,0},{384,128},{1,257},{129,385},{257,1},{385... | collective-permute-start | bytes 393224 | tf_op jit(solution)/shard_map/ppermute | solution.py:189
  121.3 6.3 %collective-permute-start.11 = (f32[256,128]{1,0:T(8,128)S(1)}, f32[256,128]{1,0:T(8,128)S(1)}, u32[]{:S(2)}, u32[]{:S(2)}) collective-permute-start(f32[256,128]{1,0:T(8,128)S(1)} %get-tuple-element.68), channel_id=1, source_target_pairs={{0,384},{128,0},{256,128},{384,256},{1,385},{129,1},{257,129},{385... | collective-permute-start | bytes 393224 | tf_op jit(solution)/shard_map/ppermute | solution.py:189
  134.4 12.9 %all-to-all-start.4 = ((f32[4,448,128]{2,1,0:T(8,128)}), f32[4,448,128]{2,1,0:T(8,128)S(1)}, u32[]{:S(2)}, u32[]{:S(2)}) async-start(f32[4,448,128]{2,1,0:T(8,128)} %broadcast_in_dim.8), calls=%async_computation.4 | async-start | bytes 1835008 | tf_op jit(solution)/shard_map/all_to_all | solution.py:179
  137.9 0.7 collective-permute-start.12
  147.3 9.2 %collective-permute-start.13 = (f32[1792,128]{1,0:T(8,128)S(1)}, f32[1792,128]{1,0:T(8,128)S(1)}, u32[]{:S(2)}, u32[]{:S(2)}) collective-permute-start(f32[1792,128]{1,0:T(8,128)S(1)} %bitcast.12), channel_id=1, source_target_pairs={{0,4},{4,0},{1,5},{5,1},{2,6},{6,2},{3,7},{7,3},{8,12},{12,8},{9,1... | collective-permute-start | bytes 2752520 | tf_op jit(solution)/shard_map/ppermute | solution.py:242

commit v10 on v9

--- a/solution.py
+++ b/solution.py
@@ -189,6 +189,14 @@
     return lax.ppermute(term, axis, [(i, (i + step) % count) for i in range(count)])
 
 
+def doubling(step):
+    return [
+        (2 * zhi + core, 2 * (zhi ^ 1 if core == step else 3 - zhi) + core)
+        for zhi in range(4)
+        for core in range(2)
+    ]
+
+
 def after(value, *others):
     return lax.optimization_barrier((value, *others))[0]
 
@@ -219,16 +227,16 @@
     back = [back[0], rotate(back[1], "space", 1), rotate(back[2], "space", 2), back[3]]
     quarter, *back = lax.optimization_barrier((moved.sum(0), *back))
 
-    moved = exchange(quarter.reshape(zhis, -1, lanes), "zhi")
+    moved = lax.ppermute(quarter, ("zhi", "core"), doubling(0))
     me = lax.axis_index("chan")
     forward = convolve(False, core, me, after(data, quarter), data_inner, weight, spaces)
     forward = [forward[0], rotate(forward[1], "chan", 1), *forward[2:]]
     back[3] = rotate(back[3], "space", 3)
     cell_count = sizes[1] * rings * cores * grad.shape[1] * grad.shape[2]
-    part = moved.sum(0) / math.sqrt(cell_count)
-    part, back, forward = lax.optimization_barrier((part, back, forward))
-
-    quarter = gather(part, "zhi").reshape(-1, lanes)
+    pair = quarter + moved
+    pair, back, forward = lax.optimization_barrier((pair, back, forward))
+
+    quarter = (pair + lax.ppermute(pair, ("zhi", "core"), doubling(1))) / math.sqrt(cell_count)
     forward = [*forward[:2], rotate(forward[2], "chan", 2), rotate(forward[3], "chan", 3)]
     input_grad = sum(back).astype(BF16).reshape(activations.shape)
     quarter, forward, _ = lax.optimization_barrier((quarter, forward, input_grad))

time: 160 us -> 147 us (0.919)
  starting transfers between devices: 96.4 us -> 87.4 us
  waiting for transfers between devices: 34.9 us -> 32.6 us
    all_to_all x5 -> x3, starting transfers between devices: 54.7 us -> 31.2 us  [exchange(): return lax.all_to_all(block, axis, split_axis=0, concat_axis=0, tiled=True)]
    ppermute x0 -> x2, starting transfers between devices: none -> 15.8 us  [the longest x1 13.9 us: shards(): moved = lax.ppermute(quarter, ('zhi', 'core'), doubling(0))]
    all_to_all x5 -> x3, waiting for transfers between devices: 22.4 us -> 13.2 us  [exchange(): return lax.all_to_all(block, axis, split_axis=0, concat_axis=0, tiled=True)]
    ppermute x0 -> x2, waiting for transfers between devices: none -> 5.23 us  [the longest x1 5.23 us: shards(): lax.ppermute(pair, ('zhi', 'core'), doubling(1))]
    ppermute x6, waiting for transfers between devices: 5.86 us -> 7.47 us  [rotate(): lax.ppermute(term, axis, [(i, (i + step) % count) for i in range(count)])]
  transfers between devices with their start and end apart: 19 -> 19, of which waited for: 12 -> 10; matrix products, arithmetic and copies ran while one was open for 3% -> 3% of each run, Pallas kernels for 3% -> 3%
where the time goes in v10:
time: 147 us; the launch traced here: 146 us
  starting transfers between devices  87.4 us (59%)
  waiting for transfers between devices  32.6 us (22%)
  blocking collectives  11.2 us (8%)
  Pallas kernels  5.83 us (4%)
  other arithmetic  5.54 us (4%)
  local copies, waits for them, and re-layouts  2.51 us (2%)
    all_to_all x3, starting transfers between devices, exchange(): return lax.all_to_all(block, axis, split_axis=0, concat_axis=0, tiled=True)  31.2 us
    ppermute x6, starting transfers between devices, rotate(): lax.ppermute(term, axis, [(i, (i + step) % count) for i in range(count)])  19.3 us
    ppermute x1, starting transfers between devices, shards(): moved = lax.ppermute(quarter, ('zhi', 'core'), doubling(0))  13.9 us
    all_to_all x3, waiting for transfers between devices, exchange(): return lax.all_to_all(block, axis, split_axis=0, concat_axis=0, tiled=True)  13.2 us
    all_gather x1, blocking collectives, shards(): grad = lax.all_gather(grad, 'chan', axis=1, tiled=True)  11.2 us
    ppermute x6, waiting for transfers between devices, rotate(): lax.ppermute(term, axis, [(i, (i + step) % count) for i in range(count)])  7.47 us
    ppermute x1, starting transfers between devices, shards(): other = lax.ppermute(half, 'core', swap)  6.23 us
    ppermute x1, waiting for transfers between devices, shards(): lax.ppermute(pair, ('zhi', 'core'), doubling(1))  5.23 us
  transfers between devices with their start and end apart: 19, of which 10 were waited for; matrix products, arithmetic and copies ran while one was open for 3% of the time, Pallas kernels for 3%

profile of v10, /device:TPU:1, one launch (start us, length us, event | category | flops | bytes accessed | tf_op | source)
XLA Modules:
  0.0 145.9 jit_solution(9966223973381816299)
XLA Ops:
  0.6 4.6 %collective-permute-start.2 = (bf16[1,8,32,128]{3,2,1,0:T(8,128)(2,1)}, bf16[1,8,32,128]{3,2,1,0:T(8,128)(2,1)S(1)}, u32[]{:S(2)}, u32[]{:S(2)}) collective-permute-start(bf16[1,8,32,128]{3,2,1,0:T(8,128)(2,1)} %param.3), channel_id=1, source_target_pairs={{4,8},{5,9},{6,10},{7,11},{8,4},{9,5},{10,6},{11,7},{12,16},{13,17... | collective-permute-start | bytes 196616 | tf_op jit(solution)/shard_map/ppermute | solution.py:210
  5.2 1.5 %collective-permute-start = (bf16[1,8,32,128]{3,2,1,0:T(8,128)(2,1)}, bf16[1,8,32,128]{3,2,1,0:T(8,128)(2,1)S(1)}, u32[]{:S(2)}, u32[]{:S(2)}) collective-permute-start(bf16[1,8,32,128]{3,2,1,0:T(8,128)(2,1)} %param.5), channel_id=1, source_target_pairs={{0,0},{1,128},{2,256},{3,384},{4,4},{5,132},{6,260},{7,388},{8,8},... | collective-permute-start | bytes 196616 | tf_op jit(solution)/shard_map/ppermute | solution.py:211
  6.7 1.9 %collective-permute-start.1 = (bf16[1,8,32,128]{3,2,1,0:T(8,128)(2,1)}, bf16[1,8,32,128]{3,2,1,0:T(8,128)(2,1)S(1)}, u32[]{:S(2)}, u32[]{:S(2)}) collective-permute-start(bf16[1,8,32,128]{3,2,1,0:T(8,128)(2,1)} %param.5), channel_id=1, source_target_pairs={{4,8},{5,136},{6,264},{7,392},{8,4},{9,132},{10,260},{11,388},{12,... | collective-permute-start | bytes 196616 | tf_op jit(solution)/shard_map/ppermute | solution.py:211
  8.6 0.0 collective-permute-done.2
  8.7 0.9 pad_maximum_fusion.2
  9.5 0.0 collective-permute-done
  9.5 3.0 %collective-permute-done.1 = bf16[1,8,32,128]{3,2,1,0:T(8,128)(2,1)S(1)} collective-permute-done((bf16[1,8,32,128]{3,2,1,0:T(8,128)(2,1)}, bf16[1,8,32,128]{3,2,1,0:T(8,128)(2,1)S(1)}, u32[]{:S(2)}, u32[]{:S(2)}) %collective-permute-start.1) | collective-permute-done | bytes 65568 | tf_op jit(solution)/shard_map/ppermute | solution.py:211
  12.5 0.9 broadcast_in_dim.4
  13.4 12.4 %all-to-all-start = ((bf16[4,2,8,32,128]{4,3,2,1,0:T(8,128)(2,1)}), bf16[4,2,8,32,128]{4,3,2,1,0:T(8,128)(2,1)S(1)}, u32[]{:S(2)}, u32[]{:S(2)}) async-start(bf16[4,2,8,32,128]{4,3,2,1,0:T(8,128)(2,1)} %broadcast_in_dim.4), calls=%async_computation | async-start | bytes 1048576 | tf_op jit(solution)/shard_map/all_to_all | solution.py:179
  25.8 11.2 %all_gather.3.pair = bf16[2,32,32,128]{3,2,1,0:T(8,128)(2,1)S(1)} all-gather(bf16[2,8,32,128]{3,2,1,0:T(8,128)(2,1)S(1)} %pad_maximum_fusion.1), channel_id=1, replica_groups=mesh['chan'=4,'zhi'=4,'ring'=4,'core'=2,'space'=4] {'chan'}, dimensions={1}, use_global_device_ids=true | all-gather | bytes 655360 | tf_op jit(solution)/shard_map/all_gather | solution.py:216
  37.0 1.9 %collective-permute-start.3 = (bf16[32,32,128]{2,1,0:T(8,128)(2,1)S(1)}, bf16[32,32,128]{2,1,0:T(8,128)(2,1)S(1)}, u32[]{:S(2)}, u32[]{:S(2)}) collective-permute-start(bf16[32,32,128]{2,1,0:T(8,128)(2,1)S(1)} %slice_bitcast_fusion), channel_id=1, source_target_pairs={{0,4},{4,0},{1,5},{5,1},{2,6},{6,2},{3,7},{7,3},{8,12},{12,8},{9,1... | collective-permute-start | bytes 786440 | tf_op jit(solution)/shard_map/ppermute | solution.py:217
  39.0 1.5 %collective-permute-done.3.inner = bf16[32,32,128]{2,1,0:T(8,128)(2,1)S(1)} collective-permute-done((bf16[32,32,128]{2,1,0:T(8,128)(2,1)S(1)}, bf16[32,32,128]{2,1,0:T(8,128)(2,1)S(1)}, u32[]{:S(2)}, u32[]{:S(2)}) %collective-permute-start.3) | collective-permute-done | bytes 262176 | tf_op jit(solution)/shard_map/ppermute | solution.py:217
  40.5 0.0 all-to-all-done.data.pair
  40.5 1.6 %filter_grad.1 = (f32[1792,128]{1,0:T(8,128)S(1)}, f32[1792,128]{1,0:T(8,128)S(1)}, bf16[32,32,128]{2,1,0:T(8,128)(2,1)S(1)}) custom-call(s32[1]{0:T(128)} %bitcast.core, bf16[4,2,8,32,128]{4,3,2,1,0:T(8,128)(2,1)S(1)} %all-to-all-done.data.pair, bf16[2,32,32,128]{3,2,1,0:T(8,128)(2,1)S(1)} %all_gather.3.pair, ...), custom_call_target="tpu_custom_call" | custom-call | flops 905969664 | bytes 3145728 | tf_op jit(solution)/shard_map/filter_grad/pallas_call | solution.py:160
  42.1 2.0 %collective-permute-start.4 = (f32[1792,128]{1,0:T(8,128)S(1)}, f32[1792,128]{1,0:T(8,128)S(1)}, u32[]{:S(2)}, u32[]{:S(2)}) collective-permute-start(f32[1792,128]{1,0:T(8,128)S(1)} %get-tuple-element.44), channel_id=1, source_target_pairs={{0,4},{4,0},{1,5},{5,1},{2,6},{6,2},{3,7},{7,3},{8,12},{12,8},{9,1... | collective-permute-start | bytes 2752520 | tf_op jit(solution)/shard_map/ppermute | solution.py:220
  44.1 2.3 %collective-permute-start.5 = (bf16[32,32,128]{2,1,0:T(8,128)(2,1)S(1)}, bf16[32,32,128]{2,1,0:T(8,128)(2,1)S(1)}, u32[]{:S(2)}, u32[]{:S(2)}) collective-permute-start(bf16[32,32,128]{2,1,0:T(8,128)(2,1)S(1)} %get-tuple-element.46), channel_id=1, source_target_pairs={{0,4},{4,0},{1,5},{5,1},{2,6},{6,2},{3,7},{7,3},{8,12},{12,8},{9,1... | collective-permute-start | bytes 786440 | tf_op jit(solution)/shard_map/ppermute | solution.py:221
  46.4 0.0 collective-permute-done.4
  46.4 0.0 copy-start
  46.4 1.0 add.27
  47.4 0.1 collective-permute-done.5.inner
  47.5 15.3 %all-to-all-start.1 = ((f32[4,448,128]{2,1,0:T(8,128)}), f32[4,448,128]{2,1,0:T(8,128)}, u32[]{:S(2)}, u32[]{:S(2)}) async-start(f32[4,448,128]{2,1,0:T(8,128)} %bitcast.2), calls=%async_computation.1 | async-start | bytes 1835008 | tf_op jit(solution)/shard_map/all_to_all | solution.py:179
  62.8 0.1 pad_add_fusion.place
  62.9 0.0 copy-done
  62.9 2.2 %input_grad.1 = (f32[256,128]{1,0:T(8,128)S(1)}, f32[256,128]{1,0:T(8,128)S(1)}, f32[256,128]{1,0:T(8,128)S(1)}, f32[256,128]{1,0:T(8,128)S(1)}) custom-call(s32[2]{0:T(128)S(1)} %pad_add_fusion.place, bf16[2,32,32,128]{3,2,1,0:T(8,128)(2,1)S(1)} %all_gather.3.pair, bf16[32,32,128]{2,1,0:T(8,128)(2,1)S(1)} %collective-permute-done.3.inner, ...), custom_call_target="tpu_custom_call" | custom-call | flops 905969664 | bytes 3145728 | tf_op jit(solution)/shard_map/input_grad/pallas_call | solution.py:106
  65.0 3.3 %collective-permute-start.6 = (f32[256,128]{1,0:T(8,128)S(1)}, f32[256,128]{1,0:T(8,128)S(1)}, u32[]{:S(2)}, u32[]{:S(2)}) collective-permute-start(f32[256,128]{1,0:T(8,128)S(1)} %get-tuple-element.50), channel_id=1, source_target_pairs={{0,1},{1,2},{2,3},{3,0},{4,5},{5,6},{6,7},{7,4},{8,9},{9,10},{10,1... | collective-permute-start | bytes 393224 | tf_op jit(solution)/shard_map/ppermute | solution.py:189
  68.4 4.0 %collective-permute-start.7 = (f32[256,128]{1,0:T(8,128)S(1)}, f32[256,128]{1,0:T(8,128)S(1)}, u32[]{:S(2)}, u32[]{:S(2)}) collective-permute-start(f32[256,128]{1,0:T(8,128)S(1)} %get-tuple-element.51), channel_id=1, source_target_pairs={{0,2},{1,3},{2,0},{3,1},{4,6},{5,7},{6,4},{7,5},{8,10},{9,11},{10,... | collective-permute-start | bytes 393224 | tf_op jit(solution)/shard_map/ppermute | solution.py:189
  72.4 3.7 %all-to-all-done.1 = f32[4,448,128]{2,1,0:T(8,128)} async-done(((f32[4,448,128]{2,1,0:T(8,128)}), f32[4,448,128]{2,1,0:T(8,128)}, u32[]{:S(2)}, u32[]{:S(2)}) %all-to-all-start.1) | async-done | bytes 917536 | tf_op jit(solution)/shard_map/all_to_all | solution.py:179
  76.0 1.3 reduce_sum.9
  77.3 0.0 collective-permute-done.6
  77.3 1.9 %collective-permute-done.7 = f32[256,128]{1,0:T(8,128)S(1)} collective-permute-done((f32[256,128]{1,0:T(8,128)S(1)}, f32[256,128]{1,0:T(8,128)S(1)}, u32[]{:S(2)}, u32[]{:S(2)}) %collective-permute-start.7) | collective-permute-done | bytes 131104 | tf_op jit(solution)/shard_map/ppermute | solution.py:189
  79.2 13.9 %collective-permute-start.8 = (f32[448,128]{1,0:T(8,128)S(1)}, f32[448,128]{1,0:T(8,128)S(1)}, u32[]{:S(2)}, u32[]{:S(2)}) collective-permute-start(f32[448,128]{1,0:T(8,128)S(1)} %reduce_sum.9), channel_id=1, source_target_pairs={{0,32},{4,100},{32,0},{36,68},{64,96},{68,36},{96,64},{100,4},{1,3... | collective-permute-start | bytes 688136 | tf_op jit(solution)/shard_map/ppermute | solution.py:230
  93.1 0.1 pad_add_fusion.1.place
  93.2 2.1 %forward.1 = (f32[256,128]{1,0:T(8,128)S(1)}, f32[256,128]{1,0:T(8,128)S(1)}, f32[256,128]{1,0:T(8,128)S(1)}, f32[256,128]{1,0:T(8,128)S(1)}) custom-call(s32[2]{0:T(128)S(1)} %pad_add_fusion.1.place, bf16[4,2,8,32,128]{4,3,2,1,0:T(8,128)(2,1)S(1)} %all-to-all-done.data.pair, bf16[32,32,128]{2,1,0:T(8,128)(2,1)S(1)} %collective-permute-done.5.inner, ...), custom_call_target="tpu_custom_call" | custom-call | flops 905969664 | bytes 3145728 | tf_op jit(solution)/shard_map/forward/pallas_call | solution.py:106
  95.3 2.0 %collective-permute-start.10 = (f32[256,128]{1,0:T(8,128)S(1)}, f32[256,128]{1,0:T(8,128)S(1)}, u32[]{:S(2)}, u32[]{:S(2)}) collective-permute-start(f32[256,128]{1,0:T(8,128)S(1)} %get-tuple-element.61), channel_id=1, source_target_pairs={{0,128},{128,256},{256,384},{384,0},{1,129},{129,257},{257,385},{3... | collective-permute-start | bytes 393224 | tf_op jit(solution)/shard_map/ppermute | solution.py:189
  97.3 3.7 %collective-permute-start.9 = (f32[256,128]{1,0:T(8,128)S(1)}, f32[256,128]{1,0:T(8,128)S(1)}, u32[]{:S(2)}, u32[]{:S(2)}) collective-permute-start(f32[256,128]{1,0:T(8,128)S(1)} %get-tuple-element.57), channel_id=1, source_target_pairs={{0,3},{1,0},{2,1},{3,2},{4,7},{5,4},{6,5},{7,6},{8,11},{9,8},{10,9... | collective-permute-start | bytes 393224 | tf_op jit(solution)/shard_map/ppermute | solution.py:189
  100.9 0.0 collective-permute-done.8
  101.0 1.2 collective-permute-done.10
  102.2 4.4 %collective-permute-done.9 = f32[256,128]{1,0:T(8,128)S(1)} collective-permute-done((f32[256,128]{1,0:T(8,128)S(1)}, f32[256,128]{1,0:T(8,128)S(1)}, u32[]{:S(2)}, u32[]{:S(2)}) %collective-permute-start.9) | collective-permute-done | bytes 131104 | tf_op jit(solution)/shard_map/ppermute | solution.py:189
  106.5 1.9 %collective-permute-start.11 = (f32[448,128]{1,0:T(8,128)S(1)}, f32[448,128]{1,0:T(8,128)S(1)}, u32[]{:S(2)}, u32[]{:S(2)}) collective-permute-start(f32[448,128]{1,0:T(8,128)S(1)} %add.28), channel_id=1, source_target_pairs={{0,96},{4,36},{32,64},{36,4},{64,32},{68,100},{96,0},{100,68},{1,9... | collective-permute-start | bytes 688136 | tf_op jit(solution)/shard_map/ppermute | solution.py:239
  108.4 3.1 %collective-permute-start.12 = (f32[256,128]{1,0:T(8,128)S(1)}, f32[256,128]{1,0:T(8,128)S(1)}, u32[]{:S(2)}, u32[]{:S(2)}) collective-permute-start(f32[256,128]{1,0:T(8,128)S(1)} %get-tuple-element.67), channel_id=1, source_target_pairs={{0,256},{128,384},{256,0},{384,128},{1,257},{129,385},{257,1},{385... | collective-permute-start | bytes 393224 | tf_op jit(solution)/shard_map/ppermute | solution.py:189
  111.5 3.2 %collective-permute-start.13 = (f32[256,128]{1,0:T(8,128)S(1)}, f32[256,128]{1,0:T(8,128)S(1)}, u32[]{:S(2)}, u32[]{:S(2)}) collective-permute-start(f32[256,128]{1,0:T(8,128)S(1)} %get-tuple-element.68), channel_id=1, source_target_pairs={{0,384},{128,0},{256,128},{384,256},{1,385},{129,1},{257,129},{385... | collective-permute-start | bytes 393224 | tf_op jit(solution)/shard_map/ppermute | solution.py:189
  114.8 0.7 add_convert_fusion.1
  115.4 5.2 %collective-permute-done.11 = f32[448,128]{1,0:T(8,128)S(1)} collective-permute-done((f32[448,128]{1,0:T(8,128)S(1)}, f32[448,128]{1,0:T(8,128)S(1)}, u32[]{:S(2)}, u32[]{:S(2)}) %collective-permute-start.11) | collective-permute-done | bytes 229408 | tf_op jit(solution)/shard_map/ppermute | solution.py:239
  120.7 0.0 collective-permute-done.12
  120.7 0.0 collective-permute-done.13
  120.7 1.0 broadcast_in_dim.5
  121.7 3.5 %all-to-all-start.2 = ((f32[4,448,128]{2,1,0:T(8,128)}), f32[4,448,128]{2,1,0:T(8,128)S(1)}, u32[]{:S(2)}, u32[]{:S(2)}) async-start(f32[4,448,128]{2,1,0:T(8,128)} %broadcast_in_dim.5), calls=%async_computation.2 | async-start | bytes 1835008 | tf_op jit(solution)/shard_map/all_to_all | solution.py:179
  125.2 0.7 collective-permute-start.14
  125.9 0.0 collective-permute-done.14
  125.9 9.6 %all-to-all-done.2 = f32[4,448,128]{2,1,0:T(8,128)S(1)} async-done(((f32[4,448,128]{2,1,0:T(8,128)}), f32[4,448,128]{2,1,0:T(8,128)S(1)}, u32[]{:S(2)}, u32[]{:S(2)}) %all-to-all-start.2) | async-done | bytes 917536 | tf_op jit(solution)/shard_map/all_to_all | solution.py:179
  135.5 6.2 %collective-permute-start.15 = (f32[1792,128]{1,0:T(8,128)S(1)}, f32[1792,128]{1,0:T(8,128)S(1)}, u32[]{:S(2)}, u32[]{:S(2)}) collective-permute-start(f32[1792,128]{1,0:T(8,128)S(1)} %bitcast.10), channel_id=1, source_target_pairs={{0,4},{4,0},{1,5},{5,1},{2,6},{6,2},{3,7},{7,3},{8,12},{12,8},{9,1... | collective-permute-start | bytes 2752520 | tf_op jit(solution)/shard_map/ppermute | solution.py:250
  141.7 2.1 %collective-permute-done.15 = f32[1792,128]{1,0:T(8,128)S(1)} collective-permute-done((f32[1792,128]{1,0:T(8,128)S(1)}, f32[1792,128]{1,0:T(8,128)S(1)}, u32[]{:S(2)}, u32[]{:S(2)}) %collective-permute-start.15) | collective-permute-done | bytes 917536 | tf_op jit(solution)/shard_map/ppermute | solution.py:250
  143.8 0.1 broadcast_select_fusion
  143.9 0.1 slice_select_fusion
  144.0 1.3 pad_maximum_fusion
  145.3 0.6 copy.7
  (5 shorter events, 0.1 us)
Async XLA Ops:
  0.6 8.0 %collective-permute-start.2 = (bf16[1,8,32,128]{3,2,1,0:T(8,128)(2,1)}, bf16[1,8,32,128]{3,2,1,0:T(8,128)(2,1)S(1)}, u32[]{:S(2)}, u32[]{:S(2)}) collective-permute-start(bf16[1,8,32,128]{3,2,1,0:T(8,128)(2,1)} %param.3), channel_id=1, source_target_pairs={{4,8},{5,9},{6,10},{7,11},{8,4},{9,5},{10,6},{11,7},{12,16},{13,17... | collective-permute-start | bytes 196616 | tf_op jit(solution)/shard_map/ppermute | solution.py:210
  5.2 4.3 %collective-permute-start = (bf16[1,8,32,128]{3,2,1,0:T(8,128)(2,1)}, bf16[1,8,32,128]{3,2,1,0:T(8,128)(2,1)S(1)}, u32[]{:S(2)}, u32[]{:S(2)}) collective-permute-start(bf16[1,8,32,128]{3,2,1,0:T(8,128)(2,1)} %param.5), channel_id=1, source_target_pairs={{0,0},{1,128},{2,256},{3,384},{4,4},{5,132},{6,260},{7,388},{8,8},... | collective-permute-start | bytes 196616 | tf_op jit(solution)/shard_map/ppermute | solution.py:211
  6.7 5.8 %collective-permute-start.1 = (bf16[1,8,32,128]{3,2,1,0:T(8,128)(2,1)}, bf16[1,8,32,128]{3,2,1,0:T(8,128)(2,1)S(1)}, u32[]{:S(2)}, u32[]{:S(2)}) collective-permute-start(bf16[1,8,32,128]{3,2,1,0:T(8,128)(2,1)} %param.5), channel_id=1, source_target_pairs={{4,8},{5,136},{6,264},{7,392},{8,4},{9,132},{10,260},{11,388},{12,... | collective-permute-start | bytes 196616 | tf_op jit(solution)/shard_map/ppermute | solution.py:211
  13.4 27.1 %all-to-all-start = ((bf16[4,2,8,32,128]{4,3,2,1,0:T(8,128)(2,1)}), bf16[4,2,8,32,128]{4,3,2,1,0:T(8,128)(2,1)S(1)}, u32[]{:S(2)}, u32[]{:S(2)}) async-start(bf16[4,2,8,32,128]{4,3,2,1,0:T(8,128)(2,1)} %broadcast_in_dim.4), calls=%async_computation | async-start | bytes 1048576 | tf_op jit(solution)/shard_map/all_to_all | solution.py:179
  37.0 3.4 %collective-permute-start.3 = (bf16[32,32,128]{2,1,0:T(8,128)(2,1)S(1)}, bf16[32,32,128]{2,1,0:T(8,128)(2,1)S(1)}, u32[]{:S(2)}, u32[]{:S(2)}) collective-permute-start(bf16[32,32,128]{2,1,0:T(8,128)(2,1)S(1)} %slice_bitcast_fusion), channel_id=1, source_target_pairs={{0,4},{4,0},{1,5},{5,1},{2,6},{6,2},{3,7},{7,3},{8,12},{12,8},{9,1... | collective-permute-start | bytes 786440 | tf_op jit(solution)/shard_map/ppermute | solution.py:217
  42.1 4.4 %collective-permute-start.4 = (f32[1792,128]{1,0:T(8,128)S(1)}, f32[1792,128]{1,0:T(8,128)S(1)}, u32[]{:S(2)}, u32[]{:S(2)}) collective-permute-start(f32[1792,128]{1,0:T(8,128)S(1)} %get-tuple-element.44), channel_id=1, source_target_pairs={{0,4},{4,0},{1,5},{5,1},{2,6},{6,2},{3,7},{7,3},{8,12},{12,8},{9,1... | collective-permute-start | bytes 2752520 | tf_op jit(solution)/shard_map/ppermute | solution.py:220
  44.1 3.4 %collective-permute-start.5 = (bf16[32,32,128]{2,1,0:T(8,128)(2,1)S(1)}, bf16[32,32,128]{2,1,0:T(8,128)(2,1)S(1)}, u32[]{:S(2)}, u32[]{:S(2)}) collective-permute-start(bf16[32,32,128]{2,1,0:T(8,128)(2,1)S(1)} %get-tuple-element.46), channel_id=1, source_target_pairs={{0,4},{4,0},{1,5},{5,1},{2,6},{6,2},{3,7},{7,3},{8,12},{12,8},{9,1... | collective-permute-start | bytes 786440 | tf_op jit(solution)/shard_map/ppermute | solution.py:221
  46.4 16.5 %copy-start = (bf16[27,128,128]{2,1,0:T(8,128)(2,1)S(1)}, bf16[27,128,128]{2,1,0:T(8,128)(2,1)}, u32[]{:S(2)}) copy-start(bf16[27,128,128]{2,1,0:T(8,128)(2,1)} %weight.3) | copy-start | bytes 2654212
  47.5 28.5 %all-to-all-start.1 = ((f32[4,448,128]{2,1,0:T(8,128)}), f32[4,448,128]{2,1,0:T(8,128)}, u32[]{:S(2)}, u32[]{:S(2)}) async-start(f32[4,448,128]{2,1,0:T(8,128)} %bitcast.2), calls=%async_computation.1 | async-start | bytes 1835008 | tf_op jit(solution)/shard_map/all_to_all | solution.py:179
  65.0 12.2 %collective-permute-start.6 = (f32[256,128]{1,0:T(8,128)S(1)}, f32[256,128]{1,0:T(8,128)S(1)}, u32[]{:S(2)}, u32[]{:S(2)}) collective-permute-start(f32[256,128]{1,0:T(8,128)S(1)} %get-tuple-element.50), channel_id=1, source_target_pairs={{0,1},{1,2},{2,3},{3,0},{4,5},{5,6},{6,7},{7,4},{8,9},{9,10},{10,1... | collective-permute-start | bytes 393224 | tf_op jit(solution)/shard_map/ppermute | solution.py:189
  68.4 10.8 %collective-permute-start.7 = (f32[256,128]{1,0:T(8,128)S(1)}, f32[256,128]{1,0:T(8,128)S(1)}, u32[]{:S(2)}, u32[]{:S(2)}) collective-permute-start(f32[256,128]{1,0:T(8,128)S(1)} %get-tuple-element.51), channel_id=1, source_target_pairs={{0,2},{1,3},{2,0},{3,1},{4,6},{5,7},{6,4},{7,5},{8,10},{9,11},{10,... | collective-permute-start | bytes 393224 | tf_op jit(solution)/shard_map/ppermute | solution.py:189
  79.2 21.7 %collective-permute-start.8 = (f32[448,128]{1,0:T(8,128)S(1)}, f32[448,128]{1,0:T(8,128)S(1)}, u32[]{:S(2)}, u32[]{:S(2)}) collective-permute-start(f32[448,128]{1,0:T(8,128)S(1)} %reduce_sum.9), channel_id=1, source_target_pairs={{0,32},{4,100},{32,0},{36,68},{64,96},{68,36},{96,64},{100,4},{1,3... | collective-permute-start | bytes 688136 | tf_op jit(solution)/shard_map/ppermute | solution.py:230
  95.3 6.9 %collective-permute-start.10 = (f32[256,128]{1,0:T(8,128)S(1)}, f32[256,128]{1,0:T(8,128)S(1)}, u32[]{:S(2)}, u32[]{:S(2)}) collective-permute-start(f32[256,128]{1,0:T(8,128)S(1)} %get-tuple-element.61), channel_id=1, source_target_pairs={{0,128},{128,256},{256,384},{384,0},{1,129},{129,257},{257,385},{3... | collective-permute-start | bytes 393224 | tf_op jit(solution)/shard_map/ppermute | solution.py:189
  97.3 9.3 %collective-permute-start.9 = (f32[256,128]{1,0:T(8,128)S(1)}, f32[256,128]{1,0:T(8,128)S(1)}, u32[]{:S(2)}, u32[]{:S(2)}) collective-permute-start(f32[256,128]{1,0:T(8,128)S(1)} %get-tuple-element.57), channel_id=1, source_target_pairs={{0,3},{1,0},{2,1},{3,2},{4,7},{5,4},{6,5},{7,6},{8,11},{9,8},{10,9... | collective-permute-start | bytes 393224 | tf_op jit(solution)/shard_map/ppermute | solution.py:189
  106.5 14.1 %collective-permute-start.11 = (f32[448,128]{1,0:T(8,128)S(1)}, f32[448,128]{1,0:T(8,128)S(1)}, u32[]{:S(2)}, u32[]{:S(2)}) collective-permute-start(f32[448,128]{1,0:T(8,128)S(1)} %add.28), channel_id=1, source_target_pairs={{0,96},{4,36},{32,64},{36,4},{64,32},{68,100},{96,0},{100,68},{1,9... | collective-permute-start | bytes 688136 | tf_op jit(solution)/shard_map/ppermute | solution.py:239
  108.4 12.2 %collective-permute-start.12 = (f32[256,128]{1,0:T(8,128)S(1)}, f32[256,128]{1,0:T(8,128)S(1)}, u32[]{:S(2)}, u32[]{:S(2)}) collective-permute-start(f32[256,128]{1,0:T(8,128)S(1)} %get-tuple-element.67), channel_id=1, source_target_pairs={{0,256},{128,384},{256,0},{384,128},{1,257},{129,385},{257,1},{385... | collective-permute-start | bytes 393224 | tf_op jit(solution)/shard_map/ppermute | solution.py:189
  111.5 9.2 %collective-permute-start.13 = (f32[256,128]{1,0:T(8,128)S(1)}, f32[256,128]{1,0:T(8,128)S(1)}, u32[]{:S(2)}, u32[]{:S(2)}) collective-permute-start(f32[256,128]{1,0:T(8,128)S(1)} %get-tuple-element.68), channel_id=1, source_target_pairs={{0,384},{128,0},{256,128},{384,256},{1,385},{129,1},{257,129},{385... | collective-permute-start | bytes 393224 | tf_op jit(solution)/shard_map/ppermute | solution.py:189
  121.7 13.8 %all-to-all-start.2 = ((f32[4,448,128]{2,1,0:T(8,128)}), f32[4,448,128]{2,1,0:T(8,128)S(1)}, u32[]{:S(2)}, u32[]{:S(2)}) async-start(f32[4,448,128]{2,1,0:T(8,128)} %broadcast_in_dim.5), calls=%async_computation.2 | async-start | bytes 1835008 | tf_op jit(solution)/shard_map/all_to_all | solution.py:179
  125.2 0.7 collective-permute-start.14
  135.5 8.3 %collective-permute-start.15 = (f32[1792,128]{1,0:T(8,128)S(1)}, f32[1792,128]{1,0:T(8,128)S(1)}, u32[]{:S(2)}, u32[]{:S(2)}) collective-permute-start(f32[1792,128]{1,0:T(8,128)S(1)} %bitcast.10), channel_id=1, source_target_pairs={{0,4},{4,0},{1,5},{5,1},{2,6},{6,2},{3,7},{7,3},{8,12},{12,8},{9,1... | collective-permute-start | bytes 2752520 | tf_op jit(solution)/shard_map/ppermute | solution.py:250

commit v11 on v10

--- a/solution.py
+++ b/solution.py
@@ -175,6 +175,68 @@
     )(core.reshape(1), data, pair, inner)
 
 
+def small_call(kernel, shape, *operands):
+    return pl.pallas_call(
+        kernel,
+        out_shape=jax.ShapeDtypeStruct(shape, F32),
+        in_specs=[VMEM] * len(operands),
+        out_specs=VMEM,
+        compiler_params=pltpu.CompilerParams(vmem_limit_bytes=8 << 20),
+        cost_estimate=pl.CostEstimate(
+            flops=operands[0].size, bytes_accessed=1 << 20, transcendentals=0
+        ),
+    )(*operands)
+
+
+def add_kernel(left, right, out):
+    out[...] = left[...] + right[...]
+
+
+def sum_kernel(parts, out):
+    out[...] = (parts[0] + parts[1]) + (parts[2] + parts[3])
+
+
+def spread_kernel(scale, left, right, out):
+    total = (left[...] + right[...]) * scale
+    for copy in range(out.shape[0]):
+        out[copy] = total
+
+
+def join_kernel(core, mine, other, out, sems):
+    size, rest = mine.shape[0], out.shape[0] - mine.shape[0]
+
+    def place(low, high):
+        copies = [
+            pltpu.make_async_copy(low, out.at[pl.ds(0, size)], sems.at[0]),
+            pltpu.make_async_copy(high.at[pl.ds(0, rest)], out.at[pl.ds(size, rest)], sems.at[1]),
+        ]
+        for copy in copies:
+            copy.start()
+        for copy in copies:
+            copy.wait()
+
+    @pl.when(core[0] == 0)
+    def _():
+        place(mine, other)
+
+    @pl.when(core[0] == 1)
+    def _():
+        place(other, mine)
+
+
+def joined(core, mine, other, shape):
+    return pl.pallas_call(
+        join_kernel,
+        out_shape=jax.ShapeDtypeStruct(shape, F32),
+        in_specs=[SMEM, VMEM, VMEM],
+        out_specs=pl.BlockSpec(memory_space=pl.ANY),
+        scratch_shapes=[pltpu.SemaphoreType.DMA((2,))],
+        compiler_params=pltpu.CompilerParams(vmem_limit_bytes=8 << 20),
+        cost_estimate=pl.CostEstimate(flops=0, bytes_accessed=4 << 20, transcendentals=0),
+        name="join",
+    )(core.reshape(1), mine, other)
+
+
 def exchange(block, axis):
     return lax.all_to_all(block, axis, split_axis=0, concat_axis=0, tiled=True)
 
@@ -219,13 +281,16 @@
     keep, send, own = filter_partial(core, data, grad, grad_inner)
     moved = lax.ppermute(send, "core", swap)
     data_inner = lax.ppermute(after(own, send), "core", swap)
-    half, data_inner = lax.optimization_barrier((keep + moved, data_inner))
+    half = small_call(add_kernel, keep.shape, keep, moved)
+    half, data_inner = lax.optimization_barrier((half, data_inner))
 
     moved = exchange(half.reshape(rings, -1, lanes), "ring")
     me = lax.axis_index("space")
     back = convolve(True, core, me, after(grad, half), grad_inner, weight, spaces)
     back = [back[0], rotate(back[1], "space", 1), rotate(back[2], "space", 2), back[3]]
-    quarter, *back = lax.optimization_barrier((moved.sum(0), *back))
+    quarter, *back = lax.optimization_barrier(
+        (small_call(sum_kernel, moved.shape[1:], moved), *back)
+    )
 
     moved = lax.ppermute(quarter, ("zhi", "core"), doubling(0))
     me = lax.axis_index("chan")
@@ -236,24 +301,22 @@
     pair = quarter + moved
     pair, back, forward = lax.optimization_barrier((pair, back, forward))
 
-    quarter = (pair + lax.ppermute(pair, ("zhi", "core"), doubling(1))) / math.sqrt(cell_count)
+    moved = lax.ppermute(pair, ("zhi", "core"), doubling(1))
+    spread = functools.partial(spread_kernel, 1 / math.sqrt(cell_count))
+    quarter = small_call(spread, (rings, *pair.shape), pair, moved)
     forward = [*forward[:2], rotate(forward[2], "chan", 2), rotate(forward[3], "chan", 3)]
     input_grad = sum(back).astype(BF16).reshape(activations.shape)
     quarter, forward, _ = lax.optimization_barrier((quarter, forward, input_grad))
 
-    half = gather(quarter, "ring").reshape(-1, lanes)
+    half = exchange(quarter, "ring").reshape(-1, lanes)
     output = lax.ppermute(
         sum(forward).astype(BF16).reshape(activations.shape), AXES, neighbour(sizes, False, True)
     )
     half = after(half, output)
 
     other = lax.ppermute(half, "core", swap)
-    first = core == 0
-    low = jnp.where(first, half, other)
-    high = jnp.where(first, other, half)
-    taps = weight.shape[0]
-    filter_grad = jnp.concatenate([low, high[: taps * lanes - low.shape[0]]], axis=0)
-    filter_grad = filter_grad.reshape(weight.shape)
+    blocks = (-1, *weight.shape[1:])
+    filter_grad = joined(core, half.reshape(blocks), other.reshape(blocks), weight.shape)
     return output, input_grad, filter_grad
 
 

time: 147 us -> 146 us (level)
  other arithmetic: 5.54 us -> 1.73 us
  Pallas kernels: 5.83 us -> 9.39 us
  starting transfers between devices: 87.4 us -> 85.7 us
  waiting for transfers between devices: 32.6 us -> 34.2 us
    pallas_call x0 -> x4, Pallas kernels: none -> 3.27 us  [the longest x3 2.05 us: small_call(): pl.pallas_call(kernel, out_shape=jax.ShapeDtypeStruct(shape, F32), in_spe...]
    ppermute x6, waiting for transfers between devices: 7.47 us -> 8.96 us  [rotate(): lax.ppermute(term, axis, [(i, (i + step) % count) for i in range(count)])]
  transfers between devices with their start and end apart: 19 -> 19, of which waited for: 10 -> 10; matrix products, arithmetic and copies ran while one was open for 3% -> 1% of each run, Pallas kernels for 3% -> 5%
where the time goes in v11:
time: 146 us; the launch traced here: 145 us
  starting transfers between devices  85.7 us (59%)
  waiting for transfers between devices  34.2 us (23%)
  blocking collectives  11.2 us (8%)
  Pallas kernels  9.39 us (6%)
  local copies, waits for them, and re-layouts  2.18 us (1%)
  other arithmetic  1.73 us (1%)
    all_to_all x3, starting transfers between devices, exchange(): return lax.all_to_all(block, axis, split_axis=0, concat_axis=0, tiled=True)  31.6 us
    ppermute x6, starting transfers between devices, rotate(): lax.ppermute(term, axis, [(i, (i + step) % count) for i in range(count)])  18.9 us
    all_to_all x3, waiting for transfers between devices, exchange(): return lax.all_to_all(block, axis, split_axis=0, concat_axis=0, tiled=True)  13.2 us
    ppermute x1, starting transfers between devices, shards(): moved = lax.ppermute(quarter, ('zhi', 'core'), doubling(0))  13.2 us
    all_gather x1, blocking collectives, shards(): grad = lax.all_gather(grad, 'chan', axis=1, tiled=True)  11.2 us
    ppermute x6, waiting for transfers between devices, rotate(): lax.ppermute(term, axis, [(i, (i + step) % count) for i in range(count)])  8.96 us
    ppermute x1, waiting for transfers between devices, shards(): moved = lax.ppermute(pair, ('zhi', 'core'), doubling(1))  5.27 us
    ppermute x1, starting transfers between devices, shards(): other = lax.ppermute(half, 'core', swap)  5.21 us
  transfers between devices with their start and end apart: 19, of which 10 were waited for; matrix products, arithmetic and copies ran while one was open for 1% of the time, Pallas kernels for 5%

profile of v11, /device:TPU:1, one launch (start us, length us, event | category | flops | bytes accessed | tf_op | source)
XLA Modules:
  0.0 145.3 jit_solution(6175401467992049808)
XLA Ops:
  0.6 4.6 %collective-permute-start.2 = (bf16[1,8,32,128]{3,2,1,0:T(8,128)(2,1)}, bf16[1,8,32,128]{3,2,1,0:T(8,128)(2,1)S(1)}, u32[]{:S(2)}, u32[]{:S(2)}) collective-permute-start(bf16[1,8,32,128]{3,2,1,0:T(8,128)(2,1)} %param.3), channel_id=1, source_target_pairs={{4,8},{5,9},{6,10},{7,11},{8,4},{9,5},{10,6},{11,7},{12,16},{13,17... | collective-permute-start | bytes 196616 | tf_op jit(solution)/shard_map/ppermute | solution.py:272
  5.2 1.5 %collective-permute-start = (bf16[1,8,32,128]{3,2,1,0:T(8,128)(2,1)}, bf16[1,8,32,128]{3,2,1,0:T(8,128)(2,1)S(1)}, u32[]{:S(2)}, u32[]{:S(2)}) collective-permute-start(bf16[1,8,32,128]{3,2,1,0:T(8,128)(2,1)} %param.5), channel_id=1, source_target_pairs={{0,0},{1,128},{2,256},{3,384},{4,4},{5,132},{6,260},{7,388},{8,8},... | collective-permute-start | bytes 196616 | tf_op jit(solution)/shard_map/ppermute | solution.py:273
  6.7 1.9 %collective-permute-start.1 = (bf16[1,8,32,128]{3,2,1,0:T(8,128)(2,1)}, bf16[1,8,32,128]{3,2,1,0:T(8,128)(2,1)S(1)}, u32[]{:S(2)}, u32[]{:S(2)}) collective-permute-start(bf16[1,8,32,128]{3,2,1,0:T(8,128)(2,1)} %param.5), channel_id=1, source_target_pairs={{4,8},{5,136},{6,264},{7,392},{8,4},{9,132},{10,260},{11,388},{12,... | collective-permute-start | bytes 196616 | tf_op jit(solution)/shard_map/ppermute | solution.py:273
  8.6 0.0 collective-permute-done.2
  8.7 0.9 pad_maximum_fusion.1
  9.5 0.0 collective-permute-done
  9.5 3.0 %collective-permute-done.1 = bf16[1,8,32,128]{3,2,1,0:T(8,128)(2,1)S(1)} collective-permute-done((bf16[1,8,32,128]{3,2,1,0:T(8,128)(2,1)}, bf16[1,8,32,128]{3,2,1,0:T(8,128)(2,1)S(1)}, u32[]{:S(2)}, u32[]{:S(2)}) %collective-permute-start.1) | collective-permute-done | bytes 65568 | tf_op jit(solution)/shard_map/ppermute | solution.py:273
  12.5 0.9 broadcast_in_dim.2
  13.4 12.4 %all-to-all-start = ((bf16[4,2,8,32,128]{4,3,2,1,0:T(8,128)(2,1)}), bf16[4,2,8,32,128]{4,3,2,1,0:T(8,128)(2,1)S(1)}, u32[]{:S(2)}, u32[]{:S(2)}) async-start(bf16[4,2,8,32,128]{4,3,2,1,0:T(8,128)(2,1)} %broadcast_in_dim.2), calls=%async_computation | async-start | bytes 1048576 | tf_op jit(solution)/shard_map/all_to_all | solution.py:241
  25.8 11.2 %all_gather.3.pair = bf16[2,32,32,128]{3,2,1,0:T(8,128)(2,1)S(1)} all-gather(bf16[2,8,32,128]{3,2,1,0:T(8,128)(2,1)S(1)} %pad_maximum_fusion), channel_id=1, replica_groups=mesh['chan'=4,'zhi'=4,'ring'=4,'core'=2,'space'=4] {'chan'}, dimensions={1}, use_global_device_ids=true | all-gather | bytes 655360 | tf_op jit(solution)/shard_map/all_gather | solution.py:278
  37.0 1.9 %collective-permute-start.3 = (bf16[32,32,128]{2,1,0:T(8,128)(2,1)S(1)}, bf16[32,32,128]{2,1,0:T(8,128)(2,1)S(1)}, u32[]{:S(2)}, u32[]{:S(2)}) collective-permute-start(bf16[32,32,128]{2,1,0:T(8,128)(2,1)S(1)} %slice_bitcast_fusion), channel_id=1, source_target_pairs={{0,4},{4,0},{1,5},{5,1},{2,6},{6,2},{3,7},{7,3},{8,12},{12,8},{9,1... | collective-permute-start | bytes 786440 | tf_op jit(solution)/shard_map/ppermute | solution.py:279
  39.0 1.5 %collective-permute-done.3.inner = bf16[32,32,128]{2,1,0:T(8,128)(2,1)S(1)} collective-permute-done((bf16[32,32,128]{2,1,0:T(8,128)(2,1)S(1)}, bf16[32,32,128]{2,1,0:T(8,128)(2,1)S(1)}, u32[]{:S(2)}, u32[]{:S(2)}) %collective-permute-start.3) | collective-permute-done | bytes 262176 | tf_op jit(solution)/shard_map/ppermute | solution.py:279
  40.5 0.0 all-to-all-done.data.pair
  40.5 1.6 %filter_grad.1 = (f32[1792,128]{1,0:T(8,128)S(1)}, f32[1792,128]{1,0:T(8,128)S(1)}, bf16[32,32,128]{2,1,0:T(8,128)(2,1)S(1)}) custom-call(s32[1]{0:T(128)} %bitcast.core, bf16[4,2,8,32,128]{4,3,2,1,0:T(8,128)(2,1)S(1)} %all-to-all-done.data.pair, bf16[2,32,32,128]{3,2,1,0:T(8,128)(2,1)S(1)} %all_gather.3.pair, ...), custom_call_target="tpu_custom_call" | custom-call | flops 905969664 | bytes 3145728 | tf_op jit(solution)/shard_map/filter_grad/pallas_call | solution.py:160
  42.1 2.0 %collective-permute-start.4 = (f32[1792,128]{1,0:T(8,128)S(1)}, f32[1792,128]{1,0:T(8,128)S(1)}, u32[]{:S(2)}, u32[]{:S(2)}) collective-permute-start(f32[1792,128]{1,0:T(8,128)S(1)} %get-tuple-element.44), channel_id=1, source_target_pairs={{0,4},{4,0},{1,5},{5,1},{2,6},{6,2},{3,7},{7,3},{8,12},{12,8},{9,1... | collective-permute-start | bytes 2752520 | tf_op jit(solution)/shard_map/ppermute | solution.py:282
  44.1 2.3 %collective-permute-start.5 = (bf16[32,32,128]{2,1,0:T(8,128)(2,1)S(1)}, bf16[32,32,128]{2,1,0:T(8,128)(2,1)S(1)}, u32[]{:S(2)}, u32[]{:S(2)}) collective-permute-start(bf16[32,32,128]{2,1,0:T(8,128)(2,1)S(1)} %get-tuple-element.46), channel_id=1, source_target_pairs={{0,4},{4,0},{1,5},{5,1},{2,6},{6,2},{3,7},{7,3},{8,12},{12,8},{9,1... | collective-permute-start | bytes 786440 | tf_op jit(solution)/shard_map/ppermute | solution.py:283
  46.4 0.0 collective-permute-done.4.right
  46.4 0.0 copy-start
  46.4 1.0 shard_map.58
  47.4 0.1 collective-permute-done.5.inner
  47.5 15.3 %all-to-all-start.1 = ((f32[4,448,128]{2,1,0:T(8,128)}), f32[4,448,128]{2,1,0:T(8,128)S(1)}, u32[]{:S(2)}, u32[]{:S(2)}) async-start(f32[4,448,128]{2,1,0:T(8,128)} %bitcast.2), calls=%async_computation.1 | async-start | bytes 1835008 | tf_op jit(solution)/shard_map/all_to_all | solution.py:241
  62.8 0.1 pad_add_fusion.place
  62.9 0.0 copy-done
  62.9 2.5 %input_grad.1 = (f32[256,128]{1,0:T(8,128)S(1)}, f32[256,128]{1,0:T(8,128)}, f32[256,128]{1,0:T(8,128)}, f32[256,128]{1,0:T(8,128)S(1)}) custom-call(s32[2]{0:T(128)S(1)} %pad_add_fusion.place, bf16[2,32,32,128]{3,2,1,0:T(8,128)(2,1)S(1)} %all_gather.3.pair, bf16[32,32,128]{2,1,0:T(8,128)(2,1)S(1)} %collective-permute-done.3.inner, ...), custom_call_target="tpu_custom_call" | custom-call | flops 905969664 | bytes 3145728 | tf_op jit(solution)/shard_map/input_grad/pallas_call | solution.py:106
  65.3 0.0 copy-start.1
  65.3 0.6 copy-done.1
  66.0 3.3 %collective-permute-start.6 = (f32[256,128]{1,0:T(8,128)}, f32[256,128]{1,0:T(8,128)S(1)}, u32[]{:S(2)}, u32[]{:S(2)}) collective-permute-start(f32[256,128]{1,0:T(8,128)} %get-tuple-element.50), channel_id=1, source_target_pairs={{0,1},{1,2},{2,3},{3,0},{4,5},{5,6},{6,7},{7,4},{8,9},{9,10},{10,1... | collective-permute-start | bytes 393224 | tf_op jit(solution)/shard_map/ppermute | solution.py:251
  69.3 4.0 %collective-permute-start.7 = (f32[256,128]{1,0:T(8,128)}, f32[256,128]{1,0:T(8,128)S(1)}, u32[]{:S(2)}, u32[]{:S(2)}) collective-permute-start(f32[256,128]{1,0:T(8,128)} %get-tuple-element.51), channel_id=1, source_target_pairs={{0,2},{1,3},{2,0},{3,1},{4,6},{5,7},{6,4},{7,5},{8,10},{9,11},{10,... | collective-permute-start | bytes 393224 | tf_op jit(solution)/shard_map/ppermute | solution.py:251
  73.3 2.6 %all-to-all-done.1.parts = f32[4,448,128]{2,1,0:T(8,128)S(1)} async-done(((f32[4,448,128]{2,1,0:T(8,128)}), f32[4,448,128]{2,1,0:T(8,128)S(1)}, u32[]{:S(2)}, u32[]{:S(2)}) %all-to-all-start.1) | async-done | bytes 917536 | tf_op jit(solution)/shard_map/all_to_all | solution.py:241
  76.0 0.0 copy-start.2
  76.0 0.0 collective-permute-done.6
  76.0 4.3 %collective-permute-done.7 = f32[256,128]{1,0:T(8,128)S(1)} collective-permute-done((f32[256,128]{1,0:T(8,128)}, f32[256,128]{1,0:T(8,128)S(1)}, u32[]{:S(2)}, u32[]{:S(2)}) %collective-permute-start.7) | collective-permute-done | bytes 131104 | tf_op jit(solution)/shard_map/ppermute | solution.py:251
  80.3 13.2 %collective-permute-start.8 = (f32[448,128]{1,0:T(8,128)S(1)}, f32[448,128]{1,0:T(8,128)S(1)}, u32[]{:S(2)}, u32[]{:S(2)}) collective-permute-start(f32[448,128]{1,0:T(8,128)S(1)} %shard_map.59), channel_id=1, source_target_pairs={{0,32},{4,100},{32,0},{36,68},{64,96},{68,36},{96,64},{100,4},{1,3... | collective-permute-start | bytes 688136 | tf_op jit(solution)/shard_map/ppermute | solution.py:295
  93.5 0.1 pad_add_fusion.1.place
  93.6 2.1 %forward.1 = (f32[256,128]{1,0:T(8,128)S(1)}, f32[256,128]{1,0:T(8,128)S(1)}, f32[256,128]{1,0:T(8,128)S(1)}, f32[256,128]{1,0:T(8,128)S(1)}) custom-call(s32[2]{0:T(128)S(1)} %pad_add_fusion.1.place, bf16[4,2,8,32,128]{4,3,2,1,0:T(8,128)(2,1)S(1)} %all-to-all-done.data.pair, bf16[32,32,128]{2,1,0:T(8,128)(2,1)S(1)} %collective-permute-done.5.inner, ...), custom_call_target="tpu_custom_call" | custom-call | flops 905969664 | bytes 3145728 | tf_op jit(solution)/shard_map/forward/pallas_call | solution.py:106
  95.7 2.0 %collective-permute-start.10 = (f32[256,128]{1,0:T(8,128)S(1)}, f32[256,128]{1,0:T(8,128)S(1)}, u32[]{:S(2)}, u32[]{:S(2)}) collective-permute-start(f32[256,128]{1,0:T(8,128)S(1)} %get-tuple-element.61), channel_id=1, source_target_pairs={{0,128},{128,256},{256,384},{384,0},{1,129},{129,257},{257,385},{3... | collective-permute-start | bytes 393224 | tf_op jit(solution)/shard_map/ppermute | solution.py:251
  97.7 0.0 copy-done.2
  97.7 3.4 %collective-permute-start.9 = (f32[256,128]{1,0:T(8,128)S(1)}, f32[256,128]{1,0:T(8,128)S(1)}, u32[]{:S(2)}, u32[]{:S(2)}) collective-permute-start(f32[256,128]{1,0:T(8,128)S(1)} %copy-done.2), channel_id=1, source_target_pairs={{0,3},{1,0},{2,1},{3,2},{4,7},{5,4},{6,5},{7,6},{8,11},{9,8},{10,9... | collective-permute-start | bytes 393224 | tf_op jit(solution)/shard_map/ppermute | solution.py:251
  101.1 0.0 collective-permute-done.8
  101.1 1.5 %collective-permute-done.10 = f32[256,128]{1,0:T(8,128)S(1)} collective-permute-done((f32[256,128]{1,0:T(8,128)S(1)}, f32[256,128]{1,0:T(8,128)S(1)}, u32[]{:S(2)}, u32[]{:S(2)}) %collective-permute-start.10) | collective-permute-done | bytes 131104 | tf_op jit(solution)/shard_map/ppermute | solution.py:251
  102.6 3.1 %collective-permute-done.9 = f32[256,128]{1,0:T(8,128)S(1)} collective-permute-done((f32[256,128]{1,0:T(8,128)S(1)}, f32[256,128]{1,0:T(8,128)S(1)}, u32[]{:S(2)}, u32[]{:S(2)}) %collective-permute-start.9) | collective-permute-done | bytes 131104 | tf_op jit(solution)/shard_map/ppermute | solution.py:251
  105.7 1.9 %collective-permute-start.11 = (f32[448,128]{1,0:T(8,128)S(1)}, f32[448,128]{1,0:T(8,128)S(1)}, u32[]{:S(2)}, u32[]{:S(2)}) collective-permute-start(f32[448,128]{1,0:T(8,128)S(1)} %add.21.left), channel_id=1, source_target_pairs={{0,96},{4,36},{32,64},{36,4},{64,32},{68,100},{96,0},{100,68},{1,9... | collective-permute-start | bytes 688136 | tf_op jit(solution)/shard_map/ppermute | solution.py:304
  107.6 3.1 %collective-permute-start.12 = (f32[256,128]{1,0:T(8,128)S(1)}, f32[256,128]{1,0:T(8,128)S(1)}, u32[]{:S(2)}, u32[]{:S(2)}) collective-permute-start(f32[256,128]{1,0:T(8,128)S(1)} %get-tuple-element.67), channel_id=1, source_target_pairs={{0,256},{128,384},{256,0},{384,128},{1,257},{129,385},{257,1},{385... | collective-permute-start | bytes 393224 | tf_op jit(solution)/shard_map/ppermute | solution.py:251
  110.8 3.2 %collective-permute-start.13 = (f32[256,128]{1,0:T(8,128)S(1)}, f32[256,128]{1,0:T(8,128)S(1)}, u32[]{:S(2)}, u32[]{:S(2)}) collective-permute-start(f32[256,128]{1,0:T(8,128)S(1)} %get-tuple-element.68), channel_id=1, source_target_pairs={{0,384},{128,0},{256,128},{384,256},{1,385},{129,1},{257,129},{385... | collective-permute-start | bytes 393224 | tf_op jit(solution)/shard_map/ppermute | solution.py:251
  113.9 0.7 add_convert_fusion.1
  114.6 5.3 %collective-permute-done.11.right = f32[448,128]{1,0:T(8,128)S(1)} collective-permute-done((f32[448,128]{1,0:T(8,128)S(1)}, f32[448,128]{1,0:T(8,128)S(1)}, u32[]{:S(2)}, u32[]{:S(2)}) %collective-permute-start.11) | collective-permute-done | bytes 229408 | tf_op jit(solution)/shard_map/ppermute | solution.py:304
  119.9 1.0 shard_map.60
  120.9 0.0 collective-permute-done.12
  120.9 0.0 collective-permute-done.13
  120.9 3.9 %all-to-all-start.2 = ((f32[4,448,128]{2,1,0:T(8,128)}), f32[4,448,128]{2,1,0:T(8,128)S(1)}, u32[]{:S(2)}, u32[]{:S(2)}) async-start(f32[4,448,128]{2,1,0:T(8,128)} %shard_map.60), calls=%async_computation.2 | async-start | bytes 1835008 | tf_op jit(solution)/shard_map/all_to_all | solution.py:241
  124.8 0.7 collective-permute-start.14
  125.5 0.0 collective-permute-done.14
  125.5 10.6 %all-to-all-done.2 = f32[4,448,128]{2,1,0:T(8,128)S(1)} async-done(((f32[4,448,128]{2,1,0:T(8,128)}), f32[4,448,128]{2,1,0:T(8,128)S(1)}, u32[]{:S(2)}, u32[]{:S(2)}) %all-to-all-start.2) | async-done | bytes 917536 | tf_op jit(solution)/shard_map/all_to_all | solution.py:241
  136.1 5.2 %collective-permute-start.15 = (f32[1792,128]{1,0:T(8,128)S(1)}, f32[1792,128]{1,0:T(8,128)S(1)}, u32[]{:S(2)}, u32[]{:S(2)}) collective-permute-start(f32[1792,128]{1,0:T(8,128)S(1)} %bitcast.11), channel_id=1, source_target_pairs={{0,4},{4,0},{1,5},{5,1},{2,6},{6,2},{3,7},{7,3},{8,12},{12,8},{9,1... | collective-permute-start | bytes 2752520 | tf_op jit(solution)/shard_map/ppermute | solution.py:317
  141.3 2.1 %collective-permute-done.15 = f32[1792,128]{1,0:T(8,128)S(1)} collective-permute-done((f32[1792,128]{1,0:T(8,128)S(1)}, f32[1792,128]{1,0:T(8,128)S(1)}, u32[]{:S(2)}, u32[]{:S(2)}) %collective-permute-start.15) | collective-permute-done | bytes 917536 | tf_op jit(solution)/shard_map/ppermute | solution.py:317
  143.4 1.2 join.1
  144.6 0.6 copy.7
  (5 shorter events, 0.1 us)
Async XLA Ops:
  0.6 8.0 %collective-permute-start.2 = (bf16[1,8,32,128]{3,2,1,0:T(8,128)(2,1)}, bf16[1,8,32,128]{3,2,1,0:T(8,128)(2,1)S(1)}, u32[]{:S(2)}, u32[]{:S(2)}) collective-permute-start(bf16[1,8,32,128]{3,2,1,0:T(8,128)(2,1)} %param.3), channel_id=1, source_target_pairs={{4,8},{5,9},{6,10},{7,11},{8,4},{9,5},{10,6},{11,7},{12,16},{13,17... | collective-permute-start | bytes 196616 | tf_op jit(solution)/shard_map/ppermute | solution.py:272
  5.2 4.3 %collective-permute-start = (bf16[1,8,32,128]{3,2,1,0:T(8,128)(2,1)}, bf16[1,8,32,128]{3,2,1,0:T(8,128)(2,1)S(1)}, u32[]{:S(2)}, u32[]{:S(2)}) collective-permute-start(bf16[1,8,32,128]{3,2,1,0:T(8,128)(2,1)} %param.5), channel_id=1, source_target_pairs={{0,0},{1,128},{2,256},{3,384},{4,4},{5,132},{6,260},{7,388},{8,8},... | collective-permute-start | bytes 196616 | tf_op jit(solution)/shard_map/ppermute | solution.py:273
  6.7 5.8 %collective-permute-start.1 = (bf16[1,8,32,128]{3,2,1,0:T(8,128)(2,1)}, bf16[1,8,32,128]{3,2,1,0:T(8,128)(2,1)S(1)}, u32[]{:S(2)}, u32[]{:S(2)}) collective-permute-start(bf16[1,8,32,128]{3,2,1,0:T(8,128)(2,1)} %param.5), channel_id=1, source_target_pairs={{4,8},{5,136},{6,264},{7,392},{8,4},{9,132},{10,260},{11,388},{12,... | collective-permute-start | bytes 196616 | tf_op jit(solution)/shard_map/ppermute | solution.py:273
  13.4 27.1 %all-to-all-start = ((bf16[4,2,8,32,128]{4,3,2,1,0:T(8,128)(2,1)}), bf16[4,2,8,32,128]{4,3,2,1,0:T(8,128)(2,1)S(1)}, u32[]{:S(2)}, u32[]{:S(2)}) async-start(bf16[4,2,8,32,128]{4,3,2,1,0:T(8,128)(2,1)} %broadcast_in_dim.2), calls=%async_computation | async-start | bytes 1048576 | tf_op jit(solution)/shard_map/all_to_all | solution.py:241
  37.0 3.4 %collective-permute-start.3 = (bf16[32,32,128]{2,1,0:T(8,128)(2,1)S(1)}, bf16[32,32,128]{2,1,0:T(8,128)(2,1)S(1)}, u32[]{:S(2)}, u32[]{:S(2)}) collective-permute-start(bf16[32,32,128]{2,1,0:T(8,128)(2,1)S(1)} %slice_bitcast_fusion), channel_id=1, source_target_pairs={{0,4},{4,0},{1,5},{5,1},{2,6},{6,2},{3,7},{7,3},{8,12},{12,8},{9,1... | collective-permute-start | bytes 786440 | tf_op jit(solution)/shard_map/ppermute | solution.py:279
  42.1 4.4 %collective-permute-start.4 = (f32[1792,128]{1,0:T(8,128)S(1)}, f32[1792,128]{1,0:T(8,128)S(1)}, u32[]{:S(2)}, u32[]{:S(2)}) collective-permute-start(f32[1792,128]{1,0:T(8,128)S(1)} %get-tuple-element.44), channel_id=1, source_target_pairs={{0,4},{4,0},{1,5},{5,1},{2,6},{6,2},{3,7},{7,3},{8,12},{12,8},{9,1... | collective-permute-start | bytes 2752520 | tf_op jit(solution)/shard_map/ppermute | solution.py:282
  44.1 3.4 %collective-permute-start.5 = (bf16[32,32,128]{2,1,0:T(8,128)(2,1)S(1)}, bf16[32,32,128]{2,1,0:T(8,128)(2,1)S(1)}, u32[]{:S(2)}, u32[]{:S(2)}) collective-permute-start(bf16[32,32,128]{2,1,0:T(8,128)(2,1)S(1)} %get-tuple-element.46), channel_id=1, source_target_pairs={{0,4},{4,0},{1,5},{5,1},{2,6},{6,2},{3,7},{7,3},{8,12},{12,8},{9,1... | collective-permute-start | bytes 786440 | tf_op jit(solution)/shard_map/ppermute | solution.py:283
  46.4 16.5 %copy-start = (bf16[27,128,128]{2,1,0:T(8,128)(2,1)S(1)}, bf16[27,128,128]{2,1,0:T(8,128)(2,1)}, u32[]{:S(2)}) copy-start(bf16[27,128,128]{2,1,0:T(8,128)(2,1)} %weight.3) | copy-start | bytes 2654212
  47.5 28.4 %all-to-all-start.1 = ((f32[4,448,128]{2,1,0:T(8,128)}), f32[4,448,128]{2,1,0:T(8,128)S(1)}, u32[]{:S(2)}, u32[]{:S(2)}) async-start(f32[4,448,128]{2,1,0:T(8,128)} %bitcast.2), calls=%async_computation.1 | async-start | bytes 1835008 | tf_op jit(solution)/shard_map/all_to_all | solution.py:241
  65.3 0.6 copy-start.1
  66.0 10.0 %collective-permute-start.6 = (f32[256,128]{1,0:T(8,128)}, f32[256,128]{1,0:T(8,128)S(1)}, u32[]{:S(2)}, u32[]{:S(2)}) collective-permute-start(f32[256,128]{1,0:T(8,128)} %get-tuple-element.50), channel_id=1, source_target_pairs={{0,1},{1,2},{2,3},{3,0},{4,5},{5,6},{6,7},{7,4},{8,9},{9,10},{10,1... | collective-permute-start | bytes 393224 | tf_op jit(solution)/shard_map/ppermute | solution.py:251
  69.3 11.0 %collective-permute-start.7 = (f32[256,128]{1,0:T(8,128)}, f32[256,128]{1,0:T(8,128)S(1)}, u32[]{:S(2)}, u32[]{:S(2)}) collective-permute-start(f32[256,128]{1,0:T(8,128)} %get-tuple-element.51), channel_id=1, source_target_pairs={{0,2},{1,3},{2,0},{3,1},{4,6},{5,7},{6,4},{7,5},{8,10},{9,11},{10,... | collective-permute-start | bytes 393224 | tf_op jit(solution)/shard_map/ppermute | solution.py:251
  76.0 21.7 %copy-start.2 = (f32[256,128]{1,0:T(8,128)S(1)}, f32[256,128]{1,0:T(8,128)}, u32[]{:S(2)}) copy-start(f32[256,128]{1,0:T(8,128)} %copy-done.1) | copy-start | bytes 393220
  80.3 20.7 %collective-permute-start.8 = (f32[448,128]{1,0:T(8,128)S(1)}, f32[448,128]{1,0:T(8,128)S(1)}, u32[]{:S(2)}, u32[]{:S(2)}) collective-permute-start(f32[448,128]{1,0:T(8,128)S(1)} %shard_map.59), channel_id=1, source_target_pairs={{0,32},{4,100},{32,0},{36,68},{64,96},{68,36},{96,64},{100,4},{1,3... | collective-permute-start | bytes 688136 | tf_op jit(solution)/shard_map/ppermute | solution.py:295
  95.7 6.9 %collective-permute-start.10 = (f32[256,128]{1,0:T(8,128)S(1)}, f32[256,128]{1,0:T(8,128)S(1)}, u32[]{:S(2)}, u32[]{:S(2)}) collective-permute-start(f32[256,128]{1,0:T(8,128)S(1)} %get-tuple-element.61), channel_id=1, source_target_pairs={{0,128},{128,256},{256,384},{384,0},{1,129},{129,257},{257,385},{3... | collective-permute-start | bytes 393224 | tf_op jit(solution)/shard_map/ppermute | solution.py:251
  97.7 8.0 %collective-permute-start.9 = (f32[256,128]{1,0:T(8,128)S(1)}, f32[256,128]{1,0:T(8,128)S(1)}, u32[]{:S(2)}, u32[]{:S(2)}) collective-permute-start(f32[256,128]{1,0:T(8,128)S(1)} %copy-done.2), channel_id=1, source_target_pairs={{0,3},{1,0},{2,1},{3,2},{4,7},{5,4},{6,5},{7,6},{8,11},{9,8},{10,9... | collective-permute-start | bytes 393224 | tf_op jit(solution)/shard_map/ppermute | solution.py:251
  105.7 14.2 %collective-permute-start.11 = (f32[448,128]{1,0:T(8,128)S(1)}, f32[448,128]{1,0:T(8,128)S(1)}, u32[]{:S(2)}, u32[]{:S(2)}) collective-permute-start(f32[448,128]{1,0:T(8,128)S(1)} %add.21.left), channel_id=1, source_target_pairs={{0,96},{4,36},{32,64},{36,4},{64,32},{68,100},{96,0},{100,68},{1,9... | collective-permute-start | bytes 688136 | tf_op jit(solution)/shard_map/ppermute | solution.py:304
  107.6 13.2 %collective-permute-start.12 = (f32[256,128]{1,0:T(8,128)S(1)}, f32[256,128]{1,0:T(8,128)S(1)}, u32[]{:S(2)}, u32[]{:S(2)}) collective-permute-start(f32[256,128]{1,0:T(8,128)S(1)} %get-tuple-element.67), channel_id=1, source_target_pairs={{0,256},{128,384},{256,0},{384,128},{1,257},{129,385},{257,1},{385... | collective-permute-start | bytes 393224 | tf_op jit(solution)/shard_map/ppermute | solution.py:251
  110.8 10.1 %collective-permute-start.13 = (f32[256,128]{1,0:T(8,128)S(1)}, f32[256,128]{1,0:T(8,128)S(1)}, u32[]{:S(2)}, u32[]{:S(2)}) collective-permute-start(f32[256,128]{1,0:T(8,128)S(1)} %get-tuple-element.68), channel_id=1, source_target_pairs={{0,384},{128,0},{256,128},{384,256},{1,385},{129,1},{257,129},{385... | collective-permute-start | bytes 393224 | tf_op jit(solution)/shard_map/ppermute | solution.py:251
  120.9 15.2 %all-to-all-start.2 = ((f32[4,448,128]{2,1,0:T(8,128)}), f32[4,448,128]{2,1,0:T(8,128)S(1)}, u32[]{:S(2)}, u32[]{:S(2)}) async-start(f32[4,448,128]{2,1,0:T(8,128)} %shard_map.60), calls=%async_computation.2 | async-start | bytes 1835008 | tf_op jit(solution)/shard_map/all_to_all | solution.py:241
  124.8 0.7 collective-permute-start.14
  136.1 7.3 %collective-permute-start.15 = (f32[1792,128]{1,0:T(8,128)S(1)}, f32[1792,128]{1,0:T(8,128)S(1)}, u32[]{:S(2)}, u32[]{:S(2)}) collective-permute-start(f32[1792,128]{1,0:T(8,128)S(1)} %bitcast.11), channel_id=1, source_target_pairs={{0,4},{4,0},{1,5},{5,1},{2,6},{6,2},{3,7},{7,3},{8,12},{12,8},{9,1... | collective-permute-start | bytes 2752520 | tf_op jit(solution)/shard_map/ppermute | solution.py:317

commit v12 on v11

--- a/solution.py
+++ b/solution.py
@@ -224,6 +224,22 @@
         place(other, mine)
 
 
+def copy_kernel(block, out):
+    out[...] = block[...]
+
+
+def published(block):
+    return pl.pallas_call(
+        copy_kernel,
+        out_shape=jax.ShapeDtypeStruct(block.shape, block.dtype),
+        in_specs=[VMEM],
+        out_specs=VMEM,
+        compiler_params=pltpu.CompilerParams(vmem_limit_bytes=8 << 20),
+        cost_estimate=pl.CostEstimate(flops=0, bytes_accessed=1 << 17, transcendentals=0),
+        name="publish",
+    )(block)
+
+
 def joined(core, mine, other, shape):
     return pl.pallas_call(
         join_kernel,
@@ -287,7 +303,7 @@
     moved = exchange(half.reshape(rings, -1, lanes), "ring")
     me = lax.axis_index("space")
     back = convolve(True, core, me, after(grad, half), grad_inner, weight, spaces)
-    back = [back[0], rotate(back[1], "space", 1), rotate(back[2], "space", 2), back[3]]
+    back = [back[0], rotate(back[1], "space", 1), back[2], rotate(back[3], "space", 3)]
     quarter, *back = lax.optimization_barrier(
         (small_call(sum_kernel, moved.shape[1:], moved), *back)
     )
@@ -296,7 +312,6 @@
     me = lax.axis_index("chan")
     forward = convolve(False, core, me, after(data, quarter), data_inner, weight, spaces)
     forward = [forward[0], rotate(forward[1], "chan", 1), *forward[2:]]
-    back[3] = rotate(back[3], "space", 3)
     cell_count = sizes[1] * rings * cores * grad.shape[1] * grad.shape[2]
     pair = quarter + moved
     pair, back, forward = lax.optimization_barrier((pair, back, forward))
@@ -305,14 +320,16 @@
     spread = functools.partial(spread_kernel, 1 / math.sqrt(cell_count))
     quarter = small_call(spread, (rings, *pair.shape), pair, moved)
     forward = [*forward[:2], rotate(forward[2], "chan", 2), rotate(forward[3], "chan", 3)]
-    input_grad = sum(back).astype(BF16).reshape(activations.shape)
-    quarter, forward, _ = lax.optimization_barrier((quarter, forward, input_grad))
+    quarter, forward, back = lax.optimization_barrier((quarter, forward, back))
 
     half = exchange(quarter, "ring").reshape(-1, lanes)
     output = lax.ppermute(
         sum(forward).astype(BF16).reshape(activations.shape), AXES, neighbour(sizes, False, True)
     )
-    half = after(half, output)
+    output = published(output)
+    back[2] = rotate(back[2], "space", 2)
+    input_grad = sum(back).astype(BF16).reshape(activations.shape)
+    half, _, _ = lax.optimization_barrier((half, output, input_grad))
 
     other = lax.ppermute(half, "core", swap)
     blocks = (-1, *weight.shape[1:])

time: 146 us -> 146 us (level); the launches traced: 145 us -> 143 us
  starting transfers between devices: 85.7 us -> 84.1 us
    all_to_all x3, waiting for transfers between devices: 13.2 us -> 5.64 us  [exchange(): return lax.all_to_all(block, axis, split_axis=0, concat_axis=0, tiled=True)]
    ppermute x1, waiting for transfers between devices: 5.27 us -> 9.19 us  [shards(): moved = lax.ppermute(pair, ('zhi', 'core'), doubling(1))]
    ppermute x6, waiting for transfers between devices: 8.96 us -> 10.9 us  [rotate(): lax.ppermute(term, axis, [(i, (i + step) % count) for i in range(count)])]
    ppermute x6, starting transfers between devices: 18.9 us -> 17.1 us  [rotate(): lax.ppermute(term, axis, [(i, (i + step) % count) for i in range(count)])]
  transfers between devices with their start and end apart: 19 -> 19, of which waited for: 10 -> 11; matrix products, arithmetic and copies ran while one was open for 1% -> 1% of each run, Pallas kernels for 5% -> 5%
where the time goes in v12:
time: 146 us; the launch traced here: 143 us
  starting transfers between devices  84.1 us (58%)
  waiting for transfers between devices  33.7 us (23%)
  blocking collectives  11.2 us (8%)
  Pallas kernels  10.4 us (7%)
  other arithmetic  1.73 us (1%)
  local copies, waits for them, and re-layouts  1.55 us (1%)
    all_to_all x3, starting transfers between devices, exchange(): return lax.all_to_all(block, axis, split_axis=0, concat_axis=0, tiled=True)  31.4 us
    ppermute x6, starting transfers between devices, rotate(): lax.ppermute(term, axis, [(i, (i + step) % count) for i in range(count)])  17.1 us
    ppermute x1, starting transfers between devices, shards(): moved = lax.ppermute(quarter, ('zhi', 'core'), doubling(0))  13.1 us
    all_gather x1, blocking collectives, shards(): grad = lax.all_gather(grad, 'chan', axis=1, tiled=True)  11.2 us
    ppermute x6, waiting for transfers between devices, rotate(): lax.ppermute(term, axis, [(i, (i + step) % count) for i in range(count)])  10.9 us
    ppermute x1, waiting for transfers between devices, shards(): moved = lax.ppermute(pair, ('zhi', 'core'), doubling(1))  9.19 us
    all_to_all x3, waiting for transfers between devices, exchange(): return lax.all_to_all(block, axis, split_axis=0, concat_axis=0, tiled=True)  5.64 us
    pallas_call x2, Pallas kernels, convolve(): pl.pallas_call(functools.partial(conv_kernel, backward), out_shape=[jax.S...  4.89 us
  transfers between devices with their start and end apart: 19, of which 11 were waited for; matrix products, arithmetic and copies ran while one was open for 1% of the time, Pallas kernels for 5%

profile of v12, /device:TPU:1, one launch (start us, length us, event | category | flops | bytes accessed | tf_op | source)
XLA Modules:
  0.0 143.4 jit_solution(5501710645766247680)
XLA Ops:
  0.6 4.6 %collective-permute-start.2 = (bf16[1,8,32,128]{3,2,1,0:T(8,128)(2,1)}, bf16[1,8,32,128]{3,2,1,0:T(8,128)(2,1)S(1)}, u32[]{:S(2)}, u32[]{:S(2)}) collective-permute-start(bf16[1,8,32,128]{3,2,1,0:T(8,128)(2,1)} %param.3), channel_id=1, source_target_pairs={{4,8},{5,9},{6,10},{7,11},{8,4},{9,5},{10,6},{11,7},{12,16},{13,17... | collective-permute-start | bytes 196616 | tf_op jit(solution)/shard_map/ppermute | solution.py:288
  5.2 1.5 %collective-permute-start = (bf16[1,8,32,128]{3,2,1,0:T(8,128)(2,1)}, bf16[1,8,32,128]{3,2,1,0:T(8,128)(2,1)S(1)}, u32[]{:S(2)}, u32[]{:S(2)}) collective-permute-start(bf16[1,8,32,128]{3,2,1,0:T(8,128)(2,1)} %param.5), channel_id=1, source_target_pairs={{0,0},{1,128},{2,256},{3,384},{4,4},{5,132},{6,260},{7,388},{8,8},... | collective-permute-start | bytes 196616 | tf_op jit(solution)/shard_map/ppermute | solution.py:289
  6.7 1.9 %collective-permute-start.1 = (bf16[1,8,32,128]{3,2,1,0:T(8,128)(2,1)}, bf16[1,8,32,128]{3,2,1,0:T(8,128)(2,1)S(1)}, u32[]{:S(2)}, u32[]{:S(2)}) collective-permute-start(bf16[1,8,32,128]{3,2,1,0:T(8,128)(2,1)} %param.5), channel_id=1, source_target_pairs={{4,8},{5,136},{6,264},{7,392},{8,4},{9,132},{10,260},{11,388},{12,... | collective-permute-start | bytes 196616 | tf_op jit(solution)/shard_map/ppermute | solution.py:289
  8.6 0.0 collective-permute-done.2
  8.7 0.9 pad_maximum_fusion.1
  9.5 0.0 collective-permute-done
  9.5 3.0 %collective-permute-done.1 = bf16[1,8,32,128]{3,2,1,0:T(8,128)(2,1)S(1)} collective-permute-done((bf16[1,8,32,128]{3,2,1,0:T(8,128)(2,1)}, bf16[1,8,32,128]{3,2,1,0:T(8,128)(2,1)S(1)}, u32[]{:S(2)}, u32[]{:S(2)}) %collective-permute-start.1) | collective-permute-done | bytes 65568 | tf_op jit(solution)/shard_map/ppermute | solution.py:289
  12.5 0.9 broadcast_in_dim.2
  13.4 12.4 %all-to-all-start = ((bf16[4,2,8,32,128]{4,3,2,1,0:T(8,128)(2,1)}), bf16[4,2,8,32,128]{4,3,2,1,0:T(8,128)(2,1)S(1)}, u32[]{:S(2)}, u32[]{:S(2)}) async-start(bf16[4,2,8,32,128]{4,3,2,1,0:T(8,128)(2,1)} %broadcast_in_dim.2), calls=%async_computation | async-start | bytes 1048576 | tf_op jit(solution)/shard_map/all_to_all | solution.py:257
  25.8 11.2 %all_gather.3.pair = bf16[2,32,32,128]{3,2,1,0:T(8,128)(2,1)S(1)} all-gather(bf16[2,8,32,128]{3,2,1,0:T(8,128)(2,1)S(1)} %pad_maximum_fusion), channel_id=1, replica_groups=mesh['chan'=4,'zhi'=4,'ring'=4,'core'=2,'space'=4] {'chan'}, dimensions={1}, use_global_device_ids=true | all-gather | bytes 655360 | tf_op jit(solution)/shard_map/all_gather | solution.py:294
  37.0 1.9 %collective-permute-start.3 = (bf16[32,32,128]{2,1,0:T(8,128)(2,1)S(1)}, bf16[32,32,128]{2,1,0:T(8,128)(2,1)S(1)}, u32[]{:S(2)}, u32[]{:S(2)}) collective-permute-start(bf16[32,32,128]{2,1,0:T(8,128)(2,1)S(1)} %slice_bitcast_fusion), channel_id=1, source_target_pairs={{0,4},{4,0},{1,5},{5,1},{2,6},{6,2},{3,7},{7,3},{8,12},{12,8},{9,1... | collective-permute-start | bytes 786440 | tf_op jit(solution)/shard_map/ppermute | solution.py:295
  39.0 1.5 %collective-permute-done.3.inner = bf16[32,32,128]{2,1,0:T(8,128)(2,1)S(1)} collective-permute-done((bf16[32,32,128]{2,1,0:T(8,128)(2,1)S(1)}, bf16[32,32,128]{2,1,0:T(8,128)(2,1)S(1)}, u32[]{:S(2)}, u32[]{:S(2)}) %collective-permute-start.3) | collective-permute-done | bytes 262176 | tf_op jit(solution)/shard_map/ppermute | solution.py:295
  40.5 0.0 all-to-all-done.data.pair
  40.5 1.6 %filter_grad.1 = (f32[1792,128]{1,0:T(8,128)S(1)}, f32[1792,128]{1,0:T(8,128)S(1)}, bf16[32,32,128]{2,1,0:T(8,128)(2,1)S(1)}) custom-call(s32[1]{0:T(128)} %bitcast.core, bf16[4,2,8,32,128]{4,3,2,1,0:T(8,128)(2,1)S(1)} %all-to-all-done.data.pair, bf16[2,32,32,128]{3,2,1,0:T(8,128)(2,1)S(1)} %all_gather.3.pair, ...), custom_call_target="tpu_custom_call" | custom-call | flops 905969664 | bytes 3145728 | tf_op jit(solution)/shard_map/filter_grad/pallas_call | solution.py:160
  42.1 2.0 %collective-permute-start.4 = (f32[1792,128]{1,0:T(8,128)S(1)}, f32[1792,128]{1,0:T(8,128)S(1)}, u32[]{:S(2)}, u32[]{:S(2)}) collective-permute-start(f32[1792,128]{1,0:T(8,128)S(1)} %get-tuple-element.48), channel_id=1, source_target_pairs={{0,4},{4,0},{1,5},{5,1},{2,6},{6,2},{3,7},{7,3},{8,12},{12,8},{9,1... | collective-permute-start | bytes 2752520 | tf_op jit(solution)/shard_map/ppermute | solution.py:298
  44.1 2.3 %collective-permute-start.5 = (bf16[32,32,128]{2,1,0:T(8,128)(2,1)S(1)}, bf16[32,32,128]{2,1,0:T(8,128)(2,1)S(1)}, u32[]{:S(2)}, u32[]{:S(2)}) collective-permute-start(bf16[32,32,128]{2,1,0:T(8,128)(2,1)S(1)} %get-tuple-element.50), channel_id=1, source_target_pairs={{0,4},{4,0},{1,5},{5,1},{2,6},{6,2},{3,7},{7,3},{8,12},{12,8},{9,1... | collective-permute-start | bytes 786440 | tf_op jit(solution)/shard_map/ppermute | solution.py:299
  46.4 0.0 collective-permute-done.4.right
  46.4 0.0 copy-start
  46.4 1.0 shard_map.58
  47.4 0.1 collective-permute-done.5.inner
  47.5 15.3 %all-to-all-start.1 = ((f32[4,448,128]{2,1,0:T(8,128)}), f32[4,448,128]{2,1,0:T(8,128)S(1)}, u32[]{:S(2)}, u32[]{:S(2)}) async-start(f32[4,448,128]{2,1,0:T(8,128)} %bitcast.2), calls=%async_computation.1 | async-start | bytes 1835008 | tf_op jit(solution)/shard_map/all_to_all | solution.py:257
  62.8 0.1 pad_add_fusion.place
  62.9 0.0 copy-done
  62.9 2.8 %input_grad.1 = (f32[256,128]{1,0:T(8,128)S(1)}, f32[256,128]{1,0:T(8,128)}, f32[256,128]{1,0:T(8,128)S(1)}, f32[256,128]{1,0:T(8,128)}) custom-call(s32[2]{0:T(128)S(1)} %pad_add_fusion.place, bf16[2,32,32,128]{3,2,1,0:T(8,128)(2,1)S(1)} %all_gather.3.pair, bf16[32,32,128]{2,1,0:T(8,128)(2,1)S(1)} %collective-permute-done.3.inner, ...), custom_call_target="tpu_custom_call" | custom-call | flops 905969664 | bytes 3145728 | tf_op jit(solution)/shard_map/input_grad/pallas_call | solution.py:106
  65.7 0.0 copy-start.1
  65.7 0.6 copy-done.1
  66.3 3.3 %collective-permute-start.6 = (f32[256,128]{1,0:T(8,128)}, f32[256,128]{1,0:T(8,128)S(1)}, u32[]{:S(2)}, u32[]{:S(2)}) collective-permute-start(f32[256,128]{1,0:T(8,128)} %get-tuple-element.54), channel_id=1, source_target_pairs={{0,1},{1,2},{2,3},{3,0},{4,5},{5,6},{6,7},{7,4},{8,9},{9,10},{10,1... | collective-permute-start | bytes 393224 | tf_op jit(solution)/shard_map/ppermute | solution.py:267
  69.6 3.8 %collective-permute-start.7 = (f32[256,128]{1,0:T(8,128)}, f32[256,128]{1,0:T(8,128)S(1)}, u32[]{:S(2)}, u32[]{:S(2)}) collective-permute-start(f32[256,128]{1,0:T(8,128)} %get-tuple-element.56), channel_id=1, source_target_pairs={{0,3},{1,0},{2,1},{3,2},{4,7},{5,4},{6,5},{7,6},{8,11},{9,8},{10,9... | collective-permute-start | bytes 393224 | tf_op jit(solution)/shard_map/ppermute | solution.py:267
  73.4 2.5 %all-to-all-done.1.parts = f32[4,448,128]{2,1,0:T(8,128)S(1)} async-done(((f32[4,448,128]{2,1,0:T(8,128)}), f32[4,448,128]{2,1,0:T(8,128)S(1)}, u32[]{:S(2)}, u32[]{:S(2)}) %all-to-all-start.1) | async-done | bytes 917536 | tf_op jit(solution)/shard_map/all_to_all | solution.py:257
  76.0 0.0 collective-permute-done.6
  76.0 2.4 %collective-permute-done.7 = f32[256,128]{1,0:T(8,128)S(1)} collective-permute-done((f32[256,128]{1,0:T(8,128)}, f32[256,128]{1,0:T(8,128)S(1)}, u32[]{:S(2)}, u32[]{:S(2)}) %collective-permute-start.7) | collective-permute-done | bytes 131104 | tf_op jit(solution)/shard_map/ppermute | solution.py:267
  78.4 13.1 %collective-permute-start.8 = (f32[448,128]{1,0:T(8,128)S(1)}, f32[448,128]{1,0:T(8,128)S(1)}, u32[]{:S(2)}, u32[]{:S(2)}) collective-permute-start(f32[448,128]{1,0:T(8,128)S(1)} %shard_map.59), channel_id=1, source_target_pairs={{0,32},{4,100},{32,0},{36,68},{64,96},{68,36},{96,64},{100,4},{1,3... | collective-permute-start | bytes 688136 | tf_op jit(solution)/shard_map/ppermute | solution.py:311
  91.5 0.1 pad_add_fusion.1.place
  91.6 2.1 %forward.1 = (f32[256,128]{1,0:T(8,128)S(1)}, f32[256,128]{1,0:T(8,128)S(1)}, f32[256,128]{1,0:T(8,128)S(1)}, f32[256,128]{1,0:T(8,128)S(1)}) custom-call(s32[2]{0:T(128)S(1)} %pad_add_fusion.1.place, bf16[4,2,8,32,128]{4,3,2,1,0:T(8,128)(2,1)S(1)} %all-to-all-done.data.pair, bf16[32,32,128]{2,1,0:T(8,128)(2,1)S(1)} %collective-permute-done.5.inner, ...), custom_call_target="tpu_custom_call" | custom-call | flops 905969664 | bytes 3145728 | tf_op jit(solution)/shard_map/forward/pallas_call | solution.py:106
  93.7 2.0 %collective-permute-start.9 = (f32[256,128]{1,0:T(8,128)S(1)}, f32[256,128]{1,0:T(8,128)S(1)}, u32[]{:S(2)}, u32[]{:S(2)}) collective-permute-start(f32[256,128]{1,0:T(8,128)S(1)} %get-tuple-element.65), channel_id=1, source_target_pairs={{0,128},{128,256},{256,384},{384,0},{1,129},{129,257},{257,385},{3... | collective-permute-start | bytes 393224 | tf_op jit(solution)/shard_map/ppermute | solution.py:267
  95.7 1.3 collective-permute-done.8
  97.0 0.0 copy-start.2
  97.0 3.6 %collective-permute-done.9 = f32[256,128]{1,0:T(8,128)S(1)} collective-permute-done((f32[256,128]{1,0:T(8,128)S(1)}, f32[256,128]{1,0:T(8,128)S(1)}, u32[]{:S(2)}, u32[]{:S(2)}) %collective-permute-start.9) | collective-permute-done | bytes 131104 | tf_op jit(solution)/shard_map/ppermute | solution.py:267
  100.6 3.0 %collective-permute-start.10 = (f32[448,128]{1,0:T(8,128)S(1)}, f32[448,128]{1,0:T(8,128)S(1)}, u32[]{:S(2)}, u32[]{:S(2)}) collective-permute-start(f32[448,128]{1,0:T(8,128)S(1)} %add.21.left), channel_id=1, source_target_pairs={{0,96},{4,36},{32,64},{36,4},{64,32},{68,100},{96,0},{100,68},{1,9... | collective-permute-start | bytes 688136 | tf_op jit(solution)/shard_map/ppermute | solution.py:319
  103.6 3.1 %collective-permute-start.11 = (f32[256,128]{1,0:T(8,128)S(1)}, f32[256,128]{1,0:T(8,128)S(1)}, u32[]{:S(2)}, u32[]{:S(2)}) collective-permute-start(f32[256,128]{1,0:T(8,128)S(1)} %get-tuple-element.71), channel_id=1, source_target_pairs={{0,256},{128,384},{256,0},{384,128},{1,257},{129,385},{257,1},{385... | collective-permute-start | bytes 393224 | tf_op jit(solution)/shard_map/ppermute | solution.py:267
  106.7 3.1 %collective-permute-start.12 = (f32[256,128]{1,0:T(8,128)S(1)}, f32[256,128]{1,0:T(8,128)S(1)}, u32[]{:S(2)}, u32[]{:S(2)}) collective-permute-start(f32[256,128]{1,0:T(8,128)S(1)} %get-tuple-element.72), channel_id=1, source_target_pairs={{0,384},{128,0},{256,128},{384,256},{1,385},{129,1},{257,129},{385... | collective-permute-start | bytes 393224 | tf_op jit(solution)/shard_map/ppermute | solution.py:267
  109.7 9.2 %collective-permute-done.10.right = f32[448,128]{1,0:T(8,128)S(1)} collective-permute-done((f32[448,128]{1,0:T(8,128)S(1)}, f32[448,128]{1,0:T(8,128)S(1)}, u32[]{:S(2)}, u32[]{:S(2)}) %collective-permute-start.10) | collective-permute-done | bytes 229408 | tf_op jit(solution)/shard_map/ppermute | solution.py:319
  118.9 1.0 shard_map.60
  119.9 0.0 collective-permute-done.11
  119.9 0.0 collective-permute-done.12
  119.9 3.7 %all-to-all-start.2 = ((f32[4,448,128]{2,1,0:T(8,128)}), f32[4,448,128]{2,1,0:T(8,128)S(1)}, u32[]{:S(2)}, u32[]{:S(2)}) async-start(f32[4,448,128]{2,1,0:T(8,128)} %shard_map.60), calls=%async_computation.2 | async-start | bytes 1835008 | tf_op jit(solution)/shard_map/all_to_all | solution.py:257
  123.6 0.0 copy-done.2
  123.6 1.9 %collective-permute-start.14 = (f32[256,128]{1,0:T(8,128)S(1)}, f32[256,128]{1,0:T(8,128)S(1)}, u32[]{:S(2)}, u32[]{:S(2)}) collective-permute-start(f32[256,128]{1,0:T(8,128)S(1)} %copy-done.2), channel_id=1, source_target_pairs={{0,2},{1,3},{2,0},{3,1},{4,6},{5,7},{6,4},{7,5},{8,10},{9,11},{10,... | collective-permute-start | bytes 393224 | tf_op jit(solution)/shard_map/ppermute | solution.py:267
  125.6 0.7 collective-permute-start.13
  126.2 0.0 collective-permute-done.13.block
  126.2 0.6 publish.1
  126.9 4.8 %collective-permute-done.14 = f32[256,128]{1,0:T(8,128)S(1)} collective-permute-done((f32[256,128]{1,0:T(8,128)S(1)}, f32[256,128]{1,0:T(8,128)S(1)}, u32[]{:S(2)}, u32[]{:S(2)}) %collective-permute-start.14) | collective-permute-done | bytes 131104 | tf_op jit(solution)/shard_map/ppermute | solution.py:267
  131.7 0.7 add_convert_fusion
  132.3 3.1 %all-to-all-done.2 = f32[4,448,128]{2,1,0:T(8,128)S(1)} async-done(((f32[4,448,128]{2,1,0:T(8,128)}), f32[4,448,128]{2,1,0:T(8,128)S(1)}, u32[]{:S(2)}, u32[]{:S(2)}) %all-to-all-start.2) | async-done | bytes 917536 | tf_op jit(solution)/shard_map/all_to_all | solution.py:257
  135.5 4.7 %collective-permute-start.15 = (f32[1792,128]{1,0:T(8,128)S(1)}, f32[1792,128]{1,0:T(8,128)S(1)}, u32[]{:S(2)}, u32[]{:S(2)}) collective-permute-start(f32[1792,128]{1,0:T(8,128)S(1)} %bitcast.11), channel_id=1, source_target_pairs={{0,4},{4,0},{1,5},{5,1},{2,6},{6,2},{3,7},{7,3},{8,12},{12,8},{9,1... | collective-permute-start | bytes 2752520 | tf_op jit(solution)/shard_map/ppermute | solution.py:334
  140.1 2.1 %collective-permute-done.15 = f32[1792,128]{1,0:T(8,128)S(1)} collective-permute-done((f32[1792,128]{1,0:T(8,128)S(1)}, f32[1792,128]{1,0:T(8,128)S(1)}, u32[]{:S(2)}, u32[]{:S(2)}) %collective-permute-start.15) | collective-permute-done | bytes 917536 | tf_op jit(solution)/shard_map/ppermute | solution.py:334
  142.2 1.2 join.1
  (5 shorter events, 0.1 us)
Async XLA Ops:
  0.6 8.0 %collective-permute-start.2 = (bf16[1,8,32,128]{3,2,1,0:T(8,128)(2,1)}, bf16[1,8,32,128]{3,2,1,0:T(8,128)(2,1)S(1)}, u32[]{:S(2)}, u32[]{:S(2)}) collective-permute-start(bf16[1,8,32,128]{3,2,1,0:T(8,128)(2,1)} %param.3), channel_id=1, source_target_pairs={{4,8},{5,9},{6,10},{7,11},{8,4},{9,5},{10,6},{11,7},{12,16},{13,17... | collective-permute-start | bytes 196616 | tf_op jit(solution)/shard_map/ppermute | solution.py:288
  5.2 4.3 %collective-permute-start = (bf16[1,8,32,128]{3,2,1,0:T(8,128)(2,1)}, bf16[1,8,32,128]{3,2,1,0:T(8,128)(2,1)S(1)}, u32[]{:S(2)}, u32[]{:S(2)}) collective-permute-start(bf16[1,8,32,128]{3,2,1,0:T(8,128)(2,1)} %param.5), channel_id=1, source_target_pairs={{0,0},{1,128},{2,256},{3,384},{4,4},{5,132},{6,260},{7,388},{8,8},... | collective-permute-start | bytes 196616 | tf_op jit(solution)/shard_map/ppermute | solution.py:289
  6.7 5.8 %collective-permute-start.1 = (bf16[1,8,32,128]{3,2,1,0:T(8,128)(2,1)}, bf16[1,8,32,128]{3,2,1,0:T(8,128)(2,1)S(1)}, u32[]{:S(2)}, u32[]{:S(2)}) collective-permute-start(bf16[1,8,32,128]{3,2,1,0:T(8,128)(2,1)} %param.5), channel_id=1, source_target_pairs={{4,8},{5,136},{6,264},{7,392},{8,4},{9,132},{10,260},{11,388},{12,... | collective-permute-start | bytes 196616 | tf_op jit(solution)/shard_map/ppermute | solution.py:289
  13.4 27.1 %all-to-all-start = ((bf16[4,2,8,32,128]{4,3,2,1,0:T(8,128)(2,1)}), bf16[4,2,8,32,128]{4,3,2,1,0:T(8,128)(2,1)S(1)}, u32[]{:S(2)}, u32[]{:S(2)}) async-start(bf16[4,2,8,32,128]{4,3,2,1,0:T(8,128)(2,1)} %broadcast_in_dim.2), calls=%async_computation | async-start | bytes 1048576 | tf_op jit(solution)/shard_map/all_to_all | solution.py:257
  37.0 3.4 %collective-permute-start.3 = (bf16[32,32,128]{2,1,0:T(8,128)(2,1)S(1)}, bf16[32,32,128]{2,1,0:T(8,128)(2,1)S(1)}, u32[]{:S(2)}, u32[]{:S(2)}) collective-permute-start(bf16[32,32,128]{2,1,0:T(8,128)(2,1)S(1)} %slice_bitcast_fusion), channel_id=1, source_target_pairs={{0,4},{4,0},{1,5},{5,1},{2,6},{6,2},{3,7},{7,3},{8,12},{12,8},{9,1... | collective-permute-start | bytes 786440 | tf_op jit(solution)/shard_map/ppermute | solution.py:295
  42.1 4.4 %collective-permute-start.4 = (f32[1792,128]{1,0:T(8,128)S(1)}, f32[1792,128]{1,0:T(8,128)S(1)}, u32[]{:S(2)}, u32[]{:S(2)}) collective-permute-start(f32[1792,128]{1,0:T(8,128)S(1)} %get-tuple-element.48), channel_id=1, source_target_pairs={{0,4},{4,0},{1,5},{5,1},{2,6},{6,2},{3,7},{7,3},{8,12},{12,8},{9,1... | collective-permute-start | bytes 2752520 | tf_op jit(solution)/shard_map/ppermute | solution.py:298
  44.1 3.4 %collective-permute-start.5 = (bf16[32,32,128]{2,1,0:T(8,128)(2,1)S(1)}, bf16[32,32,128]{2,1,0:T(8,128)(2,1)S(1)}, u32[]{:S(2)}, u32[]{:S(2)}) collective-permute-start(bf16[32,32,128]{2,1,0:T(8,128)(2,1)S(1)} %get-tuple-element.50), channel_id=1, source_target_pairs={{0,4},{4,0},{1,5},{5,1},{2,6},{6,2},{3,7},{7,3},{8,12},{12,8},{9,1... | collective-permute-start | bytes 786440 | tf_op jit(solution)/shard_map/ppermute | solution.py:299
  46.4 16.5 %copy-start = (bf16[27,128,128]{2,1,0:T(8,128)(2,1)S(1)}, bf16[27,128,128]{2,1,0:T(8,128)(2,1)}, u32[]{:S(2)}) copy-start(bf16[27,128,128]{2,1,0:T(8,128)(2,1)} %weight.3) | copy-start | bytes 2654212
  47.5 28.4 %all-to-all-start.1 = ((f32[4,448,128]{2,1,0:T(8,128)}), f32[4,448,128]{2,1,0:T(8,128)S(1)}, u32[]{:S(2)}, u32[]{:S(2)}) async-start(f32[4,448,128]{2,1,0:T(8,128)} %bitcast.2), calls=%async_computation.1 | async-start | bytes 1835008 | tf_op jit(solution)/shard_map/all_to_all | solution.py:257
  65.7 0.6 copy-start.1
  66.3 9.7 %collective-permute-start.6 = (f32[256,128]{1,0:T(8,128)}, f32[256,128]{1,0:T(8,128)S(1)}, u32[]{:S(2)}, u32[]{:S(2)}) collective-permute-start(f32[256,128]{1,0:T(8,128)} %get-tuple-element.54), channel_id=1, source_target_pairs={{0,1},{1,2},{2,3},{3,0},{4,5},{5,6},{6,7},{7,4},{8,9},{9,10},{10,1... | collective-permute-start | bytes 393224 | tf_op jit(solution)/shard_map/ppermute | solution.py:267
  69.6 8.8 %collective-permute-start.7 = (f32[256,128]{1,0:T(8,128)}, f32[256,128]{1,0:T(8,128)S(1)}, u32[]{:S(2)}, u32[]{:S(2)}) collective-permute-start(f32[256,128]{1,0:T(8,128)} %get-tuple-element.56), channel_id=1, source_target_pairs={{0,3},{1,0},{2,1},{3,2},{4,7},{5,4},{6,5},{7,6},{8,11},{9,8},{10,9... | collective-permute-start | bytes 393224 | tf_op jit(solution)/shard_map/ppermute | solution.py:267
  78.4 18.5 %collective-permute-start.8 = (f32[448,128]{1,0:T(8,128)S(1)}, f32[448,128]{1,0:T(8,128)S(1)}, u32[]{:S(2)}, u32[]{:S(2)}) collective-permute-start(f32[448,128]{1,0:T(8,128)S(1)} %shard_map.59), channel_id=1, source_target_pairs={{0,32},{4,100},{32,0},{36,68},{64,96},{68,36},{96,64},{100,4},{1,3... | collective-permute-start | bytes 688136 | tf_op jit(solution)/shard_map/ppermute | solution.py:311
  93.7 6.9 %collective-permute-start.9 = (f32[256,128]{1,0:T(8,128)S(1)}, f32[256,128]{1,0:T(8,128)S(1)}, u32[]{:S(2)}, u32[]{:S(2)}) collective-permute-start(f32[256,128]{1,0:T(8,128)S(1)} %get-tuple-element.65), channel_id=1, source_target_pairs={{0,128},{128,256},{256,384},{384,0},{1,129},{129,257},{257,385},{3... | collective-permute-start | bytes 393224 | tf_op jit(solution)/shard_map/ppermute | solution.py:267
  97.0 26.6 %copy-start.2 = (f32[256,128]{1,0:T(8,128)S(1)}, f32[256,128]{1,0:T(8,128)}, u32[]{:S(2)}) copy-start(f32[256,128]{1,0:T(8,128)} %copy-done.1) | copy-start | bytes 393220
  100.6 18.3 %collective-permute-start.10 = (f32[448,128]{1,0:T(8,128)S(1)}, f32[448,128]{1,0:T(8,128)S(1)}, u32[]{:S(2)}, u32[]{:S(2)}) collective-permute-start(f32[448,128]{1,0:T(8,128)S(1)} %add.21.left), channel_id=1, source_target_pairs={{0,96},{4,36},{32,64},{36,4},{64,32},{68,100},{96,0},{100,68},{1,9... | collective-permute-start | bytes 688136 | tf_op jit(solution)/shard_map/ppermute | solution.py:319
  103.6 16.4 %collective-permute-start.11 = (f32[256,128]{1,0:T(8,128)S(1)}, f32[256,128]{1,0:T(8,128)S(1)}, u32[]{:S(2)}, u32[]{:S(2)}) collective-permute-start(f32[256,128]{1,0:T(8,128)S(1)} %get-tuple-element.71), channel_id=1, source_target_pairs={{0,256},{128,384},{256,0},{384,128},{1,257},{129,385},{257,1},{385... | collective-permute-start | bytes 393224 | tf_op jit(solution)/shard_map/ppermute | solution.py:267
  106.7 13.3 %collective-permute-start.12 = (f32[256,128]{1,0:T(8,128)S(1)}, f32[256,128]{1,0:T(8,128)S(1)}, u32[]{:S(2)}, u32[]{:S(2)}) collective-permute-start(f32[256,128]{1,0:T(8,128)S(1)} %get-tuple-element.72), channel_id=1, source_target_pairs={{0,384},{128,0},{256,128},{384,256},{1,385},{129,1},{257,129},{385... | collective-permute-start | bytes 393224 | tf_op jit(solution)/shard_map/ppermute | solution.py:267
  119.9 15.5 %all-to-all-start.2 = ((f32[4,448,128]{2,1,0:T(8,128)}), f32[4,448,128]{2,1,0:T(8,128)S(1)}, u32[]{:S(2)}, u32[]{:S(2)}) async-start(f32[4,448,128]{2,1,0:T(8,128)} %shard_map.60), calls=%async_computation.2 | async-start | bytes 1835008 | tf_op jit(solution)/shard_map/all_to_all | solution.py:257
  123.6 8.1 %collective-permute-start.14 = (f32[256,128]{1,0:T(8,128)S(1)}, f32[256,128]{1,0:T(8,128)S(1)}, u32[]{:S(2)}, u32[]{:S(2)}) collective-permute-start(f32[256,128]{1,0:T(8,128)S(1)} %copy-done.2), channel_id=1, source_target_pairs={{0,2},{1,3},{2,0},{3,1},{4,6},{5,7},{6,4},{7,5},{8,10},{9,11},{10,... | collective-permute-start | bytes 393224 | tf_op jit(solution)/shard_map/ppermute | solution.py:267
  125.6 0.7 collective-permute-start.13
  135.5 6.8 %collective-permute-start.15 = (f32[1792,128]{1,0:T(8,128)S(1)}, f32[1792,128]{1,0:T(8,128)S(1)}, u32[]{:S(2)}, u32[]{:S(2)}) collective-permute-start(f32[1792,128]{1,0:T(8,128)S(1)} %bitcast.11), channel_id=1, source_target_pairs={{0,4},{4,0},{1,5},{5,1},{2,6},{6,2},{3,7},{7,3},{8,12},{12,8},{9,1... | collective-permute-start | bytes 2752520 | tf_op jit(solution)/shard_map/ppermute | solution.py:334

commit v13 on v12

--- a/solution.py
+++ b/solution.py
@@ -257,11 +257,6 @@
     return lax.all_to_all(block, axis, split_axis=0, concat_axis=0, tiled=True)
 
 
-def gather(block, axis):
-    count = lax.axis_size(axis)
-    return exchange(jnp.broadcast_to(block[None], (count, *block.shape)), axis)
-
-
 def rotate(term, axis, step):
     count = lax.axis_size(axis)
     return lax.ppermute(term, axis, [(i, (i + step) % count) for i in range(count)])
@@ -280,7 +275,7 @@
 
 
 def shards(sizes, activations, weight, output_grad):
-    _, zhis, rings, cores, spaces = sizes
+    chans, _, rings, cores, spaces = sizes
     planes, height, lanes = activations.shape[1:]
     core = lax.axis_index("core")
     swap = [(0, 1), (1, 0)]
@@ -289,8 +284,9 @@
     grads = [lax.ppermute(output_grad, AXES, neighbour(sizes, far, True)) for far in (False, True)]
     grad = jnp.concatenate(grads, axis=0)
     data = jnp.concatenate([activations, outer], axis=0)
+    data = jnp.broadcast_to(data[None], (spaces, *data.shape))
     grad, data = lax.optimization_barrier((grad, data))
-    data = gather(data, "space")
+    data = exchange(data, "space")
     grad = lax.all_gather(grad, "chan", axis=1, tiled=True)
     grad_inner = lax.ppermute(grad[0], "core", swap)
 
@@ -311,7 +307,7 @@
     moved = lax.ppermute(quarter, ("zhi", "core"), doubling(0))
     me = lax.axis_index("chan")
     forward = convolve(False, core, me, after(data, quarter), data_inner, weight, spaces)
-    forward = [forward[0], rotate(forward[1], "chan", 1), *forward[2:]]
+    forward = [forward[0], *(rotate(forward[step], "chan", step) for step in range(1, chans))]
     cell_count = sizes[1] * rings * cores * grad.shape[1] * grad.shape[2]
     pair = quarter + moved
     pair, back, forward = lax.optimization_barrier((pair, back, forward))
@@ -319,17 +315,14 @@
     moved = lax.ppermute(pair, ("zhi", "core"), doubling(1))
     spread = functools.partial(spread_kernel, 1 / math.sqrt(cell_count))
     quarter = small_call(spread, (rings, *pair.shape), pair, moved)
-    forward = [*forward[:2], rotate(forward[2], "chan", 2), rotate(forward[3], "chan", 3)]
-    quarter, forward, back = lax.optimization_barrier((quarter, forward, back))
+    forward = sum(forward).astype(BF16).reshape(activations.shape)
+    output = published(lax.ppermute(forward, AXES, neighbour(sizes, False, True)))
+    quarter, output, back = lax.optimization_barrier((quarter, output, back))
 
     half = exchange(quarter, "ring").reshape(-1, lanes)
-    output = lax.ppermute(
-        sum(forward).astype(BF16).reshape(activations.shape), AXES, neighbour(sizes, False, True)
-    )
-    output = published(output)
     back[2] = rotate(back[2], "space", 2)
     input_grad = sum(back).astype(BF16).reshape(activations.shape)
-    half, _, _ = lax.optimization_barrier((half, output, input_grad))
+    half = after(half, input_grad)
 
     other = lax.ppermute(half, "core", swap)
     blocks = (-1, *weight.shape[1:])

time: 146 us -> 150 us (1.027)
  the two profiles are of different devices: /device:TPU:1 before, /device:TPU:33 now
where the time goes in v13:
time: 150 us
  starting transfers between devices  80 us (53%)
  waiting for transfers between devices  43.7 us (29%)
  blocking collectives  11.3 us (8%)
  Pallas kernels  10.4 us (7%)
  other arithmetic  1.73 us (1%)
  local copies, waits for them, and re-layouts  1.55 us (1%)
    all_to_all x3, starting transfers between devices, exchange(): return lax.all_to_all(block, axis, split_axis=0, concat_axis=0, tiled=True)  28.5 us
    ppermute x6, starting transfers between devices, rotate(): lax.ppermute(term, axis, [(i, (i + step) % count) for i in range(count)])  15.6 us
    ppermute x1, starting transfers between devices, shards(): moved = lax.ppermute(quarter, ('zhi', 'core'), doubling(0))  13.5 us
    all_gather x1, blocking collectives, shards(): grad = lax.all_gather(grad, 'chan', axis=1, tiled=True)  11.3 us
    ppermute x6, waiting for transfers between devices, rotate(): lax.ppermute(term, axis, [(i, (i + step) % count) for i in range(count)])  10.9 us
    ppermute x1, waiting for transfers between devices, shards(): moved = lax.ppermute(pair, ('zhi', 'core'), doubling(1))  10.3 us
    all_to_all x3, waiting for transfers between devices, exchange(): return lax.all_to_all(block, axis, split_axis=0, concat_axis=0, tiled=True)  9.31 us
    ppermute x2, starting transfers between devices, shards(): lax.ppermute(output_grad, AXES, neighbour(sizes, far, True))  6.19 us
  transfers between devices with their start and end apart: 19, of which 12 were waited for; matrix products, arithmetic and copies ran while one was open for 1% of the time, Pallas kernels for 4%

profile of v13, /device:TPU:33, one launch (start us, length us, event | category | flops | bytes accessed | tf_op | source)
XLA Modules:
  0.0 149.6 jit_solution(12422690920920775559)
XLA Ops:
  0.6 3.8 %collective-permute-start.2 = (bf16[1,8,32,128]{3,2,1,0:T(8,128)(2,1)}, bf16[1,8,32,128]{3,2,1,0:T(8,128)(2,1)S(1)}, u32[]{:S(2)}, u32[]{:S(2)}) collective-permute-start(bf16[1,8,32,128]{3,2,1,0:T(8,128)(2,1)} %param.3), channel_id=1, source_target_pairs={{4,8},{5,9},{6,10},{7,11},{8,4},{9,5},{10,6},{11,7},{12,16},{13,17... | collective-permute-start | bytes 196616 | tf_op jit(solution)/shard_map/ppermute | solution.py:283
  4.4 2.7 %collective-permute-start = (bf16[1,8,32,128]{3,2,1,0:T(8,128)(2,1)}, bf16[1,8,32,128]{3,2,1,0:T(8,128)(2,1)S(1)}, u32[]{:S(2)}, u32[]{:S(2)}) collective-permute-start(bf16[1,8,32,128]{3,2,1,0:T(8,128)(2,1)} %param.5), channel_id=1, source_target_pairs={{0,0},{1,128},{2,256},{3,384},{4,4},{5,132},{6,260},{7,388},{8,8},... | collective-permute-start | bytes 196616 | tf_op jit(solution)/shard_map/ppermute | solution.py:284
  7.1 3.5 %collective-permute-start.1 = (bf16[1,8,32,128]{3,2,1,0:T(8,128)(2,1)}, bf16[1,8,32,128]{3,2,1,0:T(8,128)(2,1)S(1)}, u32[]{:S(2)}, u32[]{:S(2)}) collective-permute-start(bf16[1,8,32,128]{3,2,1,0:T(8,128)(2,1)} %param.5), channel_id=1, source_target_pairs={{4,8},{5,136},{6,264},{7,392},{8,4},{9,132},{10,260},{11,388},{12,... | collective-permute-start | bytes 196616 | tf_op jit(solution)/shard_map/ppermute | solution.py:284
  10.6 0.0 collective-permute-done.2
  10.6 0.9 pad_maximum_fusion.1
  11.5 0.0 collective-permute-done
  11.5 3.9 %collective-permute-done.1 = bf16[1,8,32,128]{3,2,1,0:T(8,128)(2,1)S(1)} collective-permute-done((bf16[1,8,32,128]{3,2,1,0:T(8,128)(2,1)}, bf16[1,8,32,128]{3,2,1,0:T(8,128)(2,1)S(1)}, u32[]{:S(2)}, u32[]{:S(2)}) %collective-permute-start.1) | collective-permute-done | bytes 65568 | tf_op jit(solution)/shard_map/ppermute | solution.py:284
  15.4 0.9 broadcast_in_dim.2
  16.3 8.5 %all-to-all-start = ((bf16[4,2,8,32,128]{4,3,2,1,0:T(8,128)(2,1)}), bf16[4,2,8,32,128]{4,3,2,1,0:T(8,128)(2,1)S(1)}, u32[]{:S(2)}, u32[]{:S(2)}) async-start(bf16[4,2,8,32,128]{4,3,2,1,0:T(8,128)(2,1)} %broadcast_in_dim.2), calls=%async_computation | async-start | bytes 1048576 | tf_op jit(solution)/shard_map/all_to_all | solution.py:257
  24.8 11.3 %all_gather.3.pair = bf16[2,32,32,128]{3,2,1,0:T(8,128)(2,1)S(1)} all-gather(bf16[2,8,32,128]{3,2,1,0:T(8,128)(2,1)S(1)} %pad_maximum_fusion), channel_id=1, replica_groups=mesh['chan'=4,'zhi'=4,'ring'=4,'core'=2,'space'=4] {'chan'}, dimensions={1}, use_global_device_ids=true | all-gather | bytes 655360 | tf_op jit(solution)/shard_map/all_gather | solution.py:290
  36.2 1.9 %collective-permute-start.3 = (bf16[32,32,128]{2,1,0:T(8,128)(2,1)S(1)}, bf16[32,32,128]{2,1,0:T(8,128)(2,1)S(1)}, u32[]{:S(2)}, u32[]{:S(2)}) collective-permute-start(bf16[32,32,128]{2,1,0:T(8,128)(2,1)S(1)} %slice_bitcast_fusion), channel_id=1, source_target_pairs={{0,4},{4,0},{1,5},{5,1},{2,6},{6,2},{3,7},{7,3},{8,12},{12,8},{9,1... | collective-permute-start | bytes 786440 | tf_op jit(solution)/shard_map/ppermute | solution.py:291
  38.1 1.5 collective-permute-done.3.inner
  39.6 0.0 all-to-all-done.data.pair
  39.6 1.6 %filter_grad.1 = (f32[1792,128]{1,0:T(8,128)S(1)}, f32[1792,128]{1,0:T(8,128)S(1)}, bf16[32,32,128]{2,1,0:T(8,128)(2,1)S(1)}) custom-call(s32[1]{0:T(128)} %bitcast.core, bf16[4,2,8,32,128]{4,3,2,1,0:T(8,128)(2,1)S(1)} %all-to-all-done.data.pair, bf16[2,32,32,128]{3,2,1,0:T(8,128)(2,1)S(1)} %all_gather.3.pair, ...), custom_call_target="tpu_custom_call" | custom-call | flops 905969664 | bytes 3145728 | tf_op jit(solution)/shard_map/filter_grad/pallas_call | solution.py:160
  41.2 2.0 %collective-permute-start.4 = (f32[1792,128]{1,0:T(8,128)S(1)}, f32[1792,128]{1,0:T(8,128)S(1)}, u32[]{:S(2)}, u32[]{:S(2)}) collective-permute-start(f32[1792,128]{1,0:T(8,128)S(1)} %get-tuple-element.45), channel_id=1, source_target_pairs={{0,4},{4,0},{1,5},{5,1},{2,6},{6,2},{3,7},{7,3},{8,12},{12,8},{9,1... | collective-permute-start | bytes 2752520 | tf_op jit(solution)/shard_map/ppermute | solution.py:294
  43.2 2.3 %collective-permute-start.5 = (bf16[32,32,128]{2,1,0:T(8,128)(2,1)S(1)}, bf16[32,32,128]{2,1,0:T(8,128)(2,1)S(1)}, u32[]{:S(2)}, u32[]{:S(2)}) collective-permute-start(bf16[32,32,128]{2,1,0:T(8,128)(2,1)S(1)} %get-tuple-element.47), channel_id=1, source_target_pairs={{0,4},{4,0},{1,5},{5,1},{2,6},{6,2},{3,7},{7,3},{8,12},{12,8},{9,1... | collective-permute-start | bytes 786440 | tf_op jit(solution)/shard_map/ppermute | solution.py:295
  45.5 0.0 collective-permute-done.4.right
  45.6 0.0 copy-start
  45.6 1.0 shard_map.58
  46.6 0.1 collective-permute-done.5.inner
  46.7 15.1 %all-to-all-start.1 = ((f32[4,448,128]{2,1,0:T(8,128)}), f32[4,448,128]{2,1,0:T(8,128)S(1)}, u32[]{:S(2)}, u32[]{:S(2)}) async-start(f32[4,448,128]{2,1,0:T(8,128)} %bitcast.2), calls=%async_computation.1 | async-start | bytes 1835008 | tf_op jit(solution)/shard_map/all_to_all | solution.py:257
  61.7 0.1 pad_add_fusion.place
  61.8 0.0 copy-done
  61.8 2.8 %input_grad.1 = (f32[256,128]{1,0:T(8,128)S(1)}, f32[256,128]{1,0:T(8,128)}, f32[256,128]{1,0:T(8,128)S(1)}, f32[256,128]{1,0:T(8,128)}) custom-call(s32[2]{0:T(128)S(1)} %pad_add_fusion.place, bf16[2,32,32,128]{3,2,1,0:T(8,128)(2,1)S(1)} %all_gather.3.pair, bf16[32,32,128]{2,1,0:T(8,128)(2,1)S(1)} %collective-permute-done.3.inner, ...), custom_call_target="tpu_custom_call" | custom-call | flops 905969664 | bytes 3145728 | tf_op jit(solution)/shard_map/input_grad/pallas_call | solution.py:106
  64.6 0.0 copy-start.1
  64.6 0.6 copy-done.1
  65.3 3.1 %collective-permute-start.6 = (f32[256,128]{1,0:T(8,128)}, f32[256,128]{1,0:T(8,128)S(1)}, u32[]{:S(2)}, u32[]{:S(2)}) collective-permute-start(f32[256,128]{1,0:T(8,128)} %get-tuple-element.51), channel_id=1, source_target_pairs={{0,1},{1,2},{2,3},{3,0},{4,5},{5,6},{6,7},{7,4},{8,9},{9,10},{10,1... | collective-permute-start | bytes 393224 | tf_op jit(solution)/shard_map/ppermute | solution.py:262
  68.3 2.2 %collective-permute-start.7 = (f32[256,128]{1,0:T(8,128)}, f32[256,128]{1,0:T(8,128)S(1)}, u32[]{:S(2)}, u32[]{:S(2)}) collective-permute-start(f32[256,128]{1,0:T(8,128)} %get-tuple-element.53), channel_id=1, source_target_pairs={{0,3},{1,0},{2,1},{3,2},{4,7},{5,4},{6,5},{7,6},{8,11},{9,8},{10,9... | collective-permute-start | bytes 393224 | tf_op jit(solution)/shard_map/ppermute | solution.py:262
  70.6 4.3 %all-to-all-done.1.parts = f32[4,448,128]{2,1,0:T(8,128)S(1)} async-done(((f32[4,448,128]{2,1,0:T(8,128)}), f32[4,448,128]{2,1,0:T(8,128)S(1)}, u32[]{:S(2)}, u32[]{:S(2)}) %all-to-all-start.1) | async-done | bytes 917536 | tf_op jit(solution)/shard_map/all_to_all | solution.py:257
  74.9 0.0 collective-permute-done.6
  74.9 0.4 collective-permute-done.7
  75.3 13.5 %collective-permute-start.8 = (f32[448,128]{1,0:T(8,128)S(1)}, f32[448,128]{1,0:T(8,128)S(1)}, u32[]{:S(2)}, u32[]{:S(2)}) collective-permute-start(f32[448,128]{1,0:T(8,128)S(1)} %shard_map.59), channel_id=1, source_target_pairs={{0,32},{4,100},{32,0},{36,68},{64,96},{68,36},{96,64},{100,4},{1,3... | collective-permute-start | bytes 688136 | tf_op jit(solution)/shard_map/ppermute | solution.py:307
  88.9 0.1 pad_add_fusion.1.place
  88.9 2.1 %forward.1 = (f32[256,128]{1,0:T(8,128)S(1)}, f32[256,128]{1,0:T(8,128)S(1)}, f32[256,128]{1,0:T(8,128)S(1)}, f32[256,128]{1,0:T(8,128)S(1)}) custom-call(s32[2]{0:T(128)S(1)} %pad_add_fusion.1.place, bf16[4,2,8,32,128]{4,3,2,1,0:T(8,128)(2,1)S(1)} %all-to-all-done.data.pair, bf16[32,32,128]{2,1,0:T(8,128)(2,1)S(1)} %collective-permute-done.5.inner, ...), custom_call_target="tpu_custom_call" | custom-call | flops 905969664 | bytes 3145728 | tf_op jit(solution)/shard_map/forward/pallas_call | solution.py:106
  91.0 3.1 %collective-permute-start.10 = (f32[256,128]{1,0:T(8,128)S(1)}, f32[256,128]{1,0:T(8,128)S(1)}, u32[]{:S(2)}, u32[]{:S(2)}) collective-permute-start(f32[256,128]{1,0:T(8,128)S(1)} %get-tuple-element.63), channel_id=1, source_target_pairs={{0,256},{128,384},{256,0},{384,128},{1,257},{129,385},{257,1},{385... | collective-permute-start | bytes 393224 | tf_op jit(solution)/shard_map/ppermute | solution.py:262
  94.1 3.2 %collective-permute-start.11 = (f32[256,128]{1,0:T(8,128)S(1)}, f32[256,128]{1,0:T(8,128)S(1)}, u32[]{:S(2)}, u32[]{:S(2)}) collective-permute-start(f32[256,128]{1,0:T(8,128)S(1)} %get-tuple-element.64), channel_id=1, source_target_pairs={{0,384},{128,0},{256,128},{384,256},{1,385},{129,1},{257,129},{385... | collective-permute-start | bytes 393224 | tf_op jit(solution)/shard_map/ppermute | solution.py:262
  97.3 2.1 %collective-permute-start.9 = (f32[256,128]{1,0:T(8,128)S(1)}, f32[256,128]{1,0:T(8,128)S(1)}, u32[]{:S(2)}, u32[]{:S(2)}) collective-permute-start(f32[256,128]{1,0:T(8,128)S(1)} %get-tuple-element.62), channel_id=1, source_target_pairs={{0,128},{128,256},{256,384},{384,0},{1,129},{129,257},{257,385},{3... | collective-permute-start | bytes 393224 | tf_op jit(solution)/shard_map/ppermute | solution.py:262
  99.4 0.0 collective-permute-done.8
  99.5 0.0 collective-permute-done.10
  99.5 0.7 collective-permute-done.11
  100.1 4.1 %collective-permute-done.9 = f32[256,128]{1,0:T(8,128)S(1)} collective-permute-done((f32[256,128]{1,0:T(8,128)S(1)}, f32[256,128]{1,0:T(8,128)S(1)}, u32[]{:S(2)}, u32[]{:S(2)}) %collective-permute-start.9) | collective-permute-done | bytes 131104 | tf_op jit(solution)/shard_map/ppermute | solution.py:262
  104.3 1.9 %collective-permute-start.12 = (f32[448,128]{1,0:T(8,128)S(1)}, f32[448,128]{1,0:T(8,128)S(1)}, u32[]{:S(2)}, u32[]{:S(2)}) collective-permute-start(f32[448,128]{1,0:T(8,128)S(1)} %add.21.left), channel_id=1, source_target_pairs={{0,96},{4,36},{32,64},{36,4},{64,32},{68,100},{96,0},{100,68},{1,9... | collective-permute-start | bytes 688136 | tf_op jit(solution)/shard_map/ppermute | solution.py:315
  106.2 0.0 copy-start.2
  106.2 2.4 %collective-permute-start.13 = (bf16[1,8,32,128]{3,2,1,0:T(8,128)(2,1)S(1)}, bf16[1,8,32,128]{3,2,1,0:T(8,128)(2,1)S(1)}, u32[]{:S(2)}, u32[]{:S(2)}) collective-permute-start(bf16[1,8,32,128]{3,2,1,0:T(8,128)(2,1)S(1)} %bitcast.15), channel_id=1, source_target_pairs={{0,0},{1,128},{2,256},{3,384},{4,4},{5,132},{6,260},{7,388},{8,8},... | collective-permute-start | bytes 196616 | tf_op jit(solution)/shard_map/ppermute | solution.py:319
  108.6 5.3 %collective-permute-done.13.block = bf16[1,8,32,128]{3,2,1,0:T(8,128)(2,1)S(1)} collective-permute-done((bf16[1,8,32,128]{3,2,1,0:T(8,128)(2,1)S(1)}, bf16[1,8,32,128]{3,2,1,0:T(8,128)(2,1)S(1)}, u32[]{:S(2)}, u32[]{:S(2)}) %collective-permute-start.13) | collective-permute-done | bytes 65568 | tf_op jit(solution)/shard_map/ppermute | solution.py:319
  113.9 0.6 publish.1
  114.5 10.3 %collective-permute-done.12.right = f32[448,128]{1,0:T(8,128)S(1)} collective-permute-done((f32[448,128]{1,0:T(8,128)S(1)}, f32[448,128]{1,0:T(8,128)S(1)}, u32[]{:S(2)}, u32[]{:S(2)}) %collective-permute-start.12) | collective-permute-done | bytes 229408 | tf_op jit(solution)/shard_map/ppermute | solution.py:315
  124.8 1.0 shard_map.60
  125.8 4.9 %all-to-all-start.2 = ((f32[4,448,128]{2,1,0:T(8,128)}), f32[4,448,128]{2,1,0:T(8,128)S(1)}, u32[]{:S(2)}, u32[]{:S(2)}) async-start(f32[4,448,128]{2,1,0:T(8,128)} %shard_map.60), calls=%async_computation.2 | async-start | bytes 1835008 | tf_op jit(solution)/shard_map/all_to_all | solution.py:257
  130.7 0.0 copy-done.2
  130.7 1.9 %collective-permute-start.14 = (f32[256,128]{1,0:T(8,128)S(1)}, f32[256,128]{1,0:T(8,128)S(1)}, u32[]{:S(2)}, u32[]{:S(2)}) collective-permute-start(f32[256,128]{1,0:T(8,128)S(1)} %copy-done.2), channel_id=1, source_target_pairs={{0,2},{1,3},{2,0},{3,1},{4,6},{5,7},{6,4},{7,5},{8,10},{9,11},{10,... | collective-permute-start | bytes 393224 | tf_op jit(solution)/shard_map/ppermute | solution.py:262
  132.6 5.7 %collective-permute-done.14 = f32[256,128]{1,0:T(8,128)S(1)} collective-permute-done((f32[256,128]{1,0:T(8,128)S(1)}, f32[256,128]{1,0:T(8,128)S(1)}, u32[]{:S(2)}, u32[]{:S(2)}) %collective-permute-start.14) | collective-permute-done | bytes 131104 | tf_op jit(solution)/shard_map/ppermute | solution.py:262
  138.4 0.7 add_convert_fusion
  139.0 5.0 %all-to-all-done.2 = f32[4,448,128]{2,1,0:T(8,128)S(1)} async-done(((f32[4,448,128]{2,1,0:T(8,128)}), f32[4,448,128]{2,1,0:T(8,128)S(1)}, u32[]{:S(2)}, u32[]{:S(2)}) %all-to-all-start.2) | async-done | bytes 917536 | tf_op jit(solution)/shard_map/all_to_all | solution.py:257
  144.0 2.0 %collective-permute-start.15 = (f32[1792,128]{1,0:T(8,128)S(1)}, f32[1792,128]{1,0:T(8,128)S(1)}, u32[]{:S(2)}, u32[]{:S(2)}) collective-permute-start(f32[1792,128]{1,0:T(8,128)S(1)} %bitcast.11), channel_id=1, source_target_pairs={{0,4},{4,0},{1,5},{5,1},{2,6},{6,2},{3,7},{7,3},{8,12},{12,8},{9,1... | collective-permute-start | bytes 2752520 | tf_op jit(solution)/shard_map/ppermute | solution.py:327
  146.0 2.4 %collective-permute-done.15 = f32[1792,128]{1,0:T(8,128)S(1)} collective-permute-done((f32[1792,128]{1,0:T(8,128)S(1)}, f32[1792,128]{1,0:T(8,128)S(1)}, u32[]{:S(2)}, u32[]{:S(2)}) %collective-permute-start.15) | collective-permute-done | bytes 917536 | tf_op jit(solution)/shard_map/ppermute | solution.py:327
  148.4 1.2 join.1
  (5 shorter events, 0.1 us)
Async XLA Ops:
  0.6 10.0 %collective-permute-start.2 = (bf16[1,8,32,128]{3,2,1,0:T(8,128)(2,1)}, bf16[1,8,32,128]{3,2,1,0:T(8,128)(2,1)S(1)}, u32[]{:S(2)}, u32[]{:S(2)}) collective-permute-start(bf16[1,8,32,128]{3,2,1,0:T(8,128)(2,1)} %param.3), channel_id=1, source_target_pairs={{4,8},{5,9},{6,10},{7,11},{8,4},{9,5},{10,6},{11,7},{12,16},{13,17... | collective-permute-start | bytes 196616 | tf_op jit(solution)/shard_map/ppermute | solution.py:283
  4.4 7.1 %collective-permute-start = (bf16[1,8,32,128]{3,2,1,0:T(8,128)(2,1)}, bf16[1,8,32,128]{3,2,1,0:T(8,128)(2,1)S(1)}, u32[]{:S(2)}, u32[]{:S(2)}) collective-permute-start(bf16[1,8,32,128]{3,2,1,0:T(8,128)(2,1)} %param.5), channel_id=1, source_target_pairs={{0,0},{1,128},{2,256},{3,384},{4,4},{5,132},{6,260},{7,388},{8,8},... | collective-permute-start | bytes 196616 | tf_op jit(solution)/shard_map/ppermute | solution.py:284
  7.1 8.4 %collective-permute-start.1 = (bf16[1,8,32,128]{3,2,1,0:T(8,128)(2,1)}, bf16[1,8,32,128]{3,2,1,0:T(8,128)(2,1)S(1)}, u32[]{:S(2)}, u32[]{:S(2)}) collective-permute-start(bf16[1,8,32,128]{3,2,1,0:T(8,128)(2,1)} %param.5), channel_id=1, source_target_pairs={{4,8},{5,136},{6,264},{7,392},{8,4},{9,132},{10,260},{11,388},{12,... | collective-permute-start | bytes 196616 | tf_op jit(solution)/shard_map/ppermute | solution.py:284
  16.3 23.3 %all-to-all-start = ((bf16[4,2,8,32,128]{4,3,2,1,0:T(8,128)(2,1)}), bf16[4,2,8,32,128]{4,3,2,1,0:T(8,128)(2,1)S(1)}, u32[]{:S(2)}, u32[]{:S(2)}) async-start(bf16[4,2,8,32,128]{4,3,2,1,0:T(8,128)(2,1)} %broadcast_in_dim.2), calls=%async_computation | async-start | bytes 1048576 | tf_op jit(solution)/shard_map/all_to_all | solution.py:257
  36.2 3.4 %collective-permute-start.3 = (bf16[32,32,128]{2,1,0:T(8,128)(2,1)S(1)}, bf16[32,32,128]{2,1,0:T(8,128)(2,1)S(1)}, u32[]{:S(2)}, u32[]{:S(2)}) collective-permute-start(bf16[32,32,128]{2,1,0:T(8,128)(2,1)S(1)} %slice_bitcast_fusion), channel_id=1, source_target_pairs={{0,4},{4,0},{1,5},{5,1},{2,6},{6,2},{3,7},{7,3},{8,12},{12,8},{9,1... | collective-permute-start | bytes 786440 | tf_op jit(solution)/shard_map/ppermute | solution.py:291
  41.2 4.4 %collective-permute-start.4 = (f32[1792,128]{1,0:T(8,128)S(1)}, f32[1792,128]{1,0:T(8,128)S(1)}, u32[]{:S(2)}, u32[]{:S(2)}) collective-permute-start(f32[1792,128]{1,0:T(8,128)S(1)} %get-tuple-element.45), channel_id=1, source_target_pairs={{0,4},{4,0},{1,5},{5,1},{2,6},{6,2},{3,7},{7,3},{8,12},{12,8},{9,1... | collective-permute-start | bytes 2752520 | tf_op jit(solution)/shard_map/ppermute | solution.py:294
  43.2 3.4 %collective-permute-start.5 = (bf16[32,32,128]{2,1,0:T(8,128)(2,1)S(1)}, bf16[32,32,128]{2,1,0:T(8,128)(2,1)S(1)}, u32[]{:S(2)}, u32[]{:S(2)}) collective-permute-start(bf16[32,32,128]{2,1,0:T(8,128)(2,1)S(1)} %get-tuple-element.47), channel_id=1, source_target_pairs={{0,4},{4,0},{1,5},{5,1},{2,6},{6,2},{3,7},{7,3},{8,12},{12,8},{9,1... | collective-permute-start | bytes 786440 | tf_op jit(solution)/shard_map/ppermute | solution.py:295
  45.6 16.3 %copy-start = (bf16[27,128,128]{2,1,0:T(8,128)(2,1)S(1)}, bf16[27,128,128]{2,1,0:T(8,128)(2,1)}, u32[]{:S(2)}) copy-start(bf16[27,128,128]{2,1,0:T(8,128)(2,1)} %weight.3) | copy-start | bytes 2654212
  46.7 28.2 %all-to-all-start.1 = ((f32[4,448,128]{2,1,0:T(8,128)}), f32[4,448,128]{2,1,0:T(8,128)S(1)}, u32[]{:S(2)}, u32[]{:S(2)}) async-start(f32[4,448,128]{2,1,0:T(8,128)} %bitcast.2), calls=%async_computation.1 | async-start | bytes 1835008 | tf_op jit(solution)/shard_map/all_to_all | solution.py:257
  64.6 0.6 copy-start.1
  65.3 9.6 %collective-permute-start.6 = (f32[256,128]{1,0:T(8,128)}, f32[256,128]{1,0:T(8,128)S(1)}, u32[]{:S(2)}, u32[]{:S(2)}) collective-permute-start(f32[256,128]{1,0:T(8,128)} %get-tuple-element.51), channel_id=1, source_target_pairs={{0,1},{1,2},{2,3},{3,0},{4,5},{5,6},{6,7},{7,4},{8,9},{9,10},{10,1... | collective-permute-start | bytes 393224 | tf_op jit(solution)/shard_map/ppermute | solution.py:262
  68.3 7.0 %collective-permute-start.7 = (f32[256,128]{1,0:T(8,128)}, f32[256,128]{1,0:T(8,128)S(1)}, u32[]{:S(2)}, u32[]{:S(2)}) collective-permute-start(f32[256,128]{1,0:T(8,128)} %get-tuple-element.53), channel_id=1, source_target_pairs={{0,3},{1,0},{2,1},{3,2},{4,7},{5,4},{6,5},{7,6},{8,11},{9,8},{10,9... | collective-permute-start | bytes 393224 | tf_op jit(solution)/shard_map/ppermute | solution.py:262
  75.3 24.1 %collective-permute-start.8 = (f32[448,128]{1,0:T(8,128)S(1)}, f32[448,128]{1,0:T(8,128)S(1)}, u32[]{:S(2)}, u32[]{:S(2)}) collective-permute-start(f32[448,128]{1,0:T(8,128)S(1)} %shard_map.59), channel_id=1, source_target_pairs={{0,32},{4,100},{32,0},{36,68},{64,96},{68,36},{96,64},{100,4},{1,3... | collective-permute-start | bytes 688136 | tf_op jit(solution)/shard_map/ppermute | solution.py:307
  91.0 8.4 %collective-permute-start.10 = (f32[256,128]{1,0:T(8,128)S(1)}, f32[256,128]{1,0:T(8,128)S(1)}, u32[]{:S(2)}, u32[]{:S(2)}) collective-permute-start(f32[256,128]{1,0:T(8,128)S(1)} %get-tuple-element.63), channel_id=1, source_target_pairs={{0,256},{128,384},{256,0},{384,128},{1,257},{129,385},{257,1},{385... | collective-permute-start | bytes 393224 | tf_op jit(solution)/shard_map/ppermute | solution.py:262
  94.1 6.0 %collective-permute-start.11 = (f32[256,128]{1,0:T(8,128)S(1)}, f32[256,128]{1,0:T(8,128)S(1)}, u32[]{:S(2)}, u32[]{:S(2)}) collective-permute-start(f32[256,128]{1,0:T(8,128)S(1)} %get-tuple-element.64), channel_id=1, source_target_pairs={{0,384},{128,0},{256,128},{384,256},{1,385},{129,1},{257,129},{385... | collective-permute-start | bytes 393224 | tf_op jit(solution)/shard_map/ppermute | solution.py:262
  97.3 6.9 %collective-permute-start.9 = (f32[256,128]{1,0:T(8,128)S(1)}, f32[256,128]{1,0:T(8,128)S(1)}, u32[]{:S(2)}, u32[]{:S(2)}) collective-permute-start(f32[256,128]{1,0:T(8,128)S(1)} %get-tuple-element.62), channel_id=1, source_target_pairs={{0,128},{128,256},{256,384},{384,0},{1,129},{129,257},{257,385},{3... | collective-permute-start | bytes 393224 | tf_op jit(solution)/shard_map/ppermute | solution.py:262
  104.3 20.5 %collective-permute-start.12 = (f32[448,128]{1,0:T(8,128)S(1)}, f32[448,128]{1,0:T(8,128)S(1)}, u32[]{:S(2)}, u32[]{:S(2)}) collective-permute-start(f32[448,128]{1,0:T(8,128)S(1)} %add.21.left), channel_id=1, source_target_pairs={{0,96},{4,36},{32,64},{36,4},{64,32},{68,100},{96,0},{100,68},{1,9... | collective-permute-start | bytes 688136 | tf_op jit(solution)/shard_map/ppermute | solution.py:315
  106.2 24.5 %copy-start.2 = (f32[256,128]{1,0:T(8,128)S(1)}, f32[256,128]{1,0:T(8,128)}, u32[]{:S(2)}) copy-start(f32[256,128]{1,0:T(8,128)} %copy-done.1) | copy-start | bytes 393220
  106.2 7.6 %collective-permute-start.13 = (bf16[1,8,32,128]{3,2,1,0:T(8,128)(2,1)S(1)}, bf16[1,8,32,128]{3,2,1,0:T(8,128)(2,1)S(1)}, u32[]{:S(2)}, u32[]{:S(2)}) collective-permute-start(bf16[1,8,32,128]{3,2,1,0:T(8,128)(2,1)S(1)} %bitcast.15), channel_id=1, source_target_pairs={{0,0},{1,128},{2,256},{3,384},{4,4},{5,132},{6,260},{7,388},{8,8},... | collective-permute-start | bytes 196616 | tf_op jit(solution)/shard_map/ppermute | solution.py:319
  125.8 18.2 %all-to-all-start.2 = ((f32[4,448,128]{2,1,0:T(8,128)}), f32[4,448,128]{2,1,0:T(8,128)S(1)}, u32[]{:S(2)}, u32[]{:S(2)}) async-start(f32[4,448,128]{2,1,0:T(8,128)} %shard_map.60), calls=%async_computation.2 | async-start | bytes 1835008 | tf_op jit(solution)/shard_map/all_to_all | solution.py:257
  130.7 7.7 %collective-permute-start.14 = (f32[256,128]{1,0:T(8,128)S(1)}, f32[256,128]{1,0:T(8,128)S(1)}, u32[]{:S(2)}, u32[]{:S(2)}) collective-permute-start(f32[256,128]{1,0:T(8,128)S(1)} %copy-done.2), channel_id=1, source_target_pairs={{0,2},{1,3},{2,0},{3,1},{4,6},{5,7},{6,4},{7,5},{8,10},{9,11},{10,... | collective-permute-start | bytes 393224 | tf_op jit(solution)/shard_map/ppermute | solution.py:262
  144.0 4.4 %collective-permute-start.15 = (f32[1792,128]{1,0:T(8,128)S(1)}, f32[1792,128]{1,0:T(8,128)S(1)}, u32[]{:S(2)}, u32[]{:S(2)}) collective-permute-start(f32[1792,128]{1,0:T(8,128)S(1)} %bitcast.11), channel_id=1, source_target_pairs={{0,4},{4,0},{1,5},{5,1},{2,6},{6,2},{3,7},{7,3},{8,12},{12,8},{9,1... | collective-permute-start | bytes 2752520 | tf_op jit(solution)/shard_map/ppermute | solution.py:327

commit v14 on v13

--- a/solution.py
+++ b/solution.py
@@ -275,7 +275,7 @@
 
 
 def shards(sizes, activations, weight, output_grad):
-    chans, _, rings, cores, spaces = sizes
+    _, _, rings, cores, spaces = sizes
     planes, height, lanes = activations.shape[1:]
     core = lax.axis_index("core")
     swap = [(0, 1), (1, 0)]
@@ -307,7 +307,7 @@
     moved = lax.ppermute(quarter, ("zhi", "core"), doubling(0))
     me = lax.axis_index("chan")
     forward = convolve(False, core, me, after(data, quarter), data_inner, weight, spaces)
-    forward = [forward[0], *(rotate(forward[step], "chan", step) for step in range(1, chans))]
+    forward = [forward[0], rotate(forward[1], "chan", 1), rotate(forward[2], "chan", 2), forward[3]]
     cell_count = sizes[1] * rings * cores * grad.shape[1] * grad.shape[2]
     pair = quarter + moved
     pair, back, forward = lax.optimization_barrier((pair, back, forward))
@@ -315,14 +315,15 @@
     moved = lax.ppermute(pair, ("zhi", "core"), doubling(1))
     spread = functools.partial(spread_kernel, 1 / math.sqrt(cell_count))
     quarter = small_call(spread, (rings, *pair.shape), pair, moved)
+    forward[3] = rotate(forward[3], "chan", 3)
+    quarter, forward, back = lax.optimization_barrier((quarter, forward, back))
+
+    half = exchange(quarter, "ring").reshape(-1, lanes)
     forward = sum(forward).astype(BF16).reshape(activations.shape)
     output = published(lax.ppermute(forward, AXES, neighbour(sizes, False, True)))
-    quarter, output, back = lax.optimization_barrier((quarter, output, back))
-
-    half = exchange(quarter, "ring").reshape(-1, lanes)
-    back[2] = rotate(back[2], "space", 2)
+    back[2] = rotate(after(back[2], forward), "space", 2)
+    half, _, back = lax.optimization_barrier((half, output, back))
     input_grad = sum(back).astype(BF16).reshape(activations.shape)
-    half = after(half, input_grad)
 
     other = lax.ppermute(half, "core", swap)
     blocks = (-1, *weight.shape[1:])

time: 150 us -> 146 us (0.973)
  the two profiles are of different devices: /device:TPU:33 before, /device:TPU:1 now
where the time goes in v14:
time: 146 us; the launch traced here: 144 us
  starting transfers between devices  80.1 us (55%)
  waiting for transfers between devices  38.5 us (26%)
  blocking collectives  11.2 us (8%)
  Pallas kernels  10.4 us (7%)
  other arithmetic  1.73 us (1%)
  local copies, waits for them, and re-layouts  1.55 us (1%)
    all_to_all x3, starting transfers between devices, exchange(): return lax.all_to_all(block, axis, split_axis=0, concat_axis=0, tiled=True)  31.5 us
    ppermute x6, starting transfers between devices, rotate(): lax.ppermute(term, axis, [(i, (i + step) % count) for i in range(count)])  16.7 us
    ppermute x1, waiting for transfers between devices, shards(): moved = lax.ppermute(pair, ('zhi', 'core'), doubling(1))  13.8 us
    ppermute x6, waiting for transfers between devices, rotate(): lax.ppermute(term, axis, [(i, (i + step) % count) for i in range(count)])  13.7 us
    ppermute x1, starting transfers between devices, shards(): moved = lax.ppermute(quarter, ('zhi', 'core'), doubling(0))  13.1 us
    all_gather x1, blocking collectives, shards(): grad = lax.all_gather(grad, 'chan', axis=1, tiled=True)  11.2 us
    pallas_call x2, Pallas kernels, convolve(): pl.pallas_call(functools.partial(conv_kernel, backward), out_shape=[jax.S...  4.89 us
    all_to_all x3, waiting for transfers between devices, exchange(): return lax.all_to_all(block, axis, split_axis=0, concat_axis=0, tiled=True)  4.62 us
  transfers between devices with their start and end apart: 19, of which 11 were waited for; matrix products, arithmetic and copies ran while one was open for 1% of the time, Pallas kernels for 5%

profile of v14, /device:TPU:1, one launch (start us, length us, event | category | flops | bytes accessed | tf_op | source)
XLA Modules:
  0.0 144.3 jit_solution(14079875878478963940)
XLA Ops:
  0.6 4.6 %collective-permute-start.2 = (bf16[1,8,32,128]{3,2,1,0:T(8,128)(2,1)}, bf16[1,8,32,128]{3,2,1,0:T(8,128)(2,1)S(1)}, u32[]{:S(2)}, u32[]{:S(2)}) collective-permute-start(bf16[1,8,32,128]{3,2,1,0:T(8,128)(2,1)} %param.3), channel_id=1, source_target_pairs={{4,8},{5,9},{6,10},{7,11},{8,4},{9,5},{10,6},{11,7},{12,16},{13,17... | collective-permute-start | bytes 196616 | tf_op jit(solution)/shard_map/ppermute | solution.py:283
  5.2 1.5 %collective-permute-start = (bf16[1,8,32,128]{3,2,1,0:T(8,128)(2,1)}, bf16[1,8,32,128]{3,2,1,0:T(8,128)(2,1)S(1)}, u32[]{:S(2)}, u32[]{:S(2)}) collective-permute-start(bf16[1,8,32,128]{3,2,1,0:T(8,128)(2,1)} %param.5), channel_id=1, source_target_pairs={{0,0},{1,128},{2,256},{3,384},{4,4},{5,132},{6,260},{7,388},{8,8},... | collective-permute-start | bytes 196616 | tf_op jit(solution)/shard_map/ppermute | solution.py:284
  6.7 1.9 %collective-permute-start.1 = (bf16[1,8,32,128]{3,2,1,0:T(8,128)(2,1)}, bf16[1,8,32,128]{3,2,1,0:T(8,128)(2,1)S(1)}, u32[]{:S(2)}, u32[]{:S(2)}) collective-permute-start(bf16[1,8,32,128]{3,2,1,0:T(8,128)(2,1)} %param.5), channel_id=1, source_target_pairs={{4,8},{5,136},{6,264},{7,392},{8,4},{9,132},{10,260},{11,388},{12,... | collective-permute-start | bytes 196616 | tf_op jit(solution)/shard_map/ppermute | solution.py:284
  8.6 0.0 collective-permute-done.2
  8.7 0.9 pad_maximum_fusion.1
  9.5 0.0 collective-permute-done
  9.5 3.0 %collective-permute-done.1 = bf16[1,8,32,128]{3,2,1,0:T(8,128)(2,1)S(1)} collective-permute-done((bf16[1,8,32,128]{3,2,1,0:T(8,128)(2,1)}, bf16[1,8,32,128]{3,2,1,0:T(8,128)(2,1)S(1)}, u32[]{:S(2)}, u32[]{:S(2)}) %collective-permute-start.1) | collective-permute-done | bytes 65568 | tf_op jit(solution)/shard_map/ppermute | solution.py:284
  12.5 0.9 broadcast_in_dim.2
  13.4 12.4 %all-to-all-start = ((bf16[4,2,8,32,128]{4,3,2,1,0:T(8,128)(2,1)}), bf16[4,2,8,32,128]{4,3,2,1,0:T(8,128)(2,1)S(1)}, u32[]{:S(2)}, u32[]{:S(2)}) async-start(bf16[4,2,8,32,128]{4,3,2,1,0:T(8,128)(2,1)} %broadcast_in_dim.2), calls=%async_computation | async-start | bytes 1048576 | tf_op jit(solution)/shard_map/all_to_all | solution.py:257
  25.8 11.2 %all_gather.3.pair = bf16[2,32,32,128]{3,2,1,0:T(8,128)(2,1)S(1)} all-gather(bf16[2,8,32,128]{3,2,1,0:T(8,128)(2,1)S(1)} %pad_maximum_fusion), channel_id=1, replica_groups=mesh['chan'=4,'zhi'=4,'ring'=4,'core'=2,'space'=4] {'chan'}, dimensions={1}, use_global_device_ids=true | all-gather | bytes 655360 | tf_op jit(solution)/shard_map/all_gather | solution.py:290
  37.0 1.9 %collective-permute-start.3 = (bf16[32,32,128]{2,1,0:T(8,128)(2,1)S(1)}, bf16[32,32,128]{2,1,0:T(8,128)(2,1)S(1)}, u32[]{:S(2)}, u32[]{:S(2)}) collective-permute-start(bf16[32,32,128]{2,1,0:T(8,128)(2,1)S(1)} %slice_bitcast_fusion), channel_id=1, source_target_pairs={{0,4},{4,0},{1,5},{5,1},{2,6},{6,2},{3,7},{7,3},{8,12},{12,8},{9,1... | collective-permute-start | bytes 786440 | tf_op jit(solution)/shard_map/ppermute | solution.py:291
  39.0 1.5 %collective-permute-done.3.inner = bf16[32,32,128]{2,1,0:T(8,128)(2,1)S(1)} collective-permute-done((bf16[32,32,128]{2,1,0:T(8,128)(2,1)S(1)}, bf16[32,32,128]{2,1,0:T(8,128)(2,1)S(1)}, u32[]{:S(2)}, u32[]{:S(2)}) %collective-permute-start.3) | collective-permute-done | bytes 262176 | tf_op jit(solution)/shard_map/ppermute | solution.py:291
  40.5 0.0 all-to-all-done.data.pair
  40.5 1.6 %filter_grad.1 = (f32[1792,128]{1,0:T(8,128)S(1)}, f32[1792,128]{1,0:T(8,128)S(1)}, bf16[32,32,128]{2,1,0:T(8,128)(2,1)S(1)}) custom-call(s32[1]{0:T(128)} %bitcast.core, bf16[4,2,8,32,128]{4,3,2,1,0:T(8,128)(2,1)S(1)} %all-to-all-done.data.pair, bf16[2,32,32,128]{3,2,1,0:T(8,128)(2,1)S(1)} %all_gather.3.pair, ...), custom_call_target="tpu_custom_call" | custom-call | flops 905969664 | bytes 3145728 | tf_op jit(solution)/shard_map/filter_grad/pallas_call | solution.py:160
  42.1 2.0 %collective-permute-start.4 = (f32[1792,128]{1,0:T(8,128)S(1)}, f32[1792,128]{1,0:T(8,128)S(1)}, u32[]{:S(2)}, u32[]{:S(2)}) collective-permute-start(f32[1792,128]{1,0:T(8,128)S(1)} %get-tuple-element.53), channel_id=1, source_target_pairs={{0,4},{4,0},{1,5},{5,1},{2,6},{6,2},{3,7},{7,3},{8,12},{12,8},{9,1... | collective-permute-start | bytes 2752520 | tf_op jit(solution)/shard_map/ppermute | solution.py:294
  44.1 2.3 %collective-permute-start.5 = (bf16[32,32,128]{2,1,0:T(8,128)(2,1)S(1)}, bf16[32,32,128]{2,1,0:T(8,128)(2,1)S(1)}, u32[]{:S(2)}, u32[]{:S(2)}) collective-permute-start(bf16[32,32,128]{2,1,0:T(8,128)(2,1)S(1)} %get-tuple-element.55), channel_id=1, source_target_pairs={{0,4},{4,0},{1,5},{5,1},{2,6},{6,2},{3,7},{7,3},{8,12},{12,8},{9,1... | collective-permute-start | bytes 786440 | tf_op jit(solution)/shard_map/ppermute | solution.py:295
  46.4 0.0 collective-permute-done.4.right
  46.4 0.0 copy-start
  46.4 1.0 shard_map.58
  47.4 0.1 collective-permute-done.5.inner
  47.5 15.3 %all-to-all-start.1 = ((f32[4,448,128]{2,1,0:T(8,128)}), f32[4,448,128]{2,1,0:T(8,128)S(1)}, u32[]{:S(2)}, u32[]{:S(2)}) async-start(f32[4,448,128]{2,1,0:T(8,128)} %bitcast.2), calls=%async_computation.1 | async-start | bytes 1835008 | tf_op jit(solution)/shard_map/all_to_all | solution.py:257
  62.8 0.1 pad_add_fusion.place
  62.9 0.0 copy-done
  62.9 2.8 %input_grad.1 = (f32[256,128]{1,0:T(8,128)S(1)}, f32[256,128]{1,0:T(8,128)}, f32[256,128]{1,0:T(8,128)S(1)}, f32[256,128]{1,0:T(8,128)}) custom-call(s32[2]{0:T(128)S(1)} %pad_add_fusion.place, bf16[2,32,32,128]{3,2,1,0:T(8,128)(2,1)S(1)} %all_gather.3.pair, bf16[32,32,128]{2,1,0:T(8,128)(2,1)S(1)} %collective-permute-done.3.inner, ...), custom_call_target="tpu_custom_call" | custom-call | flops 905969664 | bytes 3145728 | tf_op jit(solution)/shard_map/input_grad/pallas_call | solution.py:106
  65.7 0.0 copy-start.1
  65.7 0.6 copy-done.1
  66.3 3.3 %collective-permute-start.6 = (f32[256,128]{1,0:T(8,128)}, f32[256,128]{1,0:T(8,128)S(1)}, u32[]{:S(2)}, u32[]{:S(2)}) collective-permute-start(f32[256,128]{1,0:T(8,128)} %get-tuple-element.59), channel_id=1, source_target_pairs={{0,1},{1,2},{2,3},{3,0},{4,5},{5,6},{6,7},{7,4},{8,9},{9,10},{10,1... | collective-permute-start | bytes 393224 | tf_op jit(solution)/shard_map/ppermute | solution.py:262
  69.6 3.8 %collective-permute-start.7 = (f32[256,128]{1,0:T(8,128)}, f32[256,128]{1,0:T(8,128)S(1)}, u32[]{:S(2)}, u32[]{:S(2)}) collective-permute-start(f32[256,128]{1,0:T(8,128)} %get-tuple-element.61), channel_id=1, source_target_pairs={{0,3},{1,0},{2,1},{3,2},{4,7},{5,4},{6,5},{7,6},{8,11},{9,8},{10,9... | collective-permute-start | bytes 393224 | tf_op jit(solution)/shard_map/ppermute | solution.py:262
  73.4 2.5 %all-to-all-done.1.parts = f32[4,448,128]{2,1,0:T(8,128)S(1)} async-done(((f32[4,448,128]{2,1,0:T(8,128)}), f32[4,448,128]{2,1,0:T(8,128)S(1)}, u32[]{:S(2)}, u32[]{:S(2)}) %all-to-all-start.1) | async-done | bytes 917536 | tf_op jit(solution)/shard_map/all_to_all | solution.py:257
  76.0 0.0 collective-permute-done.6
  76.0 2.4 %collective-permute-done.7 = f32[256,128]{1,0:T(8,128)S(1)} collective-permute-done((f32[256,128]{1,0:T(8,128)}, f32[256,128]{1,0:T(8,128)S(1)}, u32[]{:S(2)}, u32[]{:S(2)}) %collective-permute-start.7) | collective-permute-done | bytes 131104 | tf_op jit(solution)/shard_map/ppermute | solution.py:262
  78.4 13.1 %collective-permute-start.8 = (f32[448,128]{1,0:T(8,128)S(1)}, f32[448,128]{1,0:T(8,128)S(1)}, u32[]{:S(2)}, u32[]{:S(2)}) collective-permute-start(f32[448,128]{1,0:T(8,128)S(1)} %shard_map.59), channel_id=1, source_target_pairs={{0,32},{4,100},{32,0},{36,68},{64,96},{68,36},{96,64},{100,4},{1,3... | collective-permute-start | bytes 688136 | tf_op jit(solution)/shard_map/ppermute | solution.py:307
  91.5 0.1 pad_add_fusion.1.place
  91.6 2.1 %forward.1 = (f32[256,128]{1,0:T(8,128)S(1)}, f32[256,128]{1,0:T(8,128)S(1)}, f32[256,128]{1,0:T(8,128)S(1)}, f32[256,128]{1,0:T(8,128)S(1)}) custom-call(s32[2]{0:T(128)S(1)} %pad_add_fusion.1.place, bf16[4,2,8,32,128]{4,3,2,1,0:T(8,128)(2,1)S(1)} %all-to-all-done.data.pair, bf16[32,32,128]{2,1,0:T(8,128)(2,1)S(1)} %collective-permute-done.5.inner, ...), custom_call_target="tpu_custom_call" | custom-call | flops 905969664 | bytes 3145728 | tf_op jit(solution)/shard_map/forward/pallas_call | solution.py:106
  93.7 3.1 %collective-permute-start.10 = (f32[256,128]{1,0:T(8,128)S(1)}, f32[256,128]{1,0:T(8,128)S(1)}, u32[]{:S(2)}, u32[]{:S(2)}) collective-permute-start(f32[256,128]{1,0:T(8,128)S(1)} %get-tuple-element.71), channel_id=1, source_target_pairs={{0,256},{128,384},{256,0},{384,128},{1,257},{129,385},{257,1},{385... | collective-permute-start | bytes 393224 | tf_op jit(solution)/shard_map/ppermute | solution.py:262
  96.8 2.6 %collective-permute-start.9 = (f32[256,128]{1,0:T(8,128)S(1)}, f32[256,128]{1,0:T(8,128)S(1)}, u32[]{:S(2)}, u32[]{:S(2)}) collective-permute-start(f32[256,128]{1,0:T(8,128)S(1)} %get-tuple-element.70), channel_id=1, source_target_pairs={{0,128},{128,256},{256,384},{384,0},{1,129},{129,257},{257,385},{3... | collective-permute-start | bytes 393224 | tf_op jit(solution)/shard_map/ppermute | solution.py:262
  99.4 0.0 collective-permute-done.8
  99.4 1.5 %collective-permute-done.10 = f32[256,128]{1,0:T(8,128)S(1)} collective-permute-done((f32[256,128]{1,0:T(8,128)S(1)}, f32[256,128]{1,0:T(8,128)S(1)}, u32[]{:S(2)}, u32[]{:S(2)}) %collective-permute-start.10) | collective-permute-done | bytes 131104 | tf_op jit(solution)/shard_map/ppermute | solution.py:262
  100.9 2.8 %collective-permute-done.9 = f32[256,128]{1,0:T(8,128)S(1)} collective-permute-done((f32[256,128]{1,0:T(8,128)S(1)}, f32[256,128]{1,0:T(8,128)S(1)}, u32[]{:S(2)}, u32[]{:S(2)}) %collective-permute-start.9) | collective-permute-done | bytes 131104 | tf_op jit(solution)/shard_map/ppermute | solution.py:262
  103.7 0.0 copy-start.2
  103.7 2.0 %collective-permute-start.11 = (f32[448,128]{1,0:T(8,128)S(1)}, f32[448,128]{1,0:T(8,128)S(1)}, u32[]{:S(2)}, u32[]{:S(2)}) collective-permute-start(f32[448,128]{1,0:T(8,128)S(1)} %add.21.left), channel_id=1, source_target_pairs={{0,96},{4,36},{32,64},{36,4},{64,32},{68,100},{96,0},{100,68},{1,9... | collective-permute-start | bytes 688136 | tf_op jit(solution)/shard_map/ppermute | solution.py:315
  105.7 2.0 %collective-permute-start.12 = (f32[256,128]{1,0:T(8,128)S(1)}, f32[256,128]{1,0:T(8,128)S(1)}, u32[]{:S(2)}, u32[]{:S(2)}) collective-permute-start(f32[256,128]{1,0:T(8,128)S(1)} %get-tuple-element.77), channel_id=1, source_target_pairs={{0,384},{128,0},{256,128},{384,256},{1,385},{129,1},{257,129},{385... | collective-permute-start | bytes 393224 | tf_op jit(solution)/shard_map/ppermute | solution.py:262
  107.7 13.8 %collective-permute-done.11.right = f32[448,128]{1,0:T(8,128)S(1)} collective-permute-done((f32[448,128]{1,0:T(8,128)S(1)}, f32[448,128]{1,0:T(8,128)S(1)}, u32[]{:S(2)}, u32[]{:S(2)}) %collective-permute-start.11) | collective-permute-done | bytes 229408 | tf_op jit(solution)/shard_map/ppermute | solution.py:315
  121.6 1.0 shard_map.60
  122.5 0.0 collective-permute-done.12
  122.5 3.8 %all-to-all-start.2 = ((f32[4,448,128]{2,1,0:T(8,128)}), f32[4,448,128]{2,1,0:T(8,128)S(1)}, u32[]{:S(2)}, u32[]{:S(2)}) async-start(f32[4,448,128]{2,1,0:T(8,128)} %shard_map.60), calls=%async_computation.2 | async-start | bytes 1835008 | tf_op jit(solution)/shard_map/all_to_all | solution.py:257
  126.4 0.0 copy-done.2
  126.4 1.9 %collective-permute-start.14 = (f32[256,128]{1,0:T(8,128)S(1)}, f32[256,128]{1,0:T(8,128)S(1)}, u32[]{:S(2)}, u32[]{:S(2)}) collective-permute-start(f32[256,128]{1,0:T(8,128)S(1)} %copy-done.2), channel_id=1, source_target_pairs={{0,2},{1,3},{2,0},{3,1},{4,6},{5,7},{6,4},{7,5},{8,10},{9,11},{10,... | collective-permute-start | bytes 393224 | tf_op jit(solution)/shard_map/ppermute | solution.py:262
  128.3 0.7 collective-permute-start.13
  129.0 0.0 collective-permute-done.13.block
  129.0 0.6 publish.1
  129.7 7.0 %collective-permute-done.14 = f32[256,128]{1,0:T(8,128)S(1)} collective-permute-done((f32[256,128]{1,0:T(8,128)S(1)}, f32[256,128]{1,0:T(8,128)S(1)}, u32[]{:S(2)}, u32[]{:S(2)}) %collective-permute-start.14) | collective-permute-done | bytes 131104 | tf_op jit(solution)/shard_map/ppermute | solution.py:262
  136.7 2.1 %all-to-all-done.2 = f32[4,448,128]{2,1,0:T(8,128)S(1)} async-done(((f32[4,448,128]{2,1,0:T(8,128)}), f32[4,448,128]{2,1,0:T(8,128)S(1)}, u32[]{:S(2)}, u32[]{:S(2)}) %all-to-all-start.2) | async-done | bytes 917536 | tf_op jit(solution)/shard_map/all_to_all | solution.py:257
  138.8 1.9 %collective-permute-start.15 = (f32[1792,128]{1,0:T(8,128)S(1)}, f32[1792,128]{1,0:T(8,128)S(1)}, u32[]{:S(2)}, u32[]{:S(2)}) collective-permute-start(f32[1792,128]{1,0:T(8,128)S(1)} %bitcast.11), channel_id=1, source_target_pairs={{0,4},{4,0},{1,5},{5,1},{2,6},{6,2},{3,7},{7,3},{8,12},{12,8},{9,1... | collective-permute-start | bytes 2752520 | tf_op jit(solution)/shard_map/ppermute | solution.py:328
  140.7 0.7 add_convert_fusion
  141.3 1.8 %collective-permute-done.15 = f32[1792,128]{1,0:T(8,128)S(1)} collective-permute-done((f32[1792,128]{1,0:T(8,128)S(1)}, f32[1792,128]{1,0:T(8,128)S(1)}, u32[]{:S(2)}, u32[]{:S(2)}) %collective-permute-start.15) | collective-permute-done | bytes 917536 | tf_op jit(solution)/shard_map/ppermute | solution.py:328
  143.1 1.2 join.1
  (5 shorter events, 0.1 us)
Async XLA Ops:
  0.6 8.0 %collective-permute-start.2 = (bf16[1,8,32,128]{3,2,1,0:T(8,128)(2,1)}, bf16[1,8,32,128]{3,2,1,0:T(8,128)(2,1)S(1)}, u32[]{:S(2)}, u32[]{:S(2)}) collective-permute-start(bf16[1,8,32,128]{3,2,1,0:T(8,128)(2,1)} %param.3), channel_id=1, source_target_pairs={{4,8},{5,9},{6,10},{7,11},{8,4},{9,5},{10,6},{11,7},{12,16},{13,17... | collective-permute-start | bytes 196616 | tf_op jit(solution)/shard_map/ppermute | solution.py:283
  5.2 4.3 %collective-permute-start = (bf16[1,8,32,128]{3,2,1,0:T(8,128)(2,1)}, bf16[1,8,32,128]{3,2,1,0:T(8,128)(2,1)S(1)}, u32[]{:S(2)}, u32[]{:S(2)}) collective-permute-start(bf16[1,8,32,128]{3,2,1,0:T(8,128)(2,1)} %param.5), channel_id=1, source_target_pairs={{0,0},{1,128},{2,256},{3,384},{4,4},{5,132},{6,260},{7,388},{8,8},... | collective-permute-start | bytes 196616 | tf_op jit(solution)/shard_map/ppermute | solution.py:284
  6.7 5.8 %collective-permute-start.1 = (bf16[1,8,32,128]{3,2,1,0:T(8,128)(2,1)}, bf16[1,8,32,128]{3,2,1,0:T(8,128)(2,1)S(1)}, u32[]{:S(2)}, u32[]{:S(2)}) collective-permute-start(bf16[1,8,32,128]{3,2,1,0:T(8,128)(2,1)} %param.5), channel_id=1, source_target_pairs={{4,8},{5,136},{6,264},{7,392},{8,4},{9,132},{10,260},{11,388},{12,... | collective-permute-start | bytes 196616 | tf_op jit(solution)/shard_map/ppermute | solution.py:284
  13.4 27.1 %all-to-all-start = ((bf16[4,2,8,32,128]{4,3,2,1,0:T(8,128)(2,1)}), bf16[4,2,8,32,128]{4,3,2,1,0:T(8,128)(2,1)S(1)}, u32[]{:S(2)}, u32[]{:S(2)}) async-start(bf16[4,2,8,32,128]{4,3,2,1,0:T(8,128)(2,1)} %broadcast_in_dim.2), calls=%async_computation | async-start | bytes 1048576 | tf_op jit(solution)/shard_map/all_to_all | solution.py:257
  37.0 3.4 %collective-permute-start.3 = (bf16[32,32,128]{2,1,0:T(8,128)(2,1)S(1)}, bf16[32,32,128]{2,1,0:T(8,128)(2,1)S(1)}, u32[]{:S(2)}, u32[]{:S(2)}) collective-permute-start(bf16[32,32,128]{2,1,0:T(8,128)(2,1)S(1)} %slice_bitcast_fusion), channel_id=1, source_target_pairs={{0,4},{4,0},{1,5},{5,1},{2,6},{6,2},{3,7},{7,3},{8,12},{12,8},{9,1... | collective-permute-start | bytes 786440 | tf_op jit(solution)/shard_map/ppermute | solution.py:291
  42.1 4.4 %collective-permute-start.4 = (f32[1792,128]{1,0:T(8,128)S(1)}, f32[1792,128]{1,0:T(8,128)S(1)}, u32[]{:S(2)}, u32[]{:S(2)}) collective-permute-start(f32[1792,128]{1,0:T(8,128)S(1)} %get-tuple-element.53), channel_id=1, source_target_pairs={{0,4},{4,0},{1,5},{5,1},{2,6},{6,2},{3,7},{7,3},{8,12},{12,8},{9,1... | collective-permute-start | bytes 2752520 | tf_op jit(solution)/shard_map/ppermute | solution.py:294
  44.1 3.4 %collective-permute-start.5 = (bf16[32,32,128]{2,1,0:T(8,128)(2,1)S(1)}, bf16[32,32,128]{2,1,0:T(8,128)(2,1)S(1)}, u32[]{:S(2)}, u32[]{:S(2)}) collective-permute-start(bf16[32,32,128]{2,1,0:T(8,128)(2,1)S(1)} %get-tuple-element.55), channel_id=1, source_target_pairs={{0,4},{4,0},{1,5},{5,1},{2,6},{6,2},{3,7},{7,3},{8,12},{12,8},{9,1... | collective-permute-start | bytes 786440 | tf_op jit(solution)/shard_map/ppermute | solution.py:295
  46.4 16.5 %copy-start = (bf16[27,128,128]{2,1,0:T(8,128)(2,1)S(1)}, bf16[27,128,128]{2,1,0:T(8,128)(2,1)}, u32[]{:S(2)}) copy-start(bf16[27,128,128]{2,1,0:T(8,128)(2,1)} %weight.3) | copy-start | bytes 2654212
  47.5 28.4 %all-to-all-start.1 = ((f32[4,448,128]{2,1,0:T(8,128)}), f32[4,448,128]{2,1,0:T(8,128)S(1)}, u32[]{:S(2)}, u32[]{:S(2)}) async-start(f32[4,448,128]{2,1,0:T(8,128)} %bitcast.2), calls=%async_computation.1 | async-start | bytes 1835008 | tf_op jit(solution)/shard_map/all_to_all | solution.py:257
  65.7 0.6 copy-start.1
  66.3 9.7 %collective-permute-start.6 = (f32[256,128]{1,0:T(8,128)}, f32[256,128]{1,0:T(8,128)S(1)}, u32[]{:S(2)}, u32[]{:S(2)}) collective-permute-start(f32[256,128]{1,0:T(8,128)} %get-tuple-element.59), channel_id=1, source_target_pairs={{0,1},{1,2},{2,3},{3,0},{4,5},{5,6},{6,7},{7,4},{8,9},{9,10},{10,1... | collective-permute-start | bytes 393224 | tf_op jit(solution)/shard_map/ppermute | solution.py:262
  69.6 8.8 %collective-permute-start.7 = (f32[256,128]{1,0:T(8,128)}, f32[256,128]{1,0:T(8,128)S(1)}, u32[]{:S(2)}, u32[]{:S(2)}) collective-permute-start(f32[256,128]{1,0:T(8,128)} %get-tuple-element.61), channel_id=1, source_target_pairs={{0,3},{1,0},{2,1},{3,2},{4,7},{5,4},{6,5},{7,6},{8,11},{9,8},{10,9... | collective-permute-start | bytes 393224 | tf_op jit(solution)/shard_map/ppermute | solution.py:262
  78.4 21.0 %collective-permute-start.8 = (f32[448,128]{1,0:T(8,128)S(1)}, f32[448,128]{1,0:T(8,128)S(1)}, u32[]{:S(2)}, u32[]{:S(2)}) collective-permute-start(f32[448,128]{1,0:T(8,128)S(1)} %shard_map.59), channel_id=1, source_target_pairs={{0,32},{4,100},{32,0},{36,68},{64,96},{68,36},{96,64},{100,4},{1,3... | collective-permute-start | bytes 688136 | tf_op jit(solution)/shard_map/ppermute | solution.py:307
  93.7 7.2 %collective-permute-start.10 = (f32[256,128]{1,0:T(8,128)S(1)}, f32[256,128]{1,0:T(8,128)S(1)}, u32[]{:S(2)}, u32[]{:S(2)}) collective-permute-start(f32[256,128]{1,0:T(8,128)S(1)} %get-tuple-element.71), channel_id=1, source_target_pairs={{0,256},{128,384},{256,0},{384,128},{1,257},{129,385},{257,1},{385... | collective-permute-start | bytes 393224 | tf_op jit(solution)/shard_map/ppermute | solution.py:262
  96.8 6.9 %collective-permute-start.9 = (f32[256,128]{1,0:T(8,128)S(1)}, f32[256,128]{1,0:T(8,128)S(1)}, u32[]{:S(2)}, u32[]{:S(2)}) collective-permute-start(f32[256,128]{1,0:T(8,128)S(1)} %get-tuple-element.70), channel_id=1, source_target_pairs={{0,128},{128,256},{256,384},{384,0},{1,129},{129,257},{257,385},{3... | collective-permute-start | bytes 393224 | tf_op jit(solution)/shard_map/ppermute | solution.py:262
  103.7 22.7 %copy-start.2 = (f32[256,128]{1,0:T(8,128)S(1)}, f32[256,128]{1,0:T(8,128)}, u32[]{:S(2)}) copy-start(f32[256,128]{1,0:T(8,128)} %copy-done.1) | copy-start | bytes 393220
  103.7 17.9 %collective-permute-start.11 = (f32[448,128]{1,0:T(8,128)S(1)}, f32[448,128]{1,0:T(8,128)S(1)}, u32[]{:S(2)}, u32[]{:S(2)}) collective-permute-start(f32[448,128]{1,0:T(8,128)S(1)} %add.21.left), channel_id=1, source_target_pairs={{0,96},{4,36},{32,64},{36,4},{64,32},{68,100},{96,0},{100,68},{1,9... | collective-permute-start | bytes 688136 | tf_op jit(solution)/shard_map/ppermute | solution.py:315
  105.7 16.8 %collective-permute-start.12 = (f32[256,128]{1,0:T(8,128)S(1)}, f32[256,128]{1,0:T(8,128)S(1)}, u32[]{:S(2)}, u32[]{:S(2)}) collective-permute-start(f32[256,128]{1,0:T(8,128)S(1)} %get-tuple-element.77), channel_id=1, source_target_pairs={{0,384},{128,0},{256,128},{384,256},{1,385},{129,1},{257,129},{385... | collective-permute-start | bytes 393224 | tf_op jit(solution)/shard_map/ppermute | solution.py:262
  122.5 16.2 %all-to-all-start.2 = ((f32[4,448,128]{2,1,0:T(8,128)}), f32[4,448,128]{2,1,0:T(8,128)S(1)}, u32[]{:S(2)}, u32[]{:S(2)}) async-start(f32[4,448,128]{2,1,0:T(8,128)} %shard_map.60), calls=%async_computation.2 | async-start | bytes 1835008 | tf_op jit(solution)/shard_map/all_to_all | solution.py:257
  126.4 10.2 %collective-permute-start.14 = (f32[256,128]{1,0:T(8,128)S(1)}, f32[256,128]{1,0:T(8,128)S(1)}, u32[]{:S(2)}, u32[]{:S(2)}) collective-permute-start(f32[256,128]{1,0:T(8,128)S(1)} %copy-done.2), channel_id=1, source_target_pairs={{0,2},{1,3},{2,0},{3,1},{4,6},{5,7},{6,4},{7,5},{8,10},{9,11},{10,... | collective-permute-start | bytes 393224 | tf_op jit(solution)/shard_map/ppermute | solution.py:262
  128.3 0.7 collective-permute-start.13
  138.8 4.4 %collective-permute-start.15 = (f32[1792,128]{1,0:T(8,128)S(1)}, f32[1792,128]{1,0:T(8,128)S(1)}, u32[]{:S(2)}, u32[]{:S(2)}) collective-permute-start(f32[1792,128]{1,0:T(8,128)S(1)} %bitcast.11), channel_id=1, source_target_pairs={{0,4},{4,0},{1,5},{5,1},{2,6},{6,2},{3,7},{7,3},{8,12},{12,8},{9,1... | collective-permute-start | bytes 2752520 | tf_op jit(solution)/shard_map/ppermute | solution.py:328

commit v15 on v14

--- a/solution.py
+++ b/solution.py
@@ -240,6 +240,24 @@
     )(block)
 
 
+def pack_kernel(own, outer, out):
+    for copy in range(out.shape[0]):
+        out[copy, 0:1] = own[...]
+        out[copy, 1:2] = outer[...]
+
+
+def packed(own, outer, copies):
+    return pl.pallas_call(
+        pack_kernel,
+        out_shape=jax.ShapeDtypeStruct((copies, 2, *own.shape[1:]), own.dtype),
+        in_specs=[VMEM, VMEM],
+        out_specs=VMEM,
+        compiler_params=pltpu.CompilerParams(vmem_limit_bytes=8 << 20),
+        cost_estimate=pl.CostEstimate(flops=0, bytes_accessed=1 << 19, transcendentals=0),
+        name="pack",
+    )(own, outer)
+
+
 def joined(core, mine, other, shape):
     return pl.pallas_call(
         join_kernel,
@@ -283,10 +301,8 @@
     outer = lax.ppermute(activations, AXES, neighbour(sizes, True, False))
     grads = [lax.ppermute(output_grad, AXES, neighbour(sizes, far, True)) for far in (False, True)]
     grad = jnp.concatenate(grads, axis=0)
-    data = jnp.concatenate([activations, outer], axis=0)
-    data = jnp.broadcast_to(data[None], (spaces, *data.shape))
-    grad, data = lax.optimization_barrier((grad, data))
-    data = exchange(data, "space")
+    grad, outer = lax.optimization_barrier((grad, outer))
+    data = exchange(packed(activations, outer, spaces), "space")
     grad = lax.all_gather(grad, "chan", axis=1, tiled=True)
     grad_inner = lax.ppermute(grad[0], "core", swap)
 

time: 146 us -> 143 us (0.979)
  starting transfers between devices: 80.1 us -> 77.4 us
    ppermute x1, waiting for transfers between devices: 0.01 us -> 3.63 us  [shards(): outer = lax.ppermute(activations, AXES, neighbour(sizes, True, False))]
    ppermute x2, waiting for transfers between devices: 2.99 us -> 0.21 us  [shards(): lax.ppermute(output_grad, AXES, neighbour(sizes, far, True))]
    ppermute x2, starting transfers between devices: 3.41 us -> 6.08 us  [shards(): lax.ppermute(output_grad, AXES, neighbour(sizes, far, True))]
    ppermute x1, starting transfers between devices: 4.59 us -> 1.92 us  [shards(): outer = lax.ppermute(activations, AXES, neighbour(sizes, True, False))]
    all_to_all x3, starting transfers between devices: 31.5 us -> 29.3 us  [exchange(): return lax.all_to_all(block, axis, split_axis=0, concat_axis=0, tiled=True)]
  transfers between devices with their start and end apart: 19 -> 19, of which waited for: 11 -> 12; matrix products, arithmetic and copies ran while one was open for 1% -> 1% of each run, Pallas kernels for 5% -> 5%
where the time goes in v15:
time: 143 us; the launch traced here: 141 us
  starting transfers between devices  77.4 us (54%)
  waiting for transfers between devices  38.6 us (27%)
  Pallas kernels  11.2 us (8%)
  blocking collectives  10.8 us (8%)
  local copies, waits for them, and re-layouts  1.52 us (1%)
    all_to_all x3, starting transfers between devices, exchange(): return lax.all_to_all(block, axis, split_axis=0, concat_axis=0, tiled=True)  29.3 us
    ppermute x6, starting transfers between devices, rotate(): lax.ppermute(term, axis, [(i, (i + step) % count) for i in range(count)])  16.4 us
    ppermute x6, waiting for transfers between devices, rotate(): lax.ppermute(term, axis, [(i, (i + step) % count) for i in range(count)])  13.8 us
    ppermute x1, waiting for transfers between devices, shards(): moved = lax.ppermute(pair, ('zhi', 'core'), doubling(1))  12.8 us
    ppermute x1, starting transfers between devices, shards(): moved = lax.ppermute(quarter, ('zhi', 'core'), doubling(0))  12.2 us
    all_gather x1, blocking collectives, shards(): grad = lax.all_gather(grad, 'chan', axis=1, tiled=True)  10.8 us
    ppermute x2, starting transfers between devices, shards(): lax.ppermute(output_grad, AXES, neighbour(sizes, far, True))  6.08 us
    pallas_call x2, Pallas kernels, convolve(): pl.pallas_call(functools.partial(conv_kernel, backward), out_shape=[jax.S...  4.9 us
  transfers between devices with their start and end apart: 19, of which 12 were waited for; matrix products, arithmetic and copies ran while one was open for 1% of the time, Pallas kernels for 5%

profile of v15, /device:TPU:1, one launch (start us, length us, event | category | flops | bytes accessed | tf_op | source)
XLA Modules:
  0.0 141.2 jit_solution(10980058334642334364)
XLA Ops:
  0.6 1.5 %collective-permute-start = (bf16[1,8,32,128]{3,2,1,0:T(8,128)(2,1)}, bf16[1,8,32,128]{3,2,1,0:T(8,128)(2,1)S(1)}, u32[]{:S(2)}, u32[]{:S(2)}) collective-permute-start(bf16[1,8,32,128]{3,2,1,0:T(8,128)(2,1)} %param.5), channel_id=1, source_target_pairs={{0,0},{1,128},{2,256},{3,384},{4,4},{5,132},{6,260},{7,388},{8,8},... | collective-permute-start | bytes 196616 | tf_op jit(solution)/shard_map/ppermute | solution.py:302
  2.1 4.6 %collective-permute-start.1 = (bf16[1,8,32,128]{3,2,1,0:T(8,128)(2,1)}, bf16[1,8,32,128]{3,2,1,0:T(8,128)(2,1)S(1)}, u32[]{:S(2)}, u32[]{:S(2)}) collective-permute-start(bf16[1,8,32,128]{3,2,1,0:T(8,128)(2,1)} %param.5), channel_id=1, source_target_pairs={{4,8},{5,136},{6,264},{7,392},{8,4},{9,132},{10,260},{11,388},{12,... | collective-permute-start | bytes 196616 | tf_op jit(solution)/shard_map/ppermute | solution.py:302
  6.7 1.9 %collective-permute-start.2 = (bf16[1,8,32,128]{3,2,1,0:T(8,128)(2,1)}, bf16[1,8,32,128]{3,2,1,0:T(8,128)(2,1)S(1)}, u32[]{:S(2)}, u32[]{:S(2)}) collective-permute-start(bf16[1,8,32,128]{3,2,1,0:T(8,128)(2,1)} %own.1), channel_id=1, source_target_pairs={{4,8},{5,9},{6,10},{7,11},{8,4},{9,5},{10,6},{11,7},{12,16},{13,17... | collective-permute-start | bytes 196616 | tf_op jit(solution)/shard_map/ppermute | solution.py:301
  8.6 0.0 collective-permute-done
  8.7 0.2 collective-permute-done.1
  8.9 3.6 %collective-permute-done.2.outer = bf16[1,8,32,128]{3,2,1,0:T(8,128)(2,1)S(1)} collective-permute-done((bf16[1,8,32,128]{3,2,1,0:T(8,128)(2,1)}, bf16[1,8,32,128]{3,2,1,0:T(8,128)(2,1)S(1)}, u32[]{:S(2)}, u32[]{:S(2)}) %collective-permute-start.2) | collective-permute-done | bytes 65568 | tf_op jit(solution)/shard_map/ppermute | solution.py:301
  12.5 0.0 copy-start
  12.5 0.8 copy-done
  13.4 0.9 pack.1
  14.2 11.4 %all-to-all-start = ((bf16[4,2,8,32,128]{4,3,2,1,0:T(8,128)(2,1)}), bf16[4,2,8,32,128]{4,3,2,1,0:T(8,128)(2,1)S(1)}, u32[]{:S(2)}, u32[]{:S(2)}) async-start(bf16[4,2,8,32,128]{4,3,2,1,0:T(8,128)(2,1)} %pack.1), calls=%async_computation | async-start | bytes 1048576 | tf_op jit(solution)/shard_map/all_to_all | solution.py:275
  25.6 10.8 %all_gather.3.pair = bf16[2,32,32,128]{3,2,1,0:T(8,128)(2,1)S(1)} all-gather(bf16[2,8,32,128]{3,2,1,0:T(8,128)(2,1)S(1)} %pad_maximum_fusion), channel_id=1, replica_groups=mesh['chan'=4,'zhi'=4,'ring'=4,'core'=2,'space'=4] {'chan'}, dimensions={1}, use_global_device_ids=true | all-gather | bytes 655360 | tf_op jit(solution)/shard_map/all_gather | solution.py:306
  36.4 1.9 %collective-permute-start.3 = (bf16[32,32,128]{2,1,0:T(8,128)(2,1)S(1)}, bf16[32,32,128]{2,1,0:T(8,128)(2,1)S(1)}, u32[]{:S(2)}, u32[]{:S(2)}) collective-permute-start(bf16[32,32,128]{2,1,0:T(8,128)(2,1)S(1)} %slice_bitcast_fusion), channel_id=1, source_target_pairs={{0,4},{4,0},{1,5},{5,1},{2,6},{6,2},{3,7},{7,3},{8,12},{12,8},{9,1... | collective-permute-start | bytes 786440 | tf_op jit(solution)/shard_map/ppermute | solution.py:307
  38.4 1.5 %collective-permute-done.3.inner = bf16[32,32,128]{2,1,0:T(8,128)(2,1)S(1)} collective-permute-done((bf16[32,32,128]{2,1,0:T(8,128)(2,1)S(1)}, bf16[32,32,128]{2,1,0:T(8,128)(2,1)S(1)}, u32[]{:S(2)}, u32[]{:S(2)}) %collective-permute-start.3) | collective-permute-done | bytes 262176 | tf_op jit(solution)/shard_map/ppermute | solution.py:307
  39.9 0.0 all-to-all-done.data.pair
  39.9 1.6 %filter_grad.1 = (f32[1792,128]{1,0:T(8,128)S(1)}, f32[1792,128]{1,0:T(8,128)S(1)}, bf16[32,32,128]{2,1,0:T(8,128)(2,1)S(1)}) custom-call(s32[1]{0:T(128)} %bitcast.core, bf16[4,2,8,32,128]{4,3,2,1,0:T(8,128)(2,1)S(1)} %all-to-all-done.data.pair, bf16[2,32,32,128]{3,2,1,0:T(8,128)(2,1)S(1)} %all_gather.3.pair, ...), custom_call_target="tpu_custom_call" | custom-call | flops 905969664 | bytes 3145728 | tf_op jit(solution)/shard_map/filter_grad/pallas_call | solution.py:160
  41.5 2.0 %collective-permute-start.4 = (f32[1792,128]{1,0:T(8,128)S(1)}, f32[1792,128]{1,0:T(8,128)S(1)}, u32[]{:S(2)}, u32[]{:S(2)}) collective-permute-start(f32[1792,128]{1,0:T(8,128)S(1)} %get-tuple-element.53), channel_id=1, source_target_pairs={{0,4},{4,0},{1,5},{5,1},{2,6},{6,2},{3,7},{7,3},{8,12},{12,8},{9,1... | collective-permute-start | bytes 2752520 | tf_op jit(solution)/shard_map/ppermute | solution.py:310
  43.5 2.3 %collective-permute-start.5 = (bf16[32,32,128]{2,1,0:T(8,128)(2,1)S(1)}, bf16[32,32,128]{2,1,0:T(8,128)(2,1)S(1)}, u32[]{:S(2)}, u32[]{:S(2)}) collective-permute-start(bf16[32,32,128]{2,1,0:T(8,128)(2,1)S(1)} %get-tuple-element.55), channel_id=1, source_target_pairs={{0,4},{4,0},{1,5},{5,1},{2,6},{6,2},{3,7},{7,3},{8,12},{12,8},{9,1... | collective-permute-start | bytes 786440 | tf_op jit(solution)/shard_map/ppermute | solution.py:311
  45.8 0.0 collective-permute-done.4.right
  45.8 0.0 copy-start.1
  45.8 1.0 shard_map.58
  46.9 0.1 collective-permute-done.5.inner
  46.9 14.1 %all-to-all-start.1 = ((f32[4,448,128]{2,1,0:T(8,128)}), f32[4,448,128]{2,1,0:T(8,128)S(1)}, u32[]{:S(2)}, u32[]{:S(2)}) async-start(f32[4,448,128]{2,1,0:T(8,128)} %bitcast.2), calls=%async_computation.1 | async-start | bytes 1835008 | tf_op jit(solution)/shard_map/all_to_all | solution.py:275
  61.1 0.1 pad_add_fusion.place
  61.1 0.0 copy-done.1
  61.1 2.8 %input_grad.1 = (f32[256,128]{1,0:T(8,128)S(1)}, f32[256,128]{1,0:T(8,128)}, f32[256,128]{1,0:T(8,128)S(1)}, f32[256,128]{1,0:T(8,128)}) custom-call(s32[2]{0:T(128)S(1)} %pad_add_fusion.place, bf16[2,32,32,128]{3,2,1,0:T(8,128)(2,1)S(1)} %all_gather.3.pair, bf16[32,32,128]{2,1,0:T(8,128)(2,1)S(1)} %collective-permute-done.3.inner, ...), custom_call_target="tpu_custom_call" | custom-call | flops 905969664 | bytes 3145728 | tf_op jit(solution)/shard_map/input_grad/pallas_call | solution.py:106
  63.9 0.0 copy-start.2
  63.9 0.6 copy-done.2
  64.6 3.4 %collective-permute-start.6 = (f32[256,128]{1,0:T(8,128)}, f32[256,128]{1,0:T(8,128)S(1)}, u32[]{:S(2)}, u32[]{:S(2)}) collective-permute-start(f32[256,128]{1,0:T(8,128)} %get-tuple-element.59), channel_id=1, source_target_pairs={{0,1},{1,2},{2,3},{3,0},{4,5},{5,6},{6,7},{7,4},{8,9},{9,10},{10,1... | collective-permute-start | bytes 393224 | tf_op jit(solution)/shard_map/ppermute | solution.py:280
  68.0 3.7 %collective-permute-start.7 = (f32[256,128]{1,0:T(8,128)}, f32[256,128]{1,0:T(8,128)S(1)}, u32[]{:S(2)}, u32[]{:S(2)}) collective-permute-start(f32[256,128]{1,0:T(8,128)} %get-tuple-element.61), channel_id=1, source_target_pairs={{0,3},{1,0},{2,1},{3,2},{4,7},{5,4},{6,5},{7,6},{8,11},{9,8},{10,9... | collective-permute-start | bytes 393224 | tf_op jit(solution)/shard_map/ppermute | solution.py:280
  71.7 2.5 %all-to-all-done.1.parts = f32[4,448,128]{2,1,0:T(8,128)S(1)} async-done(((f32[4,448,128]{2,1,0:T(8,128)}), f32[4,448,128]{2,1,0:T(8,128)S(1)}, u32[]{:S(2)}, u32[]{:S(2)}) %all-to-all-start.1) | async-done | bytes 917536 | tf_op jit(solution)/shard_map/all_to_all | solution.py:275
  74.2 0.0 collective-permute-done.6
  74.2 2.4 %collective-permute-done.7 = f32[256,128]{1,0:T(8,128)S(1)} collective-permute-done((f32[256,128]{1,0:T(8,128)}, f32[256,128]{1,0:T(8,128)S(1)}, u32[]{:S(2)}, u32[]{:S(2)}) %collective-permute-start.7) | collective-permute-done | bytes 131104 | tf_op jit(solution)/shard_map/ppermute | solution.py:280
  76.7 12.2 %collective-permute-start.8 = (f32[448,128]{1,0:T(8,128)S(1)}, f32[448,128]{1,0:T(8,128)S(1)}, u32[]{:S(2)}, u32[]{:S(2)}) collective-permute-start(f32[448,128]{1,0:T(8,128)S(1)} %shard_map.59), channel_id=1, source_target_pairs={{0,32},{4,100},{32,0},{36,68},{64,96},{68,36},{96,64},{100,4},{1,3... | collective-permute-start | bytes 688136 | tf_op jit(solution)/shard_map/ppermute | solution.py:323
  88.8 0.1 pad_add_fusion.1.place
  88.9 2.1 %forward.1 = (f32[256,128]{1,0:T(8,128)S(1)}, f32[256,128]{1,0:T(8,128)S(1)}, f32[256,128]{1,0:T(8,128)S(1)}, f32[256,128]{1,0:T(8,128)S(1)}) custom-call(s32[2]{0:T(128)S(1)} %pad_add_fusion.1.place, bf16[4,2,8,32,128]{4,3,2,1,0:T(8,128)(2,1)S(1)} %all-to-all-done.data.pair, bf16[32,32,128]{2,1,0:T(8,128)(2,1)S(1)} %collective-permute-done.5.inner, ...), custom_call_target="tpu_custom_call" | custom-call | flops 905969664 | bytes 3145728 | tf_op jit(solution)/shard_map/forward/pallas_call | solution.py:106
  91.0 3.1 %collective-permute-start.10 = (f32[256,128]{1,0:T(8,128)S(1)}, f32[256,128]{1,0:T(8,128)S(1)}, u32[]{:S(2)}, u32[]{:S(2)}) collective-permute-start(f32[256,128]{1,0:T(8,128)S(1)} %get-tuple-element.71), channel_id=1, source_target_pairs={{0,256},{128,384},{256,0},{384,128},{1,257},{129,385},{257,1},{385... | collective-permute-start | bytes 393224 | tf_op jit(solution)/shard_map/ppermute | solution.py:280
  94.1 1.9 %collective-permute-start.9 = (f32[256,128]{1,0:T(8,128)S(1)}, f32[256,128]{1,0:T(8,128)S(1)}, u32[]{:S(2)}, u32[]{:S(2)}) collective-permute-start(f32[256,128]{1,0:T(8,128)S(1)} %get-tuple-element.70), channel_id=1, source_target_pairs={{0,128},{128,256},{256,384},{384,0},{1,129},{129,257},{257,385},{3... | collective-permute-start | bytes 393224 | tf_op jit(solution)/shard_map/ppermute | solution.py:280
  96.0 0.0 collective-permute-done.8
  96.1 2.7 %collective-permute-done.10 = f32[256,128]{1,0:T(8,128)S(1)} collective-permute-done((f32[256,128]{1,0:T(8,128)S(1)}, f32[256,128]{1,0:T(8,128)S(1)}, u32[]{:S(2)}, u32[]{:S(2)}) %collective-permute-start.10) | collective-permute-done | bytes 131104 | tf_op jit(solution)/shard_map/ppermute | solution.py:280
  98.7 2.3 %collective-permute-done.9 = f32[256,128]{1,0:T(8,128)S(1)} collective-permute-done((f32[256,128]{1,0:T(8,128)S(1)}, f32[256,128]{1,0:T(8,128)S(1)}, u32[]{:S(2)}, u32[]{:S(2)}) %collective-permute-start.9) | collective-permute-done | bytes 131104 | tf_op jit(solution)/shard_map/ppermute | solution.py:280
  101.0 0.0 copy-start.3
  101.0 2.7 %collective-permute-start.11 = (f32[448,128]{1,0:T(8,128)S(1)}, f32[448,128]{1,0:T(8,128)S(1)}, u32[]{:S(2)}, u32[]{:S(2)}) collective-permute-start(f32[448,128]{1,0:T(8,128)S(1)} %add.21.left), channel_id=1, source_target_pairs={{0,96},{4,36},{32,64},{36,4},{64,32},{68,100},{96,0},{100,68},{1,9... | collective-permute-start | bytes 688136 | tf_op jit(solution)/shard_map/ppermute | solution.py:331
  103.7 2.4 %collective-permute-start.12 = (f32[256,128]{1,0:T(8,128)S(1)}, f32[256,128]{1,0:T(8,128)S(1)}, u32[]{:S(2)}, u32[]{:S(2)}) collective-permute-start(f32[256,128]{1,0:T(8,128)S(1)} %get-tuple-element.77), channel_id=1, source_target_pairs={{0,384},{128,0},{256,128},{384,256},{1,385},{129,1},{257,129},{385... | collective-permute-start | bytes 393224 | tf_op jit(solution)/shard_map/ppermute | solution.py:280
  106.1 12.8 %collective-permute-done.11.right = f32[448,128]{1,0:T(8,128)S(1)} collective-permute-done((f32[448,128]{1,0:T(8,128)S(1)}, f32[448,128]{1,0:T(8,128)S(1)}, u32[]{:S(2)}, u32[]{:S(2)}) %collective-permute-start.11) | collective-permute-done | bytes 229408 | tf_op jit(solution)/shard_map/ppermute | solution.py:331
  118.9 1.0 shard_map.60
  119.9 0.0 collective-permute-done.12
  119.9 3.8 %all-to-all-start.2 = ((f32[4,448,128]{2,1,0:T(8,128)}), f32[4,448,128]{2,1,0:T(8,128)S(1)}, u32[]{:S(2)}, u32[]{:S(2)}) async-start(f32[4,448,128]{2,1,0:T(8,128)} %shard_map.60), calls=%async_computation.2 | async-start | bytes 1835008 | tf_op jit(solution)/shard_map/all_to_all | solution.py:275
  123.7 0.0 copy-done.3
  123.7 1.9 %collective-permute-start.14 = (f32[256,128]{1,0:T(8,128)S(1)}, f32[256,128]{1,0:T(8,128)S(1)}, u32[]{:S(2)}, u32[]{:S(2)}) collective-permute-start(f32[256,128]{1,0:T(8,128)S(1)} %copy-done.3), channel_id=1, source_target_pairs={{0,2},{1,3},{2,0},{3,1},{4,6},{5,7},{6,4},{7,5},{8,10},{9,11},{10,... | collective-permute-start | bytes 393224 | tf_op jit(solution)/shard_map/ppermute | solution.py:280
  125.7 0.7 collective-permute-start.13
  126.3 0.0 collective-permute-done.13.block
  126.4 0.6 publish.1
  127.0 6.4 %collective-permute-done.14 = f32[256,128]{1,0:T(8,128)S(1)} collective-permute-done((f32[256,128]{1,0:T(8,128)S(1)}, f32[256,128]{1,0:T(8,128)S(1)}, u32[]{:S(2)}, u32[]{:S(2)}) %collective-permute-start.14) | collective-permute-done | bytes 131104 | tf_op jit(solution)/shard_map/ppermute | solution.py:280
  133.4 2.3 %all-to-all-done.2 = f32[4,448,128]{2,1,0:T(8,128)S(1)} async-done(((f32[4,448,128]{2,1,0:T(8,128)}), f32[4,448,128]{2,1,0:T(8,128)S(1)}, u32[]{:S(2)}, u32[]{:S(2)}) %all-to-all-start.2) | async-done | bytes 917536 | tf_op jit(solution)/shard_map/all_to_all | solution.py:275
  135.7 1.9 %collective-permute-start.15 = (f32[1792,128]{1,0:T(8,128)S(1)}, f32[1792,128]{1,0:T(8,128)S(1)}, u32[]{:S(2)}, u32[]{:S(2)}) collective-permute-start(f32[1792,128]{1,0:T(8,128)S(1)} %bitcast.11), channel_id=1, source_target_pairs={{0,4},{4,0},{1,5},{5,1},{2,6},{6,2},{3,7},{7,3},{8,12},{12,8},{9,1... | collective-permute-start | bytes 2752520 | tf_op jit(solution)/shard_map/ppermute | solution.py:344
  137.6 0.7 add_convert_fusion
  138.2 1.8 %collective-permute-done.15 = f32[1792,128]{1,0:T(8,128)S(1)} collective-permute-done((f32[1792,128]{1,0:T(8,128)S(1)}, f32[1792,128]{1,0:T(8,128)S(1)}, u32[]{:S(2)}, u32[]{:S(2)}) %collective-permute-start.15) | collective-permute-done | bytes 917536 | tf_op jit(solution)/shard_map/ppermute | solution.py:344
  140.0 1.2 join.1
  (5 shorter events, 0.1 us)
Async XLA Ops:
  0.6 8.0 %collective-permute-start = (bf16[1,8,32,128]{3,2,1,0:T(8,128)(2,1)}, bf16[1,8,32,128]{3,2,1,0:T(8,128)(2,1)S(1)}, u32[]{:S(2)}, u32[]{:S(2)}) collective-permute-start(bf16[1,8,32,128]{3,2,1,0:T(8,128)(2,1)} %param.5), channel_id=1, source_target_pairs={{0,0},{1,128},{2,256},{3,384},{4,4},{5,132},{6,260},{7,388},{8,8},... | collective-permute-start | bytes 196616 | tf_op jit(solution)/shard_map/ppermute | solution.py:302
  2.1 6.7 %collective-permute-start.1 = (bf16[1,8,32,128]{3,2,1,0:T(8,128)(2,1)}, bf16[1,8,32,128]{3,2,1,0:T(8,128)(2,1)S(1)}, u32[]{:S(2)}, u32[]{:S(2)}) collective-permute-start(bf16[1,8,32,128]{3,2,1,0:T(8,128)(2,1)} %param.5), channel_id=1, source_target_pairs={{4,8},{5,136},{6,264},{7,392},{8,4},{9,132},{10,260},{11,388},{12,... | collective-permute-start | bytes 196616 | tf_op jit(solution)/shard_map/ppermute | solution.py:302
  6.7 5.8 %collective-permute-start.2 = (bf16[1,8,32,128]{3,2,1,0:T(8,128)(2,1)}, bf16[1,8,32,128]{3,2,1,0:T(8,128)(2,1)S(1)}, u32[]{:S(2)}, u32[]{:S(2)}) collective-permute-start(bf16[1,8,32,128]{3,2,1,0:T(8,128)(2,1)} %own.1), channel_id=1, source_target_pairs={{4,8},{5,9},{6,10},{7,11},{8,4},{9,5},{10,6},{11,7},{12,16},{13,17... | collective-permute-start | bytes 196616 | tf_op jit(solution)/shard_map/ppermute | solution.py:301
  12.5 0.8 copy-start
  14.2 25.7 %all-to-all-start = ((bf16[4,2,8,32,128]{4,3,2,1,0:T(8,128)(2,1)}), bf16[4,2,8,32,128]{4,3,2,1,0:T(8,128)(2,1)S(1)}, u32[]{:S(2)}, u32[]{:S(2)}) async-start(bf16[4,2,8,32,128]{4,3,2,1,0:T(8,128)(2,1)} %pack.1), calls=%async_computation | async-start | bytes 1048576 | tf_op jit(solution)/shard_map/all_to_all | solution.py:275
  36.4 3.4 %collective-permute-start.3 = (bf16[32,32,128]{2,1,0:T(8,128)(2,1)S(1)}, bf16[32,32,128]{2,1,0:T(8,128)(2,1)S(1)}, u32[]{:S(2)}, u32[]{:S(2)}) collective-permute-start(bf16[32,32,128]{2,1,0:T(8,128)(2,1)S(1)} %slice_bitcast_fusion), channel_id=1, source_target_pairs={{0,4},{4,0},{1,5},{5,1},{2,6},{6,2},{3,7},{7,3},{8,12},{12,8},{9,1... | collective-permute-start | bytes 786440 | tf_op jit(solution)/shard_map/ppermute | solution.py:307
  41.5 4.4 %collective-permute-start.4 = (f32[1792,128]{1,0:T(8,128)S(1)}, f32[1792,128]{1,0:T(8,128)S(1)}, u32[]{:S(2)}, u32[]{:S(2)}) collective-permute-start(f32[1792,128]{1,0:T(8,128)S(1)} %get-tuple-element.53), channel_id=1, source_target_pairs={{0,4},{4,0},{1,5},{5,1},{2,6},{6,2},{3,7},{7,3},{8,12},{12,8},{9,1... | collective-permute-start | bytes 2752520 | tf_op jit(solution)/shard_map/ppermute | solution.py:310
  43.5 3.4 %collective-permute-start.5 = (bf16[32,32,128]{2,1,0:T(8,128)(2,1)S(1)}, bf16[32,32,128]{2,1,0:T(8,128)(2,1)S(1)}, u32[]{:S(2)}, u32[]{:S(2)}) collective-permute-start(bf16[32,32,128]{2,1,0:T(8,128)(2,1)S(1)} %get-tuple-element.55), channel_id=1, source_target_pairs={{0,4},{4,0},{1,5},{5,1},{2,6},{6,2},{3,7},{7,3},{8,12},{12,8},{9,1... | collective-permute-start | bytes 786440 | tf_op jit(solution)/shard_map/ppermute | solution.py:311
  45.8 15.3 %copy-start.1 = (bf16[27,128,128]{2,1,0:T(8,128)(2,1)S(1)}, bf16[27,128,128]{2,1,0:T(8,128)(2,1)}, u32[]{:S(2)}) copy-start(bf16[27,128,128]{2,1,0:T(8,128)(2,1)} %weight.3) | copy-start | bytes 2654212
  46.9 27.2 %all-to-all-start.1 = ((f32[4,448,128]{2,1,0:T(8,128)}), f32[4,448,128]{2,1,0:T(8,128)S(1)}, u32[]{:S(2)}, u32[]{:S(2)}) async-start(f32[4,448,128]{2,1,0:T(8,128)} %bitcast.2), calls=%async_computation.1 | async-start | bytes 1835008 | tf_op jit(solution)/shard_map/all_to_all | solution.py:275
  63.9 0.7 copy-start.2
  64.6 9.6 %collective-permute-start.6 = (f32[256,128]{1,0:T(8,128)}, f32[256,128]{1,0:T(8,128)S(1)}, u32[]{:S(2)}, u32[]{:S(2)}) collective-permute-start(f32[256,128]{1,0:T(8,128)} %get-tuple-element.59), channel_id=1, source_target_pairs={{0,1},{1,2},{2,3},{3,0},{4,5},{5,6},{6,7},{7,4},{8,9},{9,10},{10,1... | collective-permute-start | bytes 393224 | tf_op jit(solution)/shard_map/ppermute | solution.py:280
  68.0 8.7 %collective-permute-start.7 = (f32[256,128]{1,0:T(8,128)}, f32[256,128]{1,0:T(8,128)S(1)}, u32[]{:S(2)}, u32[]{:S(2)}) collective-permute-start(f32[256,128]{1,0:T(8,128)} %get-tuple-element.61), channel_id=1, source_target_pairs={{0,3},{1,0},{2,1},{3,2},{4,7},{5,4},{6,5},{7,6},{8,11},{9,8},{10,9... | collective-permute-start | bytes 393224 | tf_op jit(solution)/shard_map/ppermute | solution.py:280
  76.7 19.4 %collective-permute-start.8 = (f32[448,128]{1,0:T(8,128)S(1)}, f32[448,128]{1,0:T(8,128)S(1)}, u32[]{:S(2)}, u32[]{:S(2)}) collective-permute-start(f32[448,128]{1,0:T(8,128)S(1)} %shard_map.59), channel_id=1, source_target_pairs={{0,32},{4,100},{32,0},{36,68},{64,96},{68,36},{96,64},{100,4},{1,3... | collective-permute-start | bytes 688136 | tf_op jit(solution)/shard_map/ppermute | solution.py:323
  91.0 7.7 %collective-permute-start.10 = (f32[256,128]{1,0:T(8,128)S(1)}, f32[256,128]{1,0:T(8,128)S(1)}, u32[]{:S(2)}, u32[]{:S(2)}) collective-permute-start(f32[256,128]{1,0:T(8,128)S(1)} %get-tuple-element.71), channel_id=1, source_target_pairs={{0,256},{128,384},{256,0},{384,128},{1,257},{129,385},{257,1},{385... | collective-permute-start | bytes 393224 | tf_op jit(solution)/shard_map/ppermute | solution.py:280
  94.1 6.9 %collective-permute-start.9 = (f32[256,128]{1,0:T(8,128)S(1)}, f32[256,128]{1,0:T(8,128)S(1)}, u32[]{:S(2)}, u32[]{:S(2)}) collective-permute-start(f32[256,128]{1,0:T(8,128)S(1)} %get-tuple-element.70), channel_id=1, source_target_pairs={{0,128},{128,256},{256,384},{384,0},{1,129},{129,257},{257,385},{3... | collective-permute-start | bytes 393224 | tf_op jit(solution)/shard_map/ppermute | solution.py:280
  101.0 22.7 %copy-start.3 = (f32[256,128]{1,0:T(8,128)S(1)}, f32[256,128]{1,0:T(8,128)}, u32[]{:S(2)}) copy-start(f32[256,128]{1,0:T(8,128)} %copy-done.2) | copy-start | bytes 393220
  101.0 17.9 %collective-permute-start.11 = (f32[448,128]{1,0:T(8,128)S(1)}, f32[448,128]{1,0:T(8,128)S(1)}, u32[]{:S(2)}, u32[]{:S(2)}) collective-permute-start(f32[448,128]{1,0:T(8,128)S(1)} %add.21.left), channel_id=1, source_target_pairs={{0,96},{4,36},{32,64},{36,4},{64,32},{68,100},{96,0},{100,68},{1,9... | collective-permute-start | bytes 688136 | tf_op jit(solution)/shard_map/ppermute | solution.py:331
  103.7 16.2 %collective-permute-start.12 = (f32[256,128]{1,0:T(8,128)S(1)}, f32[256,128]{1,0:T(8,128)S(1)}, u32[]{:S(2)}, u32[]{:S(2)}) collective-permute-start(f32[256,128]{1,0:T(8,128)S(1)} %get-tuple-element.77), channel_id=1, source_target_pairs={{0,384},{128,0},{256,128},{384,256},{1,385},{129,1},{257,129},{385... | collective-permute-start | bytes 393224 | tf_op jit(solution)/shard_map/ppermute | solution.py:280
  119.9 15.7 %all-to-all-start.2 = ((f32[4,448,128]{2,1,0:T(8,128)}), f32[4,448,128]{2,1,0:T(8,128)S(1)}, u32[]{:S(2)}, u32[]{:S(2)}) async-start(f32[4,448,128]{2,1,0:T(8,128)} %shard_map.60), calls=%async_computation.2 | async-start | bytes 1835008 | tf_op jit(solution)/shard_map/all_to_all | solution.py:275
  123.7 9.6 %collective-permute-start.14 = (f32[256,128]{1,0:T(8,128)S(1)}, f32[256,128]{1,0:T(8,128)S(1)}, u32[]{:S(2)}, u32[]{:S(2)}) collective-permute-start(f32[256,128]{1,0:T(8,128)S(1)} %copy-done.3), channel_id=1, source_target_pairs={{0,2},{1,3},{2,0},{3,1},{4,6},{5,7},{6,4},{7,5},{8,10},{9,11},{10,... | collective-permute-start | bytes 393224 | tf_op jit(solution)/shard_map/ppermute | solution.py:280
  125.7 0.7 collective-permute-start.13
  135.7 4.4 %collective-permute-start.15 = (f32[1792,128]{1,0:T(8,128)S(1)}, f32[1792,128]{1,0:T(8,128)S(1)}, u32[]{:S(2)}, u32[]{:S(2)}) collective-permute-start(f32[1792,128]{1,0:T(8,128)S(1)} %bitcast.11), channel_id=1, source_target_pairs={{0,4},{4,0},{1,5},{5,1},{2,6},{6,2},{3,7},{7,3},{8,12},{12,8},{9,1... | collective-permute-start | bytes 2752520 | tf_op jit(solution)/shard_map/ppermute | solution.py:344

commit v16 on v15

--- a/solution.py
+++ b/solution.py
@@ -301,8 +301,8 @@
     outer = lax.ppermute(activations, AXES, neighbour(sizes, True, False))
     grads = [lax.ppermute(output_grad, AXES, neighbour(sizes, far, True)) for far in (False, True)]
     grad = jnp.concatenate(grads, axis=0)
-    grad, outer = lax.optimization_barrier((grad, outer))
-    data = exchange(packed(activations, outer, spaces), "space")
+    grad, outer, own = lax.optimization_barrier((grad, outer, published(activations)))
+    data = exchange(packed(own, outer, spaces), "space")
     grad = lax.all_gather(grad, "chan", axis=1, tiled=True)
     grad_inner = lax.ppermute(grad[0], "core", swap)
 

time: 143 us -> 142 us (level)
  transfers between devices with their start and end apart: 19 -> 19, of which waited for: 12 -> 11; matrix products, arithmetic and copies ran while one was open for 1% -> 1% of each run, Pallas kernels for 5% -> 5%
where the time goes in v16:
time: 142 us; the launch traced here: 140 us
  starting transfers between devices  78 us (55%)
  waiting for transfers between devices  37.6 us (26%)
  Pallas kernels  11.2 us (8%)
  blocking collectives  10.2 us (7%)
  local copies, waits for them, and re-layouts  1.52 us (1%)
    all_to_all x3, starting transfers between devices, exchange(): return lax.all_to_all(block, axis, split_axis=0, concat_axis=0, tiled=True)  29.9 us
    ppermute x6, starting transfers between devices, rotate(): lax.ppermute(term, axis, [(i, (i + step) % count) for i in range(count)])  16.4 us
    ppermute x6, waiting for transfers between devices, rotate(): lax.ppermute(term, axis, [(i, (i + step) % count) for i in range(count)])  13.7 us
    ppermute x1, waiting for transfers between devices, shards(): moved = lax.ppermute(pair, ('zhi', 'core'), doubling(1))  12.8 us
    ppermute x1, starting transfers between devices, shards(): moved = lax.ppermute(quarter, ('zhi', 'core'), doubling(0))  12.2 us
    all_gather x1, blocking collectives, shards(): grad = lax.all_gather(grad, 'chan', axis=1, tiled=True)  10.2 us
    ppermute x2, starting transfers between devices, shards(): lax.ppermute(output_grad, AXES, neighbour(sizes, far, True))  6.08 us
    pallas_call x2, Pallas kernels, convolve(): pl.pallas_call(functools.partial(conv_kernel, backward), out_shape=[jax.S...  4.9 us
  transfers between devices with their start and end apart: 19, of which 11 were waited for; matrix products, arithmetic and copies ran while one was open for 1% of the time, Pallas kernels for 5%

profile of v16, /device:TPU:1, one launch (start us, length us, event | category | flops | bytes accessed | tf_op | source)
XLA Modules:
  0.0 140.3 jit_solution(2916879534644323927)
XLA Ops:
  0.6 1.5 %collective-permute-start = (bf16[1,8,32,128]{3,2,1,0:T(8,128)(2,1)}, bf16[1,8,32,128]{3,2,1,0:T(8,128)(2,1)S(1)}, u32[]{:S(2)}, u32[]{:S(2)}) collective-permute-start(bf16[1,8,32,128]{3,2,1,0:T(8,128)(2,1)} %param.5), channel_id=1, source_target_pairs={{0,0},{1,128},{2,256},{3,384},{4,4},{5,132},{6,260},{7,388},{8,8},... | collective-permute-start | bytes 196616 | tf_op jit(solution)/shard_map/ppermute | solution.py:302
  2.1 4.6 %collective-permute-start.1 = (bf16[1,8,32,128]{3,2,1,0:T(8,128)(2,1)}, bf16[1,8,32,128]{3,2,1,0:T(8,128)(2,1)S(1)}, u32[]{:S(2)}, u32[]{:S(2)}) collective-permute-start(bf16[1,8,32,128]{3,2,1,0:T(8,128)(2,1)} %param.5), channel_id=1, source_target_pairs={{4,8},{5,136},{6,264},{7,392},{8,4},{9,132},{10,260},{11,388},{12,... | collective-permute-start | bytes 196616 | tf_op jit(solution)/shard_map/ppermute | solution.py:302
  6.7 1.9 %collective-permute-start.2 = (bf16[1,8,32,128]{3,2,1,0:T(8,128)(2,1)}, bf16[1,8,32,128]{3,2,1,0:T(8,128)(2,1)S(1)}, u32[]{:S(2)}, u32[]{:S(2)}) collective-permute-start(bf16[1,8,32,128]{3,2,1,0:T(8,128)(2,1)} %block.1), channel_id=1, source_target_pairs={{4,8},{5,9},{6,10},{7,11},{8,4},{9,5},{10,6},{11,7},{12,16},{13,17... | collective-permute-start | bytes 196616 | tf_op jit(solution)/shard_map/ppermute | solution.py:301
  8.6 0.0 copy-start
  8.7 0.8 copy-done
  9.5 0.0 collective-permute-done
  9.5 0.0 collective-permute-done.1
  9.5 3.0 %collective-permute-done.2.outer = bf16[1,8,32,128]{3,2,1,0:T(8,128)(2,1)S(1)} collective-permute-done((bf16[1,8,32,128]{3,2,1,0:T(8,128)(2,1)}, bf16[1,8,32,128]{3,2,1,0:T(8,128)(2,1)S(1)}, u32[]{:S(2)}, u32[]{:S(2)}) %collective-permute-start.2) | collective-permute-done | bytes 65568 | tf_op jit(solution)/shard_map/ppermute | solution.py:301
  12.5 0.9 pack.1
  13.4 11.4 %all-to-all-start = ((bf16[4,2,8,32,128]{4,3,2,1,0:T(8,128)(2,1)}), bf16[4,2,8,32,128]{4,3,2,1,0:T(8,128)(2,1)S(1)}, u32[]{:S(2)}, u32[]{:S(2)}) async-start(bf16[4,2,8,32,128]{4,3,2,1,0:T(8,128)(2,1)} %pack.1), calls=%async_computation | async-start | bytes 1048576 | tf_op jit(solution)/shard_map/all_to_all | solution.py:275
  24.8 10.2 %all_gather.3.pair = bf16[2,32,32,128]{3,2,1,0:T(8,128)(2,1)S(1)} all-gather(bf16[2,8,32,128]{3,2,1,0:T(8,128)(2,1)S(1)} %pad_maximum_fusion), channel_id=1, replica_groups=mesh['chan'=4,'zhi'=4,'ring'=4,'core'=2,'space'=4] {'chan'}, dimensions={1}, use_global_device_ids=true | all-gather | bytes 655360 | tf_op jit(solution)/shard_map/all_gather | solution.py:306
  35.0 1.9 %collective-permute-start.3 = (bf16[32,32,128]{2,1,0:T(8,128)(2,1)S(1)}, bf16[32,32,128]{2,1,0:T(8,128)(2,1)S(1)}, u32[]{:S(2)}, u32[]{:S(2)}) collective-permute-start(bf16[32,32,128]{2,1,0:T(8,128)(2,1)S(1)} %slice_bitcast_fusion), channel_id=1, source_target_pairs={{0,4},{4,0},{1,5},{5,1},{2,6},{6,2},{3,7},{7,3},{8,12},{12,8},{9,1... | collective-permute-start | bytes 786440 | tf_op jit(solution)/shard_map/ppermute | solution.py:307
  37.0 1.5 %collective-permute-done.3.inner = bf16[32,32,128]{2,1,0:T(8,128)(2,1)S(1)} collective-permute-done((bf16[32,32,128]{2,1,0:T(8,128)(2,1)S(1)}, bf16[32,32,128]{2,1,0:T(8,128)(2,1)S(1)}, u32[]{:S(2)}, u32[]{:S(2)}) %collective-permute-start.3) | collective-permute-done | bytes 262176 | tf_op jit(solution)/shard_map/ppermute | solution.py:307
  38.5 0.0 all-to-all-done.data.pair
  38.5 1.6 %filter_grad.1 = (f32[1792,128]{1,0:T(8,128)S(1)}, f32[1792,128]{1,0:T(8,128)S(1)}, bf16[32,32,128]{2,1,0:T(8,128)(2,1)S(1)}) custom-call(s32[1]{0:T(128)} %bitcast.core, bf16[4,2,8,32,128]{4,3,2,1,0:T(8,128)(2,1)S(1)} %all-to-all-done.data.pair, bf16[2,32,32,128]{3,2,1,0:T(8,128)(2,1)S(1)} %all_gather.3.pair, ...), custom_call_target="tpu_custom_call" | custom-call | flops 905969664 | bytes 3145728 | tf_op jit(solution)/shard_map/filter_grad/pallas_call | solution.py:160
  40.1 2.0 %collective-permute-start.4 = (f32[1792,128]{1,0:T(8,128)S(1)}, f32[1792,128]{1,0:T(8,128)S(1)}, u32[]{:S(2)}, u32[]{:S(2)}) collective-permute-start(f32[1792,128]{1,0:T(8,128)S(1)} %get-tuple-element.55), channel_id=1, source_target_pairs={{0,4},{4,0},{1,5},{5,1},{2,6},{6,2},{3,7},{7,3},{8,12},{12,8},{9,1... | collective-permute-start | bytes 2752520 | tf_op jit(solution)/shard_map/ppermute | solution.py:310
  42.1 2.3 %collective-permute-start.5 = (bf16[32,32,128]{2,1,0:T(8,128)(2,1)S(1)}, bf16[32,32,128]{2,1,0:T(8,128)(2,1)S(1)}, u32[]{:S(2)}, u32[]{:S(2)}) collective-permute-start(bf16[32,32,128]{2,1,0:T(8,128)(2,1)S(1)} %get-tuple-element.57), channel_id=1, source_target_pairs={{0,4},{4,0},{1,5},{5,1},{2,6},{6,2},{3,7},{7,3},{8,12},{12,8},{9,1... | collective-permute-start | bytes 786440 | tf_op jit(solution)/shard_map/ppermute | solution.py:311
  44.4 0.0 collective-permute-done.4.right
  44.4 0.0 copy-start.1
  44.4 1.0 shard_map.58
  45.4 0.1 collective-permute-done.5.inner
  45.5 14.7 %all-to-all-start.1 = ((f32[4,448,128]{2,1,0:T(8,128)}), f32[4,448,128]{2,1,0:T(8,128)S(1)}, u32[]{:S(2)}, u32[]{:S(2)}) async-start(f32[4,448,128]{2,1,0:T(8,128)} %bitcast.2), calls=%async_computation.1 | async-start | bytes 1835008 | tf_op jit(solution)/shard_map/all_to_all | solution.py:275
  60.2 0.1 pad_add_fusion.place
  60.3 0.0 copy-done.1
  60.3 2.8 %input_grad.1 = (f32[256,128]{1,0:T(8,128)S(1)}, f32[256,128]{1,0:T(8,128)}, f32[256,128]{1,0:T(8,128)S(1)}, f32[256,128]{1,0:T(8,128)}) custom-call(s32[2]{0:T(128)S(1)} %pad_add_fusion.place, bf16[2,32,32,128]{3,2,1,0:T(8,128)(2,1)S(1)} %all_gather.3.pair, bf16[32,32,128]{2,1,0:T(8,128)(2,1)S(1)} %collective-permute-done.3.inner, ...), custom_call_target="tpu_custom_call" | custom-call | flops 905969664 | bytes 3145728 | tf_op jit(solution)/shard_map/input_grad/pallas_call | solution.py:106
  63.1 0.0 copy-start.2
  63.1 0.6 copy-done.2
  63.7 3.4 %collective-permute-start.6 = (f32[256,128]{1,0:T(8,128)}, f32[256,128]{1,0:T(8,128)S(1)}, u32[]{:S(2)}, u32[]{:S(2)}) collective-permute-start(f32[256,128]{1,0:T(8,128)} %get-tuple-element.61), channel_id=1, source_target_pairs={{0,1},{1,2},{2,3},{3,0},{4,5},{5,6},{6,7},{7,4},{8,9},{9,10},{10,1... | collective-permute-start | bytes 393224 | tf_op jit(solution)/shard_map/ppermute | solution.py:280
  67.1 3.7 %collective-permute-start.7 = (f32[256,128]{1,0:T(8,128)}, f32[256,128]{1,0:T(8,128)S(1)}, u32[]{:S(2)}, u32[]{:S(2)}) collective-permute-start(f32[256,128]{1,0:T(8,128)} %get-tuple-element.63), channel_id=1, source_target_pairs={{0,3},{1,0},{2,1},{3,2},{4,7},{5,4},{6,5},{7,6},{8,11},{9,8},{10,9... | collective-permute-start | bytes 393224 | tf_op jit(solution)/shard_map/ppermute | solution.py:280
  70.8 2.5 %all-to-all-done.1.parts = f32[4,448,128]{2,1,0:T(8,128)S(1)} async-done(((f32[4,448,128]{2,1,0:T(8,128)}), f32[4,448,128]{2,1,0:T(8,128)S(1)}, u32[]{:S(2)}, u32[]{:S(2)}) %all-to-all-start.1) | async-done | bytes 917536 | tf_op jit(solution)/shard_map/all_to_all | solution.py:275
  73.4 0.0 collective-permute-done.6
  73.4 2.4 %collective-permute-done.7 = f32[256,128]{1,0:T(8,128)S(1)} collective-permute-done((f32[256,128]{1,0:T(8,128)}, f32[256,128]{1,0:T(8,128)S(1)}, u32[]{:S(2)}, u32[]{:S(2)}) %collective-permute-start.7) | collective-permute-done | bytes 131104 | tf_op jit(solution)/shard_map/ppermute | solution.py:280
  75.8 12.2 %collective-permute-start.8 = (f32[448,128]{1,0:T(8,128)S(1)}, f32[448,128]{1,0:T(8,128)S(1)}, u32[]{:S(2)}, u32[]{:S(2)}) collective-permute-start(f32[448,128]{1,0:T(8,128)S(1)} %shard_map.59), channel_id=1, source_target_pairs={{0,32},{4,100},{32,0},{36,68},{64,96},{68,36},{96,64},{100,4},{1,3... | collective-permute-start | bytes 688136 | tf_op jit(solution)/shard_map/ppermute | solution.py:323
  88.0 0.1 pad_add_fusion.1.place
  88.1 2.1 %forward.1 = (f32[256,128]{1,0:T(8,128)S(1)}, f32[256,128]{1,0:T(8,128)S(1)}, f32[256,128]{1,0:T(8,128)S(1)}, f32[256,128]{1,0:T(8,128)S(1)}) custom-call(s32[2]{0:T(128)S(1)} %pad_add_fusion.1.place, bf16[4,2,8,32,128]{4,3,2,1,0:T(8,128)(2,1)S(1)} %all-to-all-done.data.pair, bf16[32,32,128]{2,1,0:T(8,128)(2,1)S(1)} %collective-permute-done.5.inner, ...), custom_call_target="tpu_custom_call" | custom-call | flops 905969664 | bytes 3145728 | tf_op jit(solution)/shard_map/forward/pallas_call | solution.py:106
  90.2 3.1 %collective-permute-start.10 = (f32[256,128]{1,0:T(8,128)S(1)}, f32[256,128]{1,0:T(8,128)S(1)}, u32[]{:S(2)}, u32[]{:S(2)}) collective-permute-start(f32[256,128]{1,0:T(8,128)S(1)} %get-tuple-element.73), channel_id=1, source_target_pairs={{0,256},{128,384},{256,0},{384,128},{1,257},{129,385},{257,1},{385... | collective-permute-start | bytes 393224 | tf_op jit(solution)/shard_map/ppermute | solution.py:280
  93.3 1.9 %collective-permute-start.9 = (f32[256,128]{1,0:T(8,128)S(1)}, f32[256,128]{1,0:T(8,128)S(1)}, u32[]{:S(2)}, u32[]{:S(2)}) collective-permute-start(f32[256,128]{1,0:T(8,128)S(1)} %get-tuple-element.72), channel_id=1, source_target_pairs={{0,128},{128,256},{256,384},{384,0},{1,129},{129,257},{257,385},{3... | collective-permute-start | bytes 393224 | tf_op jit(solution)/shard_map/ppermute | solution.py:280
  95.2 0.0 collective-permute-done.8
  95.2 2.7 %collective-permute-done.10 = f32[256,128]{1,0:T(8,128)S(1)} collective-permute-done((f32[256,128]{1,0:T(8,128)S(1)}, f32[256,128]{1,0:T(8,128)S(1)}, u32[]{:S(2)}, u32[]{:S(2)}) %collective-permute-start.10) | collective-permute-done | bytes 131104 | tf_op jit(solution)/shard_map/ppermute | solution.py:280
  98.0 2.2 %collective-permute-done.9 = f32[256,128]{1,0:T(8,128)S(1)} collective-permute-done((f32[256,128]{1,0:T(8,128)S(1)}, f32[256,128]{1,0:T(8,128)S(1)}, u32[]{:S(2)}, u32[]{:S(2)}) %collective-permute-start.9) | collective-permute-done | bytes 131104 | tf_op jit(solution)/shard_map/ppermute | solution.py:280
  100.2 0.0 copy-start.3
  100.2 2.7 %collective-permute-start.11 = (f32[448,128]{1,0:T(8,128)S(1)}, f32[448,128]{1,0:T(8,128)S(1)}, u32[]{:S(2)}, u32[]{:S(2)}) collective-permute-start(f32[448,128]{1,0:T(8,128)S(1)} %add.21.left), channel_id=1, source_target_pairs={{0,96},{4,36},{32,64},{36,4},{64,32},{68,100},{96,0},{100,68},{1,9... | collective-permute-start | bytes 688136 | tf_op jit(solution)/shard_map/ppermute | solution.py:331
  102.9 2.4 %collective-permute-start.12 = (f32[256,128]{1,0:T(8,128)S(1)}, f32[256,128]{1,0:T(8,128)S(1)}, u32[]{:S(2)}, u32[]{:S(2)}) collective-permute-start(f32[256,128]{1,0:T(8,128)S(1)} %get-tuple-element.79), channel_id=1, source_target_pairs={{0,384},{128,0},{256,128},{384,256},{1,385},{129,1},{257,129},{385... | collective-permute-start | bytes 393224 | tf_op jit(solution)/shard_map/ppermute | solution.py:280
  105.3 12.8 %collective-permute-done.11.right = f32[448,128]{1,0:T(8,128)S(1)} collective-permute-done((f32[448,128]{1,0:T(8,128)S(1)}, f32[448,128]{1,0:T(8,128)S(1)}, u32[]{:S(2)}, u32[]{:S(2)}) %collective-permute-start.11) | collective-permute-done | bytes 229408 | tf_op jit(solution)/shard_map/ppermute | solution.py:331
  118.1 1.0 shard_map.60
  119.1 0.0 collective-permute-done.12
  119.1 3.8 %all-to-all-start.2 = ((f32[4,448,128]{2,1,0:T(8,128)}), f32[4,448,128]{2,1,0:T(8,128)S(1)}, u32[]{:S(2)}, u32[]{:S(2)}) async-start(f32[4,448,128]{2,1,0:T(8,128)} %shard_map.60), calls=%async_computation.2 | async-start | bytes 1835008 | tf_op jit(solution)/shard_map/all_to_all | solution.py:275
  122.9 0.0 copy-done.3
  123.0 1.9 %collective-permute-start.14 = (f32[256,128]{1,0:T(8,128)S(1)}, f32[256,128]{1,0:T(8,128)S(1)}, u32[]{:S(2)}, u32[]{:S(2)}) collective-permute-start(f32[256,128]{1,0:T(8,128)S(1)} %copy-done.3), channel_id=1, source_target_pairs={{0,2},{1,3},{2,0},{3,1},{4,6},{5,7},{6,4},{7,5},{8,10},{9,11},{10,... | collective-permute-start | bytes 393224 | tf_op jit(solution)/shard_map/ppermute | solution.py:280
  124.9 0.7 collective-permute-start.13
  125.6 0.0 collective-permute-done.13.block
  125.6 0.6 publish.3
  126.2 6.3 %collective-permute-done.14 = f32[256,128]{1,0:T(8,128)S(1)} collective-permute-done((f32[256,128]{1,0:T(8,128)S(1)}, f32[256,128]{1,0:T(8,128)S(1)}, u32[]{:S(2)}, u32[]{:S(2)}) %collective-permute-start.14) | collective-permute-done | bytes 131104 | tf_op jit(solution)/shard_map/ppermute | solution.py:280
  132.5 2.2 %all-to-all-done.2 = f32[4,448,128]{2,1,0:T(8,128)S(1)} async-done(((f32[4,448,128]{2,1,0:T(8,128)}), f32[4,448,128]{2,1,0:T(8,128)S(1)}, u32[]{:S(2)}, u32[]{:S(2)}) %all-to-all-start.2) | async-done | bytes 917536 | tf_op jit(solution)/shard_map/all_to_all | solution.py:275
  134.8 1.9 %collective-permute-start.15 = (f32[1792,128]{1,0:T(8,128)S(1)}, f32[1792,128]{1,0:T(8,128)S(1)}, u32[]{:S(2)}, u32[]{:S(2)}) collective-permute-start(f32[1792,128]{1,0:T(8,128)S(1)} %bitcast.11), channel_id=1, source_target_pairs={{0,4},{4,0},{1,5},{5,1},{2,6},{6,2},{3,7},{7,3},{8,12},{12,8},{9,1... | collective-permute-start | bytes 2752520 | tf_op jit(solution)/shard_map/ppermute | solution.py:344
  136.7 0.7 add_convert_fusion
  137.3 1.8 %collective-permute-done.15 = f32[1792,128]{1,0:T(8,128)S(1)} collective-permute-done((f32[1792,128]{1,0:T(8,128)S(1)}, f32[1792,128]{1,0:T(8,128)S(1)}, u32[]{:S(2)}, u32[]{:S(2)}) %collective-permute-start.15) | collective-permute-done | bytes 917536 | tf_op jit(solution)/shard_map/ppermute | solution.py:344
  139.1 1.2 join.1
  (6 shorter events, 0.1 us)
Async XLA Ops:
  0.6 8.9 %collective-permute-start = (bf16[1,8,32,128]{3,2,1,0:T(8,128)(2,1)}, bf16[1,8,32,128]{3,2,1,0:T(8,128)(2,1)S(1)}, u32[]{:S(2)}, u32[]{:S(2)}) collective-permute-start(bf16[1,8,32,128]{3,2,1,0:T(8,128)(2,1)} %param.5), channel_id=1, source_target_pairs={{0,0},{1,128},{2,256},{3,384},{4,4},{5,132},{6,260},{7,388},{8,8},... | collective-permute-start | bytes 196616 | tf_op jit(solution)/shard_map/ppermute | solution.py:302
  2.1 7.4 %collective-permute-start.1 = (bf16[1,8,32,128]{3,2,1,0:T(8,128)(2,1)}, bf16[1,8,32,128]{3,2,1,0:T(8,128)(2,1)S(1)}, u32[]{:S(2)}, u32[]{:S(2)}) collective-permute-start(bf16[1,8,32,128]{3,2,1,0:T(8,128)(2,1)} %param.5), channel_id=1, source_target_pairs={{4,8},{5,136},{6,264},{7,392},{8,4},{9,132},{10,260},{11,388},{12,... | collective-permute-start | bytes 196616 | tf_op jit(solution)/shard_map/ppermute | solution.py:302
  6.7 5.8 %collective-permute-start.2 = (bf16[1,8,32,128]{3,2,1,0:T(8,128)(2,1)}, bf16[1,8,32,128]{3,2,1,0:T(8,128)(2,1)S(1)}, u32[]{:S(2)}, u32[]{:S(2)}) collective-permute-start(bf16[1,8,32,128]{3,2,1,0:T(8,128)(2,1)} %block.1), channel_id=1, source_target_pairs={{4,8},{5,9},{6,10},{7,11},{8,4},{9,5},{10,6},{11,7},{12,16},{13,17... | collective-permute-start | bytes 196616 | tf_op jit(solution)/shard_map/ppermute | solution.py:301
  8.6 0.9 copy-start
  13.4 25.1 %all-to-all-start = ((bf16[4,2,8,32,128]{4,3,2,1,0:T(8,128)(2,1)}), bf16[4,2,8,32,128]{4,3,2,1,0:T(8,128)(2,1)S(1)}, u32[]{:S(2)}, u32[]{:S(2)}) async-start(bf16[4,2,8,32,128]{4,3,2,1,0:T(8,128)(2,1)} %pack.1), calls=%async_computation | async-start | bytes 1048576 | tf_op jit(solution)/shard_map/all_to_all | solution.py:275
  35.0 3.4 %collective-permute-start.3 = (bf16[32,32,128]{2,1,0:T(8,128)(2,1)S(1)}, bf16[32,32,128]{2,1,0:T(8,128)(2,1)S(1)}, u32[]{:S(2)}, u32[]{:S(2)}) collective-permute-start(bf16[32,32,128]{2,1,0:T(8,128)(2,1)S(1)} %slice_bitcast_fusion), channel_id=1, source_target_pairs={{0,4},{4,0},{1,5},{5,1},{2,6},{6,2},{3,7},{7,3},{8,12},{12,8},{9,1... | collective-permute-start | bytes 786440 | tf_op jit(solution)/shard_map/ppermute | solution.py:307
  40.1 4.4 %collective-permute-start.4 = (f32[1792,128]{1,0:T(8,128)S(1)}, f32[1792,128]{1,0:T(8,128)S(1)}, u32[]{:S(2)}, u32[]{:S(2)}) collective-permute-start(f32[1792,128]{1,0:T(8,128)S(1)} %get-tuple-element.55), channel_id=1, source_target_pairs={{0,4},{4,0},{1,5},{5,1},{2,6},{6,2},{3,7},{7,3},{8,12},{12,8},{9,1... | collective-permute-start | bytes 2752520 | tf_op jit(solution)/shard_map/ppermute | solution.py:310
  42.1 3.4 %collective-permute-start.5 = (bf16[32,32,128]{2,1,0:T(8,128)(2,1)S(1)}, bf16[32,32,128]{2,1,0:T(8,128)(2,1)S(1)}, u32[]{:S(2)}, u32[]{:S(2)}) collective-permute-start(bf16[32,32,128]{2,1,0:T(8,128)(2,1)S(1)} %get-tuple-element.57), channel_id=1, source_target_pairs={{0,4},{4,0},{1,5},{5,1},{2,6},{6,2},{3,7},{7,3},{8,12},{12,8},{9,1... | collective-permute-start | bytes 786440 | tf_op jit(solution)/shard_map/ppermute | solution.py:311
  44.4 15.9 %copy-start.1 = (bf16[27,128,128]{2,1,0:T(8,128)(2,1)S(1)}, bf16[27,128,128]{2,1,0:T(8,128)(2,1)}, u32[]{:S(2)}) copy-start(bf16[27,128,128]{2,1,0:T(8,128)(2,1)} %weight.3) | copy-start | bytes 2654212
  45.5 27.8 %all-to-all-start.1 = ((f32[4,448,128]{2,1,0:T(8,128)}), f32[4,448,128]{2,1,0:T(8,128)S(1)}, u32[]{:S(2)}, u32[]{:S(2)}) async-start(f32[4,448,128]{2,1,0:T(8,128)} %bitcast.2), calls=%async_computation.1 | async-start | bytes 1835008 | tf_op jit(solution)/shard_map/all_to_all | solution.py:275
  63.1 0.7 copy-start.2
  63.7 9.6 %collective-permute-start.6 = (f32[256,128]{1,0:T(8,128)}, f32[256,128]{1,0:T(8,128)S(1)}, u32[]{:S(2)}, u32[]{:S(2)}) collective-permute-start(f32[256,128]{1,0:T(8,128)} %get-tuple-element.61), channel_id=1, source_target_pairs={{0,1},{1,2},{2,3},{3,0},{4,5},{5,6},{6,7},{7,4},{8,9},{9,10},{10,1... | collective-permute-start | bytes 393224 | tf_op jit(solution)/shard_map/ppermute | solution.py:280
  67.1 8.7 %collective-permute-start.7 = (f32[256,128]{1,0:T(8,128)}, f32[256,128]{1,0:T(8,128)S(1)}, u32[]{:S(2)}, u32[]{:S(2)}) collective-permute-start(f32[256,128]{1,0:T(8,128)} %get-tuple-element.63), channel_id=1, source_target_pairs={{0,3},{1,0},{2,1},{3,2},{4,7},{5,4},{6,5},{7,6},{8,11},{9,8},{10,9... | collective-permute-start | bytes 393224 | tf_op jit(solution)/shard_map/ppermute | solution.py:280
  75.8 19.4 %collective-permute-start.8 = (f32[448,128]{1,0:T(8,128)S(1)}, f32[448,128]{1,0:T(8,128)S(1)}, u32[]{:S(2)}, u32[]{:S(2)}) collective-permute-start(f32[448,128]{1,0:T(8,128)S(1)} %shard_map.59), channel_id=1, source_target_pairs={{0,32},{4,100},{32,0},{36,68},{64,96},{68,36},{96,64},{100,4},{1,3... | collective-permute-start | bytes 688136 | tf_op jit(solution)/shard_map/ppermute | solution.py:323
  90.2 7.8 %collective-permute-start.10 = (f32[256,128]{1,0:T(8,128)S(1)}, f32[256,128]{1,0:T(8,128)S(1)}, u32[]{:S(2)}, u32[]{:S(2)}) collective-permute-start(f32[256,128]{1,0:T(8,128)S(1)} %get-tuple-element.73), channel_id=1, source_target_pairs={{0,256},{128,384},{256,0},{384,128},{1,257},{129,385},{257,1},{385... | collective-permute-start | bytes 393224 | tf_op jit(solution)/shard_map/ppermute | solution.py:280
  93.3 6.9 %collective-permute-start.9 = (f32[256,128]{1,0:T(8,128)S(1)}, f32[256,128]{1,0:T(8,128)S(1)}, u32[]{:S(2)}, u32[]{:S(2)}) collective-permute-start(f32[256,128]{1,0:T(8,128)S(1)} %get-tuple-element.72), channel_id=1, source_target_pairs={{0,128},{128,256},{256,384},{384,0},{1,129},{129,257},{257,385},{3... | collective-permute-start | bytes 393224 | tf_op jit(solution)/shard_map/ppermute | solution.py:280
  100.2 22.8 %copy-start.3 = (f32[256,128]{1,0:T(8,128)S(1)}, f32[256,128]{1,0:T(8,128)}, u32[]{:S(2)}) copy-start(f32[256,128]{1,0:T(8,128)} %copy-done.2) | copy-start | bytes 393220
  100.2 17.9 %collective-permute-start.11 = (f32[448,128]{1,0:T(8,128)S(1)}, f32[448,128]{1,0:T(8,128)S(1)}, u32[]{:S(2)}, u32[]{:S(2)}) collective-permute-start(f32[448,128]{1,0:T(8,128)S(1)} %add.21.left), channel_id=1, source_target_pairs={{0,96},{4,36},{32,64},{36,4},{64,32},{68,100},{96,0},{100,68},{1,9... | collective-permute-start | bytes 688136 | tf_op jit(solution)/shard_map/ppermute | solution.py:331
  102.9 16.2 %collective-permute-start.12 = (f32[256,128]{1,0:T(8,128)S(1)}, f32[256,128]{1,0:T(8,128)S(1)}, u32[]{:S(2)}, u32[]{:S(2)}) collective-permute-start(f32[256,128]{1,0:T(8,128)S(1)} %get-tuple-element.79), channel_id=1, source_target_pairs={{0,384},{128,0},{256,128},{384,256},{1,385},{129,1},{257,129},{385... | collective-permute-start | bytes 393224 | tf_op jit(solution)/shard_map/ppermute | solution.py:280
  119.1 15.7 %all-to-all-start.2 = ((f32[4,448,128]{2,1,0:T(8,128)}), f32[4,448,128]{2,1,0:T(8,128)S(1)}, u32[]{:S(2)}, u32[]{:S(2)}) async-start(f32[4,448,128]{2,1,0:T(8,128)} %shard_map.60), calls=%async_computation.2 | async-start | bytes 1835008 | tf_op jit(solution)/shard_map/all_to_all | solution.py:275
  123.0 9.6 %collective-permute-start.14 = (f32[256,128]{1,0:T(8,128)S(1)}, f32[256,128]{1,0:T(8,128)S(1)}, u32[]{:S(2)}, u32[]{:S(2)}) collective-permute-start(f32[256,128]{1,0:T(8,128)S(1)} %copy-done.3), channel_id=1, source_target_pairs={{0,2},{1,3},{2,0},{3,1},{4,6},{5,7},{6,4},{7,5},{8,10},{9,11},{10,... | collective-permute-start | bytes 393224 | tf_op jit(solution)/shard_map/ppermute | solution.py:280
  124.9 0.7 collective-permute-start.13
  134.8 4.4 %collective-permute-start.15 = (f32[1792,128]{1,0:T(8,128)S(1)}, f32[1792,128]{1,0:T(8,128)S(1)}, u32[]{:S(2)}, u32[]{:S(2)}) collective-permute-start(f32[1792,128]{1,0:T(8,128)S(1)} %bitcast.11), channel_id=1, source_target_pairs={{0,4},{4,0},{1,5},{5,1},{2,6},{6,2},{3,7},{7,3},{8,12},{12,8},{9,1... | collective-permute-start | bytes 2752520 | tf_op jit(solution)/shard_map/ppermute | solution.py:344
